TPU v7x, 32 devices: a whole 2x2x4 slice. The times are simulated.
32 devices in a mesh: groups: 2 (over y), seq: 4 (over z), mp: 2 (over x), sub: 2 (over core).
Axes of the slice: x: 2, y: 2, z: 4, core: 2. Of those that a mesh axis runs over, the one named last changes fastest.
Arguments:
- video_in: bfloat16 [1024, 4096], P(('groups', 'seq'), ('mp', 'sub')), parts along dimension 0, may hold values from -6 to 6
- audio_in: bfloat16 [256, 2048], P(('groups', 'seq'), ('mp', 'sub')), parts along dimension 0, may hold values from -6 to 6
- q_self: bfloat16 [1024, 2048], P(('groups', 'seq'), ('mp', 'sub')), parts along dimension 0
- k_self: bfloat16 [1024, 2048], P(('groups', 'seq'), ('mp', 'sub')), parts along dimension 0
- v_self: bfloat16 [1024, 2048], P(('groups', 'seq'), ('mp', 'sub')), parts along dimension 0, may hold values from -6 to 6
- q_a2v: bfloat16 [1024, 1024], P(('groups', 'seq'), ('mp', 'sub')), parts along dimension 0
- k_a2v: bfloat16 [256, 1024], P(('groups', 'seq'), ('mp', 'sub')), parts along dimension 0
- v_a2v: bfloat16 [256, 1024], P(('groups', 'seq'), ('mp', 'sub')), parts along dimension 0, may hold values from -6 to 6
- q_v2a: bfloat16 [256, 1024], P(('groups', 'seq'), ('mp', 'sub')), parts along dimension 0
- k_v2a: bfloat16 [1024, 1024], P(('groups', 'seq'), ('mp', 'sub')), parts along dimension 0
- v_v2a: bfloat16 [1024, 1024], P(('groups', 'seq'), ('mp', 'sub')), parts along dimension 0, may hold values from -6 to 6
- wo_self: bfloat16 [2048, 4096], P(('mp', 'sub')), may hold values from -0.125 to 0.125
- wo_a2v: bfloat16 [1024, 4096], P(('mp', 'sub')), may hold values from -0.1875 to 0.1875
- wo_v2a: bfloat16 [1024, 2048], P(('mp', 'sub')), may hold values from -0.1875 to 0.1875
- video_gates: bfloat16 [16, 2, 4096], replicated, may hold values from -4 to 4
- audio_gates: bfloat16 [16, 2048], replicated, may hold values from -4 to 4
- video_steps: int32 [1024], P(('groups', 'seq')), parts along dimension 0, may hold values from 0 to 15
- audio_steps: int32 [256], P(('groups', 'seq')), parts along dimension 0, may hold values from 0 to 15
- audio_len: int32 [2], P('groups'), parts along dimension 0, may hold values from 64 to 128
Outputs:
- video_out: bfloat16 [1024, 4096], P(('groups', 'seq'), ('mp', 'sub')), parts along dimension 0
- audio_out: bfloat16 [256, 2048], P(('groups', 'seq'), ('mp', 'sub')), parts along dimension 0
There are 2 independent parts, one for each index of `groups`. A program takes and returns all parts, laid end to end along the dimension named above; an argument that names none is the same for every part. Nothing has to cross between parts.
Inputs may be any that keep to these rules, and one draw needn't show every extreme that they name: Audio tokens 0 to audio_len[0] - 1 are real, the rest are padding.
All inputs are finite; a program needn't handle non-finite values.
Results may differ from a plain program's by a relative error of at most 0.0075.
Values may be sent and summed in bfloat16 or wider, within the bound.
No kernel may reach another device: no remote copies, remote signals or barrier semaphores. Data moves between devices by JAX's collectives and lax.ppermute only.
A program may use at most 64 MiB of HBM per device.

v0:
```python
import math

import jax
import jax.numpy as jnp
from jax import lax
from jax.sharding import PartitionSpec as P

DHV = 128
DHC = 64
NT = 16


def start_state(rows, heads, width):
    return (
        jnp.full((rows, heads), -1e30, jnp.float32),
        jnp.zeros((rows, heads), jnp.float32),
        jnp.zeros((rows, heads, width), jnp.float32),
    )


def update_block(state, queries, keys, values, heads, width, allowed):
    rows = queries.shape[0]
    count = keys.shape[0]
    q_heads = queries.reshape(rows, heads, width)
    k_heads = keys.reshape(count, heads, width)
    v_heads = values.reshape(count, heads, width)
    scores = jnp.einsum(
        "qhd,khd->qhk", q_heads, k_heads, preferred_element_type=jnp.float32
    ) / math.sqrt(width)
    if allowed is not None:
        scores = jnp.where(allowed[None, None, :], scores, -jnp.inf)
    peak_old, total_old, summed_old = state
    peak = jnp.maximum(peak_old, jnp.max(scores, axis=2))
    weights = jnp.exp(scores - peak[:, :, None])
    factor = jnp.exp(peak_old - peak)
    total = total_old * factor + jnp.sum(weights, axis=2)
    summed = summed_old * factor[:, :, None] + jnp.einsum(
        "qhk,khd->qhd", weights.astype(jnp.bfloat16), v_heads, preferred_element_type=jnp.float32
    )
    return (peak, total, summed)


def update_state(state, queries, keys, values, heads, width, start, limit):
    count = keys.shape[0]
    block = 1024 if count > 1024 and count % 1024 == 0 else count
    if block == count:
        allowed = None
        if limit is not None:
            allowed = jnp.arange(count, dtype=jnp.int32) < limit
        return update_block(state, queries, keys, values, heads, width, allowed)
    steps = count // block
    key_blocks = keys.reshape(steps, block, keys.shape[1])
    value_blocks = values.reshape(steps, block, values.shape[1])
    offsets = jnp.arange(steps, dtype=jnp.int32) * block

    def one_block(carry, items):
        key_rows, value_rows, offset = items
        allowed = None
        if limit is not None:
            allowed = start + offset + jnp.arange(block, dtype=jnp.int32) < limit
        return (update_block(carry, queries, key_rows, value_rows, heads, width, allowed), None)

    result, _ = lax.scan(one_block, state, (key_blocks, value_blocks, offsets))
    return result


def finish(state, heads, width):
    peak, total, summed = state
    rows = summed.shape[0]
    return (summed / total[:, :, None]).reshape(rows, heads * width).astype(jnp.bfloat16)


def on_device(
    video_in,
    audio_in,
    q_self,
    k_self,
    v_self,
    q_a2v,
    k_a2v,
    v_a2v,
    q_v2a,
    k_v2a,
    v_v2a,
    wo_self,
    wo_a2v,
    wo_v2a,
    video_gates,
    audio_gates,
    video_steps,
    audio_steps,
    audio_len,
):
    heads_self = q_self.shape[1] // DHV
    heads_cross = q_a2v.shape[1] // DHC
    rows_video = q_self.shape[0]
    rows_audio = q_v2a.shape[0]
    limit = audio_len[0]
    piece = (
        lax.all_gather(k_a2v, "seq", axis=0, tiled=True),
        lax.all_gather(v_a2v, "seq", axis=0, tiled=True),
    )
    a2v_state = update_state(
        start_state(rows_video, heads_cross, DHC),
        q_a2v,
        piece[0],
        piece[1],
        heads_cross,
        DHC,
        jnp.int32(0),
        limit,
    )
    a2v_att = finish(a2v_state, heads_cross, DHC)
    piece = (
        lax.all_gather(k_self, "seq", axis=0, tiled=True),
        lax.all_gather(v_self, "seq", axis=0, tiled=True),
    )
    self_state = update_state(
        start_state(rows_video, heads_self, DHV),
        q_self,
        piece[0],
        piece[1],
        heads_self,
        DHV,
        jnp.int32(0),
        None,
    )
    piece = (
        lax.all_gather(k_v2a, "seq", axis=0, tiled=True),
        lax.all_gather(v_v2a, "seq", axis=0, tiled=True),
    )
    v2a_state = update_state(
        start_state(rows_audio, heads_cross, DHC),
        q_v2a,
        piece[0],
        piece[1],
        heads_cross,
        DHC,
        jnp.int32(0),
        None,
    )
    self_att = finish(self_state, heads_self, DHV)
    v2a_att = finish(v2a_state, heads_cross, DHC)
    levels = jnp.arange(NT, dtype=jnp.int32)
    video_hot = (video_steps[:, None] == levels[None, :]).astype(jnp.bfloat16)
    video_gain = jnp.dot(video_hot, video_gates.reshape(NT, -1), preferred_element_type=jnp.float32)
    width_video = video_gates.shape[2]
    video_term = video_gain[:, :width_video] * jnp.dot(
        self_att, wo_self, preferred_element_type=jnp.float32
    )
    video_term = video_term + video_gain[:, width_video:] * jnp.dot(
        a2v_att, wo_a2v, preferred_element_type=jnp.float32
    )
    audio_hot = (audio_steps[:, None] == levels[None, :]).astype(jnp.bfloat16)
    audio_gain = jnp.dot(audio_hot, audio_gates, preferred_element_type=jnp.float32)
    positions = lax.axis_index("seq") * rows_audio + jnp.arange(rows_audio, dtype=jnp.int32)
    present = (positions < limit).astype(jnp.float32)
    audio_term = (
        present[:, None] * audio_gain * jnp.dot(v2a_att, wo_v2a, preferred_element_type=jnp.float32)
    )
    video_sum, audio_sum = (
        lax.psum_scatter(
            video_term.astype(jnp.bfloat16), ("mp", "sub"), scatter_dimension=1, tiled=True
        ).astype(jnp.float32),
        lax.psum_scatter(
            audio_term.astype(jnp.bfloat16), ("mp", "sub"), scatter_dimension=1, tiled=True
        ).astype(jnp.float32),
    )
    video_out = (video_in.astype(jnp.float32) + video_sum).astype(jnp.bfloat16)
    audio_out = (audio_in.astype(jnp.float32) + audio_sum).astype(jnp.bfloat16)
    return (video_out, audio_out)


def solution(mesh):
    in_specs = (
        P(("groups", "seq"), ("mp", "sub")),
        P(("groups", "seq"), ("mp", "sub")),
        P(("groups", "seq"), ("mp", "sub")),
        P(("groups", "seq"), ("mp", "sub")),
        P(("groups", "seq"), ("mp", "sub")),
        P(("groups", "seq"), ("mp", "sub")),
        P(("groups", "seq"), ("mp", "sub")),
        P(("groups", "seq"), ("mp", "sub")),
        P(("groups", "seq"), ("mp", "sub")),
        P(("groups", "seq"), ("mp", "sub")),
        P(("groups", "seq"), ("mp", "sub")),
        P(("mp", "sub"), None),
        P(("mp", "sub"), None),
        P(("mp", "sub"), None),
        P(),
        P(),
        P(("groups", "seq")),
        P(("groups", "seq")),
        P("groups"),
    )
    out_specs = (P(("groups", "seq"), ("mp", "sub")), P(("groups", "seq"), ("mp", "sub")))
    return jax.shard_map(
        on_device, mesh=mesh, in_specs=in_specs, out_specs=out_specs, check_vma=False
    )
```

profile of v0, /device:TPU:0, one launch (start us, length us, event | category | flops | bytes accessed | tf_op | source)
XLA Modules:
  0.0 149.5 jit_solution(6648957412750940869)
XLA Ops:
  8.0 16.0 %all_gather.22 = bf16[512,256]{1,0:T(8,128)(2,1)S(1)} all-gather(bf16[128,256]{1,0:T(8,128)(2,1)} %param.28), channel_id=1, replica_groups=mesh['groups'=2,'seq'=4,'mp'=2,'sub'=2] {'seq'}, dimensions={0}, use_global_device_ids=true | all-gather | bytes 327680 | tf_op jit(solution)/shard_map/all_gather | solution.py:129
  24.0 0.8 copy.40
  24.9 0.8 reshape.99
  25.7 1.2 fusion.39
  28.2 14.7 %all_gather.23 = bf16[512,256]{1,0:T(8,128)(2,1)S(1)} all-gather(bf16[128,256]{1,0:T(8,128)(2,1)} %param.29), channel_id=1, replica_groups=mesh['groups'=2,'seq'=4,'mp'=2,'sub'=2] {'seq'}, dimensions={0}, use_global_device_ids=true | all-gather | bytes 327680 | tf_op jit(solution)/shard_map/all_gather | solution.py:130
  43.0 0.8 copy.42
  43.8 1.3 fusion.15
  45.3 0.9 convolution_multiply_fusion.3
  46.2 0.9 fusion.2
  47.3 13.2 %all_gather.20 = bf16[128,256]{1,0:T(8,128)(2,1)S(1)} all-gather(bf16[32,256]{1,0:T(8,128)(2,1)S(1)} %copy-done.12), channel_id=1, replica_groups=mesh['groups'=2,'seq'=4,'mp'=2,'sub'=2] {'seq'}, dimensions={0}, use_global_device_ids=true | all-gather | bytes 81920 | tf_op jit(solution)/shard_map/all_gather | solution.py:100
  61.1 13.4 %all_gather.21 = bf16[128,256]{1,0:T(8,128)(2,1)S(1)} all-gather(bf16[32,256]{1,0:T(8,128)(2,1)S(1)} %copy-done.13), channel_id=1, replica_groups=mesh['groups'=2,'seq'=4,'mp'=2,'sub'=2] {'seq'}, dimensions={0}, use_global_device_ids=true | all-gather | bytes 81920 | tf_op jit(solution)/shard_map/all_gather | solution.py:101
  74.5 0.7 copy.38
  75.3 15.3 %all_gather.18 = bf16[512,512]{0,1:T(8,128)(2,1)S(1)} all-gather(bf16[128,512]{0,1:T(8,128)(2,1)S(1)} %copy.31), channel_id=1, replica_groups=mesh['groups'=2,'seq'=4,'mp'=2,'sub'=2] {'seq'}, dimensions={0}, use_global_device_ids=true | all-gather | bytes 655360 | tf_op jit(solution)/shard_map/all_gather | solution.py:115
  90.6 1.3 fusion.37
  92.1 0.6 exponential_multiply_fusion.2
  92.7 15.4 %all_gather.19 = bf16[512,512]{1,0:T(8,128)(2,1)} all-gather(bf16[128,512]{1,0:T(8,128)(2,1)S(1)} %copy-done.6), channel_id=1, replica_groups=mesh['groups'=2,'seq'=4,'mp'=2,'sub'=2] {'seq'}, dimensions={0}, use_global_device_ids=true | all-gather | bytes 655360 | tf_op jit(solution)/shard_map/all_gather | solution.py:116
  108.1 2.0 %copy.34 = bf16[512,512]{0,1:T(8,128)(2,1)} copy(bf16[512,512]{1,0:T(8,128)(2,1)} %all_gather.19) | data formatting | bytes 1048576 | tf_op jit(solution)/shard_map/all_gather | solution.py:116
  110.1 1.1 copy.48
  111.3 1.6 %fusion.30 = f32[128,8192]{1,0:T(8,128)S(1)} fusion(bf16[16,8192]{1,0:T(8,128)(2,1)S(1)} %bitcast.69, s32[128]{0:T(128)} %param.35), kind=kOutput, calls=%fused_computation.43 | convolution fusion | flops 33556480 | bytes 4456960 | tf_op jit(solution)/shard_map/dot_general | solution.py:146
  113.6 0.8 convolution_multiply_fusion.1
  114.4 1.6 %fusion.1 = bf16[128,4096]{1,0:T(8,128)(2,1)} fusion(f32[128,4096]{1,0:T(8,128)S(1)} %convolution_multiply_fusion.1, bf16[128,256]{0,1:T(8,128)(2,1)S(1)} %bitcast.77, bf16[256,4096]{1,0:T(8,128)(2,1)S(1)} %copy-done, f32[128,8192]{1,0:T(8,128)S(1)} %fusion.30), kind=kOutput, calls=%fused_computation.3 | convolution fusion | flops 270008320 | bytes 7405568 | tf_op jit(solution)/shard_map/dot_general | solution.py:151
  116.1 1.4 add_convert_fusion.1
  117.5 23.5 %reduce-scatter.3.cloned.1.call-done = bf16[128,1024]{1,0:T(8,128)(2,1)} async-done(((bf16[128,4096]{1,0:T(8,128)(2,1)}), bf16[128,1024]{1,0:T(8,128)(2,1)}) %reduce-scatter.3.cloned.1.call-update) | async-done | bytes 262160 | tf_op jit(solution)/shard_map/reduce_scatter | solution.py:162
  141.0 1.7 %add_convert_fusion = bf16[128,1024]{1,0:T(8,128)(2,1)} fusion(bf16[128,1024]{1,0:T(8,128)(2,1)} %reduce-scatter.3.cloned.1.call-done, bf16[128,1024]{1,0:T(8,128)(2,1)S(1)} %copy-done.5), kind=kLoop, calls=%fused_computation.29 | loop fusion | flops 524288 | bytes 786432 | tf_op jit(solution)/shard_map/convert_element_type | solution.py:169
  (57 shorter events, 3.2 us)
Async XLA Ops:
  7.2 107.2 %copy-start = (bf16[256,4096]{1,0:T(8,128)(2,1)S(1)}, bf16[256,4096]{1,0:T(8,128)(2,1)}, u32[]{:S(2)}) copy-start(bf16[256,4096]{1,0:T(8,128)(2,1)} %param.31) | copy-start | bytes 6291460
  7.2 38.1 %copy-start.8 = (bf16[16,2048]{1,0:T(8,128)(2,1)S(1)}, bf16[16,2048]{1,0:T(8,128)(2,1)}, u32[]{:S(2)}) copy-start(bf16[16,2048]{1,0:T(8,128)(2,1)} %param.34) | copy-start | bytes 196612
  7.2 39.0 %copy-start.2 = (bf16[256,2048]{1,0:T(8,128)(2,1)S(1)}, bf16[256,2048]{1,0:T(8,128)(2,1)}, u32[]{:S(2)}) copy-start(bf16[256,2048]{1,0:T(8,128)(2,1)} %param.32) | copy-start | bytes 3145732
  7.2 108.9 %reduce-scatter.5.cloned.1.call-start = ((), (), s32[]{:S(2)}) async-start(), calls=%async_computation.3 | async-start | bytes 163840 | tf_op jit(solution)/shard_map/reduce_scatter | solution.py:165
  25.7 21.5 %copy-start.12 = (bf16[32,256]{1,0:T(8,128)(2,1)S(1)}, bf16[32,256]{1,0:T(8,128)(2,1)}, u32[]{:S(2)}) copy-start(bf16[32,256]{1,0:T(8,128)(2,1)} %param.25) | copy-start | bytes 49156
  26.9 0.7 copy-start.3
  26.9 33.6 %copy-start.9 = (bf16[128,256]{1,0:T(8,128)(2,1)S(1)}, bf16[128,256]{1,0:T(8,128)(2,1)}, u32[]{:S(2)}) copy-start(bf16[128,256]{1,0:T(8,128)(2,1)} %param.24) | copy-start | bytes 196612
  26.9 0.7 copy-start.14
  43.8 17.2 %copy-start.13 = (bf16[32,256]{1,0:T(8,128)(2,1)S(1)}, bf16[32,256]{1,0:T(8,128)(2,1)}, u32[]{:S(2)}) copy-start(bf16[32,256]{1,0:T(8,128)(2,1)} %param.26) | copy-start | bytes 49156
  43.8 31.4 %copy-start.7 = (bf16[128,512]{1,0:T(8,128)(2,1)S(1)}, bf16[128,512]{1,0:T(8,128)(2,1)}, u32[]{:S(2)}) copy-start(bf16[128,512]{1,0:T(8,128)(2,1)} %param.22) | copy-start | bytes 393220
  47.2 93.8 %reduce-scatter.3.cloned.1.call-start = ((), (), s32[]{:S(2)}) async-start(), calls=%async_computation.2 | async-start | bytes 1310720 | tf_op jit(solution)/shard_map/reduce_scatter | solution.py:162
  60.9 31.7 %copy-start.6 = (bf16[128,512]{1,0:T(8,128)(2,1)S(1)}, bf16[128,512]{1,0:T(8,128)(2,1)}, u32[]{:S(2)}) copy-start(bf16[128,512]{1,0:T(8,128)(2,1)} %param.23) | copy-start | bytes 393220
  110.1 2.7 %copy-start.10 = (bf16[128,256]{0,1:T(8,128)(2,1)S(1)}, bf16[128,256]{0,1:T(8,128)(2,1)}, u32[]{:S(2)}) copy-start(bf16[128,256]{0,1:T(8,128)(2,1)} %copy.38) | copy-start | bytes 196612
  111.2 1.8 %copy-start.4 = (bf16[512,512]{0,1:T(8,128)(2,1)S(1)}, bf16[512,512]{0,1:T(8,128)(2,1)}, u32[]{:S(2)}) copy-start(bf16[512,512]{0,1:T(8,128)(2,1)} %copy.34) | copy-start | bytes 1572868
  111.2 1.8 %copy-start.15 = (f32[128,4]{0,1:T(4,128)S(1)}, f32[128,4]{0,1:T(4,128)}, u32[]{:S(2)}) copy-start(f32[128,4]{0,1:T(4,128)} %get-tuple-element.6) | copy-start | bytes 6148
  111.3 1.8 %copy-start.16 = (f32[128,4]{0,1:T(4,128)S(1)}, f32[128,4]{0,1:T(4,128)}, u32[]{:S(2)}) copy-start(f32[128,4]{0,1:T(4,128)} %get-tuple-element.7) | copy-start | bytes 6148
  111.3 2.4 %copy-start.1 = (bf16[512,4096]{1,0:T(8,128)(2,1)S(1)}, bf16[512,4096]{1,0:T(8,128)(2,1)}, u32[]{:S(2)}) copy-start(bf16[512,4096]{1,0:T(8,128)(2,1)} %param.30) | copy-start | bytes 12582916
  114.4 1.7 %copy-start.11 = (bf16[32,512]{1,0:T(8,128)(2,1)S(1)}, bf16[32,512]{1,0:T(8,128)(2,1)}, u32[]{:S(2)}) copy-start(bf16[32,512]{1,0:T(8,128)(2,1)} %param.20) | copy-start | bytes 98308
  114.4 26.5 %copy-start.5 = (bf16[128,1024]{1,0:T(8,128)(2,1)S(1)}, bf16[128,1024]{1,0:T(8,128)(2,1)}, u32[]{:S(2)}) copy-start(bf16[128,1024]{1,0:T(8,128)(2,1)} %param.19) | copy-start | bytes 786436
Sparse Core Ops, SparseCore 0:
  47.3 20.5 reduce-scatter.4
  116.2 24.7 reduce-scatter.2
where the time goes:
time: 150 us
  blocking collectives  88 us (59%)
  waiting for transfers between devices  23.5 us (16%)
  between operations  15.2 us (10%)
  matrix products  10.3 us (7%)
  local copies, waits for them, and re-layouts  7.66 us (5%)
  other arithmetic  4.72 us (3%)
    reduce_scatter x1, waiting for transfers between devices, on_device(): lax.psum_scatter(video_term.astype(jnp.bfloat16), ('mp', 'sub'), scatter_...  23.5 us
    all_gather x1, blocking collectives, on_device(): lax.all_gather(k_v2a, 'seq', axis=0, tiled=True)  16 us
    all_gather x1, blocking collectives, on_device(): lax.all_gather(v_self, 'seq', axis=0, tiled=True)  15.4 us
    all_gather x1, blocking collectives, on_device(): lax.all_gather(k_self, 'seq', axis=0, tiled=True)  15.3 us
    all_gather x1, blocking collectives, on_device(): lax.all_gather(v_v2a, 'seq', axis=0, tiled=True)  14.7 us
    all_gather x1, blocking collectives, on_device(): lax.all_gather(v_a2v, 'seq', axis=0, tiled=True)  13.4 us
    all_gather x1, blocking collectives, on_device(): lax.all_gather(k_a2v, 'seq', axis=0, tiled=True)  13.2 us
  transfers between devices with their start and end apart: 2, of which 1 were waited for; matrix products, arithmetic and copies ran while one was open for 8% of the time, Pallas kernels for 0%

commit v1 on v0

--- a/solution.py
+++ b/solution.py
@@ -1,8 +1,11 @@
+import functools
 import math
 
 import jax
 import jax.numpy as jnp
 from jax import lax
+from jax.experimental import pallas as pl
+from jax.experimental.pallas import tpu as pltpu
 from jax.sharding import PartitionSpec as P
 
 DHV = 128
@@ -70,7 +73,7 @@
     return (summed / total[:, :, None]).reshape(rows, heads * width).astype(jnp.bfloat16)
 
 
-def on_device(
+def on_device_gather(
     video_in,
     audio_in,
     q_self,
@@ -171,6 +174,337 @@
     return (video_out, audio_out)
 
 
+LOG2E = 1.4426950408889634
+VMEM = pl.BlockSpec(memory_space=pltpu.VMEM)
+SMEM = pl.BlockSpec(memory_space=pltpu.SMEM)
+
+
+def call(kernel, outs, operands, flops, scratch=(), limit=24 * 2**20):
+    size = sum(math.prod(x.shape) * x.dtype.itemsize for x in (*operands, *outs))
+    specs = [SMEM if x.ndim == 1 and x.dtype == jnp.int32 else VMEM for x in operands]
+    return pl.pallas_call(
+        kernel,
+        out_shape=tuple(outs),
+        in_specs=specs,
+        out_specs=tuple(VMEM for _ in outs),
+        scratch_shapes=list(scratch),
+        compiler_params=pltpu.CompilerParams(vmem_limit_bytes=limit),
+        cost_estimate=pl.CostEstimate(flops=flops, bytes_accessed=size, transcendentals=0),
+    )(*operands)
+
+
+def dot_t(a, b):
+    return lax.dot_general(a, b, (((1,), (1,)), ((), ())), preferred_element_type=jnp.float32)
+
+
+def dot(a, b):
+    return jnp.dot(a, b, preferred_element_type=jnp.float32)
+
+
+def pack_kernel(hops, width, me_ref, q_ref, k_ref, v_ref, ka_ref, va_ref, qa_ref, *outs):
+    rows = q_ref.shape[0]
+    rows_audio, cols_audio = ka_ref.shape
+    me = me_ref[0]
+    for hop, out in zip(hops, outs):
+        at = pl.ds(pl.multiple_of((me ^ hop) * width, width), width)
+        for i, ref in enumerate((q_ref, k_ref, v_ref)):
+            out[0:rows, i * width : (i + 1) * width] = ref[:, at]
+        top = rows
+        for part in range(cols_audio // width):
+            for i, ref in enumerate((ka_ref, va_ref, qa_ref)):
+                out[top : top + rows_audio, i * width : (i + 1) * width] = ref[
+                    :, part * width : (part + 1) * width
+                ]
+            top += rows_audio
+
+
+def softmax_parts(scores, scale, allowed=None):
+    if allowed is not None:
+        scores = jnp.where(allowed, scores, -jnp.inf)
+    peak = jnp.max(scores, axis=1, keepdims=True)
+    weights = jnp.exp2((scores - peak) * (scale * LOG2E))
+    return peak, weights, jnp.sum(weights, axis=1, keepdims=True)
+
+
+def attend_kernel(
+    hops, width, head, me_ref, limit_ref, q_ref, k_ref, v_ref, qv_ref, ka_ref, va_ref, qa_ref, kv_ref, vv_ref, *rest
+):
+    n = len(hops) + 1
+    got = rest[: n - 1]
+    sends = rest[n - 1 : 2 * n - 2]
+    own_ref, a2v_ref, own_v2a_ref, own_lse_ref = rest[2 * n - 2 : 2 * n + 2]
+    qs, ks, vs, kas, vas, qas = rest[2 * n + 2 :]
+    rows = q_ref.shape[0]
+    rows_audio, cols = ka_ref.shape
+    me, limit = me_ref[0], limit_ref[0]
+    mine = pl.ds(pl.multiple_of(me * width, width), width)
+    for dst, ref in ((qs, q_ref), (ks, k_ref), (vs, v_ref)):
+        dst[0:rows, :] = ref[:, mine]
+    for dst, ref in ((kas, ka_ref), (vas, va_ref), (qas, qa_ref)):
+        dst[0:rows_audio, :] = ref[...]
+    for j, ref in enumerate(got):
+        at = (j + 1) * rows
+        for i, dst in enumerate((qs, ks, vs)):
+            dst[at : at + rows, :] = ref[0:rows, i * width : (i + 1) * width]
+        at = (j + 1) * rows_audio
+        top = rows
+        for part in range(cols // width):
+            for i, dst in enumerate((kas, vas, qas)):
+                dst[at : at + rows_audio, part * width : (part + 1) * width] = ref[
+                    top : top + rows_audio, i * width : (i + 1) * width
+                ]
+            top += rows_audio
+    scale = 1.0 / math.sqrt(DHV)
+    for j in range(n):
+        for h in range(width // DHV):
+            cut = slice(h * DHV, (h + 1) * DHV)
+            _, p, total = softmax_parts(dot_t(qs[j * rows : (j + 1) * rows, cut], ks[:, cut]), scale)
+            o = dot(p.astype(jnp.bfloat16), vs[:, cut]) / total
+            dst = own_ref if j == 0 else sends[j - 1].at[0:rows, :]
+            dst[:, cut] = o.astype(jnp.bfloat16)
+    scale = 1.0 / math.sqrt(head)
+    pair = 128 // head
+    keys = n * rows_audio
+    column = lax.broadcasted_iota(jnp.int32, (1, keys), 1)
+    owner = jnp.full((1, keys), me, jnp.int32)
+    for j, hop in enumerate(hops):
+        owner = jnp.where(column // rows_audio == j + 1, me ^ hop, owner)
+    allowed = owner * rows_audio + column % rows_audio < limit
+    lane = lax.broadcasted_iota(jnp.int32, (1, 128), 1) // head
+    lse_column = lax.broadcasted_iota(jnp.int32, (1, 128), 1)
+    lse = jnp.zeros((n * rows_audio, 128), jnp.float32)
+    for block in range(cols // 128):
+        cut = slice(block * 128, (block + 1) * 128)
+        a2v = jnp.zeros((rows, 128), jnp.float32)
+        v2a = jnp.zeros((n * rows_audio, 128), jnp.float32)
+        for i in range(pair):
+            q = jnp.where(lane == i, qv_ref[:, cut], 0).astype(jnp.bfloat16)
+            _, p, total = softmax_parts(dot_t(q, kas[:, cut]), scale, allowed)
+            o = dot(p.astype(jnp.bfloat16), vas[:, cut]) / total
+            a2v = jnp.where(lane == i, o, a2v)
+            q = jnp.where(lane == i, qas[:, cut], 0).astype(jnp.bfloat16)
+            peak, p, total = softmax_parts(dot_t(q, kv_ref[:, cut]), scale)
+            o = dot(p.astype(jnp.bfloat16), vv_ref[:, cut]) / total
+            v2a = jnp.where(lane == i, o, v2a)
+            lse = jnp.where(
+                lse_column == block * pair + i, peak * (scale * LOG2E) + jnp.log2(total), lse
+            )
+        a2v_ref[:, cut] = a2v.astype(jnp.bfloat16)
+        own_v2a_ref[:, cut] = v2a[0:rows_audio]
+        for j, dst in enumerate(sends):
+            top = rows + block * rows_audio
+            dst[top : top + rows_audio, 0:128] = v2a[
+                (j + 1) * rows_audio : (j + 2) * rows_audio
+            ].astype(jnp.bfloat16)
+    own_lse_ref[...] = lse[0:rows_audio]
+    for j, dst in enumerate(sends):
+        rest_lse = lse[(j + 1) * rows_audio : (j + 2) * rows_audio]
+        top = rows + cols // 128 * rows_audio
+        packed = jnp.zeros((rows_audio, 128), jnp.float32)
+        for term in range(3):
+            piece = rest_lse.astype(jnp.bfloat16).astype(jnp.float32)
+            rest_lse = rest_lse - piece
+            packed = packed + (piece if term == 0 else pltpu.roll(piece, 32 * term, 1))
+        dst[top : top + rows_audio, 0:128] = packed.astype(jnp.bfloat16)
+
+
+def merge_kernel(hops, width, head, me_ref, own_ref, v2a_ref, lse_ref, *rest):
+    got, (self_ref, out_ref) = rest[: len(hops)], rest[len(hops) :]
+    rows = own_ref.shape[0]
+    rows_audio, cols = v2a_ref.shape
+    me = me_ref[0]
+    lses, top = [lse_ref[...]], rows + cols // 128 * rows_audio
+    self_ref[:, pl.ds(pl.multiple_of(me * width, width), width)] = own_ref[...]
+    for hop, ref in zip(hops, got):
+        self_ref[:, pl.ds(pl.multiple_of((me ^ hop) * width, width), width)] = ref[0:rows, :]
+        packed = ref[top : top + rows_audio, 0:128].astype(jnp.float32)
+        lses.append(packed + pltpu.roll(packed, 96, 1) + pltpu.roll(packed, 64, 1))
+    peak = functools.reduce(jnp.maximum, lses)
+    parts = [jnp.exp2(x - peak) for x in lses]
+    total = functools.reduce(jnp.add, parts)
+    parts = [x / total for x in parts]
+    pair = 128 // head
+    lane = lax.broadcasted_iota(jnp.int32, (1, 128), 1) // head
+    for block in range(cols // 128):
+        cut = slice(block * 128, (block + 1) * 128)
+        top = rows + block * rows_audio
+        summed = jnp.zeros((rows_audio, 128), jnp.float32)
+        for j in range(len(parts)):
+            if j == 0:
+                o = v2a_ref[:, cut]
+            else:
+                o = got[j - 1][top : top + rows_audio, 0:128].astype(jnp.float32)
+            share = jnp.zeros((rows_audio, 128), jnp.float32)
+            for i in range(pair):
+                at = block * pair + i
+                share = jnp.where(lane == i, parts[j][:, at : at + 1], share)
+            summed = summed + share * o
+        out_ref[:, cut] = summed.astype(jnp.bfloat16)
+
+
+def project_kernel(count, added, block_ref, att_ref, a2v_ref, v2a_ref, ws_ref, wa_ref, wv_ref, g0_ref, g1_ref, *rest):
+    extra, outs = rest[:added], rest[added:]
+    rows = att_ref.shape[0]
+    rows_audio = v2a_ref.shape[0]
+    for i in range(count):
+        out = outs[i]
+        wide = out.shape[1]
+        narrow = wv_ref.shape[1] * wide // ws_ref.shape[1]
+        at = pl.ds(pl.multiple_of(block_ref[i] * wide, wide), wide)
+        term = g0_ref[:, at].astype(jnp.float32) * dot(att_ref[...], ws_ref[:, at])
+        term = term + g1_ref[:, at].astype(jnp.float32) * dot(a2v_ref[...], wa_ref[:, at])
+        at = pl.ds(pl.multiple_of(block_ref[i] * narrow, narrow), narrow)
+        audio = dot(v2a_ref[...], wv_ref[:, at])
+        fold = wide // narrow
+        short = rows_audio // fold
+        if added:
+            term = term + extra[i][0:rows, :].astype(jnp.float32)
+        out[0:rows, :] = term.astype(out.dtype)
+        for f in range(fold):
+            piece = audio[f * short : (f + 1) * short]
+            cut = slice(f * narrow, (f + 1) * narrow)
+            if added:
+                piece = piece + extra[i][rows : rows + short, cut].astype(jnp.float32)
+            out[rows : rows + short, cut] = piece.astype(out.dtype)
+
+
+def finish_kernel(video_ref, audio_ref, gain_ref, own_ref, core_ref, chip_ref, video_out, audio_out):
+    rows = video_ref.shape[0]
+    rows_audio, narrow = audio_ref.shape
+    term = own_ref[...] + core_ref[...].astype(jnp.float32) + chip_ref[...].astype(jnp.float32)
+    video_out[...] = (video_ref[...].astype(jnp.float32) + term[0:rows]).astype(jnp.bfloat16)
+    fold = video_ref.shape[1] // narrow
+    short = rows_audio // fold
+    for f in range(fold):
+        cut = slice(f * short, (f + 1) * short)
+        piece = term[rows : rows + short, f * narrow : (f + 1) * narrow]
+        audio_out[cut, :] = (
+            audio_ref[cut, :].astype(jnp.float32) + gain_ref[cut, :] * piece
+        ).astype(jnp.bfloat16)
+
+
+def on_device_heads(
+    video_in,
+    audio_in,
+    q_self,
+    k_self,
+    v_self,
+    q_a2v,
+    k_a2v,
+    v_a2v,
+    q_v2a,
+    k_v2a,
+    v_v2a,
+    wo_self,
+    wo_a2v,
+    wo_v2a,
+    video_gates,
+    audio_gates,
+    video_steps,
+    audio_steps,
+    audio_len,
+    *,
+    n,
+    chips,
+):
+    bf16, f32 = jnp.bfloat16, jnp.float32
+    hops = [hop for hop in range(n - 1, 1, -1)] + [1]
+    rows, cols = q_self.shape
+    rows_audio, cols_cross = q_v2a.shape
+    width = cols // n
+    seq, mp, sub = (lax.axis_index(a).astype(jnp.int32) for a in ("seq", "mp", "sub"))
+    me = seq.reshape(1)
+
+    def trade(x, axis, hop, size):
+        return lax.ppermute(x, axis, [(i, i ^ hop) for i in range(size)])
+
+    tall = rows + cols_cross // width * rows_audio
+    packed = call(
+        functools.partial(pack_kernel, hops, width),
+        [jax.ShapeDtypeStruct((tall, 3 * width), bf16)] * (n - 1),
+        (me, q_self, k_self, v_self, k_a2v, v_a2v, q_v2a),
+        0,
+    )
+    got = [trade(x, "seq", hop, n) for x, hop in zip(packed, hops)]
+
+    levels = jnp.arange(NT, dtype=jnp.int32)
+    wide_all = video_gates.shape[2]
+    video_hot = (video_steps[:, None] == levels[None, :]).astype(bf16)
+    gain = jnp.dot(video_hot, video_gates.reshape(NT, -1), preferred_element_type=f32).astype(bf16)
+    gain_self, gain_a2v = gain[:, :wide_all], gain[:, wide_all:]
+    narrow = audio_in.shape[1]
+    owned = lax.dynamic_slice_in_dim(audio_gates, (mp * 2 + sub) * narrow, narrow, 1)
+    audio_hot = (audio_steps[:, None] == levels[None, :]).astype(bf16)
+    positions = seq * rows_audio + jnp.arange(rows_audio, dtype=jnp.int32)
+    present = (positions < audio_len[0]).astype(f32)
+    audio_gain = present[:, None] * jnp.dot(audio_hot, owned, preferred_element_type=f32)
+
+    back = rows + cols_cross // 128 * rows_audio + rows_audio
+    result = call(
+        functools.partial(attend_kernel, hops, width, DHC),
+        [jax.ShapeDtypeStruct((back, width), bf16)] * (n - 1)
+        + [
+            jax.ShapeDtypeStruct((rows, width), bf16),
+            jax.ShapeDtypeStruct((rows, cols_cross), bf16),
+            jax.ShapeDtypeStruct((rows_audio, cols_cross), f32),
+            jax.ShapeDtypeStruct((rows_audio, 128), f32),
+        ],
+        (me, audio_len, q_self, k_self, v_self, q_a2v, k_a2v, v_a2v, q_v2a, k_v2a, v_v2a, *got),
+        4 * n * n * rows * rows * width + 8 * n * rows * rows_audio * cols_cross,
+        scratch=[pltpu.VMEM((n * rows, width), bf16)] * 3
+        + [pltpu.VMEM((n * rows_audio, cols_cross), bf16)] * 3,
+    )
+    sends, (own, a2v_att, own_v2a, own_lse) = result[: n - 1], result[n - 1 :]
+    got = [trade(x, "seq", hop, n) for x, hop in zip(sends, hops)]
+    self_att, v2a_att = call(
+        functools.partial(merge_kernel, hops, width, DHC),
+        [jax.ShapeDtypeStruct((rows, cols), bf16), jax.ShapeDtypeStruct((rows_audio, cols_cross), bf16)],
+        (me, own, own_v2a, own_lse, *got),
+        0,
+    )
+
+    wide = video_in.shape[1]
+    short = rows_audio * narrow // wide
+    heads = (self_att, a2v_att, v2a_att, wo_self, wo_a2v, wo_v2a, gain_self, gain_a2v)
+
+    def project(blocks, kinds, extra=()):
+        return call(
+            functools.partial(project_kernel, len(kinds), len(extra)),
+            [jax.ShapeDtypeStruct((rows + short, wide), kind) for kind in kinds],
+            (jnp.stack(blocks), *heads, *extra),
+            2 * rows * (cols + cols_cross) * wide * len(kinds),
+        )
+
+    far, near = (1 - mp) * 2, mp * 2
+    (first,) = project([far + 1 - sub], [bf16])
+    first = trade(first, "sub", 1, 2)
+    second, own_sum = project([near + 1 - sub, near + sub], [bf16, f32])
+    (out_sum,) = project([far + sub], [bf16], (first,))
+    chip_sum = trade(out_sum, "mp", 1, 2)
+    core_sum = trade(second, "sub", 1, 2)
+    return call(
+        finish_kernel,
+        [jax.ShapeDtypeStruct(video_in.shape, bf16), jax.ShapeDtypeStruct(audio_in.shape, bf16)],
+        (video_in, audio_in, audio_gain, own_sum, core_sum, chip_sum),
+        0,
+    )
+
+
+def on_device(n, mp, sub, *arrays):
+    cols, cross = arrays[2].shape[1], arrays[5].shape[1]
+    width = cols // n
+    fits = (
+        n in (2, 4, 8)
+        and (mp, sub) == (2, 2)
+        and width % DHV == 0
+        and cross % width == 0
+        and cross // DHC <= 32
+    )
+    if fits:
+        return on_device_heads(*arrays, n=n, chips=mp)
+    return on_device_gather(*arrays)
+
+
 def solution(mesh):
     in_specs = (
         P(("groups", "seq"), ("mp", "sub")),
@@ -195,5 +529,5 @@
     )
     out_specs = (P(("groups", "seq"), ("mp", "sub")), P(("groups", "seq"), ("mp", "sub")))
     return jax.shard_map(
-        on_device, mesh=mesh, in_specs=in_specs, out_specs=out_specs, check_vma=False
-    )
+        functools.partial(on_device, *(mesh.shape[a] for a in ("seq", "mp", "sub"))), mesh=mesh, in_specs=in_specs, out_specs=out_specs, check_vma=False
+    )

time: 150 us -> 64.7 us (0.43)
  blocking collectives: 88 us -> 0 us
  between operations: 15.2 us -> 1.41 us
  local copies, waits for them, and re-layouts: 7.66 us -> 20.9 us
  starting transfers between devices: 0.08 us -> 12.3 us
  matrix products: 10.3 us -> 1.59 us
  Pallas kernels: 0 us -> 8.63 us
  other arithmetic: 4.72 us -> 0.08 us
  waiting for transfers between devices: 23.5 us -> 18.9 us
    all_gather x6 -> x0, blocking collectives: 88 us -> none  [the longest x1 16 us: on_device(): lax.all_gather(k_v2a, 'seq', axis=0, tiled=True)]
    reduce_scatter x2 -> x0, waiting for transfers between devices: 23.5 us -> none  [the longest x1 23.5 us: on_device(): lax.psum_scatter(video_term.astype(jnp.bfloat16), ('mp', 'sub'), scatter_...]
    ppermute x0 -> x9, waiting for transfers between devices: none -> 18.9 us  [trade(): return lax.ppermute(x, axis, [(i, i ^ hop) for i in range(size)])]
    unnamed x37 -> x55, local copies, waits for them, and re-layouts: 2.17 us -> 19.8 us
    ppermute x0 -> x9, starting transfers between devices: none -> 12.3 us  [trade(): return lax.ppermute(x, axis, [(i, i ^ hop) for i in range(size)])]
    dot_general x11 -> x2, matrix products: 10.3 us -> 1.59 us  [the longest x1 1.4 us: on_device_heads(): jnp.dot(video_hot, video_gates.reshape(NT, -1), preferred_element_type=f32)]
    pallas_call x0 -> x7, Pallas kernels: none -> 8.63 us  [call(): pl.pallas_call(kernel, out_shape=tuple(outs), in_specs=specs, out_specs=t...]
    all_gather x5 -> x0, local copies, waits for them, and re-layouts: 4.57 us -> none  [the longest x1 2.04 us: on_device(): lax.all_gather(v_self, 'seq', axis=0, tiled=True)]
  transfers between devices with their start and end apart: 2 -> 9, of which waited for: 1 -> 5; matrix products, arithmetic and copies ran while one was open for 8% -> 6% of each run, Pallas kernels for 0% -> 4%
where the time goes in v1:
time: 64.7 us; the launch traced here: 63.8 us
  local copies, waits for them, and re-layouts  20.9 us (32%)
  waiting for transfers between devices  18.9 us (29%)
  starting transfers between devices  12.3 us (19%)
  Pallas kernels  8.63 us (13%)
  matrix products  1.59 us (2%)
  between operations  1.41 us (2%)
    unnamed x55, local copies, waits for them, and re-layouts  19.8 us
    ppermute x9, waiting for transfers between devices, trade(): return lax.ppermute(x, axis, [(i, i ^ hop) for i in range(size)])  18.9 us
    ppermute x9, starting transfers between devices, trade(): return lax.ppermute(x, axis, [(i, i ^ hop) for i in range(size)])  12.3 us
    pallas_call x7, Pallas kernels, call(): pl.pallas_call(kernel, out_shape=tuple(outs), in_specs=specs, out_specs=t...  8.63 us
    dot_general x1, matrix products, on_device_heads(): jnp.dot(video_hot, video_gates.reshape(NT, -1), preferred_element_type=f32)  1.4 us
  transfers between devices with their start and end apart: 9, of which 5 were waited for; matrix products, arithmetic and copies ran while one was open for 6% of the time, Pallas kernels for 4%

profile of v1, /device:TPU:0, one launch (start us, length us, event | category | flops | bytes accessed | tf_op | source)
XLA Modules:
  0.0 63.8 jit_solution(15118380400094392199)
XLA Ops:
  0.7 0.9 %copy-done.9 = bf16[128,512]{1,0:T(8,128)(2,1)S(1)} copy-done((bf16[128,512]{1,0:T(8,128)(2,1)S(1)}, bf16[128,512]{1,0:T(8,128)(2,1)}, u32[]{:S(2)}) %copy-start.9) | copy-done | bytes 131096
  1.6 0.9 %copy-done.10 = bf16[128,512]{1,0:T(8,128)(2,1)S(1)} copy-done((bf16[128,512]{1,0:T(8,128)(2,1)S(1)}, bf16[128,512]{1,0:T(8,128)(2,1)}, u32[]{:S(2)}) %copy-start.10) | copy-done | bytes 131096
  5.6 5.1 %collective-permute-start = (bf16[192,384]{1,0:T(8,128)(2,1)S(1)}, bf16[192,384]{1,0:T(8,128)(2,1)S(1)}, u32[]{:S(2)}, u32[]{:S(2)}) collective-permute-start(bf16[192,384]{1,0:T(8,128)(2,1)S(1)} %get-tuple-element.16), channel_id=1, source_target_pairs={{0,12},{4,8},{8,4},{12,0},{1,13},{5,9},{9,5},{13,1},{2,14},{6,10},... | collective-permute-start | bytes 442376 | tf_op jit(solution)/shard_map/ppermute | solution.py:419
  12.1 1.1 %copy.21 = bf16[2,8,2,4096]{3,1,2,0:T(8,128)(2,1)S(1)} copy(bf16[2,8,2,4096]{3,2,1,0:T(2,128)(2,1)} %bitcast.11) | data formatting | bytes 524288
  13.2 1.4 %convolution_convert_fusion = bf16[128,8192]{1,0:T(8,128)(2,1)S(1)} fusion(bf16[16,8192]{1,0:T(8,128)(2,1)S(1)} %bitcast.10, s32[128]{0:T(128)} %param.35), kind=kOutput, calls=%fused_computation | convolution fusion | flops 34605056 | bytes 2359808 | tf_op jit(solution)/shard_map/dot_general | solution.py:433
  14.6 1.0 %collective-permute-done.rest_0_ = bf16[192,384]{1,0:T(8,128)(2,1)S(1)} collective-permute-done((bf16[192,384]{1,0:T(8,128)(2,1)S(1)}, bf16[192,384]{1,0:T(8,128)(2,1)S(1)}, u32[]{:S(2)}, u32[]{:S(2)}) %collective-permute-start) | collective-permute-done | bytes 147488 | tf_op jit(solution)/shard_map/ppermute | solution.py:419
  15.6 7.7 %collective-permute-done.1.rest_1_ = bf16[192,384]{1,0:T(8,128)(2,1)S(1)} collective-permute-done((bf16[192,384]{1,0:T(8,128)(2,1)S(1)}, bf16[192,384]{1,0:T(8,128)(2,1)S(1)}, u32[]{:S(2)}, u32[]{:S(2)}) %collective-permute-start.1) | collective-permute-done | bytes 147488 | tf_op jit(solution)/shard_map/ppermute | solution.py:419
  23.3 3.6 %shard_map.195 = (bf16[224,128]{1,0:T(8,128)(2,1)}, bf16[224,128]{1,0:T(8,128)(2,1)}, bf16[224,128]{1,0:T(8,128)(2,1)S(1)}, bf16[128,128]{1,0:T(8,128)(2,1)S(1)}...) custom-call(s32[1]{0:T(128)} %bitcast.3.me_ref, s32[1]{0:T(128)} %copy.22.limit_ref, ...), custom_call_target="tpu_custom_call" | custom-call | flops 167772160 | bytes 1400840 | tf_op jit(solution)/shard_map/pallas_call | solution.py:185
  28.1 2.5 %collective-permute-start.3 = (bf16[224,128]{1,0:T(8,128)(2,1)}, bf16[224,128]{1,0:T(8,128)(2,1)S(1)}, u32[]{:S(2)}, u32[]{:S(2)}) collective-permute-start(bf16[224,128]{1,0:T(8,128)(2,1)} %get-tuple-element.22), channel_id=1, source_target_pairs={{0,12},{4,8},{8,4},{12,0},{1,13},{5,9},{9,5},{13,1},{2,14},{6,10},... | collective-permute-start | bytes 172040 | tf_op jit(solution)/shard_map/ppermute | solution.py:419
  30.6 1.9 %collective-permute-start.5 = (bf16[224,128]{1,0:T(8,128)(2,1)S(1)}, bf16[224,128]{1,0:T(8,128)(2,1)S(1)}, u32[]{:S(2)}, u32[]{:S(2)}) collective-permute-start(bf16[224,128]{1,0:T(8,128)(2,1)S(1)} %get-tuple-element.24), channel_id=1, source_target_pairs={{0,4},{4,0},{8,12},{12,8},{1,5},{5,1},{9,13},{13,9},{2,6},{6,2},{1... | collective-permute-start | bytes 172040 | tf_op jit(solution)/shard_map/ppermute | solution.py:419
  32.5 1.2 %fusion.4 = (bf16[128,4096]{1,0:T(8,128)(2,1)S(1)}, bf16[128,4096]{1,0:T(8,128)(2,1)}) fusion(bf16[128,8192]{1,0:T(8,128)(2,1)S(1)} %convolution_convert_fusion), kind=kLoop, calls=%fused_computation.10 | loop fusion | bytes 4194304 | tf_op jit(solution)/shard_map/slice | solution.py:434
  33.6 0.9 %collective-permute-done.3.rest_0_ = bf16[224,128]{1,0:T(8,128)(2,1)S(1)} collective-permute-done((bf16[224,128]{1,0:T(8,128)(2,1)}, bf16[224,128]{1,0:T(8,128)(2,1)S(1)}, u32[]{:S(2)}, u32[]{:S(2)}) %collective-permute-start.3) | collective-permute-done | bytes 57376 | tf_op jit(solution)/shard_map/ppermute | solution.py:419
  34.6 1.5 %collective-permute-done.4.rest_1_ = bf16[224,128]{1,0:T(8,128)(2,1)S(1)} collective-permute-done((bf16[224,128]{1,0:T(8,128)(2,1)}, bf16[224,128]{1,0:T(8,128)(2,1)S(1)}, u32[]{:S(2)}, u32[]{:S(2)}) %collective-permute-start.4) | collective-permute-done | bytes 57376 | tf_op jit(solution)/shard_map/ppermute | solution.py:419
  39.4 2.2 %copy-done.1 = bf16[512,4096]{1,0:T(8,128)(2,1)S(1)} copy-done((bf16[512,4096]{1,0:T(8,128)(2,1)S(1)}, bf16[512,4096]{1,0:T(8,128)(2,1)}, u32[]{:S(2)}) %copy-start.1) | copy-done | bytes 4194328
  41.6 1.2 %copy-done.5 = bf16[128,4096]{1,0:T(8,128)(2,1)S(1)} copy-done((bf16[128,4096]{1,0:T(8,128)(2,1)S(1)}, bf16[128,4096]{1,0:T(8,128)(2,1)}, u32[]{:S(2)}) %copy-start.5) | copy-done | bytes 1048600
  42.8 1.2 %copy-done.7 = bf16[256,2048]{1,0:T(8,128)(2,1)S(1)} copy-done((bf16[256,2048]{1,0:T(8,128)(2,1)S(1)}, bf16[256,2048]{1,0:T(8,128)(2,1)}, u32[]{:S(2)}) %copy-start.7) | copy-done | bytes 1048600
  44.0 1.1 %shard_map.198 = bf16[144,1024]{1,0:T(8,128)(2,1)} custom-call(s32[1]{0:T(128)} %bitcast.5.block_ref, bf16[128,512]{1,0:T(8,128)(2,1)S(1)} %get-tuple-element.25.att_ref, bf16[128,256]{1,0:T(8,128)(2,1)S(1)} %get-tuple-element.26.a2v_ref, bf16[32,256]{1,0:T(8,128)(2,1)S(1)} %get-tuple-element.27.v2a_ref, bf16[512,4096]{1,0:T(8,128)(2,1)S(1)} %copy-done.1, ...), custom_call_target="tpu_custom_call" | custom-call | flops 201326592 | bytes 9945092 | tf_op jit(solution)/shard_map/pallas_call | solution.py:185
  45.2 2.2 %copy-done.2 = bf16[512,4096]{1,0:T(8,128)(2,1)S(1)} copy-done((bf16[512,4096]{1,0:T(8,128)(2,1)S(1)}, bf16[512,4096]{1,0:T(8,128)(2,1)}, u32[]{:S(2)}) %copy-start.2) | copy-done | bytes 4194328
  47.4 1.2 %copy-done.6 = bf16[128,4096]{1,0:T(8,128)(2,1)S(1)} copy-done((bf16[128,4096]{1,0:T(8,128)(2,1)S(1)}, bf16[128,4096]{1,0:T(8,128)(2,1)}, u32[]{:S(2)}) %copy-start.6) | copy-done | bytes 1048600
  48.6 1.2 %copy-done.8 = bf16[256,2048]{1,0:T(8,128)(2,1)S(1)} copy-done((bf16[256,2048]{1,0:T(8,128)(2,1)S(1)}, bf16[256,2048]{1,0:T(8,128)(2,1)}, u32[]{:S(2)}) %copy-start.8) | copy-done | bytes 1048600
  49.9 1.3 %shard_map.197 = (bf16[144,1024]{1,0:T(8,128)(2,1)S(1)}, f32[144,1024]{1,0:T(8,128)S(1)}) custom-call(s32[2]{0:T(128)S(1)} %pad_add_fusion.block_ref, bf16[128,512]{1,0:T(8,128)(2,1)S(1)} %get-tuple-element.25.att_ref, bf16[128,256]{1,0:T(8,128)(2,1)S(1)} %get-tuple-element.26.a2v_ref, bf16[32,256]{1,0:T(8,128)(2,1)S(1)} %get-tuple-element.27.v2a_ref, ...), custom_call_target="tpu_custom_call" | custom-call | flops 402653184 | bytes 10534920 | tf_op jit(solution)/shard_map/pallas_call | solution.py:185
  52.0 1.5 %shard_map.199 = bf16[144,1024]{1,0:T(8,128)(2,1)S(1)} custom-call(s32[1]{0:T(128)} %bitcast.4.block_ref, bf16[128,512]{1,0:T(8,128)(2,1)S(1)} %get-tuple-element.25.att_ref, bf16[128,256]{1,0:T(8,128)(2,1)S(1)} %get-tuple-element.26.a2v_ref, bf16[32,256]{1,0:T(8,128)(2,1)S(1)} %get-tuple-element.27.v2a_ref, bf16[512,4096]{1,0:T(8,128)(2,1)S(1)} %copy-done.3, ...), custom_call_target="tpu_custom_call" | custom-call | flops 201326592 | bytes 10240004 | tf_op jit(solution)/shard_map/pallas_call | solution.py:185
  53.5 1.6 %collective-permute-start.8 = (bf16[144,1024]{1,0:T(8,128)(2,1)S(1)}, bf16[144,1024]{1,0:T(8,128)(2,1)S(1)}, u32[]{:S(2)}, u32[]{:S(2)}) collective-permute-start(bf16[144,1024]{1,0:T(8,128)(2,1)S(1)} %shard_map.199), channel_id=1, source_target_pairs={{0,2},{2,0},{1,3},{3,1},{4,6},{6,4},{5,7},{7,5},{8,10},{10,8},{9,1... | collective-permute-start | bytes 884744 | tf_op jit(solution)/shard_map/ppermute | solution.py:419
  55.3 7.7 %collective-permute-done.8.chip_ref = bf16[144,1024]{1,0:T(8,128)(2,1)S(1)} collective-permute-done((bf16[144,1024]{1,0:T(8,128)(2,1)S(1)}, bf16[144,1024]{1,0:T(8,128)(2,1)S(1)}, u32[]{:S(2)}, u32[]{:S(2)}) %collective-permute-start.8) | collective-permute-done | bytes 294944 | tf_op jit(solution)/shard_map/ppermute | solution.py:419
  (61 shorter events, 10.3 us)
Async XLA Ops:
  0.6 54.4 %copy-start = (bf16[16,2048]{1,0:T(8,128)(2,1)S(1)}, bf16[16,2048]{1,0:T(8,128)(2,1)}, u32[]{:S(2)}) copy-start(bf16[16,2048]{1,0:T(8,128)(2,1)} %param.34) | copy-start | bytes 196612
  5.6 17.7 %copy-start.16 = (bf16[128,256]{1,0:T(8,128)(2,1)S(1)}, bf16[128,256]{1,0:T(8,128)(2,1)}, u32[]{:S(2)}) copy-start(bf16[128,256]{1,0:T(8,128)(2,1)} %qv_ref.1) | copy-start | bytes 196612
  5.6 17.7 %copy-start.17 = (bf16[128,256]{1,0:T(8,128)(2,1)S(1)}, bf16[128,256]{1,0:T(8,128)(2,1)}, u32[]{:S(2)}) copy-start(bf16[128,256]{1,0:T(8,128)(2,1)} %kv_ref.1) | copy-start | bytes 196612
  5.6 17.7 %copy-start.18 = (bf16[128,256]{1,0:T(8,128)(2,1)S(1)}, bf16[128,256]{1,0:T(8,128)(2,1)}, u32[]{:S(2)}) copy-start(bf16[128,256]{1,0:T(8,128)(2,1)} %vv_ref.1) | copy-start | bytes 196612
  5.6 9.9 %collective-permute-start = (bf16[192,384]{1,0:T(8,128)(2,1)S(1)}, bf16[192,384]{1,0:T(8,128)(2,1)S(1)}, u32[]{:S(2)}, u32[]{:S(2)}) collective-permute-start(bf16[192,384]{1,0:T(8,128)(2,1)S(1)} %get-tuple-element.16), channel_id=1, source_target_pairs={{0,12},{4,8},{8,4},{12,0},{1,13},{5,9},{9,5},{13,1},{2,14},{6,10},... | collective-permute-start | bytes 442376 | tf_op jit(solution)/shard_map/ppermute | solution.py:419
  10.8 12.5 %collective-permute-start.1 = (bf16[192,384]{1,0:T(8,128)(2,1)S(1)}, bf16[192,384]{1,0:T(8,128)(2,1)S(1)}, u32[]{:S(2)}, u32[]{:S(2)}) collective-permute-start(bf16[192,384]{1,0:T(8,128)(2,1)S(1)} %get-tuple-element.17), channel_id=1, source_target_pairs={{0,8},{4,12},{8,0},{12,4},{1,9},{5,13},{9,1},{13,5},{2,10},{6,14},... | collective-permute-start | bytes 442376 | tf_op jit(solution)/shard_map/ppermute | solution.py:419
  10.8 12.5 %collective-permute-start.2 = (bf16[192,384]{1,0:T(8,128)(2,1)S(1)}, bf16[192,384]{1,0:T(8,128)(2,1)S(1)}, u32[]{:S(2)}, u32[]{:S(2)}) collective-permute-start(bf16[192,384]{1,0:T(8,128)(2,1)S(1)} %get-tuple-element.18), channel_id=1, source_target_pairs={{0,4},{4,0},{8,12},{12,8},{1,5},{5,1},{9,13},{13,9},{2,6},{6,2},{1... | collective-permute-start | bytes 442376 | tf_op jit(solution)/shard_map/ppermute | solution.py:419
  28.1 6.5 %collective-permute-start.3 = (bf16[224,128]{1,0:T(8,128)(2,1)}, bf16[224,128]{1,0:T(8,128)(2,1)S(1)}, u32[]{:S(2)}, u32[]{:S(2)}) collective-permute-start(bf16[224,128]{1,0:T(8,128)(2,1)} %get-tuple-element.22), channel_id=1, source_target_pairs={{0,12},{4,8},{8,4},{12,0},{1,13},{5,9},{9,5},{13,1},{2,14},{6,10},... | collective-permute-start | bytes 172040 | tf_op jit(solution)/shard_map/ppermute | solution.py:419
  30.6 5.5 %collective-permute-start.4 = (bf16[224,128]{1,0:T(8,128)(2,1)}, bf16[224,128]{1,0:T(8,128)(2,1)S(1)}, u32[]{:S(2)}, u32[]{:S(2)}) collective-permute-start(bf16[224,128]{1,0:T(8,128)(2,1)} %get-tuple-element.23), channel_id=1, source_target_pairs={{0,8},{4,12},{8,0},{12,4},{1,9},{5,13},{9,1},{13,5},{2,10},{6,14},... | collective-permute-start | bytes 172040 | tf_op jit(solution)/shard_map/ppermute | solution.py:419
  30.6 8.8 %copy-start.4 = (bf16[256,4096]{1,0:T(8,128)(2,1)S(1)}, bf16[256,4096]{1,0:T(8,128)(2,1)}, u32[]{:S(2)}) copy-start(bf16[256,4096]{1,0:T(8,128)(2,1)} %wa_ref.5) | copy-start | bytes 6291460
  30.6 5.5 %collective-permute-start.5 = (bf16[224,128]{1,0:T(8,128)(2,1)S(1)}, bf16[224,128]{1,0:T(8,128)(2,1)S(1)}, u32[]{:S(2)}, u32[]{:S(2)}) collective-permute-start(bf16[224,128]{1,0:T(8,128)(2,1)S(1)} %get-tuple-element.24), channel_id=1, source_target_pairs={{0,4},{4,0},{8,12},{12,8},{1,5},{5,1},{9,13},{13,9},{2,6},{6,2},{1... | collective-permute-start | bytes 172040 | tf_op jit(solution)/shard_map/ppermute | solution.py:419
  39.4 2.2 %copy-start.1 = (bf16[512,4096]{1,0:T(8,128)(2,1)S(1)}, bf16[512,4096]{1,0:T(8,128)(2,1)}, u32[]{:S(2)}) copy-start(bf16[512,4096]{1,0:T(8,128)(2,1)} %ws_ref.5) | copy-start | bytes 12582916
  41.6 1.2 %copy-start.5 = (bf16[128,4096]{1,0:T(8,128)(2,1)S(1)}, bf16[128,4096]{1,0:T(8,128)(2,1)}, u32[]{:S(2)}) copy-start(bf16[128,4096]{1,0:T(8,128)(2,1)} %get-tuple-element.31.g0_ref) | copy-start | bytes 3145732
  42.8 1.2 %copy-start.7 = (bf16[256,2048]{1,0:T(8,128)(2,1)S(1)}, bf16[256,2048]{1,0:T(8,128)(2,1)}, u32[]{:S(2)}) copy-start(bf16[256,2048]{1,0:T(8,128)(2,1)} %wv_ref.5) | copy-start | bytes 3145732
  45.1 6.6 %collective-permute-start.7 = (bf16[144,1024]{1,0:T(8,128)(2,1)}, bf16[144,1024]{1,0:T(8,128)(2,1)}, u32[]{:S(2)}, u32[]{:S(2)}) collective-permute-start(bf16[144,1024]{1,0:T(8,128)(2,1)} %shard_map.198), channel_id=1, source_target_pairs={{0,1},{1,0},{2,3},{3,2},{4,5},{5,4},{6,7},{7,6},{8,9},{9,8},{10,11... | collective-permute-start | bytes 884744 | tf_op jit(solution)/shard_map/ppermute | solution.py:419
  45.2 2.2 %copy-start.2 = (bf16[512,4096]{1,0:T(8,128)(2,1)S(1)}, bf16[512,4096]{1,0:T(8,128)(2,1)}, u32[]{:S(2)}) copy-start(bf16[512,4096]{1,0:T(8,128)(2,1)} %ws_ref.5) | copy-start | bytes 12582916
  47.4 1.2 %copy-start.6 = (bf16[128,4096]{1,0:T(8,128)(2,1)S(1)}, bf16[128,4096]{1,0:T(8,128)(2,1)}, u32[]{:S(2)}) copy-start(bf16[128,4096]{1,0:T(8,128)(2,1)} %get-tuple-element.31.g0_ref) | copy-start | bytes 3145732
  48.6 1.2 %copy-start.8 = (bf16[256,2048]{1,0:T(8,128)(2,1)S(1)}, bf16[256,2048]{1,0:T(8,128)(2,1)}, u32[]{:S(2)}) copy-start(bf16[256,2048]{1,0:T(8,128)(2,1)} %wv_ref.5) | copy-start | bytes 3145732
  49.9 2.2 %copy-start.3 = (bf16[512,4096]{1,0:T(8,128)(2,1)S(1)}, bf16[512,4096]{1,0:T(8,128)(2,1)}, u32[]{:S(2)}) copy-start(bf16[512,4096]{1,0:T(8,128)(2,1)} %ws_ref.5) | copy-start | bytes 12582916
  51.2 4.1 %collective-permute-start.6 = (bf16[144,1024]{1,0:T(8,128)(2,1)S(1)}, bf16[144,1024]{1,0:T(8,128)(2,1)S(1)}, u32[]{:S(2)}, u32[]{:S(2)}) collective-permute-start(bf16[144,1024]{1,0:T(8,128)(2,1)S(1)} %get-tuple-element.29), channel_id=1, source_target_pairs={{0,1},{1,0},{2,3},{3,2},{4,5},{5,4},{6,7},{7,6},{8,9},{9,8},{10,11... | collective-permute-start | bytes 884744 | tf_op jit(solution)/shard_map/ppermute | solution.py:419
  52.0 3.0 %copy-start.26 = (s32[32]{0:T(128)S(1)}, s32[32]{0:T(128)}, u32[]{:S(2)}) copy-start(s32[32]{0:T(128)} %param.36) | copy-start | bytes 388
  52.0 11.0 %copy-start.12 = (bf16[128,1024]{1,0:T(8,128)(2,1)S(1)}, bf16[128,1024]{1,0:T(8,128)(2,1)}, u32[]{:S(2)}) copy-start(bf16[128,1024]{1,0:T(8,128)(2,1)} %video_ref.1) | copy-start | bytes 786436
  52.0 11.0 %copy-start.21 = (bf16[32,512]{1,0:T(8,128)(2,1)S(1)}, bf16[32,512]{1,0:T(8,128)(2,1)}, u32[]{:S(2)}) copy-start(bf16[32,512]{1,0:T(8,128)(2,1)} %audio_ref.1) | copy-start | bytes 98308
  53.5 9.5 %collective-permute-start.8 = (bf16[144,1024]{1,0:T(8,128)(2,1)S(1)}, bf16[144,1024]{1,0:T(8,128)(2,1)S(1)}, u32[]{:S(2)}, u32[]{:S(2)}) collective-permute-start(bf16[144,1024]{1,0:T(8,128)(2,1)S(1)} %shard_map.199), channel_id=1, source_target_pairs={{0,2},{2,0},{1,3},{3,1},{4,6},{6,4},{5,7},{7,5},{8,10},{10,8},{9,1... | collective-permute-start | bytes 884744 | tf_op jit(solution)/shard_map/ppermute | solution.py:419
  (12 other events, 9.1 us)

commit v2 on v0

--- a/solution.py
+++ b/solution.py
@@ -1,9 +1,13 @@
+import functools
 import math
 
 import jax
 import jax.numpy as jnp
 from jax import lax
+from jax.experimental import pallas as pl
+from jax.experimental.pallas import tpu as pltpu
 from jax.sharding import PartitionSpec as P
+
 
 DHV = 128
 DHC = 64
@@ -65,12 +69,12 @@
 
 
 def finish(state, heads, width):
-    peak, total, summed = state
+    _, total, summed = state
     rows = summed.shape[0]
     return (summed / total[:, :, None]).reshape(rows, heads * width).astype(jnp.bfloat16)
 
 
-def on_device(
+def on_device_gather(
     video_in,
     audio_in,
     q_self,
@@ -171,6 +175,402 @@
     return (video_out, audio_out)
 
 
+LOG2E = 1.4426950408889634
+VMEM = pl.BlockSpec(memory_space=pltpu.VMEM)
+SMEM = pl.BlockSpec(memory_space=pltpu.SMEM)
+HBM = pl.BlockSpec(memory_space=pltpu.HBM)
+BF16, F32 = jnp.bfloat16, jnp.float32
+
+
+def call(kernel, outs, operands, specs=None, flops=0, scratch=(), limit=8 * 2**20):
+    size = sum(math.prod(x.shape) * x.dtype.itemsize for x in (*operands, *outs))
+    if specs:
+        operands = [
+            pltpu.with_memory_space_constraint(x, pltpu.HBM) if spec is HBM else x for x, spec in zip(operands, specs)
+        ]
+    return pl.pallas_call(
+        kernel,
+        out_shape=tuple(outs),
+        in_specs=specs or [VMEM] * len(operands),
+        out_specs=tuple(VMEM for _ in outs),
+        scratch_shapes=list(scratch),
+        compiler_params=pltpu.CompilerParams(vmem_limit_bytes=limit),
+        cost_estimate=pl.CostEstimate(flops=flops, bytes_accessed=size, transcendentals=0),
+    )(*operands)
+
+
+def shape(rows, cols, kind=BF16):
+    return jax.ShapeDtypeStruct((rows, cols), kind)
+
+
+def dot_t(a, b):
+    return lax.dot_general(a, b, (((1,), (1,)), ((), ())), preferred_element_type=F32)
+
+
+def dot(a, b):
+    return jnp.dot(a, b, preferred_element_type=F32)
+
+
+def index_of(axis):
+    return lax.axis_index(axis).astype(jnp.int32)
+
+
+def columns(index, width):
+    return pl.ds(pl.multiple_of(index * width, width), width)
+
+
+def copy_all(pairs, sems):
+    copies = [pltpu.make_async_copy(src, dst, sems.at[i]) for i, (src, dst) in enumerate(pairs)]
+    for copy in copies:
+        copy.start()
+    for copy in copies:
+        copy.wait()
+
+
+def pack_kernel(hops, width, q_ref, k_ref, v_ref, qa_ref, ka_ref, va_ref, *rest):
+    outs, audio, sems = rest[: len(hops)], rest[-2], rest[-1]
+    rows = q_ref.shape[0]
+    rows_audio, cols_audio = qa_ref.shape
+    me = index_of("seq")
+    pairs = []
+    for hop, out in zip(hops, outs):
+        for i, ref in enumerate((q_ref, k_ref, v_ref)):
+            pairs.append((ref.at[:, columns(me ^ hop, width)], out.at[pl.ds(i * rows, rows), :]))
+        for i in range(cols_audio // width):
+            at = pl.ds(3 * rows + i * rows_audio, rows_audio)
+            pairs.append((qa_ref.at[:, pl.ds(i * width, width)], out.at[at, :]))
+    pairs.append((ka_ref, audio.at[pl.ds(0, rows_audio), :]))
+    pairs.append((va_ref, audio.at[pl.ds(rows_audio, rows_audio), :]))
+    copy_all(pairs, sems)
+
+
+def one_hot_t(steps_ref):
+    levels = lax.broadcasted_iota(jnp.int32, (NT, steps_ref.shape[1]), 0)
+    return (levels == steps_ref[...]).astype(BF16)
+
+
+def pick(hot_t, table):
+    return lax.dot_general(hot_t, table, (((0,), (0,)), ((), ())), preferred_element_type=F32)
+
+
+def fetch_kernel(limit_ref, vg_ref, *rest):
+    loads, gain_ref, audio_ref = rest[:8], rest[8], rest[9]
+    fetched, (vs_ref, as_ref, ag_ref, sems) = rest[10:15], rest[15:]
+    copies = [
+        pltpu.make_async_copy(src, dst, sems.at[i])
+        for i, (src, dst) in enumerate(zip(loads, (vs_ref, as_ref, ag_ref, *fetched)))
+    ]
+    for copy in copies:
+        copy.start()
+    for copy in copies[:3]:
+        copy.wait()
+    hot_t = one_hot_t(vs_ref)
+    piece = min(vg_ref.shape[1], 2048)
+    for at in range(0, vg_ref.shape[1], piece):
+        gain_ref[:, at : at + piece] = pick(hot_t, vg_ref[:, at : at + piece]).astype(BF16)
+    rows_audio, narrow = audio_ref.shape
+    part = index_of("mp") * 2 + index_of("sub")
+    gain = pick(one_hot_t(as_ref), ag_ref[:, columns(part, narrow)])
+    at = index_of("seq") * rows_audio + lax.broadcasted_iota(jnp.int32, (rows_audio, 1), 0)
+    audio_ref[...] = jnp.where(at < limit_ref[0], gain, 0.0)
+    for copy in copies[3:]:
+        copy.wait()
+
+
+def softmax_parts(scores, scale, allowed=None):
+    if allowed is not None:
+        scores = jnp.where(allowed, scores, -jnp.inf)
+    peak = jnp.max(scores, axis=1, keepdims=True)
+    weights = jnp.exp2((scores - peak) * (scale * LOG2E))
+    return peak, weights, jnp.sum(weights, axis=1, keepdims=True)
+
+
+def attend_kernel(n, head, kv_hbm, vv_hbm, *rest):
+    blocks, sends, (own_ref, own_v2a_ref, own_lse_ref) = rest[:n], rest[n : 2 * n - 1], rest[2 * n - 1 : 2 * n + 2]
+    ks, vs, qas, kv_ref, vv_ref, sems = rest[2 * n + 2 :]
+    copies = [pltpu.make_async_copy(kv_hbm, kv_ref, sems.at[0]), pltpu.make_async_copy(vv_hbm, vv_ref, sems.at[1])]
+    for copy in copies:
+        copy.start()
+    rows, cols = kv_ref.shape
+    width = blocks[0].shape[1]
+    rows_audio = qas.shape[0] // n
+    for j, ref in enumerate(blocks):
+        ks[j * rows : (j + 1) * rows, :] = ref[rows : 2 * rows, :]
+        vs[j * rows : (j + 1) * rows, :] = ref[2 * rows : 3 * rows, :]
+        for i in range(cols // width):
+            top = 3 * rows + i * rows_audio
+            qas[j * rows_audio : (j + 1) * rows_audio, i * width : (i + 1) * width] = ref[top : top + rows_audio, :]
+    scale = 1.0 / math.sqrt(DHV)
+    for j, ref in enumerate(blocks):
+        for h in range(width // DHV):
+            cut = slice(h * DHV, (h + 1) * DHV)
+            _, p, total = softmax_parts(dot_t(ref[0:rows, cut], ks[:, cut]), scale)
+            o = dot(p.astype(BF16), vs[:, cut]) / total
+            dst = own_ref if j == 0 else sends[j - 1].at[0:rows, :]
+            dst[:, cut] = o.astype(BF16)
+    for copy in copies:
+        copy.wait()
+    scale = 1.0 / math.sqrt(head)
+    pair = 128 // head
+    lane = lax.broadcasted_iota(jnp.int32, (1, 128), 1) // head
+    lse_column = lax.broadcasted_iota(jnp.int32, (1, 128), 1)
+    lse = jnp.zeros((n * rows_audio, 128), F32)
+    for block in range(cols // 128):
+        cut = slice(block * 128, (block + 1) * 128)
+        v2a = jnp.zeros((n * rows_audio, 128), F32)
+        for i in range(pair):
+            q = jnp.where(lane == i, qas[:, cut], 0).astype(BF16)
+            peak, p, total = softmax_parts(dot_t(q, kv_ref[:, cut]), scale)
+            v2a = jnp.where(lane == i, dot(p.astype(BF16), vv_ref[:, cut]) / total, v2a)
+            lse = jnp.where(lse_column == block * pair + i, peak * (scale * LOG2E) + jnp.log2(total), lse)
+        own_v2a_ref[:, cut] = v2a[0:rows_audio]
+        for j, dst in enumerate(sends):
+            top = rows + block * rows_audio
+            dst[top : top + rows_audio, 0:128] = v2a[(j + 1) * rows_audio : (j + 2) * rows_audio].astype(BF16)
+    own_lse_ref[...] = lse[0:rows_audio]
+    for j, dst in enumerate(sends):
+        rest_lse = lse[(j + 1) * rows_audio : (j + 2) * rows_audio]
+        top = rows + cols // 128 * rows_audio
+        packed = jnp.zeros((rows_audio, 128), F32)
+        for term in range(3):
+            piece = rest_lse.astype(BF16).astype(F32)
+            rest_lse = rest_lse - piece
+            packed = packed + (piece if term == 0 else pltpu.roll(piece, 32 * term, 1))
+        dst[top : top + rows_audio, 0:128] = packed.astype(BF16)
+
+
+def attend_audio_kernel(hops, head, limit_ref, q_hbm, *rest):
+    n = len(hops)
+    blocks, out_ref, ks, vs, q_ref, sem = rest[:n], *rest[n:]
+    copy = pltpu.make_async_copy(q_hbm, q_ref, sem.at[0])
+    copy.start()
+    rows_audio = blocks[0].shape[0] // 2
+    keys = n * rows_audio
+    column = lax.broadcasted_iota(jnp.int32, (1, keys), 1)
+    me, position = index_of("seq"), column
+    for j, (hop, ref) in enumerate(zip(hops, blocks)):
+        at = slice(j * rows_audio, (j + 1) * rows_audio)
+        ks[at, :] = ref[0:rows_audio, :]
+        vs[at, :] = ref[rows_audio : 2 * rows_audio, :]
+        shift = ((me ^ hop) - j) * rows_audio
+        position = jnp.where(column // rows_audio == j, column + shift, position)
+    allowed = position < limit_ref[0]
+    copy.wait()
+    scale = 1.0 / math.sqrt(head)
+    lane = lax.broadcasted_iota(jnp.int32, (1, 128), 1) // head
+    for block in range(q_ref.shape[1] // 128):
+        cut = slice(block * 128, (block + 1) * 128)
+        both = jnp.zeros((q_ref.shape[0], 128), F32)
+        for i in range(128 // head):
+            q = jnp.where(lane == i, q_ref[:, cut], 0).astype(BF16)
+            _, p, total = softmax_parts(dot_t(q, ks[:, cut]), scale, allowed)
+            both = jnp.where(lane == i, dot(p.astype(BF16), vs[:, cut]) / total, both)
+        out_ref[:, cut] = both.astype(BF16)
+
+
+def merge(hops, head, own_ref, v2a_ref, lse_ref, got, self_ref, out_ref):
+    rows, width = own_ref.shape
+    rows_audio, cols = v2a_ref.shape
+    me = index_of("seq")
+    lses, top = [lse_ref[...]], rows + cols // 128 * rows_audio
+    self_ref[:, columns(me, width)] = own_ref[...]
+    for hop, ref in zip(hops[1:], got):
+        self_ref[:, columns(me ^ hop, width)] = ref[0:rows, :]
+        packed = ref[top : top + rows_audio, 0:128].astype(F32)
+        lses.append(packed + pltpu.roll(packed, 96, 1) + pltpu.roll(packed, 64, 1))
+    peak = functools.reduce(jnp.maximum, lses)
+    parts = [jnp.exp2(x - peak) for x in lses]
+    total = functools.reduce(jnp.add, parts)
+    parts = [x / total for x in parts]
+    pair = 128 // head
+    lane = lax.broadcasted_iota(jnp.int32, (1, 128), 1) // head
+    for block in range(cols // 128):
+        cut = slice(block * 128, (block + 1) * 128)
+        top = rows + block * rows_audio
+        summed = jnp.zeros((rows_audio, 128), F32)
+        for j in range(len(parts)):
+            o = v2a_ref[:, cut] if j == 0 else got[j - 1][top : top + rows_audio, 0:128].astype(F32)
+            share = jnp.zeros((rows_audio, 128), F32)
+            for i in range(pair):
+                at = block * pair + i
+                share = jnp.where(lane == i, parts[j][:, at : at + 1], share)
+            summed = summed + share * o
+        out_ref[:, cut] = summed.astype(BF16)
+
+
+def block_of(far, other):
+    mp, sub = index_of("mp"), index_of("sub")
+    return (1 - mp if far else mp) * 2 + (1 - sub if other else sub)
+
+
+def project(block, heads, weights, gain_ref, out, extra=None):
+    (att_ref, a2v_ref, v2a_ref), (ws_ref, wa_ref, wv_ref) = heads, weights
+    rows, rows_audio, wide = att_ref.shape[0], v2a_ref.shape[0], out.shape[1]
+    all_wide = ws_ref.shape[1]
+    narrow = wv_ref.shape[1] * wide // all_wide
+    at = columns(block, wide)
+    term = gain_ref[:, at].astype(F32) * dot(att_ref[...], ws_ref[:, at])
+    gain = gain_ref[:, columns(block + all_wide // wide, wide)].astype(F32)
+    term = term + gain * dot(a2v_ref[...], wa_ref[:, at])
+    audio = dot(v2a_ref[...], wv_ref[:, columns(block, narrow)])
+    fold = wide // narrow
+    short = rows_audio // fold
+    if extra is not None:
+        term = term + extra[0:rows, :].astype(F32)
+    out[0:rows, :] = term.astype(out.dtype)
+    for f in range(fold):
+        piece = audio[f * short : (f + 1) * short]
+        cut = slice(f * narrow, (f + 1) * narrow)
+        if extra is not None:
+            piece = piece + extra[rows : rows + short, cut].astype(F32)
+        out[rows : rows + short, cut] = piece.astype(out.dtype)
+
+
+def first_kernel(hops, head, own_ref, v2a_ref, lse_ref, a2v_ref, ws_ref, wa_ref, wv_ref, gain_ref, *rest):
+    got, (out_ref, self_ref, audio_ref) = rest[: len(hops) - 1], rest[len(hops) - 1 :]
+    merge(hops, head, own_ref, v2a_ref, lse_ref, got, self_ref, audio_ref)
+    project(block_of(True, True), (self_ref, a2v_ref, audio_ref), (ws_ref, wa_ref, wv_ref), gain_ref, out_ref)
+
+
+def near_kernel(*refs):
+    heads, weights, gain_ref, (send_ref, own_ref) = refs[:3], refs[3:6], refs[6], refs[7:]
+    project(block_of(False, True), heads, weights, gain_ref, send_ref)
+    project(block_of(False, False), heads, weights, gain_ref, own_ref)
+
+
+def far_kernel(*refs):
+    heads, weights, gain_ref, extra, out_ref = refs[:3], refs[3:6], refs[6], refs[7], refs[8]
+    project(block_of(True, False), heads, weights, gain_ref, out_ref, extra)
+
+
+def finish_kernel(video_ref, audio_ref, gain_ref, own_ref, core_ref, chip_ref, video_out, audio_out):
+    rows = video_ref.shape[0]
+    rows_audio, narrow = audio_ref.shape
+    term = own_ref[...] + core_ref[...].astype(F32) + chip_ref[...].astype(F32)
+    video_out[...] = (video_ref[...].astype(F32) + term[0:rows]).astype(BF16)
+    fold = video_ref.shape[1] // narrow
+    short = rows_audio // fold
+    for f in range(fold):
+        cut = slice(f * short, (f + 1) * short)
+        piece = term[rows : rows + short, f * narrow : (f + 1) * narrow]
+        audio_out[cut, :] = (audio_ref[cut, :].astype(F32) + gain_ref[cut, :] * piece).astype(BF16)
+
+
+def on_device_heads(
+    video_in,
+    audio_in,
+    q_self,
+    k_self,
+    v_self,
+    q_a2v,
+    k_a2v,
+    v_a2v,
+    q_v2a,
+    k_v2a,
+    v_v2a,
+    wo_self,
+    wo_a2v,
+    wo_v2a,
+    video_gates,
+    audio_gates,
+    video_steps,
+    audio_steps,
+    audio_len,
+    *,
+    n,
+):
+    hops = [0] + list(range(n - 1, 0, -1))
+    rows, cols = q_self.shape
+    rows_audio, cross = q_v2a.shape
+    width = cols // n
+
+    def trade(x, axis, hop, size):
+        return lax.ppermute(x, axis, [(i, i ^ hop) for i in range(size)])
+
+    copies = n * (3 + cross // width) + 2
+    *packed, audio = call(
+        functools.partial(pack_kernel, hops, width),
+        [shape(3 * rows + cross // width * rows_audio, width)] * n + [shape(2 * rows_audio, cross)],
+        (q_self, k_self, v_self, q_v2a, k_a2v, v_a2v),
+        [HBM] * 6,
+        scratch=[pltpu.SemaphoreType.DMA((copies,))],
+    )
+    blocks = packed[:1] + [trade(x, "seq", hop, n) for x, hop in zip(packed[1:], hops[1:])]
+    audios = [audio] + [trade(audio, "seq", hop, n) for hop in hops[1:]]
+
+    late = (video_in, audio_in, wo_self, wo_a2v, wo_v2a)
+    steps = (video_steps.reshape(1, rows), audio_steps.reshape(1, rows_audio))
+    gain, audio_gain, video_own, audio_own, *weights = call(
+        fetch_kernel,
+        [shape(rows, 2 * video_gates.shape[2]), shape(*audio_in.shape, F32)]
+        + [shape(*x.shape) for x in late],
+        (audio_len, video_gates.reshape(NT, -1), *steps, audio_gates, *late),
+        [SMEM, VMEM] + [HBM] * 8,
+        scratch=[pltpu.VMEM(x.shape, x.dtype) for x in (*steps, audio_gates)]
+        + [pltpu.SemaphoreType.DMA((8,))],
+    )
+    back = rows + cross // 128 * rows_audio + rows_audio
+    result = call(
+        functools.partial(attend_kernel, n, DHC),
+        [shape(back, width)] * (n - 1)
+        + [shape(rows, width), shape(rows_audio, cross, F32), shape(rows_audio, 128, F32)],
+        (k_v2a, v_v2a, *blocks),
+        [HBM] * 2 + [VMEM] * n,
+        flops=4 * n * n * rows * rows * width,
+        scratch=[pltpu.VMEM((n * rows, width), BF16)] * 2
+        + [pltpu.VMEM((n * rows_audio, cross), BF16)]
+        + [pltpu.VMEM((rows, cross), BF16)] * 2
+        + [pltpu.SemaphoreType.DMA((2,))],
+    )
+    sends, (own, own_v2a, own_lse) = result[: n - 1], result[n - 1 :]
+    got = [trade(x, "seq", hop, n) for x, hop in zip(sends, hops[1:])]
+    (a2v_att,) = call(
+        functools.partial(attend_audio_kernel, hops, DHC),
+        [shape(rows, cross)],
+        (audio_len, q_a2v, *audios),
+        [SMEM, HBM] + [VMEM] * n,
+        flops=8 * n * rows * rows_audio * cross,
+        scratch=[pltpu.VMEM((n * rows_audio, cross), BF16)] * 2
+        + [pltpu.VMEM((rows, cross), BF16), pltpu.SemaphoreType.DMA((1,))],
+    )
+
+    wide, narrow = video_in.shape[1], audio_in.shape[1]
+    block = (rows + rows_audio * narrow // wide, wide)
+    flops = 2 * rows * (cols + cross) * wide
+    first, self_att, v2a_att = call(
+        functools.partial(first_kernel, hops, DHC),
+        [shape(*block), shape(rows, cols), shape(rows_audio, cross)],
+        (own, own_v2a, own_lse, a2v_att, *weights, gain, *got),
+        flops=flops,
+    )
+    heads = (self_att, a2v_att, v2a_att, *weights, gain)
+    first = trade(first, "sub", 1, 2)
+    second, own_sum = call(near_kernel, [shape(*block), shape(*block, F32)], heads, flops=2 * flops)
+    (far_sum,) = call(far_kernel, [shape(*block)], (*heads, first), flops=flops)
+    chip_sum = trade(far_sum, "mp", 1, 2)
+    core_sum = trade(second, "sub", 1, 2)
+    return call(
+        finish_kernel,
+        [shape(*video_in.shape), shape(*audio_in.shape)],
+        (video_own, audio_own, audio_gain, own_sum, core_sum, chip_sum),
+    )
+
+
+def on_device(n, mp, sub, *arrays):
+    cols, cross = arrays[2].shape[1], arrays[5].shape[1]
+    width = cols // n
+    fits = (
+        n in (2, 4, 8)
+        and (mp, sub) == (2, 2)
+        and width % DHV == 0
+        and cross % width == 0
+        and cross // DHC <= 32
+    )
+    if fits:
+        return on_device_heads(*arrays, n=n)
+    return on_device_gather(*arrays)
+
+
 def solution(mesh):
     in_specs = (
         P(("groups", "seq"), ("mp", "sub")),
@@ -195,5 +595,5 @@
     )
     out_specs = (P(("groups", "seq"), ("mp", "sub")), P(("groups", "seq"), ("mp", "sub")))
     return jax.shard_map(
-        on_device, mesh=mesh, in_specs=in_specs, out_specs=out_specs, check_vma=False
-    )
+        functools.partial(on_device, *(mesh.shape[a] for a in ("seq", "mp", "sub"))), mesh=mesh, in_specs=in_specs, out_specs=out_specs, check_vma=False
+    )

time: 150 us -> 46.1 us (0.31)
  blocking collectives: 88 us -> 0 us
  starting transfers between devices: 0.08 us -> 16.3 us
  between operations: 15.2 us -> 1.39 us
  Pallas kernels: 0 us -> 11.5 us
  matrix products: 10.3 us -> 0 us
  waiting for transfers between devices: 23.5 us -> 15.5 us
  local copies, waits for them, and re-layouts: 7.66 us -> 1.1 us
  other arithmetic: 4.72 us -> 0 us
    all_gather x6 -> x0, blocking collectives: 88 us -> none  [the longest x1 16 us: on_device(): lax.all_gather(k_v2a, 'seq', axis=0, tiled=True)]
    reduce_scatter x2 -> x0, waiting for transfers between devices: 23.5 us -> none  [the longest x1 23.5 us: on_device(): lax.psum_scatter(video_term.astype(jnp.bfloat16), ('mp', 'sub'), scatter_...]
    ppermute x0 -> x12, starting transfers between devices: none -> 16.3 us  [trade(): return lax.ppermute(x, axis, [(i, i ^ hop) for i in range(size)])]
    ppermute x0 -> x12, waiting for transfers between devices: none -> 15.5 us  [trade(): return lax.ppermute(x, axis, [(i, i ^ hop) for i in range(size)])]
    pallas_call x0 -> x8, Pallas kernels: none -> 11.5 us  [call(): pl.pallas_call(kernel, out_shape=tuple(outs), in_specs=specs or [VMEM] *...]
    dot_general x11 -> x0, matrix products: 10.3 us -> none  [the longest x3 2.72 us: update_block(): jnp.einsum('qhd,khd->qhk', q_heads, k_heads, preferred_element_type=jnp.f...]
    all_gather x5 -> x0, local copies, waits for them, and re-layouts: 4.57 us -> none  [the longest x1 2.04 us: on_device(): lax.all_gather(v_self, 'seq', axis=0, tiled=True)]
    convert_element_type x3 -> x0, other arithmetic: 3.11 us -> none  [the longest x1 1.72 us: on_device(): video_out = (video_in.astype(jnp.float32) + video_sum).astype(jnp.bfloat16)]
  transfers between devices with their start and end apart: 2 -> 12, of which waited for: 1 -> 4; matrix products, arithmetic and copies ran while one was open for 8% -> 2% of each run, Pallas kernels for 0% -> 20%
where the time goes in v2:
time: 46.1 us; the launch traced here: 45.8 us
  starting transfers between devices  16.3 us (35%)
  waiting for transfers between devices  15.5 us (34%)
  Pallas kernels  11.5 us (25%)
  between operations  1.39 us (3%)
  local copies, waits for them, and re-layouts  1.1 us (2%)
    ppermute x12, starting transfers between devices, trade(): return lax.ppermute(x, axis, [(i, i ^ hop) for i in range(size)])  16.3 us
    ppermute x12, waiting for transfers between devices, trade(): return lax.ppermute(x, axis, [(i, i ^ hop) for i in range(size)])  15.5 us
    pallas_call x8, Pallas kernels, call(): pl.pallas_call(kernel, out_shape=tuple(outs), in_specs=specs or [VMEM] *...  11.5 us
    unnamed x1, local copies, waits for them, and re-layouts  1.1 us
  transfers between devices with their start and end apart: 12, of which 4 were waited for; matrix products, arithmetic and copies ran while one was open for 2% of the time, Pallas kernels for 20%

profile of v2, /device:TPU:0, one launch (start us, length us, event | category | flops | bytes accessed | tf_op | source)
XLA Modules:
  0.0 45.8 jit_solution(10650429976419158468)
XLA Ops:
  0.6 1.2 %shard_map.195 = (bf16[448,128]{1,0:T(8,128)(2,1)S(1)}, bf16[448,128]{1,0:T(8,128)(2,1)S(1)}, bf16[448,128]{1,0:T(8,128)(2,1)S(1)}, bf16[448,128]{1,0:T(8,128)(2,1)S(1)}, bf16[64,256]{1,0:T(8,128)(2,1)S(1)}) custom-call(bf16[128,512]{1,0:T(8,128)(2,1)} %q_ref.1, bf16[128,512]{1,0:T(8,128)(2,1)} %k_ref.1, bf16[128,512]{1,0:T(8,128)(2,1)} %v_ref.1, ...), custom_call_target="tpu_custom_call" | custom-call | bytes 933888 | tf_op jit(solution)/shard_map/pallas_call | solution.py:191
  1.8 5.1 %collective-permute-start = (bf16[448,128]{1,0:T(8,128)(2,1)S(1)}, bf16[448,128]{1,0:T(8,128)(2,1)S(1)}, u32[]{:S(2)}, u32[]{:S(2)}) collective-permute-start(bf16[448,128]{1,0:T(8,128)(2,1)S(1)} %get-tuple-element.29), channel_id=1, source_target_pairs={{0,12},{4,8},{8,4},{12,0},{1,13},{5,9},{9,5},{13,1},{2,14},{6,10},... | collective-permute-start | bytes 344072 | tf_op jit(solution)/shard_map/ppermute | solution.py:488
  7.0 0.6 %collective-permute-start.2 = (bf16[448,128]{1,0:T(8,128)(2,1)S(1)}, bf16[448,128]{1,0:T(8,128)(2,1)S(1)}, u32[]{:S(2)}, u32[]{:S(2)}) collective-permute-start(bf16[448,128]{1,0:T(8,128)(2,1)S(1)} %get-tuple-element.31), channel_id=1, source_target_pairs={{0,4},{4,0},{8,12},{12,8},{1,5},{5,1},{9,13},{13,9},{2,6},{6,2},{1... | collective-permute-start | bytes 344072 | tf_op jit(solution)/shard_map/ppermute | solution.py:488
  7.6 1.4 %collective-permute-start.5 = (bf16[64,256]{1,0:T(8,128)(2,1)S(1)}, bf16[64,256]{1,0:T(8,128)(2,1)S(1)}, u32[]{:S(2)}, u32[]{:S(2)}) collective-permute-start(bf16[64,256]{1,0:T(8,128)(2,1)S(1)} %get-tuple-element.35.rest_0_), channel_id=1, source_target_pairs={{0,4},{4,0},{8,12},{12,8},{1,5},{5,1},{9,13},{13,9},{2,6},{6,2},{1... | collective-permute-start | bytes 98312 | tf_op jit(solution)/shard_map/ppermute | solution.py:488
  9.0 2.1 %collective-permute-done.rest_1_ = bf16[448,128]{1,0:T(8,128)(2,1)S(1)} collective-permute-done((bf16[448,128]{1,0:T(8,128)(2,1)S(1)}, bf16[448,128]{1,0:T(8,128)(2,1)S(1)}, u32[]{:S(2)}, u32[]{:S(2)}) %collective-permute-start) | collective-permute-done | bytes 114720 | tf_op jit(solution)/shard_map/ppermute | solution.py:488
  11.1 5.6 %collective-permute-done.1.rest_2_ = bf16[448,128]{1,0:T(8,128)(2,1)S(1)} collective-permute-done((bf16[448,128]{1,0:T(8,128)(2,1)S(1)}, bf16[448,128]{1,0:T(8,128)(2,1)S(1)}, u32[]{:S(2)}, u32[]{:S(2)}) %collective-permute-start.1) | collective-permute-done | bytes 114720 | tf_op jit(solution)/shard_map/ppermute | solution.py:488
  16.7 2.6 %shard_map.196 = (bf16[224,128]{1,0:T(8,128)(2,1)S(1)}, bf16[224,128]{1,0:T(8,128)(2,1)S(1)}, bf16[224,128]{1,0:T(8,128)(2,1)S(1)}, bf16[128,128]{1,0:T(8,128)(2...) custom-call(bf16[128,256]{1,0:T(8,128)(2,1)} %kv_hbm.1, bf16[128,256]{1,0:T(8,128)(2,1)} %vv_hbm.1, ...), custom_call_target="tpu_custom_call" | custom-call | flops 134217728 | bytes 843776 | tf_op jit(solution)/shard_map/pallas_call | solution.py:191
  19.3 2.5 %collective-permute-start.6 = (bf16[224,128]{1,0:T(8,128)(2,1)S(1)}, bf16[224,128]{1,0:T(8,128)(2,1)S(1)}, u32[]{:S(2)}, u32[]{:S(2)}) collective-permute-start(bf16[224,128]{1,0:T(8,128)(2,1)S(1)} %get-tuple-element.40), channel_id=1, source_target_pairs={{0,12},{4,8},{8,4},{12,0},{1,13},{5,9},{9,5},{13,1},{2,14},{6,10},... | collective-permute-start | bytes 172040 | tf_op jit(solution)/shard_map/ppermute | solution.py:488
  21.9 0.0 collective-permute-start.7
  21.9 1.9 %collective-permute-start.8 = (bf16[224,128]{1,0:T(8,128)(2,1)S(1)}, bf16[224,128]{1,0:T(8,128)(2,1)S(1)}, u32[]{:S(2)}, u32[]{:S(2)}) collective-permute-start(bf16[224,128]{1,0:T(8,128)(2,1)S(1)} %get-tuple-element.42), channel_id=1, source_target_pairs={{0,4},{4,0},{8,12},{12,8},{1,5},{5,1},{9,13},{13,9},{2,6},{6,2},{1... | collective-permute-start | bytes 172040 | tf_op jit(solution)/shard_map/ppermute | solution.py:488
  23.8 1.0 %collective-permute-start.4 = (bf16[64,256]{1,0:T(8,128)(2,1)S(1)}, bf16[64,256]{1,0:T(8,128)(2,1)S(1)}, u32[]{:S(2)}, u32[]{:S(2)}) collective-permute-start(bf16[64,256]{1,0:T(8,128)(2,1)S(1)} %get-tuple-element.35.rest_0_), channel_id=1, source_target_pairs={{0,8},{4,12},{8,0},{12,4},{1,9},{5,13},{9,1},{13,5},{2,10},{6,14},... | collective-permute-start | bytes 98312 | tf_op jit(solution)/shard_map/ppermute | solution.py:488
  24.8 1.5 %collective-permute-start.3 = (bf16[64,256]{1,0:T(8,128)(2,1)S(1)}, bf16[64,256]{1,0:T(8,128)(2,1)S(1)}, u32[]{:S(2)}, u32[]{:S(2)}) collective-permute-start(bf16[64,256]{1,0:T(8,128)(2,1)S(1)} %get-tuple-element.35.rest_0_), channel_id=1, source_target_pairs={{0,12},{4,8},{8,4},{12,0},{1,13},{5,9},{9,5},{13,1},{2,14},{6,10},... | collective-permute-start | bytes 98312 | tf_op jit(solution)/shard_map/ppermute | solution.py:488
  26.9 1.1 %copy.21 = bf16[2,8,2,4096]{3,1,2,0:T(8,128)(2,1)S(1)} copy(bf16[2,8,2,4096]{3,2,1,0:T(2,128)(2,1)} %bitcast.5) | data formatting | bytes 524288
  28.0 3.3 %shard_map.194 = (bf16[128,8192]{1,0:T(8,128)(2,1)S(1)}, f32[32,512]{1,0:T(8,128)S(1)}, bf16[128,1024]{1,0:T(8,128)(2,1)S(1)}, bf16[32,512]{1,0:T(8,128)(2,1)S(1...) custom-call(s32[1]{0:T(128)S(6)} %copy.22.limit_ref, ...), custom_call_target="tpu_custom_call" | custom-call | bytes 17760900 | tf_op jit(solution)/shard_map/pallas_call | solution.py:191
  31.4 1.9 %shard_map.197.a2v_ref.refs_1_ = bf16[128,256]{1,0:T(8,128)(2,1)S(1)} custom-call(s32[1]{0:T(128)S(6)} %copy.22.limit_ref, bf16[128,256]{1,0:T(8,128)(2,1)} %q_hbm.1, bf16[64,256]{1,0:T(8,128)(2,1)S(1)} %get-tuple-element.35.rest_0_, bf16[64,256]{1,0:T(8,128)(2,1)S(1)} %collective-permute-done.3.rest_1_, bf16[64,256]{1,0:T(8,128)(2,1)S(1)} %collective-permute-done.4.rest_2_, ...), custom_call_target="tpu_custom_call" | custom-call | flops 33554432 | bytes 262148 | tf_op jit(solution)/shard_map/pallas_call | solution.py:191
  33.3 0.4 shard_map.198
  33.8 0.1 collective-permute-start.10
  33.9 0.7 %shard_map.199 = (bf16[144,1024]{1,0:T(8,128)(2,1)S(1)}, f32[144,1024]{1,0:T(8,128)S(1)}) custom-call(bf16[128,512]{1,0:T(8,128)(2,1)S(1)} %get-tuple-element.43.refs_0_, bf16[128,256]{1,0:T(8,128)(2,1)S(1)} %shard_map.197.a2v_ref.refs_1_, bf16[32,256]{1,0:T(8,128)(2,1)S(1)} %get-tuple-element.44.refs_2_, ...), custom_call_target="tpu_custom_call" | custom-call | flops 402653184 | bytes 10534912 | tf_op jit(solution)/shard_map/pallas_call | solution.py:191
  34.6 0.5 %collective-permute-start.9 = (bf16[144,1024]{1,0:T(8,128)(2,1)S(1)}, bf16[144,1024]{1,0:T(8,128)(2,1)S(1)}, u32[]{:S(2)}, u32[]{:S(2)}) collective-permute-start(bf16[144,1024]{1,0:T(8,128)(2,1)S(1)} %get-tuple-element.46), channel_id=1, source_target_pairs={{0,1},{1,0},{2,3},{3,2},{4,5},{5,4},{6,7},{7,6},{8,9},{9,8},{10,11... | collective-permute-start | bytes 884744 | tf_op jit(solution)/shard_map/ppermute | solution.py:488
  35.1 0.3 collective-permute-done.10.refs_7_
  35.4 0.4 shard_map.200
  35.9 1.6 %collective-permute-start.11 = (bf16[144,1024]{1,0:T(8,128)(2,1)S(1)}, bf16[144,1024]{1,0:T(8,128)(2,1)S(1)}, u32[]{:S(2)}, u32[]{:S(2)}) collective-permute-start(bf16[144,1024]{1,0:T(8,128)(2,1)S(1)} %shard_map.200), channel_id=1, source_target_pairs={{0,2},{2,0},{1,3},{3,1},{4,6},{6,4},{5,7},{7,5},{8,10},{10,8},{9,1... | collective-permute-start | bytes 884744 | tf_op jit(solution)/shard_map/ppermute | solution.py:488
  37.4 7.6 %collective-permute-done.11.chip_ref = bf16[144,1024]{1,0:T(8,128)(2,1)S(1)} collective-permute-done((bf16[144,1024]{1,0:T(8,128)(2,1)S(1)}, bf16[144,1024]{1,0:T(8,128)(2,1)S(1)}, u32[]{:S(2)}, u32[]{:S(2)}) %collective-permute-start.11) | collective-permute-done | bytes 294944 | tf_op jit(solution)/shard_map/ppermute | solution.py:488
  45.0 0.8 %shard_map.201 = (bf16[128,1024]{1,0:T(8,128)(2,1)}, bf16[32,512]{1,0:T(8,128)(2,1)}) custom-call(bf16[128,1024]{1,0:T(8,128)(2,1)S(1)} %get-tuple-element.25.video_ref, bf16[32,512]{1,0:T(8,128)(2,1)S(1)} %get-tuple-element.26.audio_ref, f32[32,512]{1,0:T(8,128)S(1)} %get-tuple-element.27.gain_ref, f32[144,1024]{1,0:T(8,128)S(1)} %get-tuple-element.45.own_ref, ...), custom_call_target="tpu_custom_call" | custom-call | bytes 1835008 | tf_op jit(solution)/shard_map/pallas_call | solution.py:191
  (9 shorter events, 0.0 us)
Async XLA Ops:
  1.8 9.2 %collective-permute-start = (bf16[448,128]{1,0:T(8,128)(2,1)S(1)}, bf16[448,128]{1,0:T(8,128)(2,1)S(1)}, u32[]{:S(2)}, u32[]{:S(2)}) collective-permute-start(bf16[448,128]{1,0:T(8,128)(2,1)S(1)} %get-tuple-element.29), channel_id=1, source_target_pairs={{0,12},{4,8},{8,4},{12,0},{1,13},{5,9},{9,5},{13,1},{2,14},{6,10},... | collective-permute-start | bytes 344072 | tf_op jit(solution)/shard_map/ppermute | solution.py:488
  7.0 9.7 %collective-permute-start.1 = (bf16[448,128]{1,0:T(8,128)(2,1)S(1)}, bf16[448,128]{1,0:T(8,128)(2,1)S(1)}, u32[]{:S(2)}, u32[]{:S(2)}) collective-permute-start(bf16[448,128]{1,0:T(8,128)(2,1)S(1)} %get-tuple-element.30), channel_id=1, source_target_pairs={{0,8},{4,12},{8,0},{12,4},{1,9},{5,13},{9,1},{13,5},{2,10},{6,14},... | collective-permute-start | bytes 344072 | tf_op jit(solution)/shard_map/ppermute | solution.py:488
  7.0 9.7 %collective-permute-start.2 = (bf16[448,128]{1,0:T(8,128)(2,1)S(1)}, bf16[448,128]{1,0:T(8,128)(2,1)S(1)}, u32[]{:S(2)}, u32[]{:S(2)}) collective-permute-start(bf16[448,128]{1,0:T(8,128)(2,1)S(1)} %get-tuple-element.31), channel_id=1, source_target_pairs={{0,4},{4,0},{8,12},{12,8},{1,5},{5,1},{9,13},{13,9},{2,6},{6,2},{1... | collective-permute-start | bytes 344072 | tf_op jit(solution)/shard_map/ppermute | solution.py:488
  7.6 17.2 %collective-permute-start.5 = (bf16[64,256]{1,0:T(8,128)(2,1)S(1)}, bf16[64,256]{1,0:T(8,128)(2,1)S(1)}, u32[]{:S(2)}, u32[]{:S(2)}) collective-permute-start(bf16[64,256]{1,0:T(8,128)(2,1)S(1)} %get-tuple-element.35.rest_0_), channel_id=1, source_target_pairs={{0,4},{4,0},{8,12},{12,8},{1,5},{5,1},{9,13},{13,9},{2,6},{6,2},{1... | collective-permute-start | bytes 98312 | tf_op jit(solution)/shard_map/ppermute | solution.py:488
  19.3 14.0 %collective-permute-start.6 = (bf16[224,128]{1,0:T(8,128)(2,1)S(1)}, bf16[224,128]{1,0:T(8,128)(2,1)S(1)}, u32[]{:S(2)}, u32[]{:S(2)}) collective-permute-start(bf16[224,128]{1,0:T(8,128)(2,1)S(1)} %get-tuple-element.40), channel_id=1, source_target_pairs={{0,12},{4,8},{8,4},{12,0},{1,13},{5,9},{9,5},{13,1},{2,14},{6,10},... | collective-permute-start | bytes 172040 | tf_op jit(solution)/shard_map/ppermute | solution.py:488
  21.9 11.5 %collective-permute-start.7 = (bf16[224,128]{1,0:T(8,128)(2,1)S(1)}, bf16[224,128]{1,0:T(8,128)(2,1)S(1)}, u32[]{:S(2)}, u32[]{:S(2)}) collective-permute-start(bf16[224,128]{1,0:T(8,128)(2,1)S(1)} %get-tuple-element.41), channel_id=1, source_target_pairs={{0,8},{4,12},{8,0},{12,4},{1,9},{5,13},{9,1},{13,5},{2,10},{6,14},... | collective-permute-start | bytes 172040 | tf_op jit(solution)/shard_map/ppermute | solution.py:488
  21.9 11.5 %collective-permute-start.8 = (bf16[224,128]{1,0:T(8,128)(2,1)S(1)}, bf16[224,128]{1,0:T(8,128)(2,1)S(1)}, u32[]{:S(2)}, u32[]{:S(2)}) collective-permute-start(bf16[224,128]{1,0:T(8,128)(2,1)S(1)} %get-tuple-element.42), channel_id=1, source_target_pairs={{0,4},{4,0},{8,12},{12,8},{1,5},{5,1},{9,13},{13,9},{2,6},{6,2},{1... | collective-permute-start | bytes 172040 | tf_op jit(solution)/shard_map/ppermute | solution.py:488
  23.8 7.6 %collective-permute-start.4 = (bf16[64,256]{1,0:T(8,128)(2,1)S(1)}, bf16[64,256]{1,0:T(8,128)(2,1)S(1)}, u32[]{:S(2)}, u32[]{:S(2)}) collective-permute-start(bf16[64,256]{1,0:T(8,128)(2,1)S(1)} %get-tuple-element.35.rest_0_), channel_id=1, source_target_pairs={{0,8},{4,12},{8,0},{12,4},{1,9},{5,13},{9,1},{13,5},{2,10},{6,14},... | collective-permute-start | bytes 98312 | tf_op jit(solution)/shard_map/ppermute | solution.py:488
  24.8 6.6 %collective-permute-start.3 = (bf16[64,256]{1,0:T(8,128)(2,1)S(1)}, bf16[64,256]{1,0:T(8,128)(2,1)S(1)}, u32[]{:S(2)}, u32[]{:S(2)}) collective-permute-start(bf16[64,256]{1,0:T(8,128)(2,1)S(1)} %get-tuple-element.35.rest_0_), channel_id=1, source_target_pairs={{0,12},{4,8},{8,4},{12,0},{1,13},{5,9},{9,5},{13,1},{2,14},{6,10},... | collective-permute-start | bytes 98312 | tf_op jit(solution)/shard_map/ppermute | solution.py:488
  33.8 1.6 %collective-permute-start.10 = (bf16[144,1024]{1,0:T(8,128)(2,1)S(1)}, bf16[144,1024]{1,0:T(8,128)(2,1)S(1)}, u32[]{:S(2)}, u32[]{:S(2)}) collective-permute-start(bf16[144,1024]{1,0:T(8,128)(2,1)S(1)} %get-tuple-element.47), channel_id=1, source_target_pairs={{0,1},{1,0},{2,3},{3,2},{4,5},{5,4},{6,7},{7,6},{8,9},{9,8},{10,11... | collective-permute-start | bytes 884744 | tf_op jit(solution)/shard_map/ppermute | solution.py:488
  34.6 2.8 %collective-permute-start.9 = (bf16[144,1024]{1,0:T(8,128)(2,1)S(1)}, bf16[144,1024]{1,0:T(8,128)(2,1)S(1)}, u32[]{:S(2)}, u32[]{:S(2)}) collective-permute-start(bf16[144,1024]{1,0:T(8,128)(2,1)S(1)} %get-tuple-element.46), channel_id=1, source_target_pairs={{0,1},{1,0},{2,3},{3,2},{4,5},{5,4},{6,7},{7,6},{8,9},{9,8},{10,11... | collective-permute-start | bytes 884744 | tf_op jit(solution)/shard_map/ppermute | solution.py:488
  35.9 9.1 %collective-permute-start.11 = (bf16[144,1024]{1,0:T(8,128)(2,1)S(1)}, bf16[144,1024]{1,0:T(8,128)(2,1)S(1)}, u32[]{:S(2)}, u32[]{:S(2)}) collective-permute-start(bf16[144,1024]{1,0:T(8,128)(2,1)S(1)} %shard_map.200), channel_id=1, source_target_pairs={{0,2},{2,0},{1,3},{3,1},{4,6},{6,4},{5,7},{7,5},{8,10},{10,8},{9,1... | collective-permute-start | bytes 884744 | tf_op jit(solution)/shard_map/ppermute | solution.py:488

commit v3 on v2

--- a/solution.py
+++ b/solution.py
@@ -254,8 +254,9 @@
 
 
 def fetch_kernel(limit_ref, vg_ref, *rest):
-    loads, gain_ref, audio_ref = rest[:8], rest[8], rest[9]
-    fetched, (vs_ref, as_ref, ag_ref, sems) = rest[10:15], rest[15:]
+    count = (len(rest) - 9) // 2
+    loads, gain_ref, audio_ref = rest[: count + 3], rest[count + 3], rest[count + 4]
+    fetched, (vs_ref, as_ref, ag_ref, sems) = rest[count + 5 : -4], rest[-4:]
     copies = [
         pltpu.make_async_copy(src, dst, sems.at[i])
         for i, (src, dst) in enumerate(zip(loads, (vs_ref, as_ref, ag_ref, *fetched)))
@@ -285,12 +286,9 @@
     return peak, weights, jnp.sum(weights, axis=1, keepdims=True)
 
 
-def attend_kernel(n, head, kv_hbm, vv_hbm, *rest):
+def attend_kernel(n, head, kv_ref, vv_ref, *rest):
     blocks, sends, (own_ref, own_v2a_ref, own_lse_ref) = rest[:n], rest[n : 2 * n - 1], rest[2 * n - 1 : 2 * n + 2]
-    ks, vs, qas, kv_ref, vv_ref, sems = rest[2 * n + 2 :]
-    copies = [pltpu.make_async_copy(kv_hbm, kv_ref, sems.at[0]), pltpu.make_async_copy(vv_hbm, vv_ref, sems.at[1])]
-    for copy in copies:
-        copy.start()
+    ks, vs, qas = rest[2 * n + 2 :]
     rows, cols = kv_ref.shape
     width = blocks[0].shape[1]
     rows_audio = qas.shape[0] // n
@@ -308,8 +306,6 @@
             o = dot(p.astype(BF16), vs[:, cut]) / total
             dst = own_ref if j == 0 else sends[j - 1].at[0:rows, :]
             dst[:, cut] = o.astype(BF16)
-    for copy in copies:
-        copy.wait()
     scale = 1.0 / math.sqrt(head)
     pair = 128 // head
     lane = lax.broadcasted_iota(jnp.int32, (1, 128), 1) // head
@@ -339,11 +335,9 @@
         dst[top : top + rows_audio, 0:128] = packed.astype(BF16)
 
 
-def attend_audio_kernel(hops, head, limit_ref, q_hbm, *rest):
+def attend_audio_kernel(hops, head, limit_ref, q_ref, *rest):
     n = len(hops)
-    blocks, out_ref, ks, vs, q_ref, sem = rest[:n], *rest[n:]
-    copy = pltpu.make_async_copy(q_hbm, q_ref, sem.at[0])
-    copy.start()
+    blocks, out_ref, ks, vs = rest[:n], *rest[n:]
     rows_audio = blocks[0].shape[0] // 2
     keys = n * rows_audio
     column = lax.broadcasted_iota(jnp.int32, (1, keys), 1)
@@ -355,7 +349,6 @@
         shift = ((me ^ hop) - j) * rows_audio
         position = jnp.where(column // rows_audio == j, column + shift, position)
     allowed = position < limit_ref[0]
-    copy.wait()
     scale = 1.0 / math.sqrt(head)
     lane = lax.broadcasted_iota(jnp.int32, (1, 128), 1) // head
     for block in range(q_ref.shape[1] // 128):
@@ -368,15 +361,12 @@
         out_ref[:, cut] = both.astype(BF16)
 
 
-def merge(hops, head, own_ref, v2a_ref, lse_ref, got, self_ref, out_ref):
-    rows, width = own_ref.shape
+def merge_audio(head, top, v2a_ref, lse_ref, got, out_ref):
     rows_audio, cols = v2a_ref.shape
-    me = index_of("seq")
-    lses, top = [lse_ref[...]], rows + cols // 128 * rows_audio
-    self_ref[:, columns(me, width)] = own_ref[...]
-    for hop, ref in zip(hops[1:], got):
-        self_ref[:, columns(me ^ hop, width)] = ref[0:rows, :]
-        packed = ref[top : top + rows_audio, 0:128].astype(F32)
+    lses = [lse_ref[...]]
+    for ref in got:
+        at = top + cols // 128 * rows_audio
+        packed = ref[at : at + rows_audio, 0:128].astype(F32)
         lses.append(packed + pltpu.roll(packed, 96, 1) + pltpu.roll(packed, 64, 1))
     peak = functools.reduce(jnp.maximum, lses)
     parts = [jnp.exp2(x - peak) for x in lses]
@@ -386,14 +376,14 @@
     lane = lax.broadcasted_iota(jnp.int32, (1, 128), 1) // head
     for block in range(cols // 128):
         cut = slice(block * 128, (block + 1) * 128)
-        top = rows + block * rows_audio
+        at = top + block * rows_audio
         summed = jnp.zeros((rows_audio, 128), F32)
         for j in range(len(parts)):
-            o = v2a_ref[:, cut] if j == 0 else got[j - 1][top : top + rows_audio, 0:128].astype(F32)
+            o = v2a_ref[:, cut] if j == 0 else got[j - 1][at : at + rows_audio, 0:128].astype(F32)
             share = jnp.zeros((rows_audio, 128), F32)
             for i in range(pair):
-                at = block * pair + i
-                share = jnp.where(lane == i, parts[j][:, at : at + 1], share)
+                column = block * pair + i
+                share = jnp.where(lane == i, parts[j][:, column : column + 1], share)
             summed = summed + share * o
         out_ref[:, cut] = summed.astype(BF16)
 
@@ -403,57 +393,70 @@
     return (1 - mp if far else mp) * 2 + (1 - sub if other else sub)
 
 
-def project(block, heads, weights, gain_ref, out, extra=None):
-    (att_ref, a2v_ref, v2a_ref), (ws_ref, wa_ref, wv_ref) = heads, weights
-    rows, rows_audio, wide = att_ref.shape[0], v2a_ref.shape[0], out.shape[1]
-    all_wide = ws_ref.shape[1]
-    narrow = wv_ref.shape[1] * wide // all_wide
-    at = columns(block, wide)
+def project(block, half, heads, weights, gain_ref):
+    (att_ref, a2v_ref), (ws_ref, wa_ref) = heads, weights
+    wide = ws_ref.shape[1]
+    cut = wide // 8
+    at = columns(block * 2 + half, cut)
     term = gain_ref[:, at].astype(F32) * dot(att_ref[...], ws_ref[:, at])
-    gain = gain_ref[:, columns(block + all_wide // wide, wide)].astype(F32)
-    term = term + gain * dot(a2v_ref[...], wa_ref[:, at])
-    audio = dot(v2a_ref[...], wv_ref[:, columns(block, narrow)])
-    fold = wide // narrow
-    short = rows_audio // fold
-    if extra is not None:
-        term = term + extra[0:rows, :].astype(F32)
-    out[0:rows, :] = term.astype(out.dtype)
-    for f in range(fold):
-        piece = audio[f * short : (f + 1) * short]
-        cut = slice(f * narrow, (f + 1) * narrow)
-        if extra is not None:
-            piece = piece + extra[rows : rows + short, cut].astype(F32)
-        out[rows : rows + short, cut] = piece.astype(out.dtype)
-
-
-def first_kernel(hops, head, own_ref, v2a_ref, lse_ref, a2v_ref, ws_ref, wa_ref, wv_ref, gain_ref, *rest):
-    got, (out_ref, self_ref, audio_ref) = rest[: len(hops) - 1], rest[len(hops) - 1 :]
-    merge(hops, head, own_ref, v2a_ref, lse_ref, got, self_ref, audio_ref)
-    project(block_of(True, True), (self_ref, a2v_ref, audio_ref), (ws_ref, wa_ref, wv_ref), gain_ref, out_ref)
-
-
-def near_kernel(*refs):
-    heads, weights, gain_ref, (send_ref, own_ref) = refs[:3], refs[3:6], refs[6], refs[7:]
-    project(block_of(False, True), heads, weights, gain_ref, send_ref)
-    project(block_of(False, False), heads, weights, gain_ref, own_ref)
-
-
-def far_kernel(*refs):
-    heads, weights, gain_ref, extra, out_ref = refs[:3], refs[3:6], refs[6], refs[7], refs[8]
-    project(block_of(True, False), heads, weights, gain_ref, out_ref, extra)
-
-
-def finish_kernel(video_ref, audio_ref, gain_ref, own_ref, core_ref, chip_ref, video_out, audio_out):
+    gain = gain_ref[:, columns(block * 2 + half + 8, cut)].astype(F32)
+    return term + gain * dot(a2v_ref[...], wa_ref[:, at])
+
+
+def project_audio(block, v2a_ref, wv_ref):
+    return dot(v2a_ref[...], wv_ref[:, columns(block, wv_ref.shape[1] // 4)])
+
+
+def first_kernel(hops, own_ref, a2v_ref, ws_ref, wa_ref, gain_ref, *rest):
+    got, (self_ref, out_ref) = rest[: len(hops) - 1], rest[len(hops) - 1 :]
+    rows, width = own_ref.shape
+    me = index_of("seq")
+    self_ref[:, columns(me, width)] = own_ref[...]
+    for hop, ref in zip(hops[1:], got):
+        self_ref[:, columns(me ^ hop, width)] = ref[0:rows, :]
+    out_ref[...] = project(block_of(True, True), 0, (self_ref, a2v_ref), (ws_ref, wa_ref), gain_ref).astype(BF16)
+
+
+def second_kernel(head, self_ref, a2v_ref, ws_ref, wa_ref, wv_ref, gain_ref, v2a_ref, lse_ref, *rest):
+    got, (out_ref, audio_ref) = rest[:-2], rest[-2:]
+    rows = self_ref.shape[0]
+    block = block_of(True, True)
+    out_ref[0:rows, :] = project(block, 1, (self_ref, a2v_ref), (ws_ref, wa_ref), gain_ref).astype(BF16)
+    merge_audio(head, rows, v2a_ref, lse_ref, got, audio_ref)
+    out_ref[rows:, :] = project_audio(block, audio_ref, wv_ref).astype(BF16)
+
+
+def near_kernel(self_ref, a2v_ref, audio_ref, ws_ref, wa_ref, wv_ref, gain_ref, send_ref, own_ref):
+    rows = self_ref.shape[0]
+    for out, other in ((send_ref, True), (own_ref, False)):
+        block = block_of(False, other)
+        for half in range(2):
+            term = project(block, half, (self_ref, a2v_ref), (ws_ref, wa_ref), gain_ref)
+            out[half * rows : (half + 1) * rows, :] = term.astype(out.dtype)
+        out[2 * rows :, :] = project_audio(block, audio_ref, wv_ref).astype(out.dtype)
+
+
+def far_kernel(half, self_ref, a2v_ref, ws_ref, wa_ref, gain_ref, extra_ref, *rest):
+    rows, out_ref = self_ref.shape[0], rest[-1]
+    block = block_of(True, False)
+    term = project(block, half, (self_ref, a2v_ref), (ws_ref, wa_ref), gain_ref)
+    out_ref[0:rows, :] = (term + extra_ref[0:rows, :].astype(F32)).astype(BF16)
+    if half == 1:
+        audio_ref, wv_ref = rest[:2]
+        term = project_audio(block, audio_ref, wv_ref)
+        out_ref[rows:, :] = (term + extra_ref[rows:, :].astype(F32)).astype(BF16)
+
+
+def finish_kernel(video_ref, audio_ref, gain_ref, own_ref, core_ref, low_ref, high_ref, video_out, audio_out):
     rows = video_ref.shape[0]
-    rows_audio, narrow = audio_ref.shape
-    term = own_ref[...] + core_ref[...].astype(F32) + chip_ref[...].astype(F32)
-    video_out[...] = (video_ref[...].astype(F32) + term[0:rows]).astype(BF16)
-    fold = video_ref.shape[1] // narrow
-    short = rows_audio // fold
-    for f in range(fold):
-        cut = slice(f * short, (f + 1) * short)
-        piece = term[rows : rows + short, f * narrow : (f + 1) * narrow]
-        audio_out[cut, :] = (audio_ref[cut, :].astype(F32) + gain_ref[cut, :] * piece).astype(BF16)
+    cut = video_ref.shape[1] // 2
+    near = own_ref[...] + core_ref[...].astype(F32)
+    for half, ref in enumerate((low_ref, high_ref)):
+        at = slice(half * cut, (half + 1) * cut)
+        term = near[half * rows : (half + 1) * rows] + ref[0:rows, :].astype(F32)
+        video_out[:, at] = (video_ref[:, at].astype(F32) + term).astype(BF16)
+    term = near[2 * rows :] + high_ref[rows:, :].astype(F32)
+    audio_out[...] = (audio_ref[...].astype(F32) + gain_ref[...] * term).astype(BF16)
 
 
 def on_device_heads(
@@ -479,7 +482,7 @@
     *,
     n,
 ):
-    hops = [0] + list(range(n - 1, 0, -1))
+    hops = [0] + order_of(n)
     rows, cols = q_self.shape
     rows_audio, cross = q_v2a.shape
     width = cols // n
@@ -498,61 +501,78 @@
     blocks = packed[:1] + [trade(x, "seq", hop, n) for x, hop in zip(packed[1:], hops[1:])]
     audios = [audio] + [trade(audio, "seq", hop, n) for hop in hops[1:]]
 
-    late = (video_in, audio_in, wo_self, wo_a2v, wo_v2a)
+    late = (k_v2a, v_v2a, q_a2v, wo_self, wo_a2v, wo_v2a, video_in, audio_in)
     steps = (video_steps.reshape(1, rows), audio_steps.reshape(1, rows_audio))
-    gain, audio_gain, video_own, audio_own, *weights = call(
+    gain, audio_gain, k_own, v_own, q_own, ws, wa, wv, video_own, audio_own = call(
         fetch_kernel,
         [shape(rows, 2 * video_gates.shape[2]), shape(*audio_in.shape, F32)]
         + [shape(*x.shape) for x in late],
         (audio_len, video_gates.reshape(NT, -1), *steps, audio_gates, *late),
-        [SMEM, VMEM] + [HBM] * 8,
+        [SMEM, VMEM] + [HBM] * (3 + len(late)),
         scratch=[pltpu.VMEM(x.shape, x.dtype) for x in (*steps, audio_gates)]
-        + [pltpu.SemaphoreType.DMA((8,))],
+        + [pltpu.SemaphoreType.DMA((3 + len(late),))],
     )
     back = rows + cross // 128 * rows_audio + rows_audio
     result = call(
         functools.partial(attend_kernel, n, DHC),
         [shape(back, width)] * (n - 1)
         + [shape(rows, width), shape(rows_audio, cross, F32), shape(rows_audio, 128, F32)],
-        (k_v2a, v_v2a, *blocks),
-        [HBM] * 2 + [VMEM] * n,
+        (k_own, v_own, *blocks),
         flops=4 * n * n * rows * rows * width,
-        scratch=[pltpu.VMEM((n * rows, width), BF16)] * 2
-        + [pltpu.VMEM((n * rows_audio, cross), BF16)]
-        + [pltpu.VMEM((rows, cross), BF16)] * 2
-        + [pltpu.SemaphoreType.DMA((2,))],
+        scratch=[pltpu.VMEM((n * rows, width), BF16)] * 2 + [pltpu.VMEM((n * rows_audio, cross), BF16)],
     )
     sends, (own, own_v2a, own_lse) = result[: n - 1], result[n - 1 :]
     got = [trade(x, "seq", hop, n) for x, hop in zip(sends, hops[1:])]
     (a2v_att,) = call(
         functools.partial(attend_audio_kernel, hops, DHC),
         [shape(rows, cross)],
-        (audio_len, q_a2v, *audios),
-        [SMEM, HBM] + [VMEM] * n,
+        (audio_len, q_own, *audios),
+        [SMEM] + [VMEM] * (n + 1),
         flops=8 * n * rows * rows_audio * cross,
-        scratch=[pltpu.VMEM((n * rows_audio, cross), BF16)] * 2
-        + [pltpu.VMEM((rows, cross), BF16), pltpu.SemaphoreType.DMA((1,))],
-    )
-
-    wide, narrow = video_in.shape[1], audio_in.shape[1]
-    block = (rows + rows_audio * narrow // wide, wide)
-    flops = 2 * rows * (cols + cross) * wide
-    first, self_att, v2a_att = call(
-        functools.partial(first_kernel, hops, DHC),
-        [shape(*block), shape(rows, cols), shape(rows_audio, cross)],
-        (own, own_v2a, own_lse, a2v_att, *weights, gain, *got),
+        scratch=[pltpu.VMEM((n * rows_audio, cross), BF16)] * 2,
+    )
+
+    half = video_in.shape[1] // 2
+    flops = 2 * rows * (cols + cross) * half
+    self_att, first = call(
+        functools.partial(first_kernel, hops),
+        [shape(rows, cols), shape(rows, half)],
+        (own, a2v_att, ws, wa, gain, *got),
         flops=flops,
     )
-    heads = (self_att, a2v_att, v2a_att, *weights, gain)
     first = trade(first, "sub", 1, 2)
-    second, own_sum = call(near_kernel, [shape(*block), shape(*block, F32)], heads, flops=2 * flops)
-    (far_sum,) = call(far_kernel, [shape(*block)], (*heads, first), flops=flops)
-    chip_sum = trade(far_sum, "mp", 1, 2)
-    core_sum = trade(second, "sub", 1, 2)
+    second, v2a_att = call(
+        functools.partial(second_kernel, DHC),
+        [shape(rows + rows_audio, half), shape(rows_audio, cross)],
+        (self_att, a2v_att, ws, wa, wv, gain, own_v2a, own_lse, *got),
+        flops=flops,
+    )
+    second = trade(second, "sub", 1, 2)
+    near, own_sum = call(
+        near_kernel,
+        [shape(2 * rows + rows_audio, half), shape(2 * rows + rows_audio, half, F32)],
+        (self_att, a2v_att, v2a_att, ws, wa, wv, gain),
+        flops=4 * flops,
+    )
+    (low,) = call(
+        functools.partial(far_kernel, 0),
+        [shape(rows, half)],
+        (self_att, a2v_att, ws, wa, gain, first),
+        flops=flops,
+    )
+    low = trade(low, "mp", 1, 2)
+    (high,) = call(
+        functools.partial(far_kernel, 1),
+        [shape(rows + rows_audio, half)],
+        (self_att, a2v_att, ws, wa, gain, second, v2a_att, wv),
+        flops=flops,
+    )
+    high = trade(high, "mp", 1, 2)
+    near = trade(near, "sub", 1, 2)
     return call(
         finish_kernel,
         [shape(*video_in.shape), shape(*audio_in.shape)],
-        (video_own, audio_own, audio_gain, own_sum, core_sum, chip_sum),
+        (video_own, audio_own, audio_gain, own_sum, near, low, high),
     )
 
 
@@ -565,10 +585,15 @@
         and width % DHV == 0
         and cross % width == 0
         and cross // DHC <= 32
+        and arrays[0].shape[1] == 2 * arrays[1].shape[1]
     )
     if fits:
         return on_device_heads(*arrays, n=n)
     return on_device_gather(*arrays)
+
+
+def order_of(n):
+    return list(range(n // 2, n)) + list(range(n // 2 - 1, 0, -1))
 
 
 def solution(mesh):

time: 46.1 us -> 44 us (0.954)
  waiting for transfers between devices: 15.5 us -> 12.1 us
  starting transfers between devices: 16.3 us -> 18.6 us
  Pallas kernels: 11.5 us -> 10.6 us
    ppermute x12 -> x14, waiting for transfers between devices: 15.5 us -> 12.1 us  [trade(): return lax.ppermute(x, axis, [(i, i ^ hop) for i in range(size)])]
    ppermute x12 -> x14, starting transfers between devices: 16.3 us -> 18.6 us  [trade(): return lax.ppermute(x, axis, [(i, i ^ hop) for i in range(size)])]
    pallas_call x8 -> x10, Pallas kernels: 11.5 us -> 10.6 us  [call(): pl.pallas_call(kernel, out_shape=tuple(outs), in_specs=specs or [VMEM] *...]
  transfers between devices with their start and end apart: 12 -> 14, of which waited for: 4 -> 5; matrix products, arithmetic and copies ran while one was open for 2% -> 3% of each run, Pallas kernels for 20% -> 18%
where the time goes in v3:
time: 44 us; the launch traced here: 43.7 us
  starting transfers between devices  18.6 us (42%)
  waiting for transfers between devices  12.1 us (28%)
  Pallas kernels  10.6 us (24%)
  between operations  1.38 us (3%)
  local copies, waits for them, and re-layouts  1.1 us (3%)
    ppermute x14, starting transfers between devices, trade(): return lax.ppermute(x, axis, [(i, i ^ hop) for i in range(size)])  18.6 us
    ppermute x14, waiting for transfers between devices, trade(): return lax.ppermute(x, axis, [(i, i ^ hop) for i in range(size)])  12.1 us
    pallas_call x10, Pallas kernels, call(): pl.pallas_call(kernel, out_shape=tuple(outs), in_specs=specs or [VMEM] *...  10.6 us
    unnamed x1, local copies, waits for them, and re-layouts  1.1 us
  transfers between devices with their start and end apart: 14, of which 5 were waited for; matrix products, arithmetic and copies ran while one was open for 3% of the time, Pallas kernels for 18%

profile of v3, /device:TPU:0, one launch (start us, length us, event | category | flops | bytes accessed | tf_op | source)
XLA Modules:
  0.0 43.7 jit_solution(13517801117603203498)
XLA Ops:
  0.6 1.2 %shard_map.195 = (bf16[448,128]{1,0:T(8,128)(2,1)S(1)}, bf16[448,128]{1,0:T(8,128)(2,1)S(1)}, bf16[448,128]{1,0:T(8,128)(2,1)S(1)}, bf16[448,128]{1,0:T(8,128)(2,1)S(1)}, bf16[64,256]{1,0:T(8,128)(2,1)S(1)}) custom-call(bf16[128,512]{1,0:T(8,128)(2,1)} %q_ref.1, bf16[128,512]{1,0:T(8,128)(2,1)} %k_ref.1, bf16[128,512]{1,0:T(8,128)(2,1)} %v_ref.1, ...), custom_call_target="tpu_custom_call" | custom-call | bytes 933888 | tf_op jit(solution)/shard_map/pallas_call | solution.py:191
  1.8 4.1 %collective-permute-start = (bf16[448,128]{1,0:T(8,128)(2,1)S(1)}, bf16[448,128]{1,0:T(8,128)(2,1)S(1)}, u32[]{:S(2)}, u32[]{:S(2)}) collective-permute-start(bf16[448,128]{1,0:T(8,128)(2,1)S(1)} %get-tuple-element.35), channel_id=1, source_target_pairs={{0,8},{4,12},{8,0},{12,4},{1,9},{5,13},{9,1},{13,5},{2,10},{6,14},... | collective-permute-start | bytes 344072 | tf_op jit(solution)/shard_map/ppermute | solution.py:491
  6.0 1.3 %collective-permute-start.1 = (bf16[448,128]{1,0:T(8,128)(2,1)S(1)}, bf16[448,128]{1,0:T(8,128)(2,1)S(1)}, u32[]{:S(2)}, u32[]{:S(2)}) collective-permute-start(bf16[448,128]{1,0:T(8,128)(2,1)S(1)} %get-tuple-element.36), channel_id=1, source_target_pairs={{0,12},{4,8},{8,4},{12,0},{1,13},{5,9},{9,5},{13,1},{2,14},{6,10},... | collective-permute-start | bytes 344072 | tf_op jit(solution)/shard_map/ppermute | solution.py:491
  7.6 1.8 %collective-permute-start.5 = (bf16[64,256]{1,0:T(8,128)(2,1)S(1)}, bf16[64,256]{1,0:T(8,128)(2,1)S(1)}, u32[]{:S(2)}, u32[]{:S(2)}) collective-permute-start(bf16[64,256]{1,0:T(8,128)(2,1)S(1)} %get-tuple-element.40.rest_0_), channel_id=1, source_target_pairs={{0,4},{4,0},{8,12},{12,8},{1,5},{5,1},{9,13},{13,9},{2,6},{6,2},{1... | collective-permute-start | bytes 98312 | tf_op jit(solution)/shard_map/ppermute | solution.py:491
  10.0 1.1 %copy.21 = bf16[2,8,2,4096]{3,1,2,0:T(8,128)(2,1)S(1)} copy(bf16[2,8,2,4096]{3,2,1,0:T(2,128)(2,1)} %bitcast.5) | data formatting | bytes 524288
  11.1 3.4 %shard_map.194 = (bf16[128,8192]{1,0:T(8,128)(2,1)S(1)}, f32[32,512]{1,0:T(8,128)S(1)}, bf16[128,256]{1,0:T(8,128)(2,1)S(1)}, bf16[128,256]{1,0:T(8,128)(2,1)S(1...) custom-call(s32[1]{0:T(128)S(6)} %copy.22.limit_ref, ...), custom_call_target="tpu_custom_call" | custom-call | bytes 18154116 | tf_op jit(solution)/shard_map/pallas_call | solution.py:191
  14.5 0.4 collective-permute-done.rest_1_
  14.9 0.8 %collective-permute-done.2.rest_3_ = bf16[448,128]{1,0:T(8,128)(2,1)S(1)} collective-permute-done((bf16[448,128]{1,0:T(8,128)(2,1)S(1)}, bf16[448,128]{1,0:T(8,128)(2,1)S(1)}, u32[]{:S(2)}, u32[]{:S(2)}) %collective-permute-start.2) | collective-permute-done | bytes 114720 | tf_op jit(solution)/shard_map/ppermute | solution.py:491
  15.8 2.0 %shard_map.196 = (bf16[224,128]{1,0:T(8,128)(2,1)S(1)}, bf16[224,128]{1,0:T(8,128)(2,1)S(1)}, bf16[224,128]{1,0:T(8,128)(2,1)S(1)}, bf16[128,128]{1,0:T(8,128)(2...) custom-call(bf16[128,256]{1,0:T(8,128)(2,1)S(1)} %get-tuple-element.32.kv_ref, ...), custom_call_target="tpu_custom_call" | custom-call | flops 134217728 | bytes 843776 | tf_op jit(solution)/shard_map/pallas_call | solution.py:191
  17.8 3.5 %collective-permute-start.6 = (bf16[224,128]{1,0:T(8,128)(2,1)S(1)}, bf16[224,128]{1,0:T(8,128)(2,1)S(1)}, u32[]{:S(2)}, u32[]{:S(2)}) collective-permute-start(bf16[224,128]{1,0:T(8,128)(2,1)S(1)} %get-tuple-element.44), channel_id=1, source_target_pairs={{0,8},{4,12},{8,0},{12,4},{1,9},{5,13},{9,1},{13,5},{2,10},{6,14},... | collective-permute-start | bytes 172040 | tf_op jit(solution)/shard_map/ppermute | solution.py:491
  21.2 0.4 %collective-permute-start.7 = (bf16[224,128]{1,0:T(8,128)(2,1)S(1)}, bf16[224,128]{1,0:T(8,128)(2,1)S(1)}, u32[]{:S(2)}, u32[]{:S(2)}) collective-permute-start(bf16[224,128]{1,0:T(8,128)(2,1)S(1)} %get-tuple-element.45), channel_id=1, source_target_pairs={{0,12},{4,8},{8,4},{12,0},{1,13},{5,9},{9,5},{13,1},{2,14},{6,10},... | collective-permute-start | bytes 172040 | tf_op jit(solution)/shard_map/ppermute | solution.py:491
  21.9 3.2 %collective-permute-start.4 = (bf16[64,256]{1,0:T(8,128)(2,1)S(1)}, bf16[64,256]{1,0:T(8,128)(2,1)S(1)}, u32[]{:S(2)}, u32[]{:S(2)}) collective-permute-start(bf16[64,256]{1,0:T(8,128)(2,1)S(1)} %get-tuple-element.40.rest_0_), channel_id=1, source_target_pairs={{0,12},{4,8},{8,4},{12,0},{1,13},{5,9},{9,5},{13,1},{2,14},{6,10},... | collective-permute-start | bytes 98312 | tf_op jit(solution)/shard_map/ppermute | solution.py:491
  25.1 0.6 %collective-permute-start.3 = (bf16[64,256]{1,0:T(8,128)(2,1)S(1)}, bf16[64,256]{1,0:T(8,128)(2,1)S(1)}, u32[]{:S(2)}, u32[]{:S(2)}) collective-permute-start(bf16[64,256]{1,0:T(8,128)(2,1)S(1)} %get-tuple-element.40.rest_0_), channel_id=1, source_target_pairs={{0,8},{4,12},{8,0},{12,4},{1,9},{5,13},{9,1},{13,5},{2,10},{6,14},... | collective-permute-start | bytes 98312 | tf_op jit(solution)/shard_map/ppermute | solution.py:491
  25.6 3.2 %collective-permute-done.4.rest_2_ = bf16[64,256]{1,0:T(8,128)(2,1)S(1)} collective-permute-done((bf16[64,256]{1,0:T(8,128)(2,1)S(1)}, bf16[64,256]{1,0:T(8,128)(2,1)S(1)}, u32[]{:S(2)}, u32[]{:S(2)}) %collective-permute-start.4) | collective-permute-done | bytes 32800 | tf_op jit(solution)/shard_map/ppermute | solution.py:491
  28.9 1.0 %collective-permute-done.3.rest_1_ = bf16[64,256]{1,0:T(8,128)(2,1)S(1)} collective-permute-done((bf16[64,256]{1,0:T(8,128)(2,1)S(1)}, bf16[64,256]{1,0:T(8,128)(2,1)S(1)}, u32[]{:S(2)}, u32[]{:S(2)}) %collective-permute-start.3) | collective-permute-done | bytes 32800 | tf_op jit(solution)/shard_map/ppermute | solution.py:491
  29.9 1.1 %shard_map.197.a2v_ref = bf16[128,256]{1,0:T(8,128)(2,1)S(1)} custom-call(s32[1]{0:T(128)S(6)} %copy.22.limit_ref, bf16[128,256]{1,0:T(8,128)(2,1)S(1)} %get-tuple-element.39.q_ref, bf16[64,256]{1,0:T(8,128)(2,1)S(1)} %get-tuple-element.40.rest_0_, bf16[64,256]{1,0:T(8,128)(2,1)S(1)} %collective-permute-done.3.rest_1_, ...), custom_call_target="tpu_custom_call" | custom-call | flops 33554432 | bytes 262148 | tf_op jit(solution)/shard_map/pallas_call | solution.py:191
  31.0 0.3 shard_map.198
  31.3 0.4 shard_map.199
  31.7 0.8 %shard_map.200 = (bf16[288,512]{1,0:T(8,128)(2,1)S(1)}, f32[288,512]{1,0:T(8,128)S(1)}) custom-call(bf16[128,512]{1,0:T(8,128)(2,1)S(1)} %get-tuple-element.47.self_ref, bf16[128,256]{1,0:T(8,128)(2,1)S(1)} %shard_map.197.a2v_ref, bf16[32,256]{1,0:T(8,128)(2,1)S(1)} %get-tuple-element.51.audio_ref.rest_0_, bf16[512,4096]{1,0:T(8,128)(2,1)S(1)} %get-tuple-element.41.ws_ref, ...), custom_call_target="tpu_custom_call" | custom-call | flops 402653184 | bytes 10534912 | tf_op jit(solution)/shard_map/pallas_call | solution.py:191
  32.5 0.6 %collective-permute-start.9 = (bf16[288,512]{1,0:T(8,128)(2,1)S(1)}, bf16[288,512]{1,0:T(8,128)(2,1)S(1)}, u32[]{:S(2)}, u32[]{:S(2)}) collective-permute-start(bf16[288,512]{1,0:T(8,128)(2,1)S(1)} %get-tuple-element.53), channel_id=1, source_target_pairs={{0,1},{1,0},{2,3},{3,2},{4,5},{5,4},{6,7},{7,6},{8,9},{9,8},{10,11... | collective-permute-start | bytes 884744 | tf_op jit(solution)/shard_map/ppermute | solution.py:491
  33.5 1.6 %collective-permute-start.13 = (bf16[160,512]{1,0:T(8,128)(2,1)S(1)}, bf16[160,512]{1,0:T(8,128)(2,1)S(1)}, u32[]{:S(2)}, u32[]{:S(2)}) collective-permute-start(bf16[160,512]{1,0:T(8,128)(2,1)S(1)} %shard_map.202), channel_id=1, source_target_pairs={{0,2},{2,0},{1,3},{3,1},{4,6},{6,4},{5,7},{7,5},{8,10},{10,8},{9,1... | collective-permute-start | bytes 491528 | tf_op jit(solution)/shard_map/ppermute | solution.py:491
  35.3 1.0 %collective-permute-start.11 = (bf16[128,512]{1,0:T(8,128)(2,1)S(1)}, bf16[128,512]{1,0:T(8,128)(2,1)S(1)}, u32[]{:S(2)}, u32[]{:S(2)}) collective-permute-start(bf16[128,512]{1,0:T(8,128)(2,1)S(1)} %shard_map.201), channel_id=1, source_target_pairs={{0,2},{2,0},{1,3},{3,1},{4,6},{6,4},{5,7},{7,5},{8,10},{10,8},{9,1... | collective-permute-start | bytes 393224 | tf_op jit(solution)/shard_map/ppermute | solution.py:491
  36.3 6.5 %collective-permute-done.11.low_ref = bf16[128,512]{1,0:T(8,128)(2,1)S(1)} collective-permute-done((bf16[128,512]{1,0:T(8,128)(2,1)S(1)}, bf16[128,512]{1,0:T(8,128)(2,1)S(1)}, u32[]{:S(2)}, u32[]{:S(2)}) %collective-permute-start.11) | collective-permute-done | bytes 131104 | tf_op jit(solution)/shard_map/ppermute | solution.py:491
  42.9 0.8 %shard_map.203 = (bf16[128,1024]{1,0:T(8,128)(2,1)}, bf16[32,512]{1,0:T(8,128)(2,1)}) custom-call(bf16[128,1024]{1,0:T(8,128)(2,1)S(1)} %get-tuple-element.29.video_ref, bf16[32,512]{1,0:T(8,128)(2,1)S(1)} %get-tuple-element.30.audio_ref, f32[32,512]{1,0:T(8,128)S(1)} %get-tuple-element.31.gain_ref, f32[288,512]{1,0:T(8,128)S(1)} %get-tuple-element.52.own_ref, ...), custom_call_target="tpu_custom_call" | custom-call | bytes 1835008 | tf_op jit(solution)/shard_map/pallas_call | solution.py:191
  (15 shorter events, 1.1 us)
Async XLA Ops:
  1.8 13.1 %collective-permute-start = (bf16[448,128]{1,0:T(8,128)(2,1)S(1)}, bf16[448,128]{1,0:T(8,128)(2,1)S(1)}, u32[]{:S(2)}, u32[]{:S(2)}) collective-permute-start(bf16[448,128]{1,0:T(8,128)(2,1)S(1)} %get-tuple-element.35), channel_id=1, source_target_pairs={{0,8},{4,12},{8,0},{12,4},{1,9},{5,13},{9,1},{13,5},{2,10},{6,14},... | collective-permute-start | bytes 344072 | tf_op jit(solution)/shard_map/ppermute | solution.py:491
  6.0 9.0 %collective-permute-start.1 = (bf16[448,128]{1,0:T(8,128)(2,1)S(1)}, bf16[448,128]{1,0:T(8,128)(2,1)S(1)}, u32[]{:S(2)}, u32[]{:S(2)}) collective-permute-start(bf16[448,128]{1,0:T(8,128)(2,1)S(1)} %get-tuple-element.36), channel_id=1, source_target_pairs={{0,12},{4,8},{8,4},{12,0},{1,13},{5,9},{9,5},{13,1},{2,14},{6,10},... | collective-permute-start | bytes 344072 | tf_op jit(solution)/shard_map/ppermute | solution.py:491
  7.3 8.5 %collective-permute-start.2 = (bf16[448,128]{1,0:T(8,128)(2,1)S(1)}, bf16[448,128]{1,0:T(8,128)(2,1)S(1)}, u32[]{:S(2)}, u32[]{:S(2)}) collective-permute-start(bf16[448,128]{1,0:T(8,128)(2,1)S(1)} %get-tuple-element.37), channel_id=1, source_target_pairs={{0,4},{4,0},{8,12},{12,8},{1,5},{5,1},{9,13},{13,9},{2,6},{6,2},{1... | collective-permute-start | bytes 344072 | tf_op jit(solution)/shard_map/ppermute | solution.py:491
  7.6 17.5 %collective-permute-start.5 = (bf16[64,256]{1,0:T(8,128)(2,1)S(1)}, bf16[64,256]{1,0:T(8,128)(2,1)S(1)}, u32[]{:S(2)}, u32[]{:S(2)}) collective-permute-start(bf16[64,256]{1,0:T(8,128)(2,1)S(1)} %get-tuple-element.40.rest_0_), channel_id=1, source_target_pairs={{0,4},{4,0},{8,12},{12,8},{1,5},{5,1},{9,13},{13,9},{2,6},{6,2},{1... | collective-permute-start | bytes 98312 | tf_op jit(solution)/shard_map/ppermute | solution.py:491
  17.8 13.2 %collective-permute-start.6 = (bf16[224,128]{1,0:T(8,128)(2,1)S(1)}, bf16[224,128]{1,0:T(8,128)(2,1)S(1)}, u32[]{:S(2)}, u32[]{:S(2)}) collective-permute-start(bf16[224,128]{1,0:T(8,128)(2,1)S(1)} %get-tuple-element.44), channel_id=1, source_target_pairs={{0,8},{4,12},{8,0},{12,4},{1,9},{5,13},{9,1},{13,5},{2,10},{6,14},... | collective-permute-start | bytes 172040 | tf_op jit(solution)/shard_map/ppermute | solution.py:491
  21.2 9.7 %collective-permute-start.7 = (bf16[224,128]{1,0:T(8,128)(2,1)S(1)}, bf16[224,128]{1,0:T(8,128)(2,1)S(1)}, u32[]{:S(2)}, u32[]{:S(2)}) collective-permute-start(bf16[224,128]{1,0:T(8,128)(2,1)S(1)} %get-tuple-element.45), channel_id=1, source_target_pairs={{0,12},{4,8},{8,4},{12,0},{1,13},{5,9},{9,5},{13,1},{2,14},{6,10},... | collective-permute-start | bytes 172040 | tf_op jit(solution)/shard_map/ppermute | solution.py:491
  21.7 9.3 %collective-permute-start.8 = (bf16[224,128]{1,0:T(8,128)(2,1)S(1)}, bf16[224,128]{1,0:T(8,128)(2,1)S(1)}, u32[]{:S(2)}, u32[]{:S(2)}) collective-permute-start(bf16[224,128]{1,0:T(8,128)(2,1)S(1)} %get-tuple-element.46), channel_id=1, source_target_pairs={{0,4},{4,0},{8,12},{12,8},{1,5},{5,1},{9,13},{13,9},{2,6},{6,2},{1... | collective-permute-start | bytes 172040 | tf_op jit(solution)/shard_map/ppermute | solution.py:491
  21.9 7.0 %collective-permute-start.4 = (bf16[64,256]{1,0:T(8,128)(2,1)S(1)}, bf16[64,256]{1,0:T(8,128)(2,1)S(1)}, u32[]{:S(2)}, u32[]{:S(2)}) collective-permute-start(bf16[64,256]{1,0:T(8,128)(2,1)S(1)} %get-tuple-element.40.rest_0_), channel_id=1, source_target_pairs={{0,12},{4,8},{8,4},{12,0},{1,13},{5,9},{9,5},{13,1},{2,14},{6,10},... | collective-permute-start | bytes 98312 | tf_op jit(solution)/shard_map/ppermute | solution.py:491
  25.1 4.8 %collective-permute-start.3 = (bf16[64,256]{1,0:T(8,128)(2,1)S(1)}, bf16[64,256]{1,0:T(8,128)(2,1)S(1)}, u32[]{:S(2)}, u32[]{:S(2)}) collective-permute-start(bf16[64,256]{1,0:T(8,128)(2,1)S(1)} %get-tuple-element.40.rest_0_), channel_id=1, source_target_pairs={{0,8},{4,12},{8,0},{12,4},{1,9},{5,13},{9,1},{13,5},{2,10},{6,14},... | collective-permute-start | bytes 98312 | tf_op jit(solution)/shard_map/ppermute | solution.py:491
  31.7 1.4 %collective-permute-start.12 = (bf16[160,512]{1,0:T(8,128)(2,1)S(1)}, bf16[160,512]{1,0:T(8,128)(2,1)S(1)}, u32[]{:S(2)}, u32[]{:S(2)}) collective-permute-start(bf16[160,512]{1,0:T(8,128)(2,1)S(1)} %get-tuple-element.55), channel_id=1, source_target_pairs={{0,1},{1,0},{2,3},{3,2},{4,5},{5,4},{6,7},{7,6},{8,9},{9,8},{10,11... | collective-permute-start | bytes 491528 | tf_op jit(solution)/shard_map/ppermute | solution.py:491
  32.5 10.4 %collective-permute-start.9 = (bf16[288,512]{1,0:T(8,128)(2,1)S(1)}, bf16[288,512]{1,0:T(8,128)(2,1)S(1)}, u32[]{:S(2)}, u32[]{:S(2)}) collective-permute-start(bf16[288,512]{1,0:T(8,128)(2,1)S(1)} %get-tuple-element.53), channel_id=1, source_target_pairs={{0,1},{1,0},{2,3},{3,2},{4,5},{5,4},{6,7},{7,6},{8,9},{9,8},{10,11... | collective-permute-start | bytes 884744 | tf_op jit(solution)/shard_map/ppermute | solution.py:491
  33.1 2.0 %collective-permute-start.10 = (bf16[128,512]{1,0:T(8,128)(2,1)S(1)}, bf16[128,512]{1,0:T(8,128)(2,1)S(1)}, u32[]{:S(2)}, u32[]{:S(2)}) collective-permute-start(bf16[128,512]{1,0:T(8,128)(2,1)S(1)} %get-tuple-element.54), channel_id=1, source_target_pairs={{0,1},{1,0},{2,3},{3,2},{4,5},{5,4},{6,7},{7,6},{8,9},{9,8},{10,11... | collective-permute-start | bytes 393224 | tf_op jit(solution)/shard_map/ppermute | solution.py:491
  33.5 9.4 %collective-permute-start.13 = (bf16[160,512]{1,0:T(8,128)(2,1)S(1)}, bf16[160,512]{1,0:T(8,128)(2,1)S(1)}, u32[]{:S(2)}, u32[]{:S(2)}) collective-permute-start(bf16[160,512]{1,0:T(8,128)(2,1)S(1)} %shard_map.202), channel_id=1, source_target_pairs={{0,2},{2,0},{1,3},{3,1},{4,6},{6,4},{5,7},{7,5},{8,10},{10,8},{9,1... | collective-permute-start | bytes 491528 | tf_op jit(solution)/shard_map/ppermute | solution.py:491
  35.3 7.5 %collective-permute-start.11 = (bf16[128,512]{1,0:T(8,128)(2,1)S(1)}, bf16[128,512]{1,0:T(8,128)(2,1)S(1)}, u32[]{:S(2)}, u32[]{:S(2)}) collective-permute-start(bf16[128,512]{1,0:T(8,128)(2,1)S(1)} %shard_map.201), channel_id=1, source_target_pairs={{0,2},{2,0},{1,3},{3,1},{4,6},{6,4},{5,7},{7,5},{8,10},{10,8},{9,1... | collective-permute-start | bytes 393224 | tf_op jit(solution)/shard_map/ppermute | solution.py:491

commit v4 on v3

--- a/solution.py
+++ b/solution.py
@@ -180,6 +180,7 @@
 SMEM = pl.BlockSpec(memory_space=pltpu.SMEM)
 HBM = pl.BlockSpec(memory_space=pltpu.HBM)
 BF16, F32 = jnp.bfloat16, jnp.float32
+LSE_ROWS = 16
 
 
 def call(kernel, outs, operands, specs=None, flops=0, scratch=(), limit=8 * 2**20):
@@ -278,112 +279,158 @@
         copy.wait()
 
 
-def softmax_parts(scores, scale, allowed=None):
+def softmax_t(scores, scale, allowed=None):
     if allowed is not None:
-        scores = jnp.where(allowed, scores, -jnp.inf)
-    peak = jnp.max(scores, axis=1, keepdims=True)
-    weights = jnp.exp2((scores - peak) * (scale * LOG2E))
-    return peak, weights, jnp.sum(weights, axis=1, keepdims=True)
+        scores = [jnp.where(ok, x, -jnp.inf) for ok, x in zip(allowed, scores)]
+    peak = functools.reduce(jnp.maximum, [jnp.max(x, axis=0, keepdims=True) for x in scores])
+    weights = [jnp.exp2((x - peak) * (scale * LOG2E)) for x in scores]
+    total = functools.reduce(jnp.add, [jnp.sum(x, axis=0, keepdims=True) for x in weights])
+    return peak, [x.astype(BF16) for x in weights], total
+
+
+def turn(x):
+    return x.astype(F32).T.astype(BF16)
+
+
+def pair_rows(x, head):
+    lane = lax.broadcasted_iota(jnp.int32, (1, 128), 1) // head
+    return jnp.concatenate([jnp.where(lane == i, x, 0).astype(BF16) for i in range(128 // head)], axis=0)
+
+
+def pair_columns(x, head):
+    pair = 128 // head
+    rows = x.shape[1] // pair
+    return jnp.concatenate([x[i * head : (i + 1) * head, i * rows : (i + 1) * rows] for i in range(pair)], axis=0)
 
 
 def attend_kernel(n, head, kv_ref, vv_ref, *rest):
     blocks, sends, (own_ref, own_v2a_ref, own_lse_ref) = rest[:n], rest[n : 2 * n - 1], rest[2 * n - 1 : 2 * n + 2]
-    ks, vs, qas = rest[2 * n + 2 :]
+    vt_ref, vvt_ref, s_ref, p_ref = rest[2 * n + 2 :]
     rows, cols = kv_ref.shape
     width = blocks[0].shape[1]
-    rows_audio = qas.shape[0] // n
-    for j, ref in enumerate(blocks):
-        ks[j * rows : (j + 1) * rows, :] = ref[rows : 2 * rows, :]
-        vs[j * rows : (j + 1) * rows, :] = ref[2 * rows : 3 * rows, :]
-        for i in range(cols // width):
-            top = 3 * rows + i * rows_audio
-            qas[j * rows_audio : (j + 1) * rows_audio, i * width : (i + 1) * width] = ref[top : top + rows_audio, :]
-    scale = 1.0 / math.sqrt(DHV)
-    for j, ref in enumerate(blocks):
+    rows_audio = own_v2a_ref.shape[0]
+    for h in range(width // DHV):
+        cut = slice(h * DHV, (h + 1) * DHV)
+        for i, ref in enumerate(blocks):
+            vt_ref[cut, i * rows : (i + 1) * rows] = turn(ref[2 * rows : 3 * rows, cut])
+    for block in range(cols // 128):
+        cut = slice(block * 128, (block + 1) * 128)
+        vvt_ref[cut, :] = turn(vv_ref[:, cut])
+    pair, row = 128 // head, 0
+    parts = []
+    for block in range(cols // 128):
+        cut = slice(block * 128, (block + 1) * 128)
+        top, part = 3 * rows + (block * 128 // width) * rows_audio, slice(block * 128 % width, block * 128 % width + 128)
+        q = pair_rows(jnp.concatenate([ref[top : top + rows_audio, part] for ref in blocks], axis=0), head)
+        scores = dot_t(kv_ref[:, cut], q)
+        for i in range(pair):
+            at = slice(i * n * rows_audio, (i + 1) * n * rows_audio)
+            s_ref[row + i * rows : row + (i + 1) * rows, :] = scores[:, at]
+            parts.append((row + i * rows, rows, jnp.max(scores[:, at], axis=0, keepdims=True), 1.0 / math.sqrt(head)))
+        row += pair * rows
+    for ref in blocks:
         for h in range(width // DHV):
             cut = slice(h * DHV, (h + 1) * DHV)
-            _, p, total = softmax_parts(dot_t(ref[0:rows, cut], ks[:, cut]), scale)
-            o = dot(p.astype(BF16), vs[:, cut]) / total
-            dst = own_ref if j == 0 else sends[j - 1].at[0:rows, :]
-            dst[:, cut] = o.astype(BF16)
-    scale = 1.0 / math.sqrt(head)
-    pair = 128 // head
-    lane = lax.broadcasted_iota(jnp.int32, (1, 128), 1) // head
-    lse_column = lax.broadcasted_iota(jnp.int32, (1, 128), 1)
-    lse = jnp.zeros((n * rows_audio, 128), F32)
+            peak = None
+            for i, other in enumerate(blocks):
+                scores = dot_t(other[rows : 2 * rows, cut], ref[0:rows, cut])
+                s_ref[row + i * rows : row + (i + 1) * rows, :] = scores
+                top = jnp.max(scores, axis=0, keepdims=True)
+                peak = top if i == 0 else jnp.maximum(peak, top)
+            parts.append((row, n * rows, peak, 1.0 / math.sqrt(DHV)))
+            row += n * rows
+
+    def weigh(part):
+        start, count, peak, scale = part
+        total = None
+        for at in range(start, start + count, 128):
+            p = jnp.exp2((s_ref[at : at + 128, :] - peak) * (scale * LOG2E))
+            p_ref[at : at + 128, :] = p.astype(BF16)
+            summed = jnp.sum(p, axis=0, keepdims=True)
+            total = summed if at == start else total + summed
+        return total
+
+    lses, at = [], 0
     for block in range(cols // 128):
-        cut = slice(block * 128, (block + 1) * 128)
-        v2a = jnp.zeros((n * rows_audio, 128), F32)
+        both = []
         for i in range(pair):
-            q = jnp.where(lane == i, qas[:, cut], 0).astype(BF16)
-            peak, p, total = softmax_parts(dot_t(q, kv_ref[:, cut]), scale)
-            v2a = jnp.where(lane == i, dot(p.astype(BF16), vv_ref[:, cut]) / total, v2a)
-            lse = jnp.where(lse_column == block * pair + i, peak * (scale * LOG2E) + jnp.log2(total), lse)
-        own_v2a_ref[:, cut] = v2a[0:rows_audio]
+            start, count, peak, scale = parts[at]
+            total = weigh(parts[at])
+            lses.append(peak * (scale * LOG2E) + jnp.log2(total))
+            column = block * 128 + i * head
+            o = dot(vvt_ref[column : column + head, :], p_ref[start : start + count, :])
+            both.append(o * (1.0 / total))
+            at += 1
+        v2a = jnp.concatenate(both, axis=0).T
+        own_v2a_ref[:, block * 128 : (block + 1) * 128] = v2a[0:rows_audio]
         for j, dst in enumerate(sends):
             top = rows + block * rows_audio
             dst[top : top + rows_audio, 0:128] = v2a[(j + 1) * rows_audio : (j + 2) * rows_audio].astype(BF16)
-    own_lse_ref[...] = lse[0:rows_audio]
+    for j in range(n):
+        for h in range(width // DHV):
+            cut = slice(h * DHV, (h + 1) * DHV)
+            start, count, _, _ = parts[at]
+            total = weigh(parts[at])
+            o = dot(vt_ref[cut, :], p_ref[start : start + count, :]) * (1.0 / total)
+            dst = own_ref if j == 0 else sends[j - 1].at[0:rows, :]
+            dst[:, cut] = o.T.astype(BF16)
+            at += 1
+    heads = len(lses)
+    lse = jnp.concatenate(lses, axis=0)
+    own_lse_ref[...] = lse
+    pieces, left = [], lse
+    for _ in range(3):
+        pieces.append(left.astype(BF16).astype(F32))
+        left = left - pieces[-1]
+    packed = jnp.concatenate(pieces + [jnp.zeros((LSE_ROWS - 3 * heads, lse.shape[1]), F32)], axis=0)
     for j, dst in enumerate(sends):
-        rest_lse = lse[(j + 1) * rows_audio : (j + 2) * rows_audio]
         top = rows + cols // 128 * rows_audio
-        packed = jnp.zeros((rows_audio, 128), F32)
-        for term in range(3):
-            piece = rest_lse.astype(BF16).astype(F32)
-            rest_lse = rest_lse - piece
-            packed = packed + (piece if term == 0 else pltpu.roll(piece, 32 * term, 1))
-        dst[top : top + rows_audio, 0:128] = packed.astype(BF16)
+        dst[top : top + LSE_ROWS, 0:128] = pltpu.roll(packed, 128 - (j + 1) * rows_audio, 1).astype(BF16)
 
 
 def attend_audio_kernel(hops, head, limit_ref, q_ref, *rest):
     n = len(hops)
-    blocks, out_ref, ks, vs = rest[:n], *rest[n:]
+    blocks, out_ref = rest[:n], rest[n]
     rows_audio = blocks[0].shape[0] // 2
-    keys = n * rows_audio
-    column = lax.broadcasted_iota(jnp.int32, (1, keys), 1)
-    me, position = index_of("seq"), column
-    for j, (hop, ref) in enumerate(zip(hops, blocks)):
-        at = slice(j * rows_audio, (j + 1) * rows_audio)
-        ks[at, :] = ref[0:rows_audio, :]
-        vs[at, :] = ref[rows_audio : 2 * rows_audio, :]
-        shift = ((me ^ hop) - j) * rows_audio
-        position = jnp.where(column // rows_audio == j, column + shift, position)
-    allowed = position < limit_ref[0]
+    me, row = index_of("seq"), lax.broadcasted_iota(jnp.int32, (rows_audio, 1), 0)
+    allowed = [(me ^ hop) * rows_audio + row < limit_ref[0] for hop in hops]
     scale = 1.0 / math.sqrt(head)
-    lane = lax.broadcasted_iota(jnp.int32, (1, 128), 1) // head
     for block in range(q_ref.shape[1] // 128):
         cut = slice(block * 128, (block + 1) * 128)
-        both = jnp.zeros((q_ref.shape[0], 128), F32)
-        for i in range(128 // head):
-            q = jnp.where(lane == i, q_ref[:, cut], 0).astype(BF16)
-            _, p, total = softmax_parts(dot_t(q, ks[:, cut]), scale, allowed)
-            both = jnp.where(lane == i, dot(p.astype(BF16), vs[:, cut]) / total, both)
-        out_ref[:, cut] = both.astype(BF16)
+        q = pair_rows(q_ref[:, cut], head)
+        _, p, total = softmax_t([dot_t(ref[0:rows_audio, cut], q) for ref in blocks], scale, allowed)
+        vt = turn(jnp.concatenate([ref[rows_audio : 2 * rows_audio, cut] for ref in blocks], axis=0))
+        o = dot(vt, jnp.concatenate(p, axis=0)) * (1.0 / total)
+        out_ref[:, cut] = pair_columns(o, head).T.astype(BF16)
 
 
 def merge_audio(head, top, v2a_ref, lse_ref, got, out_ref):
     rows_audio, cols = v2a_ref.shape
+    heads = cols // head
     lses = [lse_ref[...]]
     for ref in got:
         at = top + cols // 128 * rows_audio
-        packed = ref[at : at + rows_audio, 0:128].astype(F32)
-        lses.append(packed + pltpu.roll(packed, 96, 1) + pltpu.roll(packed, 64, 1))
+        packed = ref[at : at + LSE_ROWS, 0:128].astype(F32)
+        lses.append(packed[0:heads] + packed[heads : 2 * heads] + packed[2 * heads : 3 * heads])
     peak = functools.reduce(jnp.maximum, lses)
     parts = [jnp.exp2(x - peak) for x in lses]
     total = functools.reduce(jnp.add, parts)
-    parts = [x / total for x in parts]
+    inverse = 1.0 / total
+    parts = [x * inverse for x in parts]
+    parts.append(jnp.zeros((128 - len(parts) * heads, 128), F32))
+    shares = jnp.concatenate(parts, axis=0).T[0:rows_audio]
     pair = 128 // head
     lane = lax.broadcasted_iota(jnp.int32, (1, 128), 1) // head
     for block in range(cols // 128):
         cut = slice(block * 128, (block + 1) * 128)
         at = top + block * rows_audio
         summed = jnp.zeros((rows_audio, 128), F32)
-        for j in range(len(parts)):
+        for j in range(len(lses)):
             o = v2a_ref[:, cut] if j == 0 else got[j - 1][at : at + rows_audio, 0:128].astype(F32)
             share = jnp.zeros((rows_audio, 128), F32)
             for i in range(pair):
-                column = block * pair + i
-                share = jnp.where(lane == i, parts[j][:, column : column + 1], share)
+                column = j * heads + block * pair + i
+                share = jnp.where(lane == i, shares[:, column : column + 1], share)
             summed = summed + share * o
         out_ref[:, cut] = summed.astype(BF16)
 
@@ -418,12 +465,17 @@
 
 
 def second_kernel(head, self_ref, a2v_ref, ws_ref, wa_ref, wv_ref, gain_ref, v2a_ref, lse_ref, *rest):
-    got, (out_ref, audio_ref) = rest[:-2], rest[-2:]
+    got, (out_ref, audio_ref, low_ref) = rest[:-3], rest[-3:]
     rows = self_ref.shape[0]
     block = block_of(True, True)
     out_ref[0:rows, :] = project(block, 1, (self_ref, a2v_ref), (ws_ref, wa_ref), gain_ref).astype(BF16)
     merge_audio(head, rows, v2a_ref, lse_ref, got, audio_ref)
     out_ref[rows:, :] = project_audio(block, audio_ref, wv_ref).astype(BF16)
+    low_ref[...] = project(block_of(True, False), 0, (self_ref, a2v_ref), (ws_ref, wa_ref), gain_ref)
+
+
+def far_low_kernel(low_ref, extra_ref, out_ref):
+    out_ref[...] = (low_ref[...] + extra_ref[...].astype(F32)).astype(BF16)
 
 
 def near_kernel(self_ref, a2v_ref, audio_ref, ws_ref, wa_ref, wv_ref, gain_ref, send_ref, own_ref):
@@ -436,15 +488,13 @@
         out[2 * rows :, :] = project_audio(block, audio_ref, wv_ref).astype(out.dtype)
 
 
-def far_kernel(half, self_ref, a2v_ref, ws_ref, wa_ref, gain_ref, extra_ref, *rest):
-    rows, out_ref = self_ref.shape[0], rest[-1]
+def far_high_kernel(self_ref, a2v_ref, ws_ref, wa_ref, gain_ref, extra_ref, audio_ref, wv_ref, out_ref):
+    rows = self_ref.shape[0]
     block = block_of(True, False)
-    term = project(block, half, (self_ref, a2v_ref), (ws_ref, wa_ref), gain_ref)
+    term = project(block, 1, (self_ref, a2v_ref), (ws_ref, wa_ref), gain_ref)
     out_ref[0:rows, :] = (term + extra_ref[0:rows, :].astype(F32)).astype(BF16)
-    if half == 1:
-        audio_ref, wv_ref = rest[:2]
-        term = project_audio(block, audio_ref, wv_ref)
-        out_ref[rows:, :] = (term + extra_ref[rows:, :].astype(F32)).astype(BF16)
+    term = project_audio(block, audio_ref, wv_ref)
+    out_ref[rows:, :] = (term + extra_ref[rows:, :].astype(F32)).astype(BF16)
 
 
 def finish_kernel(video_ref, audio_ref, gain_ref, own_ref, core_ref, low_ref, high_ref, video_out, audio_out):
@@ -512,14 +562,15 @@
         scratch=[pltpu.VMEM(x.shape, x.dtype) for x in (*steps, audio_gates)]
         + [pltpu.SemaphoreType.DMA((3 + len(late),))],
     )
-    back = rows + cross // 128 * rows_audio + rows_audio
+    back = rows + cross // 128 * rows_audio + LSE_ROWS
     result = call(
         functools.partial(attend_kernel, n, DHC),
         [shape(back, width)] * (n - 1)
-        + [shape(rows, width), shape(rows_audio, cross, F32), shape(rows_audio, 128, F32)],
+        + [shape(rows, width), shape(rows_audio, cross, F32), shape(cross // DHC, 128, F32)],
         (k_own, v_own, *blocks),
         flops=4 * n * n * rows * rows * width,
-        scratch=[pltpu.VMEM((n * rows, width), BF16)] * 2 + [pltpu.VMEM((n * rows_audio, cross), BF16)],
+        scratch=[pltpu.VMEM((width, n * rows), BF16), pltpu.VMEM((cross, rows), BF16)]
+        + [pltpu.VMEM((n * n * rows * width // DHV + cross // DHC * rows, 128), kind) for kind in (F32, BF16)],
     )
     sends, (own, own_v2a, own_lse) = result[: n - 1], result[n - 1 :]
     got = [trade(x, "seq", hop, n) for x, hop in zip(sends, hops[1:])]
@@ -529,7 +580,6 @@
         (audio_len, q_own, *audios),
         [SMEM] + [VMEM] * (n + 1),
         flops=8 * n * rows * rows_audio * cross,
-        scratch=[pltpu.VMEM((n * rows_audio, cross), BF16)] * 2,
     )
 
     half = video_in.shape[1] // 2
@@ -541,33 +591,28 @@
         flops=flops,
     )
     first = trade(first, "sub", 1, 2)
-    second, v2a_att = call(
+    second, v2a_att, own_low = call(
         functools.partial(second_kernel, DHC),
-        [shape(rows + rows_audio, half), shape(rows_audio, cross)],
+        [shape(rows + rows_audio, half), shape(rows_audio, cross), shape(rows, half, F32)],
         (self_att, a2v_att, ws, wa, wv, gain, own_v2a, own_lse, *got),
+        flops=2 * flops,
+    )
+    second = trade(second, "sub", 1, 2)
+    (low,) = call(far_low_kernel, [shape(rows, half)], (own_low, first))
+    low = trade(low, "mp", 1, 2)
+    (high,) = call(
+        far_high_kernel,
+        [shape(rows + rows_audio, half)],
+        (self_att, a2v_att, ws, wa, gain, second, v2a_att, wv),
         flops=flops,
     )
-    second = trade(second, "sub", 1, 2)
+    high = trade(high, "mp", 1, 2)
     near, own_sum = call(
         near_kernel,
         [shape(2 * rows + rows_audio, half), shape(2 * rows + rows_audio, half, F32)],
         (self_att, a2v_att, v2a_att, ws, wa, wv, gain),
         flops=4 * flops,
     )
-    (low,) = call(
-        functools.partial(far_kernel, 0),
-        [shape(rows, half)],
-        (self_att, a2v_att, ws, wa, gain, first),
-        flops=flops,
-    )
-    low = trade(low, "mp", 1, 2)
-    (high,) = call(
-        functools.partial(far_kernel, 1),
-        [shape(rows + rows_audio, half)],
-        (self_att, a2v_att, ws, wa, gain, second, v2a_att, wv),
-        flops=flops,
-    )
-    high = trade(high, "mp", 1, 2)
     near = trade(near, "sub", 1, 2)
     return call(
         finish_kernel,
@@ -584,7 +629,8 @@
         and (mp, sub) == (2, 2)
         and width % DHV == 0
         and cross % width == 0
-        and cross // DHC <= 32
+        and 3 * (cross // DHC) <= LSE_ROWS
+        and n * arrays[8].shape[0] == arrays[2].shape[0] == 128
         and arrays[0].shape[1] == 2 * arrays[1].shape[1]
     )
     if fits:

time: 44 us -> 42.8 us (0.973)
  Pallas kernels: 10.6 us -> 9.11 us
    pallas_call x10, Pallas kernels: 10.6 us -> 9.11 us  [call(): pl.pallas_call(kernel, out_shape=tuple(outs), in_specs=specs or [VMEM] *...]
  transfers between devices with their start and end apart: 14 -> 14, of which waited for: 5 -> 5; matrix products, arithmetic and copies ran while one was open for 3% -> 3% of each run, Pallas kernels for 18% -> 14%
where the time goes in v4:
time: 42.8 us; the launch traced here: 42.6 us
  starting transfers between devices  18.6 us (43%)
  waiting for transfers between devices  12.4 us (29%)
  Pallas kernels  9.11 us (21%)
  between operations  1.39 us (3%)
  local copies, waits for them, and re-layouts  1.1 us (3%)
    ppermute x14, starting transfers between devices, trade(): return lax.ppermute(x, axis, [(i, i ^ hop) for i in range(size)])  18.6 us
    ppermute x14, waiting for transfers between devices, trade(): return lax.ppermute(x, axis, [(i, i ^ hop) for i in range(size)])  12.4 us
    pallas_call x10, Pallas kernels, call(): pl.pallas_call(kernel, out_shape=tuple(outs), in_specs=specs or [VMEM] *...  9.11 us
    unnamed x1, local copies, waits for them, and re-layouts  1.1 us
  transfers between devices with their start and end apart: 14, of which 5 were waited for; matrix products, arithmetic and copies ran while one was open for 3% of the time, Pallas kernels for 14%

profile of v4, /device:TPU:0, one launch (start us, length us, event | category | flops | bytes accessed | tf_op | source)
XLA Modules:
  0.0 42.6 jit_solution(14435244161222819186)
XLA Ops:
  0.6 1.2 %shard_map.195 = (bf16[448,128]{1,0:T(8,128)(2,1)S(1)}, bf16[448,128]{1,0:T(8,128)(2,1)S(1)}, bf16[448,128]{1,0:T(8,128)(2,1)S(1)}, bf16[448,128]{1,0:T(8,128)(2,1)S(1)}, bf16[64,256]{1,0:T(8,128)(2,1)S(1)}) custom-call(bf16[128,512]{1,0:T(8,128)(2,1)} %q_ref.1, bf16[128,512]{1,0:T(8,128)(2,1)} %k_ref.1, bf16[128,512]{1,0:T(8,128)(2,1)} %v_ref.1, ...), custom_call_target="tpu_custom_call" | custom-call | bytes 933888 | tf_op jit(solution)/shard_map/pallas_call | solution.py:192
  1.8 4.1 %collective-permute-start = (bf16[448,128]{1,0:T(8,128)(2,1)S(1)}, bf16[448,128]{1,0:T(8,128)(2,1)S(1)}, u32[]{:S(2)}, u32[]{:S(2)}) collective-permute-start(bf16[448,128]{1,0:T(8,128)(2,1)S(1)} %get-tuple-element.36), channel_id=1, source_target_pairs={{0,8},{4,12},{8,0},{12,4},{1,9},{5,13},{9,1},{13,5},{2,10},{6,14},... | collective-permute-start | bytes 344072 | tf_op jit(solution)/shard_map/ppermute | solution.py:541
  6.0 1.3 %collective-permute-start.1 = (bf16[448,128]{1,0:T(8,128)(2,1)S(1)}, bf16[448,128]{1,0:T(8,128)(2,1)S(1)}, u32[]{:S(2)}, u32[]{:S(2)}) collective-permute-start(bf16[448,128]{1,0:T(8,128)(2,1)S(1)} %get-tuple-element.37), channel_id=1, source_target_pairs={{0,12},{4,8},{8,4},{12,0},{1,13},{5,9},{9,5},{13,1},{2,14},{6,10},... | collective-permute-start | bytes 344072 | tf_op jit(solution)/shard_map/ppermute | solution.py:541
  7.6 1.8 %collective-permute-start.5 = (bf16[64,256]{1,0:T(8,128)(2,1)S(1)}, bf16[64,256]{1,0:T(8,128)(2,1)S(1)}, u32[]{:S(2)}, u32[]{:S(2)}) collective-permute-start(bf16[64,256]{1,0:T(8,128)(2,1)S(1)} %get-tuple-element.41.rest_0_), channel_id=1, source_target_pairs={{0,4},{4,0},{8,12},{12,8},{1,5},{5,1},{9,13},{13,9},{2,6},{6,2},{1... | collective-permute-start | bytes 98312 | tf_op jit(solution)/shard_map/ppermute | solution.py:541
  10.0 1.1 %copy.21 = bf16[2,8,2,4096]{3,1,2,0:T(8,128)(2,1)S(1)} copy(bf16[2,8,2,4096]{3,2,1,0:T(2,128)(2,1)} %bitcast.5) | data formatting | bytes 524288
  11.1 3.4 %shard_map.194 = (bf16[128,8192]{1,0:T(8,128)(2,1)S(1)}, f32[32,512]{1,0:T(8,128)S(1)}, bf16[128,256]{1,0:T(8,128)(2,1)S(1)}, bf16[128,256]{1,0:T(8,128)(2,1)S(1...) custom-call(s32[1]{0:T(128)S(6)} %copy.22.limit_ref, ...), custom_call_target="tpu_custom_call" | custom-call | bytes 18154116 | tf_op jit(solution)/shard_map/pallas_call | solution.py:192
  14.5 0.4 collective-permute-done.rest_1_
  14.9 0.8 %collective-permute-done.2.rest_3_ = bf16[448,128]{1,0:T(8,128)(2,1)S(1)} collective-permute-done((bf16[448,128]{1,0:T(8,128)(2,1)S(1)}, bf16[448,128]{1,0:T(8,128)(2,1)S(1)}, u32[]{:S(2)}, u32[]{:S(2)}) %collective-permute-start.2) | collective-permute-done | bytes 114720 | tf_op jit(solution)/shard_map/ppermute | solution.py:541
  15.8 0.9 %shard_map.196 = (bf16[208,128]{1,0:T(8,128)(2,1)S(1)}, bf16[208,128]{1,0:T(8,128)(2,1)S(1)}, bf16[208,128]{1,0:T(8,128)(2,1)S(1)}, bf16[128,128]{1,0:T(8,128)(2...) custom-call(bf16[128,256]{1,0:T(8,128)(2,1)S(1)} %get-tuple-element.33.kv_ref, ...), custom_call_target="tpu_custom_call" | custom-call | flops 134217728 | bytes 817152 | tf_op jit(solution)/shard_map/pallas_call | solution.py:192
  16.7 3.5 %collective-permute-start.6 = (bf16[208,128]{1,0:T(8,128)(2,1)S(1)}, bf16[208,128]{1,0:T(8,128)(2,1)S(1)}, u32[]{:S(2)}, u32[]{:S(2)}) collective-permute-start(bf16[208,128]{1,0:T(8,128)(2,1)S(1)} %get-tuple-element.45), channel_id=1, source_target_pairs={{0,8},{4,12},{8,0},{12,4},{1,9},{5,13},{9,1},{13,5},{2,10},{6,14},... | collective-permute-start | bytes 159752 | tf_op jit(solution)/shard_map/ppermute | solution.py:541
  20.2 0.4 %collective-permute-start.7 = (bf16[208,128]{1,0:T(8,128)(2,1)S(1)}, bf16[208,128]{1,0:T(8,128)(2,1)S(1)}, u32[]{:S(2)}, u32[]{:S(2)}) collective-permute-start(bf16[208,128]{1,0:T(8,128)(2,1)S(1)} %get-tuple-element.46), channel_id=1, source_target_pairs={{0,12},{4,8},{8,4},{12,0},{1,13},{5,9},{9,5},{13,1},{2,14},{6,10},... | collective-permute-start | bytes 159752 | tf_op jit(solution)/shard_map/ppermute | solution.py:541
  20.8 3.2 %collective-permute-start.4 = (bf16[64,256]{1,0:T(8,128)(2,1)S(1)}, bf16[64,256]{1,0:T(8,128)(2,1)S(1)}, u32[]{:S(2)}, u32[]{:S(2)}) collective-permute-start(bf16[64,256]{1,0:T(8,128)(2,1)S(1)} %get-tuple-element.41.rest_0_), channel_id=1, source_target_pairs={{0,12},{4,8},{8,4},{12,0},{1,13},{5,9},{9,5},{13,1},{2,14},{6,10},... | collective-permute-start | bytes 98312 | tf_op jit(solution)/shard_map/ppermute | solution.py:541
  24.0 0.6 %collective-permute-start.3 = (bf16[64,256]{1,0:T(8,128)(2,1)S(1)}, bf16[64,256]{1,0:T(8,128)(2,1)S(1)}, u32[]{:S(2)}, u32[]{:S(2)}) collective-permute-start(bf16[64,256]{1,0:T(8,128)(2,1)S(1)} %get-tuple-element.41.rest_0_), channel_id=1, source_target_pairs={{0,8},{4,12},{8,0},{12,4},{1,9},{5,13},{9,1},{13,5},{2,10},{6,14},... | collective-permute-start | bytes 98312 | tf_op jit(solution)/shard_map/ppermute | solution.py:541
  24.6 3.1 %collective-permute-done.4.rest_2_ = bf16[64,256]{1,0:T(8,128)(2,1)S(1)} collective-permute-done((bf16[64,256]{1,0:T(8,128)(2,1)S(1)}, bf16[64,256]{1,0:T(8,128)(2,1)S(1)}, u32[]{:S(2)}, u32[]{:S(2)}) %collective-permute-start.4) | collective-permute-done | bytes 32800 | tf_op jit(solution)/shard_map/ppermute | solution.py:541
  27.7 1.1 %collective-permute-done.3.rest_1_ = bf16[64,256]{1,0:T(8,128)(2,1)S(1)} collective-permute-done((bf16[64,256]{1,0:T(8,128)(2,1)S(1)}, bf16[64,256]{1,0:T(8,128)(2,1)S(1)}, u32[]{:S(2)}, u32[]{:S(2)}) %collective-permute-start.3) | collective-permute-done | bytes 32800 | tf_op jit(solution)/shard_map/ppermute | solution.py:541
  28.8 0.7 %shard_map.197.a2v_ref = bf16[128,256]{1,0:T(8,128)(2,1)S(1)} custom-call(s32[1]{0:T(128)S(6)} %copy.22.limit_ref, bf16[128,256]{1,0:T(8,128)(2,1)S(1)} %get-tuple-element.40.q_ref, bf16[64,256]{1,0:T(8,128)(2,1)S(1)} %get-tuple-element.41.rest_0_, bf16[64,256]{1,0:T(8,128)(2,1)S(1)} %collective-permute-done.3.rest_1_, ...), custom_call_target="tpu_custom_call" | custom-call | flops 33554432 | bytes 262148 | tf_op jit(solution)/shard_map/pallas_call | solution.py:192
  29.6 0.3 shard_map.198
  29.9 0.6 %shard_map.199 = (bf16[160,512]{1,0:T(8,128)(2,1)S(1)}, bf16[32,256]{1,0:T(8,128)(2,1)S(1)}, f32[128,512]{1,0:T(8,128)S(1)}) custom-call(bf16[128,512]{1,0:T(8,128)(2,1)S(1)} %get-tuple-element.48.self_ref, bf16[128,256]{1,0:T(8,128)(2,1)S(1)} %shard_map.197.a2v_ref, bf16[512,4096]{1,0:T(8,128)(2,1)S(1)} %get-tuple-element.42.ws_ref, ...), custom_call_target="tpu_custom_call" | custom-call | flops 201326592 | bytes 10270720 | tf_op jit(solution)/shard_map/pallas_call | solution.py:192
  30.6 0.8 %shard_map.200 = (bf16[288,512]{1,0:T(8,128)(2,1)S(1)}, f32[288,512]{1,0:T(8,128)S(1)}) custom-call(bf16[128,512]{1,0:T(8,128)(2,1)S(1)} %get-tuple-element.48.self_ref, bf16[128,256]{1,0:T(8,128)(2,1)S(1)} %shard_map.197.a2v_ref, bf16[32,256]{1,0:T(8,128)(2,1)S(1)} %get-tuple-element.52.audio_ref, bf16[512,4096]{1,0:T(8,128)(2,1)S(1)} %get-tuple-element.42.ws_ref, ...), custom_call_target="tpu_custom_call" | custom-call | flops 402653184 | bytes 10534912 | tf_op jit(solution)/shard_map/pallas_call | solution.py:192
  31.4 0.5 %collective-permute-start.9 = (bf16[288,512]{1,0:T(8,128)(2,1)S(1)}, bf16[288,512]{1,0:T(8,128)(2,1)S(1)}, u32[]{:S(2)}, u32[]{:S(2)}) collective-permute-start(bf16[288,512]{1,0:T(8,128)(2,1)S(1)} %get-tuple-element.54), channel_id=1, source_target_pairs={{0,1},{1,0},{2,3},{3,2},{4,5},{5,4},{6,7},{7,6},{8,9},{9,8},{10,11... | collective-permute-start | bytes 884744 | tf_op jit(solution)/shard_map/ppermute | solution.py:541
  32.3 1.6 %collective-permute-start.13 = (bf16[160,512]{1,0:T(8,128)(2,1)S(1)}, bf16[160,512]{1,0:T(8,128)(2,1)S(1)}, u32[]{:S(2)}, u32[]{:S(2)}) collective-permute-start(bf16[160,512]{1,0:T(8,128)(2,1)S(1)} %shard_map.202), channel_id=1, source_target_pairs={{0,2},{2,0},{1,3},{3,1},{4,6},{6,4},{5,7},{7,5},{8,10},{10,8},{9,1... | collective-permute-start | bytes 491528 | tf_op jit(solution)/shard_map/ppermute | solution.py:541
  33.9 1.0 %collective-permute-start.11 = (bf16[128,512]{1,0:T(8,128)(2,1)S(1)}, bf16[128,512]{1,0:T(8,128)(2,1)S(1)}, u32[]{:S(2)}, u32[]{:S(2)}) collective-permute-start(bf16[128,512]{1,0:T(8,128)(2,1)S(1)} %shard_map.201), channel_id=1, source_target_pairs={{0,2},{2,0},{1,3},{3,1},{4,6},{6,4},{5,7},{7,5},{8,10},{10,8},{9,1... | collective-permute-start | bytes 393224 | tf_op jit(solution)/shard_map/ppermute | solution.py:541
  34.9 6.8 %collective-permute-done.11.low_ref = bf16[128,512]{1,0:T(8,128)(2,1)S(1)} collective-permute-done((bf16[128,512]{1,0:T(8,128)(2,1)S(1)}, bf16[128,512]{1,0:T(8,128)(2,1)S(1)}, u32[]{:S(2)}, u32[]{:S(2)}) %collective-permute-start.11) | collective-permute-done | bytes 131104 | tf_op jit(solution)/shard_map/ppermute | solution.py:541
  41.7 0.8 %shard_map.203 = (bf16[128,1024]{1,0:T(8,128)(2,1)}, bf16[32,512]{1,0:T(8,128)(2,1)}) custom-call(bf16[128,1024]{1,0:T(8,128)(2,1)S(1)} %get-tuple-element.30.video_ref, bf16[32,512]{1,0:T(8,128)(2,1)S(1)} %get-tuple-element.31.audio_ref, f32[32,512]{1,0:T(8,128)S(1)} %get-tuple-element.32.gain_ref, f32[288,512]{1,0:T(8,128)S(1)} %get-tuple-element.53.own_ref, ...), custom_call_target="tpu_custom_call" | custom-call | bytes 1835008 | tf_op jit(solution)/shard_map/pallas_call | solution.py:192
  (15 shorter events, 1.0 us)
Async XLA Ops:
  1.8 13.1 %collective-permute-start = (bf16[448,128]{1,0:T(8,128)(2,1)S(1)}, bf16[448,128]{1,0:T(8,128)(2,1)S(1)}, u32[]{:S(2)}, u32[]{:S(2)}) collective-permute-start(bf16[448,128]{1,0:T(8,128)(2,1)S(1)} %get-tuple-element.36), channel_id=1, source_target_pairs={{0,8},{4,12},{8,0},{12,4},{1,9},{5,13},{9,1},{13,5},{2,10},{6,14},... | collective-permute-start | bytes 344072 | tf_op jit(solution)/shard_map/ppermute | solution.py:541
  6.0 9.0 %collective-permute-start.1 = (bf16[448,128]{1,0:T(8,128)(2,1)S(1)}, bf16[448,128]{1,0:T(8,128)(2,1)S(1)}, u32[]{:S(2)}, u32[]{:S(2)}) collective-permute-start(bf16[448,128]{1,0:T(8,128)(2,1)S(1)} %get-tuple-element.37), channel_id=1, source_target_pairs={{0,12},{4,8},{8,4},{12,0},{1,13},{5,9},{9,5},{13,1},{2,14},{6,10},... | collective-permute-start | bytes 344072 | tf_op jit(solution)/shard_map/ppermute | solution.py:541
  7.3 8.5 %collective-permute-start.2 = (bf16[448,128]{1,0:T(8,128)(2,1)S(1)}, bf16[448,128]{1,0:T(8,128)(2,1)S(1)}, u32[]{:S(2)}, u32[]{:S(2)}) collective-permute-start(bf16[448,128]{1,0:T(8,128)(2,1)S(1)} %get-tuple-element.38), channel_id=1, source_target_pairs={{0,4},{4,0},{8,12},{12,8},{1,5},{5,1},{9,13},{13,9},{2,6},{6,2},{1... | collective-permute-start | bytes 344072 | tf_op jit(solution)/shard_map/ppermute | solution.py:541
  7.6 16.5 %collective-permute-start.5 = (bf16[64,256]{1,0:T(8,128)(2,1)S(1)}, bf16[64,256]{1,0:T(8,128)(2,1)S(1)}, u32[]{:S(2)}, u32[]{:S(2)}) collective-permute-start(bf16[64,256]{1,0:T(8,128)(2,1)S(1)} %get-tuple-element.41.rest_0_), channel_id=1, source_target_pairs={{0,4},{4,0},{8,12},{12,8},{1,5},{5,1},{9,13},{13,9},{2,6},{6,2},{1... | collective-permute-start | bytes 98312 | tf_op jit(solution)/shard_map/ppermute | solution.py:541
  16.7 12.8 %collective-permute-start.6 = (bf16[208,128]{1,0:T(8,128)(2,1)S(1)}, bf16[208,128]{1,0:T(8,128)(2,1)S(1)}, u32[]{:S(2)}, u32[]{:S(2)}) collective-permute-start(bf16[208,128]{1,0:T(8,128)(2,1)S(1)} %get-tuple-element.45), channel_id=1, source_target_pairs={{0,8},{4,12},{8,0},{12,4},{1,9},{5,13},{9,1},{13,5},{2,10},{6,14},... | collective-permute-start | bytes 159752 | tf_op jit(solution)/shard_map/ppermute | solution.py:541
  20.2 9.4 %collective-permute-start.7 = (bf16[208,128]{1,0:T(8,128)(2,1)S(1)}, bf16[208,128]{1,0:T(8,128)(2,1)S(1)}, u32[]{:S(2)}, u32[]{:S(2)}) collective-permute-start(bf16[208,128]{1,0:T(8,128)(2,1)S(1)} %get-tuple-element.46), channel_id=1, source_target_pairs={{0,12},{4,8},{8,4},{12,0},{1,13},{5,9},{9,5},{13,1},{2,14},{6,10},... | collective-permute-start | bytes 159752 | tf_op jit(solution)/shard_map/ppermute | solution.py:541
  20.6 8.9 %collective-permute-start.8 = (bf16[208,128]{1,0:T(8,128)(2,1)S(1)}, bf16[208,128]{1,0:T(8,128)(2,1)S(1)}, u32[]{:S(2)}, u32[]{:S(2)}) collective-permute-start(bf16[208,128]{1,0:T(8,128)(2,1)S(1)} %get-tuple-element.47), channel_id=1, source_target_pairs={{0,4},{4,0},{8,12},{12,8},{1,5},{5,1},{9,13},{13,9},{2,6},{6,2},{1... | collective-permute-start | bytes 159752 | tf_op jit(solution)/shard_map/ppermute | solution.py:541
  20.8 6.9 %collective-permute-start.4 = (bf16[64,256]{1,0:T(8,128)(2,1)S(1)}, bf16[64,256]{1,0:T(8,128)(2,1)S(1)}, u32[]{:S(2)}, u32[]{:S(2)}) collective-permute-start(bf16[64,256]{1,0:T(8,128)(2,1)S(1)} %get-tuple-element.41.rest_0_), channel_id=1, source_target_pairs={{0,12},{4,8},{8,4},{12,0},{1,13},{5,9},{9,5},{13,1},{2,14},{6,10},... | collective-permute-start | bytes 98312 | tf_op jit(solution)/shard_map/ppermute | solution.py:541
  24.0 4.8 %collective-permute-start.3 = (bf16[64,256]{1,0:T(8,128)(2,1)S(1)}, bf16[64,256]{1,0:T(8,128)(2,1)S(1)}, u32[]{:S(2)}, u32[]{:S(2)}) collective-permute-start(bf16[64,256]{1,0:T(8,128)(2,1)S(1)} %get-tuple-element.41.rest_0_), channel_id=1, source_target_pairs={{0,8},{4,12},{8,0},{12,4},{1,9},{5,13},{9,1},{13,5},{2,10},{6,14},... | collective-permute-start | bytes 98312 | tf_op jit(solution)/shard_map/ppermute | solution.py:541
  30.5 1.5 %collective-permute-start.12 = (bf16[160,512]{1,0:T(8,128)(2,1)S(1)}, bf16[160,512]{1,0:T(8,128)(2,1)S(1)}, u32[]{:S(2)}, u32[]{:S(2)}) collective-permute-start(bf16[160,512]{1,0:T(8,128)(2,1)S(1)} %get-tuple-element.57), channel_id=1, source_target_pairs={{0,1},{1,0},{2,3},{3,2},{4,5},{5,4},{6,7},{7,6},{8,9},{9,8},{10,11... | collective-permute-start | bytes 491528 | tf_op jit(solution)/shard_map/ppermute | solution.py:541
  31.4 10.4 %collective-permute-start.9 = (bf16[288,512]{1,0:T(8,128)(2,1)S(1)}, bf16[288,512]{1,0:T(8,128)(2,1)S(1)}, u32[]{:S(2)}, u32[]{:S(2)}) collective-permute-start(bf16[288,512]{1,0:T(8,128)(2,1)S(1)} %get-tuple-element.54), channel_id=1, source_target_pairs={{0,1},{1,0},{2,3},{3,2},{4,5},{5,4},{6,7},{7,6},{8,9},{9,8},{10,11... | collective-permute-start | bytes 884744 | tf_op jit(solution)/shard_map/ppermute | solution.py:541
  31.9 2.0 %collective-permute-start.10 = (bf16[128,512]{1,0:T(8,128)(2,1)S(1)}, bf16[128,512]{1,0:T(8,128)(2,1)S(1)}, u32[]{:S(2)}, u32[]{:S(2)}) collective-permute-start(bf16[128,512]{1,0:T(8,128)(2,1)S(1)} %get-tuple-element.56), channel_id=1, source_target_pairs={{0,1},{1,0},{2,3},{3,2},{4,5},{5,4},{6,7},{7,6},{8,9},{9,8},{10,11... | collective-permute-start | bytes 393224 | tf_op jit(solution)/shard_map/ppermute | solution.py:541
  32.3 9.4 %collective-permute-start.13 = (bf16[160,512]{1,0:T(8,128)(2,1)S(1)}, bf16[160,512]{1,0:T(8,128)(2,1)S(1)}, u32[]{:S(2)}, u32[]{:S(2)}) collective-permute-start(bf16[160,512]{1,0:T(8,128)(2,1)S(1)} %shard_map.202), channel_id=1, source_target_pairs={{0,2},{2,0},{1,3},{3,1},{4,6},{6,4},{5,7},{7,5},{8,10},{10,8},{9,1... | collective-permute-start | bytes 491528 | tf_op jit(solution)/shard_map/ppermute | solution.py:541
  33.9 7.8 %collective-permute-start.11 = (bf16[128,512]{1,0:T(8,128)(2,1)S(1)}, bf16[128,512]{1,0:T(8,128)(2,1)S(1)}, u32[]{:S(2)}, u32[]{:S(2)}) collective-permute-start(bf16[128,512]{1,0:T(8,128)(2,1)S(1)} %shard_map.201), channel_id=1, source_target_pairs={{0,2},{2,0},{1,3},{3,1},{4,6},{6,4},{5,7},{7,5},{8,10},{10,8},{9,1... | collective-permute-start | bytes 393224 | tf_op jit(solution)/shard_map/ppermute | solution.py:541

commit v5 on v4

--- a/solution.py
+++ b/solution.py
@@ -181,6 +181,7 @@
 HBM = pl.BlockSpec(memory_space=pltpu.HBM)
 BF16, F32 = jnp.bfloat16, jnp.float32
 LSE_ROWS = 16
+SEQ, FORWARDED, OUT_ORDER = 4, 3, [2, 3, 1]
 
 
 def call(kernel, outs, operands, specs=None, flops=0, scratch=(), limit=8 * 2**20):
@@ -229,7 +230,7 @@
 
 
 def pack_kernel(hops, width, q_ref, k_ref, v_ref, qa_ref, ka_ref, va_ref, *rest):
-    outs, audio, sems = rest[: len(hops)], rest[-2], rest[-1]
+    outs, sems = rest[:-1], rest[-1]
     rows = q_ref.shape[0]
     rows_audio, cols_audio = qa_ref.shape
     me = index_of("seq")
@@ -237,12 +238,33 @@
     for hop, out in zip(hops, outs):
         for i, ref in enumerate((q_ref, k_ref, v_ref)):
             pairs.append((ref.at[:, columns(me ^ hop, width)], out.at[pl.ds(i * rows, rows), :]))
-        for i in range(cols_audio // width):
-            at = pl.ds(3 * rows + i * rows_audio, rows_audio)
-            pairs.append((qa_ref.at[:, pl.ds(i * width, width)], out.at[at, :]))
-    pairs.append((ka_ref, audio.at[pl.ds(0, rows_audio), :]))
-    pairs.append((va_ref, audio.at[pl.ds(rows_audio, rows_audio), :]))
+        if hop == FORWARDED:
+            continue
+        at = 3 * rows
+        for ref in (qa_ref, ka_ref, va_ref):
+            for i in range(cols_audio // width):
+                pairs.append((ref.at[:, pl.ds(i * width, width)], out.at[pl.ds(at, rows_audio), :]))
+                at += rows_audio
     copy_all(pairs, sems)
+
+
+def relay_kernel(got_ref, out_ref):
+    out_ref[...] = got_ref[got_ref.shape[0] - out_ref.shape[0] :, :]
+
+
+class Audio:
+    def __init__(self, ref, rows, cols):
+        self.ref, self.rows, self.blocks = ref, rows, cols // ref.shape[1]
+        self.top = ref.shape[0] - 3 * self.blocks * rows
+
+    def block(self, kind, block):
+        at, column = divmod(block * 128, self.ref.shape[1])
+        top = self.top + (kind * self.blocks + at) * self.rows
+        return self.ref[top : top + self.rows, column : column + 128]
+
+
+def by_hop(blocks, forwarded, rows, cols):
+    return [Audio(forwarded if hop == FORWARDED else ref, rows, cols) for hop, ref in blocks]
 
 
 def one_hot_t(steps_ref):
@@ -303,12 +325,14 @@
     return jnp.concatenate([x[i * head : (i + 1) * head, i * rows : (i + 1) * rows] for i in range(pair)], axis=0)
 
 
-def attend_kernel(n, head, kv_ref, vv_ref, *rest):
+def attend_kernel(hops, head, kv_ref, vv_ref, forwarded, *rest):
+    n = len(hops)
     blocks, sends, (own_ref, own_v2a_ref, own_lse_ref) = rest[:n], rest[n : 2 * n - 1], rest[2 * n - 1 : 2 * n + 2]
     vt_ref, vvt_ref, s_ref, p_ref = rest[2 * n + 2 :]
     rows, cols = kv_ref.shape
     width = blocks[0].shape[1]
     rows_audio = own_v2a_ref.shape[0]
+    audios = by_hop(zip(hops, blocks), forwarded, rows_audio, cols)
     for h in range(width // DHV):
         cut = slice(h * DHV, (h + 1) * DHV)
         for i, ref in enumerate(blocks):
@@ -320,8 +344,7 @@
     parts = []
     for block in range(cols // 128):
         cut = slice(block * 128, (block + 1) * 128)
-        top, part = 3 * rows + (block * 128 // width) * rows_audio, slice(block * 128 % width, block * 128 % width + 128)
-        q = pair_rows(jnp.concatenate([ref[top : top + rows_audio, part] for ref in blocks], axis=0), head)
+        q = pair_rows(jnp.concatenate([audio.block(0, block) for audio in audios], axis=0), head)
         scores = dot_t(kv_ref[:, cut], q)
         for i in range(pair):
             at = slice(i * n * rows_audio, (i + 1) * n * rows_audio)
@@ -388,18 +411,19 @@
         dst[top : top + LSE_ROWS, 0:128] = pltpu.roll(packed, 128 - (j + 1) * rows_audio, 1).astype(BF16)
 
 
-def attend_audio_kernel(hops, head, limit_ref, q_ref, *rest):
-    n = len(hops)
-    blocks, out_ref = rest[:n], rest[n]
-    rows_audio = blocks[0].shape[0] // 2
+def attend_audio_kernel(hops, rows_audio, head, limit_ref, q_ref, forwarded, *rest):
+    blocks, out_ref = rest[:-1], rest[-1]
+    near = iter(blocks)
+    pairs = [(hop, None if hop == FORWARDED else next(near)) for hop in hops]
+    audios = by_hop(pairs, forwarded, rows_audio, q_ref.shape[1])
     me, row = index_of("seq"), lax.broadcasted_iota(jnp.int32, (rows_audio, 1), 0)
     allowed = [(me ^ hop) * rows_audio + row < limit_ref[0] for hop in hops]
     scale = 1.0 / math.sqrt(head)
     for block in range(q_ref.shape[1] // 128):
         cut = slice(block * 128, (block + 1) * 128)
         q = pair_rows(q_ref[:, cut], head)
-        _, p, total = softmax_t([dot_t(ref[0:rows_audio, cut], q) for ref in blocks], scale, allowed)
-        vt = turn(jnp.concatenate([ref[rows_audio : 2 * rows_audio, cut] for ref in blocks], axis=0))
+        _, p, total = softmax_t([dot_t(audio.block(1, block), q) for audio in audios], scale, allowed)
+        vt = turn(jnp.concatenate([audio.block(2, block) for audio in audios], axis=0))
         o = dot(vt, jnp.concatenate(p, axis=0)) * (1.0 / total)
         out_ref[:, cut] = pair_columns(o, head).T.astype(BF16)
 
@@ -532,7 +556,7 @@
     *,
     n,
 ):
-    hops = [0] + order_of(n)
+    hops = [0] + OUT_ORDER
     rows, cols = q_self.shape
     rows_audio, cross = q_v2a.shape
     width = cols // n
@@ -540,16 +564,19 @@
     def trade(x, axis, hop, size):
         return lax.ppermute(x, axis, [(i, i ^ hop) for i in range(size)])
 
-    copies = n * (3 + cross // width) + 2
-    *packed, audio = call(
+    video, audio = 3 * rows, 3 * cross // width * rows_audio
+    packed = call(
         functools.partial(pack_kernel, hops, width),
-        [shape(3 * rows + cross // width * rows_audio, width)] * n + [shape(2 * rows_audio, cross)],
+        [shape(video if hop == FORWARDED else video + audio, width) for hop in hops],
         (q_self, k_self, v_self, q_v2a, k_a2v, v_a2v),
         [HBM] * 6,
-        scratch=[pltpu.SemaphoreType.DMA((copies,))],
-    )
-    blocks = packed[:1] + [trade(x, "seq", hop, n) for x, hop in zip(packed[1:], hops[1:])]
-    audios = [audio] + [trade(audio, "seq", hop, n) for hop in hops[1:]]
+        scratch=[pltpu.SemaphoreType.DMA((3 * n + (n - 1) * audio // rows_audio,))],
+    )
+    blocks = dict(zip(hops, packed))
+    for hop in hops[1:]:
+        blocks[hop] = trade(blocks[hop], "seq", hop, n)
+    (forwarded,) = call(relay_kernel, [shape(audio, width)], (blocks[FORWARDED ^ 1],))
+    forwarded = trade(forwarded, "seq", 1, n)
 
     late = (k_v2a, v_v2a, q_a2v, wo_self, wo_a2v, wo_v2a, video_in, audio_in)
     steps = (video_steps.reshape(1, rows), audio_steps.reshape(1, rows_audio))
@@ -564,21 +591,22 @@
     )
     back = rows + cross // 128 * rows_audio + LSE_ROWS
     result = call(
-        functools.partial(attend_kernel, n, DHC),
+        functools.partial(attend_kernel, hops, DHC),
         [shape(back, width)] * (n - 1)
         + [shape(rows, width), shape(rows_audio, cross, F32), shape(cross // DHC, 128, F32)],
-        (k_own, v_own, *blocks),
+        (k_own, v_own, forwarded, *blocks.values()),
         flops=4 * n * n * rows * rows * width,
         scratch=[pltpu.VMEM((width, n * rows), BF16), pltpu.VMEM((cross, rows), BF16)]
         + [pltpu.VMEM((n * n * rows * width // DHV + cross // DHC * rows, 128), kind) for kind in (F32, BF16)],
     )
     sends, (own, own_v2a, own_lse) = result[: n - 1], result[n - 1 :]
     got = [trade(x, "seq", hop, n) for x, hop in zip(sends, hops[1:])]
+    near = [blocks[hop] for hop in hops if hop != FORWARDED]
     (a2v_att,) = call(
-        functools.partial(attend_audio_kernel, hops, DHC),
+        functools.partial(attend_audio_kernel, hops, rows_audio, DHC),
         [shape(rows, cross)],
-        (audio_len, q_own, *audios),
-        [SMEM] + [VMEM] * (n + 1),
+        (audio_len, q_own, forwarded, *near),
+        [SMEM] + [VMEM] * (len(near) + 2),
         flops=8 * n * rows * rows_audio * cross,
     )
 
@@ -625,7 +653,7 @@
     cols, cross = arrays[2].shape[1], arrays[5].shape[1]
     width = cols // n
     fits = (
-        n in (2, 4, 8)
+        n == SEQ
         and (mp, sub) == (2, 2)
         and width % DHV == 0
         and cross % width == 0
@@ -636,10 +664,6 @@
     if fits:
         return on_device_heads(*arrays, n=n)
     return on_device_gather(*arrays)
-
-
-def order_of(n):
-    return list(range(n // 2, n)) + list(range(n // 2 - 1, 0, -1))
 
 
 def solution(mesh):
@@ -665,6 +689,7 @@
         P("groups"),
     )
     out_specs = (P(("groups", "seq"), ("mp", "sub")), P(("groups", "seq"), ("mp", "sub")))
-    return jax.shard_map(
+    step = jax.shard_map(
         functools.partial(on_device, *(mesh.shape[a] for a in ("seq", "mp", "sub"))), mesh=mesh, in_specs=in_specs, out_specs=out_specs, check_vma=False
     )
+    return step if mesh.shape["seq"] == SEQ else step

time: 42.8 us -> 43.8 us (1.023)
  waiting for transfers between devices: 12.4 us -> 18.3 us
  starting transfers between devices: 18.6 us -> 13.5 us
    ppermute x14 -> x12, waiting for transfers between devices: 12.4 us -> 18.3 us  [trade(): return lax.ppermute(x, axis, [(i, i ^ hop) for i in range(size)])]
    ppermute x14 -> x12, starting transfers between devices: 18.6 us -> 13.5 us  [trade(): return lax.ppermute(x, axis, [(i, i ^ hop) for i in range(size)])]
    pallas_call x10 -> x11, Pallas kernels: 9.11 us -> 9.22 us  [call(): pl.pallas_call(kernel, out_shape=tuple(outs), in_specs=specs or [VMEM] *...]
  transfers between devices with their start and end apart: 14 -> 12, of which waited for: 5 -> 4; matrix products, arithmetic and copies ran while one was open for 3% -> 3% of each run, Pallas kernels for 14% -> 12%
where the time goes in v5:
time: 43.8 us; the launch traced here: 43.5 us
  waiting for transfers between devices  18.3 us (42%)
  starting transfers between devices  13.5 us (31%)
  Pallas kernels  9.22 us (21%)
  between operations  1.39 us (3%)
  local copies, waits for them, and re-layouts  1.1 us (3%)
    ppermute x12, waiting for transfers between devices, trade(): return lax.ppermute(x, axis, [(i, i ^ hop) for i in range(size)])  18.3 us
    ppermute x12, starting transfers between devices, trade(): return lax.ppermute(x, axis, [(i, i ^ hop) for i in range(size)])  13.5 us
    pallas_call x11, Pallas kernels, call(): pl.pallas_call(kernel, out_shape=tuple(outs), in_specs=specs or [VMEM] *...  9.22 us
    unnamed x1, local copies, waits for them, and re-layouts  1.1 us
  transfers between devices with their start and end apart: 12, of which 4 were waited for; matrix products, arithmetic and copies ran while one was open for 3% of the time, Pallas kernels for 12%

profile of v5, /device:TPU:0, one launch (start us, length us, event | category | flops | bytes accessed | tf_op | source)
XLA Modules:
  0.0 43.5 jit_solution(10417255592153107209)
XLA Ops:
  0.6 1.3 %shard_map.195 = (bf16[576,128]{1,0:T(8,128)(2,1)S(1)}, bf16[576,128]{1,0:T(8,128)(2,1)S(1)}, bf16[384,128]{1,0:T(8,128)(2,1)S(1)}, bf16[576,128]{1,0:T(8,128)(2,1)S(1)}) custom-call(bf16[128,512]{1,0:T(8,128)(2,1)} %q_ref.1, bf16[128,512]{1,0:T(8,128)(2,1)} %k_ref.1, bf16[128,512]{1,0:T(8,128)(2,1)} %v_ref.1, bf16[32,256]{1,0:T(8,128)(2,1)} %qa_ref.1, ...), custom_call_target="tpu_custom_call" | custom-call | bytes 983040 | tf_op jit(solution)/shard_map/pallas_call | solution.py:193
  2.0 4.1 %collective-permute-start = (bf16[576,128]{1,0:T(8,128)(2,1)S(1)}, bf16[576,128]{1,0:T(8,128)(2,1)S(1)}, u32[]{:S(2)}, u32[]{:S(2)}) collective-permute-start(bf16[576,128]{1,0:T(8,128)(2,1)S(1)} %get-tuple-element.34), channel_id=1, source_target_pairs={{0,8},{4,12},{8,0},{12,4},{1,9},{5,13},{9,1},{13,5},{2,10},{6,14},... | collective-permute-start | bytes 442376 | tf_op jit(solution)/shard_map/ppermute | solution.py:565
  6.1 1.6 %collective-permute-start.3 = (bf16[576,128]{1,0:T(8,128)(2,1)S(1)}, bf16[576,128]{1,0:T(8,128)(2,1)S(1)}, u32[]{:S(2)}, u32[]{:S(2)}) collective-permute-start(bf16[576,128]{1,0:T(8,128)(2,1)S(1)} %get-tuple-element.37), channel_id=1, source_target_pairs={{0,4},{4,0},{8,12},{12,8},{1,5},{5,1},{9,13},{13,9},{2,6},{6,2},{1... | collective-permute-start | bytes 442376 | tf_op jit(solution)/shard_map/ppermute | solution.py:565
  7.7 7.1 %collective-permute-done.got_ref.rest_1_ = bf16[576,128]{1,0:T(8,128)(2,1)S(1)} collective-permute-done((bf16[576,128]{1,0:T(8,128)(2,1)S(1)}, bf16[576,128]{1,0:T(8,128)(2,1)S(1)}, u32[]{:S(2)}, u32[]{:S(2)}) %collective-permute-start) | collective-permute-done | bytes 147488 | tf_op jit(solution)/shard_map/ppermute | solution.py:565
  15.5 1.1 %copy.21 = bf16[2,8,2,4096]{3,1,2,0:T(8,128)(2,1)S(1)} copy(bf16[2,8,2,4096]{3,2,1,0:T(2,128)(2,1)} %bitcast.5) | data formatting | bytes 524288
  16.6 3.4 %shard_map.194 = (bf16[128,8192]{1,0:T(8,128)(2,1)S(1)}, f32[32,512]{1,0:T(8,128)S(1)}, bf16[128,256]{1,0:T(8,128)(2,1)S(1)}, bf16[128,256]{1,0:T(8,128)(2,1)S(1...) custom-call(s32[1]{0:T(128)S(6)} %copy.22.limit_ref, ...), custom_call_target="tpu_custom_call" | custom-call | bytes 18154116 | tf_op jit(solution)/shard_map/pallas_call | solution.py:193
  20.0 0.0 collective-permute-done.2.rest_2_
  20.0 0.9 %shard_map.197 = (bf16[208,128]{1,0:T(8,128)(2,1)S(1)}, bf16[208,128]{1,0:T(8,128)(2,1)S(1)}, bf16[208,128]{1,0:T(8,128)(2,1)S(1)}, bf16[128,128]{1,0:T(8,128)(2...) custom-call(bf16[128,256]{1,0:T(8,128)(2,1)S(1)} %get-tuple-element.32.kv_ref, ...), custom_call_target="tpu_custom_call" | custom-call | flops 134217728 | bytes 948224 | tf_op jit(solution)/shard_map/pallas_call | solution.py:193
  20.9 3.6 %collective-permute-start.4 = (bf16[208,128]{1,0:T(8,128)(2,1)S(1)}, bf16[208,128]{1,0:T(8,128)(2,1)S(1)}, u32[]{:S(2)}, u32[]{:S(2)}) collective-permute-start(bf16[208,128]{1,0:T(8,128)(2,1)S(1)} %get-tuple-element.43), channel_id=1, source_target_pairs={{0,8},{4,12},{8,0},{12,4},{1,9},{5,13},{9,1},{13,5},{2,10},{6,14},... | collective-permute-start | bytes 159752 | tf_op jit(solution)/shard_map/ppermute | solution.py:565
  24.6 0.8 %collective-permute-start.5 = (bf16[208,128]{1,0:T(8,128)(2,1)S(1)}, bf16[208,128]{1,0:T(8,128)(2,1)S(1)}, u32[]{:S(2)}, u32[]{:S(2)}) collective-permute-start(bf16[208,128]{1,0:T(8,128)(2,1)S(1)} %get-tuple-element.44), channel_id=1, source_target_pairs={{0,12},{4,8},{8,4},{12,0},{1,13},{5,9},{9,5},{13,1},{2,14},{6,10},... | collective-permute-start | bytes 159752 | tf_op jit(solution)/shard_map/ppermute | solution.py:565
  25.4 0.7 %shard_map.198.a2v_ref = bf16[128,256]{1,0:T(8,128)(2,1)S(1)} custom-call(s32[1]{0:T(128)S(6)} %copy.22.limit_ref, bf16[128,256]{1,0:T(8,128)(2,1)S(1)} %get-tuple-element.39.q_ref, bf16[192,128]{1,0:T(8,128)(2,1)S(1)} %collective-permute-done.1.forwarded, bf16[576,128]{1,0:T(8,128)(2,1)S(1)} %get-tuple-element.35.rest_0_, ...), custom_call_target="tpu_custom_call" | custom-call | flops 33554432 | bytes 622596 | tf_op jit(solution)/shard_map/pallas_call | solution.py:193
  26.1 1.7 %collective-permute-done.4.rest_0_ = bf16[208,128]{1,0:T(8,128)(2,1)S(1)} collective-permute-done((bf16[208,128]{1,0:T(8,128)(2,1)S(1)}, bf16[208,128]{1,0:T(8,128)(2,1)S(1)}, u32[]{:S(2)}, u32[]{:S(2)}) %collective-permute-start.4) | collective-permute-done | bytes 53280 | tf_op jit(solution)/shard_map/ppermute | solution.py:565
  27.8 2.7 %collective-permute-done.5.rest_1_ = bf16[208,128]{1,0:T(8,128)(2,1)S(1)} collective-permute-done((bf16[208,128]{1,0:T(8,128)(2,1)S(1)}, bf16[208,128]{1,0:T(8,128)(2,1)S(1)}, u32[]{:S(2)}, u32[]{:S(2)}) %collective-permute-start.5) | collective-permute-done | bytes 53280 | tf_op jit(solution)/shard_map/ppermute | solution.py:565
  30.5 0.3 shard_map.199
  30.8 0.6 %shard_map.200 = (bf16[160,512]{1,0:T(8,128)(2,1)S(1)}, bf16[32,256]{1,0:T(8,128)(2,1)S(1)}, f32[128,512]{1,0:T(8,128)S(1)}) custom-call(bf16[128,512]{1,0:T(8,128)(2,1)S(1)} %get-tuple-element.46.self_ref, bf16[128,256]{1,0:T(8,128)(2,1)S(1)} %shard_map.198.a2v_ref, bf16[512,4096]{1,0:T(8,128)(2,1)S(1)} %get-tuple-element.40.ws_ref, ...), custom_call_target="tpu_custom_call" | custom-call | flops 201326592 | bytes 10270720 | tf_op jit(solution)/shard_map/pallas_call | solution.py:193
  31.4 0.1 collective-permute-start.10
  31.5 0.8 %shard_map.201 = (bf16[288,512]{1,0:T(8,128)(2,1)S(1)}, f32[288,512]{1,0:T(8,128)S(1)}) custom-call(bf16[128,512]{1,0:T(8,128)(2,1)S(1)} %get-tuple-element.46.self_ref, bf16[128,256]{1,0:T(8,128)(2,1)S(1)} %shard_map.198.a2v_ref, bf16[32,256]{1,0:T(8,128)(2,1)S(1)} %get-tuple-element.50.audio_ref, bf16[512,4096]{1,0:T(8,128)(2,1)S(1)} %get-tuple-element.40.ws_ref, ...), custom_call_target="tpu_custom_call" | custom-call | flops 402653184 | bytes 10534912 | tf_op jit(solution)/shard_map/pallas_call | solution.py:193
  32.3 0.6 %collective-permute-start.7 = (bf16[288,512]{1,0:T(8,128)(2,1)S(1)}, bf16[288,512]{1,0:T(8,128)(2,1)S(1)}, u32[]{:S(2)}, u32[]{:S(2)}) collective-permute-start(bf16[288,512]{1,0:T(8,128)(2,1)S(1)} %get-tuple-element.52), channel_id=1, source_target_pairs={{0,1},{1,0},{2,3},{3,2},{4,5},{5,4},{6,7},{7,6},{8,9},{9,8},{10,11... | collective-permute-start | bytes 884744 | tf_op jit(solution)/shard_map/ppermute | solution.py:565
  32.9 0.1 collective-permute-start.8
  32.9 0.3 shard_map.203
  33.3 1.6 %collective-permute-start.11 = (bf16[160,512]{1,0:T(8,128)(2,1)S(1)}, bf16[160,512]{1,0:T(8,128)(2,1)S(1)}, u32[]{:S(2)}, u32[]{:S(2)}) collective-permute-start(bf16[160,512]{1,0:T(8,128)(2,1)S(1)} %shard_map.203), channel_id=1, source_target_pairs={{0,2},{2,0},{1,3},{3,1},{4,6},{6,4},{5,7},{7,5},{8,10},{10,8},{9,1... | collective-permute-start | bytes 491528 | tf_op jit(solution)/shard_map/ppermute | solution.py:565
  34.9 1.0 %collective-permute-start.9 = (bf16[128,512]{1,0:T(8,128)(2,1)S(1)}, bf16[128,512]{1,0:T(8,128)(2,1)S(1)}, u32[]{:S(2)}, u32[]{:S(2)}) collective-permute-start(bf16[128,512]{1,0:T(8,128)(2,1)S(1)} %shard_map.202), channel_id=1, source_target_pairs={{0,2},{2,0},{1,3},{3,1},{4,6},{6,4},{5,7},{7,5},{8,10},{10,8},{9,1... | collective-permute-start | bytes 393224 | tf_op jit(solution)/shard_map/ppermute | solution.py:565
  35.9 6.8 %collective-permute-done.9.low_ref = bf16[128,512]{1,0:T(8,128)(2,1)S(1)} collective-permute-done((bf16[128,512]{1,0:T(8,128)(2,1)S(1)}, bf16[128,512]{1,0:T(8,128)(2,1)S(1)}, u32[]{:S(2)}, u32[]{:S(2)}) %collective-permute-start.9) | collective-permute-done | bytes 131104 | tf_op jit(solution)/shard_map/ppermute | solution.py:565
  42.7 0.8 %shard_map.204 = (bf16[128,1024]{1,0:T(8,128)(2,1)}, bf16[32,512]{1,0:T(8,128)(2,1)}) custom-call(bf16[128,1024]{1,0:T(8,128)(2,1)S(1)} %get-tuple-element.29.video_ref, bf16[32,512]{1,0:T(8,128)(2,1)S(1)} %get-tuple-element.30.audio_ref, f32[32,512]{1,0:T(8,128)S(1)} %get-tuple-element.31.gain_ref, f32[288,512]{1,0:T(8,128)S(1)} %get-tuple-element.51.own_ref, ...), custom_call_target="tpu_custom_call" | custom-call | bytes 1835008 | tf_op jit(solution)/shard_map/pallas_call | solution.py:193
  (12 shorter events, 0.1 us)
Async XLA Ops:
  2.0 12.8 %collective-permute-start = (bf16[576,128]{1,0:T(8,128)(2,1)S(1)}, bf16[576,128]{1,0:T(8,128)(2,1)S(1)}, u32[]{:S(2)}, u32[]{:S(2)}) collective-permute-start(bf16[576,128]{1,0:T(8,128)(2,1)S(1)} %get-tuple-element.34), channel_id=1, source_target_pairs={{0,8},{4,12},{8,0},{12,4},{1,9},{5,13},{9,1},{13,5},{2,10},{6,14},... | collective-permute-start | bytes 442376 | tf_op jit(solution)/shard_map/ppermute | solution.py:565
  6.1 13.9 %collective-permute-start.3 = (bf16[576,128]{1,0:T(8,128)(2,1)S(1)}, bf16[576,128]{1,0:T(8,128)(2,1)S(1)}, u32[]{:S(2)}, u32[]{:S(2)}) collective-permute-start(bf16[576,128]{1,0:T(8,128)(2,1)S(1)} %get-tuple-element.37), channel_id=1, source_target_pairs={{0,4},{4,0},{8,12},{12,8},{1,5},{5,1},{9,13},{13,9},{2,6},{6,2},{1... | collective-permute-start | bytes 442376 | tf_op jit(solution)/shard_map/ppermute | solution.py:565
  7.7 12.3 %collective-permute-start.2 = (bf16[384,128]{1,0:T(8,128)(2,1)S(1)}, bf16[384,128]{1,0:T(8,128)(2,1)S(1)}, u32[]{:S(2)}, u32[]{:S(2)}) collective-permute-start(bf16[384,128]{1,0:T(8,128)(2,1)S(1)} %get-tuple-element.36), channel_id=1, source_target_pairs={{0,12},{4,8},{8,4},{12,0},{1,13},{5,9},{9,5},{13,1},{2,14},{6,10},... | collective-permute-start | bytes 294920 | tf_op jit(solution)/shard_map/ppermute | solution.py:565
  14.8 5.2 %collective-permute-start.1 = (bf16[192,128]{1,0:T(8,128)(2,1)S(1)}, bf16[192,128]{1,0:T(8,128)(2,1)S(1)}, u32[]{:S(2)}, u32[]{:S(2)}) collective-permute-start(bf16[192,128]{1,0:T(8,128)(2,1)S(1)} %shard_map.196), channel_id=1, source_target_pairs={{0,4},{4,0},{8,12},{12,8},{1,5},{5,1},{9,13},{13,9},{2,6},{6,2},{1... | collective-permute-start | bytes 147464 | tf_op jit(solution)/shard_map/ppermute | solution.py:565
  20.9 6.8 %collective-permute-start.4 = (bf16[208,128]{1,0:T(8,128)(2,1)S(1)}, bf16[208,128]{1,0:T(8,128)(2,1)S(1)}, u32[]{:S(2)}, u32[]{:S(2)}) collective-permute-start(bf16[208,128]{1,0:T(8,128)(2,1)S(1)} %get-tuple-element.43), channel_id=1, source_target_pairs={{0,8},{4,12},{8,0},{12,4},{1,9},{5,13},{9,1},{13,5},{2,10},{6,14},... | collective-permute-start | bytes 159752 | tf_op jit(solution)/shard_map/ppermute | solution.py:565
  24.6 5.9 %collective-permute-start.5 = (bf16[208,128]{1,0:T(8,128)(2,1)S(1)}, bf16[208,128]{1,0:T(8,128)(2,1)S(1)}, u32[]{:S(2)}, u32[]{:S(2)}) collective-permute-start(bf16[208,128]{1,0:T(8,128)(2,1)S(1)} %get-tuple-element.44), channel_id=1, source_target_pairs={{0,12},{4,8},{8,4},{12,0},{1,13},{5,9},{9,5},{13,1},{2,14},{6,10},... | collective-permute-start | bytes 159752 | tf_op jit(solution)/shard_map/ppermute | solution.py:565
  25.4 5.1 %collective-permute-start.6 = (bf16[208,128]{1,0:T(8,128)(2,1)S(1)}, bf16[208,128]{1,0:T(8,128)(2,1)S(1)}, u32[]{:S(2)}, u32[]{:S(2)}) collective-permute-start(bf16[208,128]{1,0:T(8,128)(2,1)S(1)} %get-tuple-element.45), channel_id=1, source_target_pairs={{0,4},{4,0},{8,12},{12,8},{1,5},{5,1},{9,13},{13,9},{2,6},{6,2},{1... | collective-permute-start | bytes 159752 | tf_op jit(solution)/shard_map/ppermute | solution.py:565
  31.4 1.5 %collective-permute-start.10 = (bf16[160,512]{1,0:T(8,128)(2,1)S(1)}, bf16[160,512]{1,0:T(8,128)(2,1)S(1)}, u32[]{:S(2)}, u32[]{:S(2)}) collective-permute-start(bf16[160,512]{1,0:T(8,128)(2,1)S(1)} %get-tuple-element.55), channel_id=1, source_target_pairs={{0,1},{1,0},{2,3},{3,2},{4,5},{5,4},{6,7},{7,6},{8,9},{9,8},{10,11... | collective-permute-start | bytes 491528 | tf_op jit(solution)/shard_map/ppermute | solution.py:565
  32.3 10.4 %collective-permute-start.7 = (bf16[288,512]{1,0:T(8,128)(2,1)S(1)}, bf16[288,512]{1,0:T(8,128)(2,1)S(1)}, u32[]{:S(2)}, u32[]{:S(2)}) collective-permute-start(bf16[288,512]{1,0:T(8,128)(2,1)S(1)} %get-tuple-element.52), channel_id=1, source_target_pairs={{0,1},{1,0},{2,3},{3,2},{4,5},{5,4},{6,7},{7,6},{8,9},{9,8},{10,11... | collective-permute-start | bytes 884744 | tf_op jit(solution)/shard_map/ppermute | solution.py:565
  32.9 2.0 %collective-permute-start.8 = (bf16[128,512]{1,0:T(8,128)(2,1)S(1)}, bf16[128,512]{1,0:T(8,128)(2,1)S(1)}, u32[]{:S(2)}, u32[]{:S(2)}) collective-permute-start(bf16[128,512]{1,0:T(8,128)(2,1)S(1)} %get-tuple-element.54), channel_id=1, source_target_pairs={{0,1},{1,0},{2,3},{3,2},{4,5},{5,4},{6,7},{7,6},{8,9},{9,8},{10,11... | collective-permute-start | bytes 393224 | tf_op jit(solution)/shard_map/ppermute | solution.py:565
  33.3 9.4 %collective-permute-start.11 = (bf16[160,512]{1,0:T(8,128)(2,1)S(1)}, bf16[160,512]{1,0:T(8,128)(2,1)S(1)}, u32[]{:S(2)}, u32[]{:S(2)}) collective-permute-start(bf16[160,512]{1,0:T(8,128)(2,1)S(1)} %shard_map.203), channel_id=1, source_target_pairs={{0,2},{2,0},{1,3},{3,1},{4,6},{6,4},{5,7},{7,5},{8,10},{10,8},{9,1... | collective-permute-start | bytes 491528 | tf_op jit(solution)/shard_map/ppermute | solution.py:565
  34.9 7.8 %collective-permute-start.9 = (bf16[128,512]{1,0:T(8,128)(2,1)S(1)}, bf16[128,512]{1,0:T(8,128)(2,1)S(1)}, u32[]{:S(2)}, u32[]{:S(2)}) collective-permute-start(bf16[128,512]{1,0:T(8,128)(2,1)S(1)} %shard_map.202), channel_id=1, source_target_pairs={{0,2},{2,0},{1,3},{3,1},{4,6},{6,4},{5,7},{7,5},{8,10},{10,8},{9,1... | collective-permute-start | bytes 393224 | tf_op jit(solution)/shard_map/ppermute | solution.py:565

commit v6 on v5

--- a/solution.py
+++ b/solution.py
@@ -181,7 +181,7 @@
 HBM = pl.BlockSpec(memory_space=pltpu.HBM)
 BF16, F32 = jnp.bfloat16, jnp.float32
 LSE_ROWS = 16
-SEQ, FORWARDED, OUT_ORDER = 4, 3, [2, 3, 1]
+SEQ, FORWARDED, OUT_ORDER = 4, 3, [3, 2, 1]
 
 
 def call(kernel, outs, operands, specs=None, flops=0, scratch=(), limit=8 * 2**20):
@@ -238,10 +238,8 @@
     for hop, out in zip(hops, outs):
         for i, ref in enumerate((q_ref, k_ref, v_ref)):
             pairs.append((ref.at[:, columns(me ^ hop, width)], out.at[pl.ds(i * rows, rows), :]))
-        if hop == FORWARDED:
-            continue
         at = 3 * rows
-        for ref in (qa_ref, ka_ref, va_ref):
+        for ref in (qa_ref,) if hop == FORWARDED else (qa_ref, ka_ref, va_ref):
             for i in range(cols_audio // width):
                 pairs.append((ref.at[:, pl.ds(i * width, width)], out.at[pl.ds(at, rows_audio), :]))
                 at += rows_audio
@@ -252,19 +250,10 @@
     out_ref[...] = got_ref[got_ref.shape[0] - out_ref.shape[0] :, :]
 
 
-class Audio:
-    def __init__(self, ref, rows, cols):
-        self.ref, self.rows, self.blocks = ref, rows, cols // ref.shape[1]
-        self.top = ref.shape[0] - 3 * self.blocks * rows
-
-    def block(self, kind, block):
-        at, column = divmod(block * 128, self.ref.shape[1])
-        top = self.top + (kind * self.blocks + at) * self.rows
-        return self.ref[top : top + self.rows, column : column + 128]
-
-
-def by_hop(blocks, forwarded, rows, cols):
-    return [Audio(forwarded if hop == FORWARDED else ref, rows, cols) for hop, ref in blocks]
+def audio_block(ref, end, rows, cols, block):
+    at, column = divmod(block * 128, ref.shape[1])
+    top = ref.shape[0] - end * (cols // ref.shape[1]) * rows + at * rows
+    return ref[top : top + rows, column : column + 128]
 
 
 def one_hot_t(steps_ref):
@@ -325,14 +314,14 @@
     return jnp.concatenate([x[i * head : (i + 1) * head, i * rows : (i + 1) * rows] for i in range(pair)], axis=0)
 
 
-def attend_kernel(hops, head, kv_ref, vv_ref, forwarded, *rest):
+def attend_kernel(hops, head, kv_ref, vv_ref, *rest):
     n = len(hops)
     blocks, sends, (own_ref, own_v2a_ref, own_lse_ref) = rest[:n], rest[n : 2 * n - 1], rest[2 * n - 1 : 2 * n + 2]
     vt_ref, vvt_ref, s_ref, p_ref = rest[2 * n + 2 :]
     rows, cols = kv_ref.shape
     width = blocks[0].shape[1]
     rows_audio = own_v2a_ref.shape[0]
-    audios = by_hop(zip(hops, blocks), forwarded, rows_audio, cols)
+    ends = [1 if hop == FORWARDED else 3 for hop in hops]
     for h in range(width // DHV):
         cut = slice(h * DHV, (h + 1) * DHV)
         for i, ref in enumerate(blocks):
@@ -344,7 +333,8 @@
     parts = []
     for block in range(cols // 128):
         cut = slice(block * 128, (block + 1) * 128)
-        q = pair_rows(jnp.concatenate([audio.block(0, block) for audio in audios], axis=0), head)
+        q = [audio_block(ref, end, rows_audio, cols, block) for ref, end in zip(blocks, ends)]
+        q = pair_rows(jnp.concatenate(q, axis=0), head)
         scores = dot_t(kv_ref[:, cut], q)
         for i in range(pair):
             at = slice(i * n * rows_audio, (i + 1) * n * rows_audio)
@@ -411,19 +401,17 @@
         dst[top : top + LSE_ROWS, 0:128] = pltpu.roll(packed, 128 - (j + 1) * rows_audio, 1).astype(BF16)
 
 
-def attend_audio_kernel(hops, rows_audio, head, limit_ref, q_ref, forwarded, *rest):
+def attend_audio_kernel(hops, rows_audio, head, limit_ref, q_ref, *rest):
     blocks, out_ref = rest[:-1], rest[-1]
-    near = iter(blocks)
-    pairs = [(hop, None if hop == FORWARDED else next(near)) for hop in hops]
-    audios = by_hop(pairs, forwarded, rows_audio, q_ref.shape[1])
+    cols = q_ref.shape[1]
     me, row = index_of("seq"), lax.broadcasted_iota(jnp.int32, (rows_audio, 1), 0)
     allowed = [(me ^ hop) * rows_audio + row < limit_ref[0] for hop in hops]
     scale = 1.0 / math.sqrt(head)
     for block in range(q_ref.shape[1] // 128):
         cut = slice(block * 128, (block + 1) * 128)
         q = pair_rows(q_ref[:, cut], head)
-        _, p, total = softmax_t([dot_t(audio.block(1, block), q) for audio in audios], scale, allowed)
-        vt = turn(jnp.concatenate([audio.block(2, block) for audio in audios], axis=0))
+        _, p, total = softmax_t([dot_t(audio_block(ref, 2, rows_audio, cols, block), q) for ref in blocks], scale, allowed)
+        vt = turn(jnp.concatenate([audio_block(ref, 1, rows_audio, cols, block) for ref in blocks], axis=0))
         o = dot(vt, jnp.concatenate(p, axis=0)) * (1.0 / total)
         out_ref[:, cut] = pair_columns(o, head).T.astype(BF16)
 
@@ -564,18 +552,18 @@
     def trade(x, axis, hop, size):
         return lax.ppermute(x, axis, [(i, i ^ hop) for i in range(size)])
 
-    video, audio = 3 * rows, 3 * cross // width * rows_audio
+    video, audio = 3 * rows, cross // width * rows_audio
     packed = call(
         functools.partial(pack_kernel, hops, width),
-        [shape(video if hop == FORWARDED else video + audio, width) for hop in hops],
+        [shape(video + (1 if hop == FORWARDED else 3) * audio, width) for hop in hops],
         (q_self, k_self, v_self, q_v2a, k_a2v, v_a2v),
         [HBM] * 6,
-        scratch=[pltpu.SemaphoreType.DMA((3 * n + (n - 1) * audio // rows_audio,))],
+        scratch=[pltpu.SemaphoreType.DMA((3 * n + (3 * n - 2) * audio // rows_audio,))],
     )
     blocks = dict(zip(hops, packed))
     for hop in hops[1:]:
         blocks[hop] = trade(blocks[hop], "seq", hop, n)
-    (forwarded,) = call(relay_kernel, [shape(audio, width)], (blocks[FORWARDED ^ 1],))
+    (forwarded,) = call(relay_kernel, [shape(2 * audio, width)], (blocks[FORWARDED ^ 1],))
     forwarded = trade(forwarded, "seq", 1, n)
 
     late = (k_v2a, v_v2a, q_a2v, wo_self, wo_a2v, wo_v2a, video_in, audio_in)
@@ -594,19 +582,19 @@
         functools.partial(attend_kernel, hops, DHC),
         [shape(back, width)] * (n - 1)
         + [shape(rows, width), shape(rows_audio, cross, F32), shape(cross // DHC, 128, F32)],
-        (k_own, v_own, forwarded, *blocks.values()),
+        (k_own, v_own, *blocks.values()),
         flops=4 * n * n * rows * rows * width,
         scratch=[pltpu.VMEM((width, n * rows), BF16), pltpu.VMEM((cross, rows), BF16)]
         + [pltpu.VMEM((n * n * rows * width // DHV + cross // DHC * rows, 128), kind) for kind in (F32, BF16)],
     )
     sends, (own, own_v2a, own_lse) = result[: n - 1], result[n - 1 :]
     got = [trade(x, "seq", hop, n) for x, hop in zip(sends, hops[1:])]
-    near = [blocks[hop] for hop in hops if hop != FORWARDED]
+    audios = [forwarded if hop == FORWARDED else blocks[hop] for hop in hops]
     (a2v_att,) = call(
         functools.partial(attend_audio_kernel, hops, rows_audio, DHC),
         [shape(rows, cross)],
-        (audio_len, q_own, forwarded, *near),
-        [SMEM] + [VMEM] * (len(near) + 2),
+        (audio_len, q_own, *audios),
+        [SMEM] + [VMEM] * (n + 1),
         flops=8 * n * rows * rows_audio * cross,
     )
 
@@ -689,7 +677,6 @@
         P("groups"),
     )
     out_specs = (P(("groups", "seq"), ("mp", "sub")), P(("groups", "seq"), ("mp", "sub")))
-    step = jax.shard_map(
+    return jax.shard_map(
         functools.partial(on_device, *(mesh.shape[a] for a in ("seq", "mp", "sub"))), mesh=mesh, in_specs=in_specs, out_specs=out_specs, check_vma=False
     )
-    return step if mesh.shape["seq"] == SEQ else step

time: 43.8 us -> 40.8 us (0.932)
  waiting for transfers between devices: 18.3 us -> 13.8 us
  starting transfers between devices: 13.5 us -> 15 us
    ppermute x12, waiting for transfers between devices: 18.3 us -> 13.8 us  [trade(): return lax.ppermute(x, axis, [(i, i ^ hop) for i in range(size)])]
    ppermute x12, starting transfers between devices: 13.5 us -> 15 us  [trade(): return lax.ppermute(x, axis, [(i, i ^ hop) for i in range(size)])]
  transfers between devices with their start and end apart: 12 -> 12, of which waited for: 4 -> 3; matrix products, arithmetic and copies ran while one was open for 3% -> 3% of each run, Pallas kernels for 12% -> 13%
where the time goes in v6:
time: 40.8 us; the launch traced here: 40.6 us
  starting transfers between devices  15 us (37%)
  waiting for transfers between devices  13.8 us (34%)
  Pallas kernels  9.25 us (23%)
  between operations  1.39 us (3%)
  local copies, waits for them, and re-layouts  1.1 us (3%)
    ppermute x12, starting transfers between devices, trade(): return lax.ppermute(x, axis, [(i, i ^ hop) for i in range(size)])  15 us
    ppermute x12, waiting for transfers between devices, trade(): return lax.ppermute(x, axis, [(i, i ^ hop) for i in range(size)])  13.8 us
    pallas_call x11, Pallas kernels, call(): pl.pallas_call(kernel, out_shape=tuple(outs), in_specs=specs or [VMEM] *...  9.25 us
    unnamed x1, local copies, waits for them, and re-layouts  1.1 us
  transfers between devices with their start and end apart: 12, of which 3 were waited for; matrix products, arithmetic and copies ran while one was open for 3% of the time, Pallas kernels for 13%

profile of v6, /device:TPU:0, one launch (start us, length us, event | category | flops | bytes accessed | tf_op | source)
XLA Modules:
  0.0 40.6 jit_solution(10228174003894413809)
XLA Ops:
  0.6 1.4 %shard_map.195 = (bf16[576,128]{1,0:T(8,128)(2,1)S(1)}, bf16[448,128]{1,0:T(8,128)(2,1)S(1)}, bf16[576,128]{1,0:T(8,128)(2,1)S(1)}, bf16[576,128]{1,0:T(8,128)(2,1)S(1)}) custom-call(bf16[128,512]{1,0:T(8,128)(2,1)} %q_ref.1, bf16[128,512]{1,0:T(8,128)(2,1)} %k_ref.1, bf16[128,512]{1,0:T(8,128)(2,1)} %v_ref.1, bf16[32,256]{1,0:T(8,128)(2,1)} %qa_ref.1, ...), custom_call_target="tpu_custom_call" | custom-call | bytes 999424 | tf_op jit(solution)/shard_map/pallas_call | solution.py:193
  2.0 4.1 %collective-permute-start.1 = (bf16[576,128]{1,0:T(8,128)(2,1)S(1)}, bf16[576,128]{1,0:T(8,128)(2,1)S(1)}, u32[]{:S(2)}, u32[]{:S(2)}) collective-permute-start(bf16[576,128]{1,0:T(8,128)(2,1)S(1)} %get-tuple-element.36), channel_id=1, source_target_pairs={{0,8},{4,12},{8,0},{12,4},{1,9},{5,13},{9,1},{13,5},{2,10},{6,14},... | collective-permute-start | bytes 442376 | tf_op jit(solution)/shard_map/ppermute | solution.py:553
  6.1 1.6 %collective-permute-start.2 = (bf16[576,128]{1,0:T(8,128)(2,1)S(1)}, bf16[576,128]{1,0:T(8,128)(2,1)S(1)}, u32[]{:S(2)}, u32[]{:S(2)}) collective-permute-start(bf16[576,128]{1,0:T(8,128)(2,1)S(1)} %get-tuple-element.37), channel_id=1, source_target_pairs={{0,4},{4,0},{8,12},{12,8},{1,5},{5,1},{9,13},{13,9},{2,6},{6,2},{1... | collective-permute-start | bytes 442376 | tf_op jit(solution)/shard_map/ppermute | solution.py:553
  8.4 1.1 %copy.21 = bf16[2,8,2,4096]{3,1,2,0:T(8,128)(2,1)S(1)} copy(bf16[2,8,2,4096]{3,2,1,0:T(2,128)(2,1)} %bitcast.5) | data formatting | bytes 524288
  9.5 3.4 %shard_map.194 = (bf16[128,8192]{1,0:T(8,128)(2,1)S(1)}, f32[32,512]{1,0:T(8,128)S(1)}, bf16[128,256]{1,0:T(8,128)(2,1)S(1)}, bf16[128,256]{1,0:T(8,128)(2,1)S(1...) custom-call(s32[1]{0:T(128)S(6)} %copy.22.limit_ref, ...), custom_call_target="tpu_custom_call" | custom-call | bytes 18154116 | tf_op jit(solution)/shard_map/pallas_call | solution.py:193
  12.9 3.9 %collective-permute-done.rest_1_ = bf16[448,128]{1,0:T(8,128)(2,1)S(1)} collective-permute-done((bf16[448,128]{1,0:T(8,128)(2,1)S(1)}, bf16[448,128]{1,0:T(8,128)(2,1)S(1)}, u32[]{:S(2)}, u32[]{:S(2)}) %collective-permute-start) | collective-permute-done | bytes 114720 | tf_op jit(solution)/shard_map/ppermute | solution.py:553
  16.8 0.9 %shard_map.196 = (bf16[208,128]{1,0:T(8,128)(2,1)S(1)}, bf16[208,128]{1,0:T(8,128)(2,1)S(1)}, bf16[208,128]{1,0:T(8,128)(2,1)S(1)}, bf16[128,128]{1,0:T(8,128)(2...) custom-call(bf16[128,256]{1,0:T(8,128)(2,1)S(1)} %get-tuple-element.32.kv_ref, ...), custom_call_target="tpu_custom_call" | custom-call | flops 134217728 | bytes 915456 | tf_op jit(solution)/shard_map/pallas_call | solution.py:193
  17.8 2.5 %collective-permute-start.4 = (bf16[208,128]{1,0:T(8,128)(2,1)S(1)}, bf16[208,128]{1,0:T(8,128)(2,1)S(1)}, u32[]{:S(2)}, u32[]{:S(2)}) collective-permute-start(bf16[208,128]{1,0:T(8,128)(2,1)S(1)} %get-tuple-element.43), channel_id=1, source_target_pairs={{0,12},{4,8},{8,4},{12,0},{1,13},{5,9},{9,5},{13,1},{2,14},{6,10},... | collective-permute-start | bytes 159752 | tf_op jit(solution)/shard_map/ppermute | solution.py:553
  20.3 1.5 %collective-permute-start.5 = (bf16[208,128]{1,0:T(8,128)(2,1)S(1)}, bf16[208,128]{1,0:T(8,128)(2,1)S(1)}, u32[]{:S(2)}, u32[]{:S(2)}) collective-permute-start(bf16[208,128]{1,0:T(8,128)(2,1)S(1)} %get-tuple-element.44), channel_id=1, source_target_pairs={{0,8},{4,12},{8,0},{12,4},{1,9},{5,13},{9,1},{13,5},{2,10},{6,14},... | collective-permute-start | bytes 159752 | tf_op jit(solution)/shard_map/ppermute | solution.py:553
  21.8 0.5 %collective-permute-start.6 = (bf16[208,128]{1,0:T(8,128)(2,1)S(1)}, bf16[208,128]{1,0:T(8,128)(2,1)S(1)}, u32[]{:S(2)}, u32[]{:S(2)}) collective-permute-start(bf16[208,128]{1,0:T(8,128)(2,1)S(1)} %get-tuple-element.45), channel_id=1, source_target_pairs={{0,4},{4,0},{8,12},{12,8},{1,5},{5,1},{9,13},{13,9},{2,6},{6,2},{1... | collective-permute-start | bytes 159752 | tf_op jit(solution)/shard_map/ppermute | solution.py:553
  22.3 1.5 %collective-permute-start.3 = (bf16[128,128]{1,0:T(8,128)(2,1)S(1)}, bf16[128,128]{1,0:T(8,128)(2,1)S(1)}, u32[]{:S(2)}, u32[]{:S(2)}) collective-permute-start(bf16[128,128]{1,0:T(8,128)(2,1)S(1)} %shard_map.197), channel_id=1, source_target_pairs={{0,4},{4,0},{8,12},{12,8},{1,5},{5,1},{9,13},{13,9},{2,6},{6,2},{1... | collective-permute-start | bytes 98312 | tf_op jit(solution)/shard_map/ppermute | solution.py:553
  23.8 3.0 %collective-permute-done.3.rest_1_ = bf16[128,128]{1,0:T(8,128)(2,1)S(1)} collective-permute-done((bf16[128,128]{1,0:T(8,128)(2,1)S(1)}, bf16[128,128]{1,0:T(8,128)(2,1)S(1)}, u32[]{:S(2)}, u32[]{:S(2)}) %collective-permute-start.3) | collective-permute-done | bytes 32800 | tf_op jit(solution)/shard_map/ppermute | solution.py:553
  26.9 0.7 %shard_map.198.a2v_ref = bf16[128,256]{1,0:T(8,128)(2,1)S(1)} custom-call(s32[1]{0:T(128)S(6)} %copy.22.limit_ref, bf16[128,256]{1,0:T(8,128)(2,1)S(1)} %get-tuple-element.39.q_ref, bf16[576,128]{1,0:T(8,128)(2,1)S(1)} %get-tuple-element.34.rest_0_, bf16[128,128]{1,0:T(8,128)(2,1)S(1)} %collective-permute-done.3.rest_1_, ...), custom_call_target="tpu_custom_call" | custom-call | flops 33554432 | bytes 606212 | tf_op jit(solution)/shard_map/pallas_call | solution.py:193
  27.6 0.3 shard_map.199
  27.9 0.6 %shard_map.200 = (bf16[160,512]{1,0:T(8,128)(2,1)S(1)}, bf16[32,256]{1,0:T(8,128)(2,1)S(1)}, f32[128,512]{1,0:T(8,128)S(1)}) custom-call(bf16[128,512]{1,0:T(8,128)(2,1)S(1)} %get-tuple-element.46.self_ref, bf16[128,256]{1,0:T(8,128)(2,1)S(1)} %shard_map.198.a2v_ref, bf16[512,4096]{1,0:T(8,128)(2,1)S(1)} %get-tuple-element.40.ws_ref, ...), custom_call_target="tpu_custom_call" | custom-call | flops 201326592 | bytes 10270720 | tf_op jit(solution)/shard_map/pallas_call | solution.py:193
  28.5 0.1 collective-permute-start.10
  28.6 0.8 %shard_map.201 = (bf16[288,512]{1,0:T(8,128)(2,1)S(1)}, f32[288,512]{1,0:T(8,128)S(1)}) custom-call(bf16[128,512]{1,0:T(8,128)(2,1)S(1)} %get-tuple-element.46.self_ref, bf16[128,256]{1,0:T(8,128)(2,1)S(1)} %shard_map.198.a2v_ref, bf16[32,256]{1,0:T(8,128)(2,1)S(1)} %get-tuple-element.50.audio_ref, bf16[512,4096]{1,0:T(8,128)(2,1)S(1)} %get-tuple-element.40.ws_ref, ...), custom_call_target="tpu_custom_call" | custom-call | flops 402653184 | bytes 10534912 | tf_op jit(solution)/shard_map/pallas_call | solution.py:193
  29.4 0.6 %collective-permute-start.7 = (bf16[288,512]{1,0:T(8,128)(2,1)S(1)}, bf16[288,512]{1,0:T(8,128)(2,1)S(1)}, u32[]{:S(2)}, u32[]{:S(2)}) collective-permute-start(bf16[288,512]{1,0:T(8,128)(2,1)S(1)} %get-tuple-element.52), channel_id=1, source_target_pairs={{0,1},{1,0},{2,3},{3,2},{4,5},{5,4},{6,7},{7,6},{8,9},{9,8},{10,11... | collective-permute-start | bytes 884744 | tf_op jit(solution)/shard_map/ppermute | solution.py:553
  29.9 0.1 collective-permute-start.8
  30.0 0.3 shard_map.203
  30.3 1.5 %collective-permute-start.11 = (bf16[160,512]{1,0:T(8,128)(2,1)S(1)}, bf16[160,512]{1,0:T(8,128)(2,1)S(1)}, u32[]{:S(2)}, u32[]{:S(2)}) collective-permute-start(bf16[160,512]{1,0:T(8,128)(2,1)S(1)} %shard_map.203), channel_id=1, source_target_pairs={{0,2},{2,0},{1,3},{3,1},{4,6},{6,4},{5,7},{7,5},{8,10},{10,8},{9,1... | collective-permute-start | bytes 491528 | tf_op jit(solution)/shard_map/ppermute | solution.py:553
  31.9 1.0 %collective-permute-start.9 = (bf16[128,512]{1,0:T(8,128)(2,1)S(1)}, bf16[128,512]{1,0:T(8,128)(2,1)S(1)}, u32[]{:S(2)}, u32[]{:S(2)}) collective-permute-start(bf16[128,512]{1,0:T(8,128)(2,1)S(1)} %shard_map.202), channel_id=1, source_target_pairs={{0,2},{2,0},{1,3},{3,1},{4,6},{6,4},{5,7},{7,5},{8,10},{10,8},{9,1... | collective-permute-start | bytes 393224 | tf_op jit(solution)/shard_map/ppermute | solution.py:553
  32.9 6.8 %collective-permute-done.9.low_ref = bf16[128,512]{1,0:T(8,128)(2,1)S(1)} collective-permute-done((bf16[128,512]{1,0:T(8,128)(2,1)S(1)}, bf16[128,512]{1,0:T(8,128)(2,1)S(1)}, u32[]{:S(2)}, u32[]{:S(2)}) %collective-permute-start.9) | collective-permute-done | bytes 131104 | tf_op jit(solution)/shard_map/ppermute | solution.py:553
  39.8 0.8 %shard_map.204 = (bf16[128,1024]{1,0:T(8,128)(2,1)}, bf16[32,512]{1,0:T(8,128)(2,1)}) custom-call(bf16[128,1024]{1,0:T(8,128)(2,1)S(1)} %get-tuple-element.29.video_ref, bf16[32,512]{1,0:T(8,128)(2,1)S(1)} %get-tuple-element.30.audio_ref, f32[32,512]{1,0:T(8,128)S(1)} %get-tuple-element.31.gain_ref, f32[288,512]{1,0:T(8,128)S(1)} %get-tuple-element.51.own_ref, ...), custom_call_target="tpu_custom_call" | custom-call | bytes 1835008 | tf_op jit(solution)/shard_map/pallas_call | solution.py:193
  (12 shorter events, 0.1 us)
Async XLA Ops:
  2.0 14.8 %collective-permute-start.1 = (bf16[576,128]{1,0:T(8,128)(2,1)S(1)}, bf16[576,128]{1,0:T(8,128)(2,1)S(1)}, u32[]{:S(2)}, u32[]{:S(2)}) collective-permute-start(bf16[576,128]{1,0:T(8,128)(2,1)S(1)} %get-tuple-element.36), channel_id=1, source_target_pairs={{0,8},{4,12},{8,0},{12,4},{1,9},{5,13},{9,1},{13,5},{2,10},{6,14},... | collective-permute-start | bytes 442376 | tf_op jit(solution)/shard_map/ppermute | solution.py:553
  6.1 10.7 %collective-permute-start.2 = (bf16[576,128]{1,0:T(8,128)(2,1)S(1)}, bf16[576,128]{1,0:T(8,128)(2,1)S(1)}, u32[]{:S(2)}, u32[]{:S(2)}) collective-permute-start(bf16[576,128]{1,0:T(8,128)(2,1)S(1)} %get-tuple-element.37), channel_id=1, source_target_pairs={{0,4},{4,0},{8,12},{12,8},{1,5},{5,1},{9,13},{13,9},{2,6},{6,2},{1... | collective-permute-start | bytes 442376 | tf_op jit(solution)/shard_map/ppermute | solution.py:553
  7.7 9.1 %collective-permute-start = (bf16[448,128]{1,0:T(8,128)(2,1)S(1)}, bf16[448,128]{1,0:T(8,128)(2,1)S(1)}, u32[]{:S(2)}, u32[]{:S(2)}) collective-permute-start(bf16[448,128]{1,0:T(8,128)(2,1)S(1)} %get-tuple-element.35), channel_id=1, source_target_pairs={{0,12},{4,8},{8,4},{12,0},{1,13},{5,9},{9,5},{13,1},{2,14},{6,10},... | collective-permute-start | bytes 344072 | tf_op jit(solution)/shard_map/ppermute | solution.py:553
  17.8 9.8 %collective-permute-start.4 = (bf16[208,128]{1,0:T(8,128)(2,1)S(1)}, bf16[208,128]{1,0:T(8,128)(2,1)S(1)}, u32[]{:S(2)}, u32[]{:S(2)}) collective-permute-start(bf16[208,128]{1,0:T(8,128)(2,1)S(1)} %get-tuple-element.43), channel_id=1, source_target_pairs={{0,12},{4,8},{8,4},{12,0},{1,13},{5,9},{9,5},{13,1},{2,14},{6,10},... | collective-permute-start | bytes 159752 | tf_op jit(solution)/shard_map/ppermute | solution.py:553
  20.3 7.3 %collective-permute-start.5 = (bf16[208,128]{1,0:T(8,128)(2,1)S(1)}, bf16[208,128]{1,0:T(8,128)(2,1)S(1)}, u32[]{:S(2)}, u32[]{:S(2)}) collective-permute-start(bf16[208,128]{1,0:T(8,128)(2,1)S(1)} %get-tuple-element.44), channel_id=1, source_target_pairs={{0,8},{4,12},{8,0},{12,4},{1,9},{5,13},{9,1},{13,5},{2,10},{6,14},... | collective-permute-start | bytes 159752 | tf_op jit(solution)/shard_map/ppermute | solution.py:553
  21.8 5.8 %collective-permute-start.6 = (bf16[208,128]{1,0:T(8,128)(2,1)S(1)}, bf16[208,128]{1,0:T(8,128)(2,1)S(1)}, u32[]{:S(2)}, u32[]{:S(2)}) collective-permute-start(bf16[208,128]{1,0:T(8,128)(2,1)S(1)} %get-tuple-element.45), channel_id=1, source_target_pairs={{0,4},{4,0},{8,12},{12,8},{1,5},{5,1},{9,13},{13,9},{2,6},{6,2},{1... | collective-permute-start | bytes 159752 | tf_op jit(solution)/shard_map/ppermute | solution.py:553
  22.3 4.6 %collective-permute-start.3 = (bf16[128,128]{1,0:T(8,128)(2,1)S(1)}, bf16[128,128]{1,0:T(8,128)(2,1)S(1)}, u32[]{:S(2)}, u32[]{:S(2)}) collective-permute-start(bf16[128,128]{1,0:T(8,128)(2,1)S(1)} %shard_map.197), channel_id=1, source_target_pairs={{0,4},{4,0},{8,12},{12,8},{1,5},{5,1},{9,13},{13,9},{2,6},{6,2},{1... | collective-permute-start | bytes 98312 | tf_op jit(solution)/shard_map/ppermute | solution.py:553
  28.5 1.5 %collective-permute-start.10 = (bf16[160,512]{1,0:T(8,128)(2,1)S(1)}, bf16[160,512]{1,0:T(8,128)(2,1)S(1)}, u32[]{:S(2)}, u32[]{:S(2)}) collective-permute-start(bf16[160,512]{1,0:T(8,128)(2,1)S(1)} %get-tuple-element.55), channel_id=1, source_target_pairs={{0,1},{1,0},{2,3},{3,2},{4,5},{5,4},{6,7},{7,6},{8,9},{9,8},{10,11... | collective-permute-start | bytes 491528 | tf_op jit(solution)/shard_map/ppermute | solution.py:553
  29.4 10.4 %collective-permute-start.7 = (bf16[288,512]{1,0:T(8,128)(2,1)S(1)}, bf16[288,512]{1,0:T(8,128)(2,1)S(1)}, u32[]{:S(2)}, u32[]{:S(2)}) collective-permute-start(bf16[288,512]{1,0:T(8,128)(2,1)S(1)} %get-tuple-element.52), channel_id=1, source_target_pairs={{0,1},{1,0},{2,3},{3,2},{4,5},{5,4},{6,7},{7,6},{8,9},{9,8},{10,11... | collective-permute-start | bytes 884744 | tf_op jit(solution)/shard_map/ppermute | solution.py:553
  29.9 2.0 %collective-permute-start.8 = (bf16[128,512]{1,0:T(8,128)(2,1)S(1)}, bf16[128,512]{1,0:T(8,128)(2,1)S(1)}, u32[]{:S(2)}, u32[]{:S(2)}) collective-permute-start(bf16[128,512]{1,0:T(8,128)(2,1)S(1)} %get-tuple-element.54), channel_id=1, source_target_pairs={{0,1},{1,0},{2,3},{3,2},{4,5},{5,4},{6,7},{7,6},{8,9},{9,8},{10,11... | collective-permute-start | bytes 393224 | tf_op jit(solution)/shard_map/ppermute | solution.py:553
  30.3 9.4 %collective-permute-start.11 = (bf16[160,512]{1,0:T(8,128)(2,1)S(1)}, bf16[160,512]{1,0:T(8,128)(2,1)S(1)}, u32[]{:S(2)}, u32[]{:S(2)}) collective-permute-start(bf16[160,512]{1,0:T(8,128)(2,1)S(1)} %shard_map.203), channel_id=1, source_target_pairs={{0,2},{2,0},{1,3},{3,1},{4,6},{6,4},{5,7},{7,5},{8,10},{10,8},{9,1... | collective-permute-start | bytes 491528 | tf_op jit(solution)/shard_map/ppermute | solution.py:553
  31.9 7.8 %collective-permute-start.9 = (bf16[128,512]{1,0:T(8,128)(2,1)S(1)}, bf16[128,512]{1,0:T(8,128)(2,1)S(1)}, u32[]{:S(2)}, u32[]{:S(2)}) collective-permute-start(bf16[128,512]{1,0:T(8,128)(2,1)S(1)} %shard_map.202), channel_id=1, source_target_pairs={{0,2},{2,0},{1,3},{3,1},{4,6},{6,4},{5,7},{7,5},{8,10},{10,8},{9,1... | collective-permute-start | bytes 393224 | tf_op jit(solution)/shard_map/ppermute | solution.py:553

commit v7 on v6

--- a/solution.py
+++ b/solution.py
@@ -181,6 +181,7 @@
 HBM = pl.BlockSpec(memory_space=pltpu.HBM)
 BF16, F32 = jnp.bfloat16, jnp.float32
 LSE_ROWS = 16
+LEAST = float(jnp.finfo(jnp.float32).min)
 SEQ, FORWARDED, OUT_ORDER = 4, 3, [3, 2, 1]
 
 
@@ -244,10 +245,6 @@
                 pairs.append((ref.at[:, pl.ds(i * width, width)], out.at[pl.ds(at, rows_audio), :]))
                 at += rows_audio
     copy_all(pairs, sems)
-
-
-def relay_kernel(got_ref, out_ref):
-    out_ref[...] = got_ref[got_ref.shape[0] - out_ref.shape[0] :, :]
 
 
 def audio_block(ref, end, rows, cols, block):
@@ -292,7 +289,7 @@
 
 def softmax_t(scores, scale, allowed=None):
     if allowed is not None:
-        scores = [jnp.where(ok, x, -jnp.inf) for ok, x in zip(allowed, scores)]
+        scores = [jnp.where(ok, x, LEAST) for ok, x in zip(allowed, scores)]
     peak = functools.reduce(jnp.maximum, [jnp.max(x, axis=0, keepdims=True) for x in scores])
     weights = [jnp.exp2((x - peak) * (scale * LOG2E)) for x in scores]
     total = functools.reduce(jnp.add, [jnp.sum(x, axis=0, keepdims=True) for x in weights])
@@ -388,6 +385,9 @@
             dst = own_ref if j == 0 else sends[j - 1].at[0:rows, :]
             dst[:, cut] = o.T.astype(BF16)
             at += 1
+    relayed = 2 * cols // width * rows_audio
+    dst, src = sends[hops.index(1) - 1], blocks[hops.index(FORWARDED ^ 1)]
+    dst[dst.shape[0] - relayed :, :] = src[src.shape[0] - relayed :, :]
     heads = len(lses)
     lse = jnp.concatenate(lses, axis=0)
     own_lse_ref[...] = lse
@@ -401,19 +401,51 @@
         dst[top : top + LSE_ROWS, 0:128] = pltpu.roll(packed, 128 - (j + 1) * rows_audio, 1).astype(BF16)
 
 
+def audio_allowed(hop, rows_audio, limit):
+    row = lax.broadcasted_iota(jnp.int32, (rows_audio, 1), 0)
+    return (index_of("seq") ^ hop) * rows_audio + row < limit
+
+
+def spread(x, head):
+    pair = 128 // head
+    rows = x.shape[1] // pair
+    parts = [jnp.broadcast_to(x[:, i * rows : (i + 1) * rows], (head, rows)) for i in range(pair)]
+    return jnp.concatenate(parts, axis=0)
+
+
 def attend_audio_kernel(hops, rows_audio, head, limit_ref, q_ref, *rest):
-    blocks, out_ref = rest[:-1], rest[-1]
+    blocks, part_ref, stats_ref = rest[:-2], rest[-2], rest[-1]
     cols = q_ref.shape[1]
-    me, row = index_of("seq"), lax.broadcasted_iota(jnp.int32, (rows_audio, 1), 0)
-    allowed = [(me ^ hop) * rows_audio + row < limit_ref[0] for hop in hops]
+    allowed = [audio_allowed(hop, rows_audio, limit_ref[0]) for hop in hops]
     scale = 1.0 / math.sqrt(head)
-    for block in range(q_ref.shape[1] // 128):
+    for block in range(cols // 128):
         cut = slice(block * 128, (block + 1) * 128)
         q = pair_rows(q_ref[:, cut], head)
-        _, p, total = softmax_t([dot_t(audio_block(ref, 2, rows_audio, cols, block), q) for ref in blocks], scale, allowed)
+        scores = [dot_t(audio_block(ref, 2, rows_audio, cols, block), q) for ref in blocks]
+        peak, p, total = softmax_t(scores, scale, allowed)
         vt = turn(jnp.concatenate([audio_block(ref, 1, rows_audio, cols, block) for ref in blocks], axis=0))
-        o = dot(vt, jnp.concatenate(p, axis=0)) * (1.0 / total)
-        out_ref[:, cut] = pair_columns(o, head).T.astype(BF16)
+        part_ref[cut, :] = pair_columns(dot(vt, jnp.concatenate(p, axis=0)), head)
+        stats_ref[2 * block : 2 * block + 1, :] = peak
+        stats_ref[2 * block + 1 : 2 * block + 2, :] = total
+
+
+def finish_audio(head, limit, q_ref, part_ref, stats_ref, last_ref, rows_audio, out_ref):
+    cols = q_ref.shape[1]
+    scale = 1.0 / math.sqrt(head)
+    allowed = audio_allowed(FORWARDED, rows_audio, limit)
+    for block in range(cols // 128):
+        cut = slice(block * 128, (block + 1) * 128)
+        q = pair_rows(q_ref[:, cut], head)
+        scores = jnp.where(allowed, dot_t(audio_block(last_ref, 2, rows_audio, cols, block), q), LEAST)
+        before, summed = stats_ref[2 * block : 2 * block + 1, :], stats_ref[2 * block + 1 : 2 * block + 2, :]
+        peak = jnp.maximum(before, jnp.max(scores, axis=0, keepdims=True))
+        factor = jnp.exp2((before - peak) * (scale * LOG2E))
+        p = jnp.exp2((scores - peak) * (scale * LOG2E))
+        inverse = 1.0 / (summed * factor + jnp.sum(p, axis=0, keepdims=True))
+        vt = turn(audio_block(last_ref, 1, rows_audio, cols, block))
+        last = pair_columns(dot(vt, p.astype(BF16)), head)
+        both = part_ref[cut, :] * spread(factor, head) + last
+        out_ref[:, cut] = (both * spread(inverse, head)).T.astype(BF16)
 
 
 def merge_audio(head, top, v2a_ref, lse_ref, got, out_ref):
@@ -466,9 +498,11 @@
     return dot(v2a_ref[...], wv_ref[:, columns(block, wv_ref.shape[1] // 4)])
 
 
-def first_kernel(hops, own_ref, a2v_ref, ws_ref, wa_ref, gain_ref, *rest):
-    got, (self_ref, out_ref) = rest[: len(hops) - 1], rest[len(hops) - 1 :]
+def first_kernel(hops, rows_audio, head, limit_ref, q_ref, part_ref, stats_ref, own_ref, ws_ref, wa_ref, gain_ref, *rest):
+    got, (self_ref, a2v_ref, out_ref) = rest[: len(hops) - 1], rest[len(hops) - 1 :]
     rows, width = own_ref.shape
+    last_ref = got[hops.index(1) - 1]
+    finish_audio(head, limit_ref[0], q_ref, part_ref, stats_ref, last_ref, rows_audio, a2v_ref)
     me = index_of("seq")
     self_ref[:, columns(me, width)] = own_ref[...]
     for hop, ref in zip(hops[1:], got):
@@ -553,18 +587,23 @@
         return lax.ppermute(x, axis, [(i, i ^ hop) for i in range(size)])
 
     video, audio = 3 * rows, cross // width * rows_audio
-    packed = call(
-        functools.partial(pack_kernel, hops, width),
-        [shape(video + (1 if hop == FORWARDED else 3) * audio, width) for hop in hops],
-        (q_self, k_self, v_self, q_v2a, k_a2v, v_a2v),
-        [HBM] * 6,
-        scratch=[pltpu.SemaphoreType.DMA((3 * n + (3 * n - 2) * audio // rows_audio,))],
-    )
+
+    def pack(some):
+        ends = [1 if hop == FORWARDED else 3 for hop in some]
+        return call(
+            functools.partial(pack_kernel, some, width),
+            [shape(video + end * audio, width) for end in ends],
+            (q_self, k_self, v_self, q_v2a, k_a2v, v_a2v),
+            [HBM] * 6,
+            scratch=[pltpu.SemaphoreType.DMA((3 * len(some) + sum(ends) * audio // rows_audio,))],
+        )
+
+    packed = pack(hops[1:2])
+    rest = pack(hops[:1] + hops[2:])
+    packed = [rest[0], *packed, *rest[1:]]
     blocks = dict(zip(hops, packed))
     for hop in hops[1:]:
         blocks[hop] = trade(blocks[hop], "seq", hop, n)
-    (forwarded,) = call(relay_kernel, [shape(2 * audio, width)], (blocks[FORWARDED ^ 1],))
-    forwarded = trade(forwarded, "seq", 1, n)
 
     late = (k_v2a, v_v2a, q_a2v, wo_self, wo_a2v, wo_v2a, video_in, audio_in)
     steps = (video_steps.reshape(1, rows), audio_steps.reshape(1, rows_audio))
@@ -580,7 +619,7 @@
     back = rows + cross // 128 * rows_audio + LSE_ROWS
     result = call(
         functools.partial(attend_kernel, hops, DHC),
-        [shape(back, width)] * (n - 1)
+        [shape(back + 2 * audio if hop == 1 else back, width) for hop in hops[1:]]
         + [shape(rows, width), shape(rows_audio, cross, F32), shape(cross // DHC, 128, F32)],
         (k_own, v_own, *blocks.values()),
         flops=4 * n * n * rows * rows * width,
@@ -589,21 +628,22 @@
     )
     sends, (own, own_v2a, own_lse) = result[: n - 1], result[n - 1 :]
     got = [trade(x, "seq", hop, n) for x, hop in zip(sends, hops[1:])]
-    audios = [forwarded if hop == FORWARDED else blocks[hop] for hop in hops]
-    (a2v_att,) = call(
-        functools.partial(attend_audio_kernel, hops, rows_audio, DHC),
-        [shape(rows, cross)],
-        (audio_len, q_own, *audios),
-        [SMEM] + [VMEM] * (n + 1),
+    near = [hop for hop in hops if hop != FORWARDED]
+    a2v_part, a2v_stats = call(
+        functools.partial(attend_audio_kernel, near, rows_audio, DHC),
+        [shape(cross, rows, F32), shape(cross // 64, 128 // DHC * rows, F32)],
+        (audio_len, q_own, *(blocks[hop] for hop in near)),
+        [SMEM] + [VMEM] * n,
         flops=8 * n * rows * rows_audio * cross,
     )
 
     half = video_in.shape[1] // 2
     flops = 2 * rows * (cols + cross) * half
-    self_att, first = call(
-        functools.partial(first_kernel, hops),
-        [shape(rows, cols), shape(rows, half)],
-        (own, a2v_att, ws, wa, gain, *got),
+    self_att, a2v_att, first = call(
+        functools.partial(first_kernel, hops, rows_audio, DHC),
+        [shape(rows, cols), shape(rows, cross), shape(rows, half)],
+        (audio_len, q_own, a2v_part, a2v_stats, own, ws, wa, gain, *got),
+        [SMEM] + [VMEM] * (n + 6),
         flops=flops,
     )
     first = trade(first, "sub", 1, 2)

time: 40.8 us -> 42.4 us (1.039)
  waiting for transfers between devices: 13.8 us -> 14.9 us
  Pallas kernels: 9.25 us -> 10.3 us
  starting transfers between devices: 15 us -> 14.5 us
    ppermute x12 -> x11, waiting for transfers between devices: 13.8 us -> 14.9 us  [trade(): return lax.ppermute(x, axis, [(i, i ^ hop) for i in range(size)])]
    pallas_call x11, Pallas kernels: 9.25 us -> 10.3 us  [call(): pl.pallas_call(kernel, out_shape=tuple(outs), in_specs=specs or [VMEM] *...]
    ppermute x12 -> x11, starting transfers between devices: 15 us -> 14.5 us  [trade(): return lax.ppermute(x, axis, [(i, i ^ hop) for i in range(size)])]
  transfers between devices with their start and end apart: 12 -> 11, of which waited for: 3 -> 4; matrix products, arithmetic and copies ran while one was open for 3% -> 3% of each run, Pallas kernels for 13% -> 14%
where the time goes in v7:
time: 42.4 us; the launch traced here: 42.1 us
  waiting for transfers between devices  14.9 us (35%)
  starting transfers between devices  14.5 us (34%)
  Pallas kernels  10.3 us (24%)
  between operations  1.37 us (3%)
  local copies, waits for them, and re-layouts  1.1 us (3%)
    ppermute x11, waiting for transfers between devices, trade(): return lax.ppermute(x, axis, [(i, i ^ hop) for i in range(size)])  14.9 us
    ppermute x11, starting transfers between devices, trade(): return lax.ppermute(x, axis, [(i, i ^ hop) for i in range(size)])  14.5 us
    pallas_call x11, Pallas kernels, call(): pl.pallas_call(kernel, out_shape=tuple(outs), in_specs=specs or [VMEM] *...  10.3 us
    unnamed x1, local copies, waits for them, and re-layouts  1.1 us
  transfers between devices with their start and end apart: 11, of which 4 were waited for; matrix products, arithmetic and copies ran while one was open for 3% of the time, Pallas kernels for 14%

profile of v7, /device:TPU:0, one launch (start us, length us, event | category | flops | bytes accessed | tf_op | source)
XLA Modules:
  0.0 42.1 jit_solution(387358481973798810)
XLA Ops:
  0.6 1.3 %shard_map.195 = (bf16[576,128]{1,0:T(8,128)(2,1)S(1)}, bf16[576,128]{1,0:T(8,128)(2,1)S(1)}, bf16[576,128]{1,0:T(8,128)(2,1)S(1)}) custom-call(bf16[128,512]{1,0:T(8,128)(2,1)} %q_ref.3, bf16[128,512]{1,0:T(8,128)(2,1)} %k_ref.3, bf16[128,512]{1,0:T(8,128)(2,1)} %v_ref.3, bf16[32,256]{1,0:T(8,128)(2,1)} %qa_ref.3, bf16[32,256]{1,0:T(8,128)(2,1)} %ka_ref.3, ...), custom_call_target="tpu_custom_call" | custom-call | bytes 884736 | tf_op jit(solution)/shard_map/pallas_call | solution.py:194
  1.9 4.1 %collective-permute-start = (bf16[576,128]{1,0:T(8,128)(2,1)S(1)}, bf16[576,128]{1,0:T(8,128)(2,1)S(1)}, u32[]{:S(2)}, u32[]{:S(2)}) collective-permute-start(bf16[576,128]{1,0:T(8,128)(2,1)S(1)} %get-tuple-element.36), channel_id=1, source_target_pairs={{0,8},{4,12},{8,0},{12,4},{1,9},{5,13},{9,1},{13,5},{2,10},{6,14},... | collective-permute-start | bytes 442376 | tf_op jit(solution)/shard_map/ppermute | solution.py:587
  6.0 1.6 %collective-permute-start.1 = (bf16[576,128]{1,0:T(8,128)(2,1)S(1)}, bf16[576,128]{1,0:T(8,128)(2,1)S(1)}, u32[]{:S(2)}, u32[]{:S(2)}) collective-permute-start(bf16[576,128]{1,0:T(8,128)(2,1)S(1)} %get-tuple-element.37), channel_id=1, source_target_pairs={{0,4},{4,0},{8,12},{12,8},{1,5},{5,1},{9,13},{13,9},{2,6},{6,2},{1... | collective-permute-start | bytes 442376 | tf_op jit(solution)/shard_map/ppermute | solution.py:587
  7.6 0.8 %shard_map.197 = bf16[448,128]{1,0:T(8,128)(2,1)S(1)} custom-call(bf16[128,512]{1,0:T(8,128)(2,1)} %q_ref.3, bf16[128,512]{1,0:T(8,128)(2,1)} %k_ref.3, bf16[128,512]{1,0:T(8,128)(2,1)} %v_ref.3, bf16[32,256]{1,0:T(8,128)(2,1)} %qa_ref.3, bf16[32,256]{1,0:T(8,128)(2,1)} %ka_ref.3, bf16[32,256]{1,0:T(8,128)(2,1)} %va_ref.3), custom_call_target="tpu_custom_call" | custom-call | bytes 557056 | tf_op jit(solution)/shard_map/pallas_call | solution.py:194
  8.5 0.1 collective-permute-start.2
  9.2 1.1 %copy.21 = bf16[2,8,2,4096]{3,1,2,0:T(8,128)(2,1)S(1)} copy(bf16[2,8,2,4096]{3,2,1,0:T(2,128)(2,1)} %bitcast.5) | data formatting | bytes 524288
  10.3 3.4 %shard_map.194 = (bf16[128,8192]{1,0:T(8,128)(2,1)S(1)}, f32[32,512]{1,0:T(8,128)S(1)}, bf16[128,256]{1,0:T(8,128)(2,1)S(1)}, bf16[128,256]{1,0:T(8,128)(2,1)S(1...) custom-call(s32[1]{0:T(128)S(6)} %copy.22.limit_ref, ...), custom_call_target="tpu_custom_call" | custom-call | bytes 18154116 | tf_op jit(solution)/shard_map/pallas_call | solution.py:194
  13.7 3.0 %collective-permute-done.2.rest_1_ = bf16[448,128]{1,0:T(8,128)(2,1)S(1)} collective-permute-done((bf16[448,128]{1,0:T(8,128)(2,1)S(1)}, bf16[448,128]{1,0:T(8,128)(2,1)S(1)}, u32[]{:S(2)}, u32[]{:S(2)}) %collective-permute-start.2) | collective-permute-done | bytes 114720 | tf_op jit(solution)/shard_map/ppermute | solution.py:587
  16.7 0.9 %shard_map.198 = (bf16[208,128]{1,0:T(8,128)(2,1)S(1)}, bf16[208,128]{1,0:T(8,128)(2,1)S(1)}, bf16[336,128]{1,0:T(8,128)(2,1)S(1)}, bf16[128,128]{1,0:T(8,128)(2...) custom-call(bf16[128,256]{1,0:T(8,128)(2,1)S(1)} %get-tuple-element.40.kv_ref, ...), custom_call_target="tpu_custom_call" | custom-call | flops 134217728 | bytes 948224 | tf_op jit(solution)/shard_map/pallas_call | solution.py:194
  17.6 2.0 %collective-permute-start.5 = (bf16[336,128]{1,0:T(8,128)(2,1)S(1)}, bf16[336,128]{1,0:T(8,128)(2,1)S(1)}, u32[]{:S(2)}, u32[]{:S(2)}) collective-permute-start(bf16[336,128]{1,0:T(8,128)(2,1)S(1)} %get-tuple-element.48), channel_id=1, source_target_pairs={{0,4},{4,0},{8,12},{12,8},{1,5},{5,1},{9,13},{13,9},{2,6},{6,2},{1... | collective-permute-start | bytes 258056 | tf_op jit(solution)/shard_map/ppermute | solution.py:587
  19.7 3.4 %collective-permute-start.3 = (bf16[208,128]{1,0:T(8,128)(2,1)S(1)}, bf16[208,128]{1,0:T(8,128)(2,1)S(1)}, u32[]{:S(2)}, u32[]{:S(2)}) collective-permute-start(bf16[208,128]{1,0:T(8,128)(2,1)S(1)} %get-tuple-element.46), channel_id=1, source_target_pairs={{0,12},{4,8},{8,4},{12,0},{1,13},{5,9},{9,5},{13,1},{2,14},{6,10},... | collective-permute-start | bytes 159752 | tf_op jit(solution)/shard_map/ppermute | solution.py:587
  23.1 0.6 %shard_map.196 = (f32[256,128]{1,0:T(8,128)S(1)}, f32[4,256]{1,0:T(4,128)S(1)}) custom-call(s32[1]{0:T(128)S(6)} %copy.22.limit_ref, bf16[128,256]{1,0:T(8,128)(2,1)S(1)} %get-tuple-element.34.q_ref, bf16[576,128]{1,0:T(8,128)(2,1)S(1)} %get-tuple-element.35.rest_0_, bf16[576,128]{1,0:T(8,128)(2,1)S(1)} %collective-permute-done.rest_1_.rest_2_, ...), custom_call_target="tpu_custom_call" | custom-call | flops 33554432 | bytes 643076 | tf_op jit(solution)/shard_map/pallas_call | solution.py:194
  23.7 3.6 %collective-permute-done.3.rest_0_ = bf16[208,128]{1,0:T(8,128)(2,1)S(1)} collective-permute-done((bf16[208,128]{1,0:T(8,128)(2,1)S(1)}, bf16[208,128]{1,0:T(8,128)(2,1)S(1)}, u32[]{:S(2)}, u32[]{:S(2)}) %collective-permute-start.3) | collective-permute-done | bytes 53280 | tf_op jit(solution)/shard_map/ppermute | solution.py:587
  27.3 1.4 %collective-permute-done.4.rest_1_ = bf16[208,128]{1,0:T(8,128)(2,1)S(1)} collective-permute-done((bf16[208,128]{1,0:T(8,128)(2,1)S(1)}, bf16[208,128]{1,0:T(8,128)(2,1)S(1)}, u32[]{:S(2)}, u32[]{:S(2)}) %collective-permute-start.4) | collective-permute-done | bytes 53280 | tf_op jit(solution)/shard_map/ppermute | solution.py:587
  28.7 0.8 %shard_map.199 = (bf16[128,512]{1,0:T(8,128)(2,1)S(1)}, bf16[128,256]{1,0:T(8,128)(2,1)S(1)}, bf16[128,512]{1,0:T(8,128)(2,1)S(1)}) custom-call(s32[1]{0:T(128)S(6)} %copy.22.limit_ref, bf16[128,256]{1,0:T(8,128)(2,1)S(1)} %get-tuple-element.34.q_ref, f32[256,128]{1,0:T(8,128)S(1)} %get-tuple-element.38.part_ref, f32[4,256]{1,0:T(4,128)S(1)} %get-tuple-element.39.stats_ref, ...), custom_call_target="tpu_custom_call" | custom-call | flops 100663296 | bytes 9142276 | tf_op jit(solution)/shard_map/pallas_call | solution.py:194
  29.5 0.6 %shard_map.200 = (bf16[160,512]{1,0:T(8,128)(2,1)S(1)}, bf16[32,256]{1,0:T(8,128)(2,1)S(1)}, f32[128,512]{1,0:T(8,128)S(1)}) custom-call(bf16[128,512]{1,0:T(8,128)(2,1)S(1)} %get-tuple-element.49.self_ref, bf16[128,256]{1,0:T(8,128)(2,1)S(1)} %get-tuple-element.50.a2v_ref, bf16[512,4096]{1,0:T(8,128)(2,1)S(1)} %get-tuple-element.43.ws_ref, ...), custom_call_target="tpu_custom_call" | custom-call | flops 201326592 | bytes 10303488 | tf_op jit(solution)/shard_map/pallas_call | solution.py:194
  30.1 0.7 %shard_map.201 = (bf16[288,512]{1,0:T(8,128)(2,1)S(1)}, f32[288,512]{1,0:T(8,128)S(1)}) custom-call(bf16[128,512]{1,0:T(8,128)(2,1)S(1)} %get-tuple-element.49.self_ref, bf16[128,256]{1,0:T(8,128)(2,1)S(1)} %get-tuple-element.50.a2v_ref, bf16[32,256]{1,0:T(8,128)(2,1)S(1)} %get-tuple-element.54.audio_ref, bf16[512,4096]{1,0:T(8,128)(2,1)S(1)} %get-tuple-element.43.ws_ref, ...), custom_call_target="tpu_custom_call" | custom-call | flops 402653184 | bytes 10534912 | tf_op jit(solution)/shard_map/pallas_call | solution.py:194
  30.9 0.6 %collective-permute-start.6 = (bf16[288,512]{1,0:T(8,128)(2,1)S(1)}, bf16[288,512]{1,0:T(8,128)(2,1)S(1)}, u32[]{:S(2)}, u32[]{:S(2)}) collective-permute-start(bf16[288,512]{1,0:T(8,128)(2,1)S(1)} %get-tuple-element.56), channel_id=1, source_target_pairs={{0,1},{1,0},{2,3},{3,2},{4,5},{5,4},{6,7},{7,6},{8,9},{9,8},{10,11... | collective-permute-start | bytes 884744 | tf_op jit(solution)/shard_map/ppermute | solution.py:587
  31.4 0.1 collective-permute-start.7
  31.5 0.3 shard_map.203
  31.8 1.6 %collective-permute-start.10 = (bf16[160,512]{1,0:T(8,128)(2,1)S(1)}, bf16[160,512]{1,0:T(8,128)(2,1)S(1)}, u32[]{:S(2)}, u32[]{:S(2)}) collective-permute-start(bf16[160,512]{1,0:T(8,128)(2,1)S(1)} %shard_map.203), channel_id=1, source_target_pairs={{0,2},{2,0},{1,3},{3,1},{4,6},{6,4},{5,7},{7,5},{8,10},{10,8},{9,1... | collective-permute-start | bytes 491528 | tf_op jit(solution)/shard_map/ppermute | solution.py:587
  33.4 1.0 %collective-permute-start.8 = (bf16[128,512]{1,0:T(8,128)(2,1)S(1)}, bf16[128,512]{1,0:T(8,128)(2,1)S(1)}, u32[]{:S(2)}, u32[]{:S(2)}) collective-permute-start(bf16[128,512]{1,0:T(8,128)(2,1)S(1)} %shard_map.202), channel_id=1, source_target_pairs={{0,2},{2,0},{1,3},{3,1},{4,6},{6,4},{5,7},{7,5},{8,10},{10,8},{9,1... | collective-permute-start | bytes 393224 | tf_op jit(solution)/shard_map/ppermute | solution.py:587
  34.4 6.8 %collective-permute-done.8.low_ref = bf16[128,512]{1,0:T(8,128)(2,1)S(1)} collective-permute-done((bf16[128,512]{1,0:T(8,128)(2,1)S(1)}, bf16[128,512]{1,0:T(8,128)(2,1)S(1)}, u32[]{:S(2)}, u32[]{:S(2)}) %collective-permute-start.8) | collective-permute-done | bytes 131104 | tf_op jit(solution)/shard_map/ppermute | solution.py:587
  41.3 0.8 %shard_map.204 = (bf16[128,1024]{1,0:T(8,128)(2,1)}, bf16[32,512]{1,0:T(8,128)(2,1)}) custom-call(bf16[128,1024]{1,0:T(8,128)(2,1)S(1)} %get-tuple-element.31.video_ref, bf16[32,512]{1,0:T(8,128)(2,1)S(1)} %get-tuple-element.32.audio_ref, f32[32,512]{1,0:T(8,128)S(1)} %get-tuple-element.33.gain_ref, f32[288,512]{1,0:T(8,128)S(1)} %get-tuple-element.55.own_ref, ...), custom_call_target="tpu_custom_call" | custom-call | bytes 1835008 | tf_op jit(solution)/shard_map/pallas_call | solution.py:194
  (10 shorter events, 0.1 us)
Async XLA Ops:
  1.9 14.8 %collective-permute-start = (bf16[576,128]{1,0:T(8,128)(2,1)S(1)}, bf16[576,128]{1,0:T(8,128)(2,1)S(1)}, u32[]{:S(2)}, u32[]{:S(2)}) collective-permute-start(bf16[576,128]{1,0:T(8,128)(2,1)S(1)} %get-tuple-element.36), channel_id=1, source_target_pairs={{0,8},{4,12},{8,0},{12,4},{1,9},{5,13},{9,1},{13,5},{2,10},{6,14},... | collective-permute-start | bytes 442376 | tf_op jit(solution)/shard_map/ppermute | solution.py:587
  6.0 10.7 %collective-permute-start.1 = (bf16[576,128]{1,0:T(8,128)(2,1)S(1)}, bf16[576,128]{1,0:T(8,128)(2,1)S(1)}, u32[]{:S(2)}, u32[]{:S(2)}) collective-permute-start(bf16[576,128]{1,0:T(8,128)(2,1)S(1)} %get-tuple-element.37), channel_id=1, source_target_pairs={{0,4},{4,0},{8,12},{12,8},{1,5},{5,1},{9,13},{13,9},{2,6},{6,2},{1... | collective-permute-start | bytes 442376 | tf_op jit(solution)/shard_map/ppermute | solution.py:587
  8.5 8.3 %collective-permute-start.2 = (bf16[448,128]{1,0:T(8,128)(2,1)S(1)}, bf16[448,128]{1,0:T(8,128)(2,1)S(1)}, u32[]{:S(2)}, u32[]{:S(2)}) collective-permute-start(bf16[448,128]{1,0:T(8,128)(2,1)S(1)} %shard_map.197), channel_id=1, source_target_pairs={{0,12},{4,8},{8,4},{12,0},{1,13},{5,9},{9,5},{13,1},{2,14},{6,10},... | collective-permute-start | bytes 344072 | tf_op jit(solution)/shard_map/ppermute | solution.py:587
  17.6 11.1 %collective-permute-start.5 = (bf16[336,128]{1,0:T(8,128)(2,1)S(1)}, bf16[336,128]{1,0:T(8,128)(2,1)S(1)}, u32[]{:S(2)}, u32[]{:S(2)}) collective-permute-start(bf16[336,128]{1,0:T(8,128)(2,1)S(1)} %get-tuple-element.48), channel_id=1, source_target_pairs={{0,4},{4,0},{8,12},{12,8},{1,5},{5,1},{9,13},{13,9},{2,6},{6,2},{1... | collective-permute-start | bytes 258056 | tf_op jit(solution)/shard_map/ppermute | solution.py:587
  19.7 7.6 %collective-permute-start.3 = (bf16[208,128]{1,0:T(8,128)(2,1)S(1)}, bf16[208,128]{1,0:T(8,128)(2,1)S(1)}, u32[]{:S(2)}, u32[]{:S(2)}) collective-permute-start(bf16[208,128]{1,0:T(8,128)(2,1)S(1)} %get-tuple-element.46), channel_id=1, source_target_pairs={{0,12},{4,8},{8,4},{12,0},{1,13},{5,9},{9,5},{13,1},{2,14},{6,10},... | collective-permute-start | bytes 159752 | tf_op jit(solution)/shard_map/ppermute | solution.py:587
  23.1 5.6 %collective-permute-start.4 = (bf16[208,128]{1,0:T(8,128)(2,1)S(1)}, bf16[208,128]{1,0:T(8,128)(2,1)S(1)}, u32[]{:S(2)}, u32[]{:S(2)}) collective-permute-start(bf16[208,128]{1,0:T(8,128)(2,1)S(1)} %get-tuple-element.47), channel_id=1, source_target_pairs={{0,8},{4,12},{8,0},{12,4},{1,9},{5,13},{9,1},{13,5},{2,10},{6,14},... | collective-permute-start | bytes 159752 | tf_op jit(solution)/shard_map/ppermute | solution.py:587
  30.1 1.5 %collective-permute-start.9 = (bf16[160,512]{1,0:T(8,128)(2,1)S(1)}, bf16[160,512]{1,0:T(8,128)(2,1)S(1)}, u32[]{:S(2)}, u32[]{:S(2)}) collective-permute-start(bf16[160,512]{1,0:T(8,128)(2,1)S(1)} %get-tuple-element.59), channel_id=1, source_target_pairs={{0,1},{1,0},{2,3},{3,2},{4,5},{5,4},{6,7},{7,6},{8,9},{9,8},{10,11... | collective-permute-start | bytes 491528 | tf_op jit(solution)/shard_map/ppermute | solution.py:587
  30.9 10.4 %collective-permute-start.6 = (bf16[288,512]{1,0:T(8,128)(2,1)S(1)}, bf16[288,512]{1,0:T(8,128)(2,1)S(1)}, u32[]{:S(2)}, u32[]{:S(2)}) collective-permute-start(bf16[288,512]{1,0:T(8,128)(2,1)S(1)} %get-tuple-element.56), channel_id=1, source_target_pairs={{0,1},{1,0},{2,3},{3,2},{4,5},{5,4},{6,7},{7,6},{8,9},{9,8},{10,11... | collective-permute-start | bytes 884744 | tf_op jit(solution)/shard_map/ppermute | solution.py:587
  31.4 2.0 %collective-permute-start.7 = (bf16[128,512]{1,0:T(8,128)(2,1)S(1)}, bf16[128,512]{1,0:T(8,128)(2,1)S(1)}, u32[]{:S(2)}, u32[]{:S(2)}) collective-permute-start(bf16[128,512]{1,0:T(8,128)(2,1)S(1)} %get-tuple-element.58), channel_id=1, source_target_pairs={{0,1},{1,0},{2,3},{3,2},{4,5},{5,4},{6,7},{7,6},{8,9},{9,8},{10,11... | collective-permute-start | bytes 393224 | tf_op jit(solution)/shard_map/ppermute | solution.py:587
  31.8 9.4 %collective-permute-start.10 = (bf16[160,512]{1,0:T(8,128)(2,1)S(1)}, bf16[160,512]{1,0:T(8,128)(2,1)S(1)}, u32[]{:S(2)}, u32[]{:S(2)}) collective-permute-start(bf16[160,512]{1,0:T(8,128)(2,1)S(1)} %shard_map.203), channel_id=1, source_target_pairs={{0,2},{2,0},{1,3},{3,1},{4,6},{6,4},{5,7},{7,5},{8,10},{10,8},{9,1... | collective-permute-start | bytes 491528 | tf_op jit(solution)/shard_map/ppermute | solution.py:587
  33.4 7.8 %collective-permute-start.8 = (bf16[128,512]{1,0:T(8,128)(2,1)S(1)}, bf16[128,512]{1,0:T(8,128)(2,1)S(1)}, u32[]{:S(2)}, u32[]{:S(2)}) collective-permute-start(bf16[128,512]{1,0:T(8,128)(2,1)S(1)} %shard_map.202), channel_id=1, source_target_pairs={{0,2},{2,0},{1,3},{3,1},{4,6},{6,4},{5,7},{7,5},{8,10},{10,8},{9,1... | collective-permute-start | bytes 393224 | tf_op jit(solution)/shard_map/ppermute | solution.py:587

commit v8 on v7

--- a/solution.py
+++ b/solution.py
@@ -484,14 +484,21 @@
     return (1 - mp if far else mp) * 2 + (1 - sub if other else sub)
 
 
+def project_self(block, half, att_ref, ws_ref, gain_ref):
+    cut = ws_ref.shape[1] // 8
+    at = columns(block * 2 + half, cut)
+    return gain_ref[:, at].astype(F32) * dot(att_ref[...], ws_ref[:, at])
+
+
+def project_a2v(block, half, a2v_ref, wa_ref, gain_ref):
+    cut = wa_ref.shape[1] // 8
+    gain = gain_ref[:, columns(block * 2 + half + 8, cut)].astype(F32)
+    return gain * dot(a2v_ref[...], wa_ref[:, columns(block * 2 + half, cut)])
+
+
 def project(block, half, heads, weights, gain_ref):
-    (att_ref, a2v_ref), (ws_ref, wa_ref) = heads, weights
-    wide = ws_ref.shape[1]
-    cut = wide // 8
-    at = columns(block * 2 + half, cut)
-    term = gain_ref[:, at].astype(F32) * dot(att_ref[...], ws_ref[:, at])
-    gain = gain_ref[:, columns(block * 2 + half + 8, cut)].astype(F32)
-    return term + gain * dot(a2v_ref[...], wa_ref[:, at])
+    term = project_self(block, half, heads[0], weights[0], gain_ref)
+    return term + project_a2v(block, half, heads[1], weights[1], gain_ref)
 
 
 def project_audio(block, v2a_ref, wv_ref):
@@ -499,15 +506,16 @@
 
 
 def first_kernel(hops, rows_audio, head, limit_ref, q_ref, part_ref, stats_ref, own_ref, ws_ref, wa_ref, gain_ref, *rest):
-    got, (self_ref, a2v_ref, out_ref) = rest[: len(hops) - 1], rest[len(hops) - 1 :]
+    got, (self_ref, a2v_ref, out_ref, term_ref) = rest[: len(hops) - 1], rest[len(hops) - 1 :]
     rows, width = own_ref.shape
     last_ref = got[hops.index(1) - 1]
+    self_ref[:, columns(index_of("seq"), width)] = own_ref[...]
+    for hop, ref in zip(hops[1:], got):
+        self_ref[:, columns(index_of("seq") ^ hop, width)] = ref[0:rows, :]
+    block = block_of(True, True)
+    term_ref[...] = project_self(block, 0, self_ref, ws_ref, gain_ref)
     finish_audio(head, limit_ref[0], q_ref, part_ref, stats_ref, last_ref, rows_audio, a2v_ref)
-    me = index_of("seq")
-    self_ref[:, columns(me, width)] = own_ref[...]
-    for hop, ref in zip(hops[1:], got):
-        self_ref[:, columns(me ^ hop, width)] = ref[0:rows, :]
-    out_ref[...] = project(block_of(True, True), 0, (self_ref, a2v_ref), (ws_ref, wa_ref), gain_ref).astype(BF16)
+    out_ref[...] = (term_ref[...] + project_a2v(block, 0, a2v_ref, wa_ref, gain_ref)).astype(BF16)
 
 
 def second_kernel(head, self_ref, a2v_ref, ws_ref, wa_ref, wv_ref, gain_ref, v2a_ref, lse_ref, *rest):
@@ -645,6 +653,7 @@
         (audio_len, q_own, a2v_part, a2v_stats, own, ws, wa, gain, *got),
         [SMEM] + [VMEM] * (n + 6),
         flops=flops,
+        scratch=[pltpu.VMEM((rows, half), F32)],
     )
     first = trade(first, "sub", 1, 2)
     second, v2a_att, own_low = call(

time: 42.4 us -> 42.3 us (level)
  no operation moved by 1% of the time
where the time goes in v8:
time: 42.3 us; the launch traced here: 42 us
  waiting for transfers between devices  14.9 us (35%)
  starting transfers between devices  14.5 us (34%)
  Pallas kernels  10.2 us (24%)
  between operations  1.37 us (3%)
  local copies, waits for them, and re-layouts  1.1 us (3%)
    ppermute x11, waiting for transfers between devices, trade(): return lax.ppermute(x, axis, [(i, i ^ hop) for i in range(size)])  14.9 us
    ppermute x11, starting transfers between devices, trade(): return lax.ppermute(x, axis, [(i, i ^ hop) for i in range(size)])  14.5 us
    pallas_call x11, Pallas kernels, call(): pl.pallas_call(kernel, out_shape=tuple(outs), in_specs=specs or [VMEM] *...  10.2 us
    unnamed x1, local copies, waits for them, and re-layouts  1.1 us
  transfers between devices with their start and end apart: 11, of which 4 were waited for; matrix products, arithmetic and copies ran while one was open for 3% of the time, Pallas kernels for 14%

profile of v8, /device:TPU:0, one launch (start us, length us, event | category | flops | bytes accessed | tf_op | source)
XLA Modules:
  0.0 42.0 jit_solution(11914654510045025449)
XLA Ops:
  0.6 1.3 %shard_map.195 = (bf16[576,128]{1,0:T(8,128)(2,1)S(1)}, bf16[576,128]{1,0:T(8,128)(2,1)S(1)}, bf16[576,128]{1,0:T(8,128)(2,1)S(1)}) custom-call(bf16[128,512]{1,0:T(8,128)(2,1)} %q_ref.3, bf16[128,512]{1,0:T(8,128)(2,1)} %k_ref.3, bf16[128,512]{1,0:T(8,128)(2,1)} %v_ref.3, bf16[32,256]{1,0:T(8,128)(2,1)} %qa_ref.3, bf16[32,256]{1,0:T(8,128)(2,1)} %ka_ref.3, ...), custom_call_target="tpu_custom_call" | custom-call | bytes 884736 | tf_op jit(solution)/shard_map/pallas_call | solution.py:194
  1.9 4.1 %collective-permute-start = (bf16[576,128]{1,0:T(8,128)(2,1)S(1)}, bf16[576,128]{1,0:T(8,128)(2,1)S(1)}, u32[]{:S(2)}, u32[]{:S(2)}) collective-permute-start(bf16[576,128]{1,0:T(8,128)(2,1)S(1)} %get-tuple-element.36), channel_id=1, source_target_pairs={{0,8},{4,12},{8,0},{12,4},{1,9},{5,13},{9,1},{13,5},{2,10},{6,14},... | collective-permute-start | bytes 442376 | tf_op jit(solution)/shard_map/ppermute | solution.py:595
  6.0 1.6 %collective-permute-start.1 = (bf16[576,128]{1,0:T(8,128)(2,1)S(1)}, bf16[576,128]{1,0:T(8,128)(2,1)S(1)}, u32[]{:S(2)}, u32[]{:S(2)}) collective-permute-start(bf16[576,128]{1,0:T(8,128)(2,1)S(1)} %get-tuple-element.37), channel_id=1, source_target_pairs={{0,4},{4,0},{8,12},{12,8},{1,5},{5,1},{9,13},{13,9},{2,6},{6,2},{1... | collective-permute-start | bytes 442376 | tf_op jit(solution)/shard_map/ppermute | solution.py:595
  7.6 0.8 %shard_map.197 = bf16[448,128]{1,0:T(8,128)(2,1)S(1)} custom-call(bf16[128,512]{1,0:T(8,128)(2,1)} %q_ref.3, bf16[128,512]{1,0:T(8,128)(2,1)} %k_ref.3, bf16[128,512]{1,0:T(8,128)(2,1)} %v_ref.3, bf16[32,256]{1,0:T(8,128)(2,1)} %qa_ref.3, bf16[32,256]{1,0:T(8,128)(2,1)} %ka_ref.3, bf16[32,256]{1,0:T(8,128)(2,1)} %va_ref.3), custom_call_target="tpu_custom_call" | custom-call | bytes 557056 | tf_op jit(solution)/shard_map/pallas_call | solution.py:194
  8.5 0.1 collective-permute-start.2
  9.2 1.1 %copy.21 = bf16[2,8,2,4096]{3,1,2,0:T(8,128)(2,1)S(1)} copy(bf16[2,8,2,4096]{3,2,1,0:T(2,128)(2,1)} %bitcast.5) | data formatting | bytes 524288
  10.3 3.4 %shard_map.194 = (bf16[128,8192]{1,0:T(8,128)(2,1)S(1)}, f32[32,512]{1,0:T(8,128)S(1)}, bf16[128,256]{1,0:T(8,128)(2,1)S(1)}, bf16[128,256]{1,0:T(8,128)(2,1)S(1...) custom-call(s32[1]{0:T(128)S(6)} %copy.22.limit_ref, ...), custom_call_target="tpu_custom_call" | custom-call | bytes 18154116 | tf_op jit(solution)/shard_map/pallas_call | solution.py:194
  13.7 3.0 %collective-permute-done.2.rest_1_ = bf16[448,128]{1,0:T(8,128)(2,1)S(1)} collective-permute-done((bf16[448,128]{1,0:T(8,128)(2,1)S(1)}, bf16[448,128]{1,0:T(8,128)(2,1)S(1)}, u32[]{:S(2)}, u32[]{:S(2)}) %collective-permute-start.2) | collective-permute-done | bytes 114720 | tf_op jit(solution)/shard_map/ppermute | solution.py:595
  16.7 0.9 %shard_map.198 = (bf16[208,128]{1,0:T(8,128)(2,1)S(1)}, bf16[208,128]{1,0:T(8,128)(2,1)S(1)}, bf16[336,128]{1,0:T(8,128)(2,1)S(1)}, bf16[128,128]{1,0:T(8,128)(2...) custom-call(bf16[128,256]{1,0:T(8,128)(2,1)S(1)} %get-tuple-element.40.kv_ref, ...), custom_call_target="tpu_custom_call" | custom-call | flops 134217728 | bytes 948224 | tf_op jit(solution)/shard_map/pallas_call | solution.py:194
  17.6 2.0 %collective-permute-start.5 = (bf16[336,128]{1,0:T(8,128)(2,1)S(1)}, bf16[336,128]{1,0:T(8,128)(2,1)S(1)}, u32[]{:S(2)}, u32[]{:S(2)}) collective-permute-start(bf16[336,128]{1,0:T(8,128)(2,1)S(1)} %get-tuple-element.48), channel_id=1, source_target_pairs={{0,4},{4,0},{8,12},{12,8},{1,5},{5,1},{9,13},{13,9},{2,6},{6,2},{1... | collective-permute-start | bytes 258056 | tf_op jit(solution)/shard_map/ppermute | solution.py:595
  19.7 3.4 %collective-permute-start.3 = (bf16[208,128]{1,0:T(8,128)(2,1)S(1)}, bf16[208,128]{1,0:T(8,128)(2,1)S(1)}, u32[]{:S(2)}, u32[]{:S(2)}) collective-permute-start(bf16[208,128]{1,0:T(8,128)(2,1)S(1)} %get-tuple-element.46), channel_id=1, source_target_pairs={{0,12},{4,8},{8,4},{12,0},{1,13},{5,9},{9,5},{13,1},{2,14},{6,10},... | collective-permute-start | bytes 159752 | tf_op jit(solution)/shard_map/ppermute | solution.py:595
  23.1 0.6 %shard_map.196 = (f32[256,128]{1,0:T(8,128)S(1)}, f32[4,256]{1,0:T(4,128)S(1)}) custom-call(s32[1]{0:T(128)S(6)} %copy.22.limit_ref, bf16[128,256]{1,0:T(8,128)(2,1)S(1)} %get-tuple-element.34.q_ref, bf16[576,128]{1,0:T(8,128)(2,1)S(1)} %get-tuple-element.35.rest_0_, bf16[576,128]{1,0:T(8,128)(2,1)S(1)} %collective-permute-done.rest_1_.rest_2_, ...), custom_call_target="tpu_custom_call" | custom-call | flops 33554432 | bytes 643076 | tf_op jit(solution)/shard_map/pallas_call | solution.py:194
  23.7 3.6 %collective-permute-done.3.rest_0_ = bf16[208,128]{1,0:T(8,128)(2,1)S(1)} collective-permute-done((bf16[208,128]{1,0:T(8,128)(2,1)S(1)}, bf16[208,128]{1,0:T(8,128)(2,1)S(1)}, u32[]{:S(2)}, u32[]{:S(2)}) %collective-permute-start.3) | collective-permute-done | bytes 53280 | tf_op jit(solution)/shard_map/ppermute | solution.py:595
  27.3 1.4 %collective-permute-done.4.rest_1_ = bf16[208,128]{1,0:T(8,128)(2,1)S(1)} collective-permute-done((bf16[208,128]{1,0:T(8,128)(2,1)S(1)}, bf16[208,128]{1,0:T(8,128)(2,1)S(1)}, u32[]{:S(2)}, u32[]{:S(2)}) %collective-permute-start.4) | collective-permute-done | bytes 53280 | tf_op jit(solution)/shard_map/ppermute | solution.py:595
  28.7 0.7 %shard_map.199 = (bf16[128,512]{1,0:T(8,128)(2,1)S(1)}, bf16[128,256]{1,0:T(8,128)(2,1)S(1)}, bf16[128,512]{1,0:T(8,128)(2,1)S(1)}) custom-call(s32[1]{0:T(128)S(6)} %copy.22.limit_ref, bf16[128,256]{1,0:T(8,128)(2,1)S(1)} %get-tuple-element.34.q_ref, f32[256,128]{1,0:T(8,128)S(1)} %get-tuple-element.38.part_ref, f32[4,256]{1,0:T(4,128)S(1)} %get-tuple-element.39.stats_ref, ...), custom_call_target="tpu_custom_call" | custom-call | flops 100663296 | bytes 9142276 | tf_op jit(solution)/shard_map/pallas_call | solution.py:194
  29.4 0.6 %shard_map.200 = (bf16[160,512]{1,0:T(8,128)(2,1)S(1)}, bf16[32,256]{1,0:T(8,128)(2,1)S(1)}, f32[128,512]{1,0:T(8,128)S(1)}) custom-call(bf16[128,512]{1,0:T(8,128)(2,1)S(1)} %get-tuple-element.49.self_ref, bf16[128,256]{1,0:T(8,128)(2,1)S(1)} %get-tuple-element.50.a2v_ref, bf16[512,4096]{1,0:T(8,128)(2,1)S(1)} %get-tuple-element.43.ws_ref, ...), custom_call_target="tpu_custom_call" | custom-call | flops 201326592 | bytes 10303488 | tf_op jit(solution)/shard_map/pallas_call | solution.py:194
  30.1 0.8 %shard_map.201 = (bf16[288,512]{1,0:T(8,128)(2,1)S(1)}, f32[288,512]{1,0:T(8,128)S(1)}) custom-call(bf16[128,512]{1,0:T(8,128)(2,1)S(1)} %get-tuple-element.49.self_ref, bf16[128,256]{1,0:T(8,128)(2,1)S(1)} %get-tuple-element.50.a2v_ref, bf16[32,256]{1,0:T(8,128)(2,1)S(1)} %get-tuple-element.54.audio_ref, bf16[512,4096]{1,0:T(8,128)(2,1)S(1)} %get-tuple-element.43.ws_ref, ...), custom_call_target="tpu_custom_call" | custom-call | flops 402653184 | bytes 10534912 | tf_op jit(solution)/shard_map/pallas_call | solution.py:194
  30.8 0.5 %collective-permute-start.6 = (bf16[288,512]{1,0:T(8,128)(2,1)S(1)}, bf16[288,512]{1,0:T(8,128)(2,1)S(1)}, u32[]{:S(2)}, u32[]{:S(2)}) collective-permute-start(bf16[288,512]{1,0:T(8,128)(2,1)S(1)} %get-tuple-element.56), channel_id=1, source_target_pairs={{0,1},{1,0},{2,3},{3,2},{4,5},{5,4},{6,7},{7,6},{8,9},{9,8},{10,11... | collective-permute-start | bytes 884744 | tf_op jit(solution)/shard_map/ppermute | solution.py:595
  31.4 0.1 collective-permute-start.7
  31.4 0.3 shard_map.203
  31.8 1.6 %collective-permute-start.10 = (bf16[160,512]{1,0:T(8,128)(2,1)S(1)}, bf16[160,512]{1,0:T(8,128)(2,1)S(1)}, u32[]{:S(2)}, u32[]{:S(2)}) collective-permute-start(bf16[160,512]{1,0:T(8,128)(2,1)S(1)} %shard_map.203), channel_id=1, source_target_pairs={{0,2},{2,0},{1,3},{3,1},{4,6},{6,4},{5,7},{7,5},{8,10},{10,8},{9,1... | collective-permute-start | bytes 491528 | tf_op jit(solution)/shard_map/ppermute | solution.py:595
  33.4 1.0 %collective-permute-start.8 = (bf16[128,512]{1,0:T(8,128)(2,1)S(1)}, bf16[128,512]{1,0:T(8,128)(2,1)S(1)}, u32[]{:S(2)}, u32[]{:S(2)}) collective-permute-start(bf16[128,512]{1,0:T(8,128)(2,1)S(1)} %shard_map.202), channel_id=1, source_target_pairs={{0,2},{2,0},{1,3},{3,1},{4,6},{6,4},{5,7},{7,5},{8,10},{10,8},{9,1... | collective-permute-start | bytes 393224 | tf_op jit(solution)/shard_map/ppermute | solution.py:595
  34.4 6.8 %collective-permute-done.8.low_ref = bf16[128,512]{1,0:T(8,128)(2,1)S(1)} collective-permute-done((bf16[128,512]{1,0:T(8,128)(2,1)S(1)}, bf16[128,512]{1,0:T(8,128)(2,1)S(1)}, u32[]{:S(2)}, u32[]{:S(2)}) %collective-permute-start.8) | collective-permute-done | bytes 131104 | tf_op jit(solution)/shard_map/ppermute | solution.py:595
  41.2 0.8 %shard_map.204 = (bf16[128,1024]{1,0:T(8,128)(2,1)}, bf16[32,512]{1,0:T(8,128)(2,1)}) custom-call(bf16[128,1024]{1,0:T(8,128)(2,1)S(1)} %get-tuple-element.31.video_ref, bf16[32,512]{1,0:T(8,128)(2,1)S(1)} %get-tuple-element.32.audio_ref, f32[32,512]{1,0:T(8,128)S(1)} %get-tuple-element.33.gain_ref, f32[288,512]{1,0:T(8,128)S(1)} %get-tuple-element.55.own_ref, ...), custom_call_target="tpu_custom_call" | custom-call | bytes 1835008 | tf_op jit(solution)/shard_map/pallas_call | solution.py:194
  (10 shorter events, 0.1 us)
Async XLA Ops:
  1.9 14.8 %collective-permute-start = (bf16[576,128]{1,0:T(8,128)(2,1)S(1)}, bf16[576,128]{1,0:T(8,128)(2,1)S(1)}, u32[]{:S(2)}, u32[]{:S(2)}) collective-permute-start(bf16[576,128]{1,0:T(8,128)(2,1)S(1)} %get-tuple-element.36), channel_id=1, source_target_pairs={{0,8},{4,12},{8,0},{12,4},{1,9},{5,13},{9,1},{13,5},{2,10},{6,14},... | collective-permute-start | bytes 442376 | tf_op jit(solution)/shard_map/ppermute | solution.py:595
  6.0 10.7 %collective-permute-start.1 = (bf16[576,128]{1,0:T(8,128)(2,1)S(1)}, bf16[576,128]{1,0:T(8,128)(2,1)S(1)}, u32[]{:S(2)}, u32[]{:S(2)}) collective-permute-start(bf16[576,128]{1,0:T(8,128)(2,1)S(1)} %get-tuple-element.37), channel_id=1, source_target_pairs={{0,4},{4,0},{8,12},{12,8},{1,5},{5,1},{9,13},{13,9},{2,6},{6,2},{1... | collective-permute-start | bytes 442376 | tf_op jit(solution)/shard_map/ppermute | solution.py:595
  8.5 8.3 %collective-permute-start.2 = (bf16[448,128]{1,0:T(8,128)(2,1)S(1)}, bf16[448,128]{1,0:T(8,128)(2,1)S(1)}, u32[]{:S(2)}, u32[]{:S(2)}) collective-permute-start(bf16[448,128]{1,0:T(8,128)(2,1)S(1)} %shard_map.197), channel_id=1, source_target_pairs={{0,12},{4,8},{8,4},{12,0},{1,13},{5,9},{9,5},{13,1},{2,14},{6,10},... | collective-permute-start | bytes 344072 | tf_op jit(solution)/shard_map/ppermute | solution.py:595
  17.6 11.1 %collective-permute-start.5 = (bf16[336,128]{1,0:T(8,128)(2,1)S(1)}, bf16[336,128]{1,0:T(8,128)(2,1)S(1)}, u32[]{:S(2)}, u32[]{:S(2)}) collective-permute-start(bf16[336,128]{1,0:T(8,128)(2,1)S(1)} %get-tuple-element.48), channel_id=1, source_target_pairs={{0,4},{4,0},{8,12},{12,8},{1,5},{5,1},{9,13},{13,9},{2,6},{6,2},{1... | collective-permute-start | bytes 258056 | tf_op jit(solution)/shard_map/ppermute | solution.py:595
  19.7 7.6 %collective-permute-start.3 = (bf16[208,128]{1,0:T(8,128)(2,1)S(1)}, bf16[208,128]{1,0:T(8,128)(2,1)S(1)}, u32[]{:S(2)}, u32[]{:S(2)}) collective-permute-start(bf16[208,128]{1,0:T(8,128)(2,1)S(1)} %get-tuple-element.46), channel_id=1, source_target_pairs={{0,12},{4,8},{8,4},{12,0},{1,13},{5,9},{9,5},{13,1},{2,14},{6,10},... | collective-permute-start | bytes 159752 | tf_op jit(solution)/shard_map/ppermute | solution.py:595
  23.1 5.6 %collective-permute-start.4 = (bf16[208,128]{1,0:T(8,128)(2,1)S(1)}, bf16[208,128]{1,0:T(8,128)(2,1)S(1)}, u32[]{:S(2)}, u32[]{:S(2)}) collective-permute-start(bf16[208,128]{1,0:T(8,128)(2,1)S(1)} %get-tuple-element.47), channel_id=1, source_target_pairs={{0,8},{4,12},{8,0},{12,4},{1,9},{5,13},{9,1},{13,5},{2,10},{6,14},... | collective-permute-start | bytes 159752 | tf_op jit(solution)/shard_map/ppermute | solution.py:595
  30.0 1.5 %collective-permute-start.9 = (bf16[160,512]{1,0:T(8,128)(2,1)S(1)}, bf16[160,512]{1,0:T(8,128)(2,1)S(1)}, u32[]{:S(2)}, u32[]{:S(2)}) collective-permute-start(bf16[160,512]{1,0:T(8,128)(2,1)S(1)} %get-tuple-element.59), channel_id=1, source_target_pairs={{0,1},{1,0},{2,3},{3,2},{4,5},{5,4},{6,7},{7,6},{8,9},{9,8},{10,11... | collective-permute-start | bytes 491528 | tf_op jit(solution)/shard_map/ppermute | solution.py:595
  30.8 10.3 %collective-permute-start.6 = (bf16[288,512]{1,0:T(8,128)(2,1)S(1)}, bf16[288,512]{1,0:T(8,128)(2,1)S(1)}, u32[]{:S(2)}, u32[]{:S(2)}) collective-permute-start(bf16[288,512]{1,0:T(8,128)(2,1)S(1)} %get-tuple-element.56), channel_id=1, source_target_pairs={{0,1},{1,0},{2,3},{3,2},{4,5},{5,4},{6,7},{7,6},{8,9},{9,8},{10,11... | collective-permute-start | bytes 884744 | tf_op jit(solution)/shard_map/ppermute | solution.py:595
  31.4 2.0 %collective-permute-start.7 = (bf16[128,512]{1,0:T(8,128)(2,1)S(1)}, bf16[128,512]{1,0:T(8,128)(2,1)S(1)}, u32[]{:S(2)}, u32[]{:S(2)}) collective-permute-start(bf16[128,512]{1,0:T(8,128)(2,1)S(1)} %get-tuple-element.58), channel_id=1, source_target_pairs={{0,1},{1,0},{2,3},{3,2},{4,5},{5,4},{6,7},{7,6},{8,9},{9,8},{10,11... | collective-permute-start | bytes 393224 | tf_op jit(solution)/shard_map/ppermute | solution.py:595
  31.8 9.4 %collective-permute-start.10 = (bf16[160,512]{1,0:T(8,128)(2,1)S(1)}, bf16[160,512]{1,0:T(8,128)(2,1)S(1)}, u32[]{:S(2)}, u32[]{:S(2)}) collective-permute-start(bf16[160,512]{1,0:T(8,128)(2,1)S(1)} %shard_map.203), channel_id=1, source_target_pairs={{0,2},{2,0},{1,3},{3,1},{4,6},{6,4},{5,7},{7,5},{8,10},{10,8},{9,1... | collective-permute-start | bytes 491528 | tf_op jit(solution)/shard_map/ppermute | solution.py:595
  33.4 7.8 %collective-permute-start.8 = (bf16[128,512]{1,0:T(8,128)(2,1)S(1)}, bf16[128,512]{1,0:T(8,128)(2,1)S(1)}, u32[]{:S(2)}, u32[]{:S(2)}) collective-permute-start(bf16[128,512]{1,0:T(8,128)(2,1)S(1)} %shard_map.202), channel_id=1, source_target_pairs={{0,2},{2,0},{1,3},{3,1},{4,6},{6,4},{5,7},{7,5},{8,10},{10,8},{9,1... | collective-permute-start | bytes 393224 | tf_op jit(solution)/shard_map/ppermute | solution.py:595

commit v9 on v8

--- a/solution.py
+++ b/solution.py
@@ -182,7 +182,7 @@
 BF16, F32 = jnp.bfloat16, jnp.float32
 LSE_ROWS = 16
 LEAST = float(jnp.finfo(jnp.float32).min)
-SEQ, FORWARDED, OUT_ORDER = 4, 3, [3, 2, 1]
+SEQ, FORWARDED, OUT_ORDER, LAST = 4, 3, [3, 2, 1], 2
 
 
 def call(kernel, outs, operands, specs=None, flops=0, scratch=(), limit=8 * 2**20):
@@ -311,94 +311,131 @@
     return jnp.concatenate([x[i * head : (i + 1) * head, i * rows : (i + 1) * rows] for i in range(pair)], axis=0)
 
 
-def attend_kernel(hops, head, kv_ref, vv_ref, *rest):
-    n = len(hops)
-    blocks, sends, (own_ref, own_v2a_ref, own_lse_ref) = rest[:n], rest[n : 2 * n - 1], rest[2 * n - 1 : 2 * n + 2]
-    vt_ref, vvt_ref, s_ref, p_ref = rest[2 * n + 2 :]
-    rows, cols = kv_ref.shape
-    width = blocks[0].shape[1]
-    rows_audio = own_v2a_ref.shape[0]
-    ends = [1 if hop == FORWARDED else 3 for hop in hops]
-    for h in range(width // DHV):
-        cut = slice(h * DHV, (h + 1) * DHV)
-        for i, ref in enumerate(blocks):
-            vt_ref[cut, i * rows : (i + 1) * rows] = turn(ref[2 * rows : 3 * rows, cut])
+def audio_part(q, keys, values_t, head):
+    pair, rows = 128 // head, q.shape[0]
+    scale = 1.0 / math.sqrt(head)
+    both = pair_rows(q, head)
+    both = jnp.concatenate([both] * (128 // both.shape[0]), axis=0)
+    peak, p, total = softmax_t([dot_t(keys, both)], scale)
+    o = dot(values_t, p[0]) * (1.0 / total)
+    lse = peak * (scale * LOG2E) + jnp.log2(total)
+    o = [o[i * head : (i + 1) * head] for i in range(pair)]
+    o = [x if i == 0 else pltpu.roll(x, 128 - i * rows, 1) for i, x in enumerate(o)]
+    lses = [lse if i == 0 else pltpu.roll(lse, 128 - i * rows, 1) for i in range(pair)]
+    return jnp.concatenate(o, axis=0).T[0:rows], lses
+
+
+def audio_parts(ref, end, kv_ref, vvt_ref, rows_audio, head):
+    cols = kv_ref.shape[1]
+    outs, lses = [], []
     for block in range(cols // 128):
         cut = slice(block * 128, (block + 1) * 128)
-        vvt_ref[cut, :] = turn(vv_ref[:, cut])
-    pair, row = 128 // head, 0
-    parts = []
-    for block in range(cols // 128):
-        cut = slice(block * 128, (block + 1) * 128)
-        q = [audio_block(ref, end, rows_audio, cols, block) for ref, end in zip(blocks, ends)]
-        q = pair_rows(jnp.concatenate(q, axis=0), head)
-        scores = dot_t(kv_ref[:, cut], q)
-        for i in range(pair):
-            at = slice(i * n * rows_audio, (i + 1) * n * rows_audio)
-            s_ref[row + i * rows : row + (i + 1) * rows, :] = scores[:, at]
-            parts.append((row + i * rows, rows, jnp.max(scores[:, at], axis=0, keepdims=True), 1.0 / math.sqrt(head)))
-        row += pair * rows
-    for ref in blocks:
-        for h in range(width // DHV):
-            cut = slice(h * DHV, (h + 1) * DHV)
-            peak = None
-            for i, other in enumerate(blocks):
-                scores = dot_t(other[rows : 2 * rows, cut], ref[0:rows, cut])
-                s_ref[row + i * rows : row + (i + 1) * rows, :] = scores
-                top = jnp.max(scores, axis=0, keepdims=True)
-                peak = top if i == 0 else jnp.maximum(peak, top)
-            parts.append((row, n * rows, peak, 1.0 / math.sqrt(DHV)))
-            row += n * rows
-
-    def weigh(part):
-        start, count, peak, scale = part
-        total = None
-        for at in range(start, start + count, 128):
-            p = jnp.exp2((s_ref[at : at + 128, :] - peak) * (scale * LOG2E))
-            p_ref[at : at + 128, :] = p.astype(BF16)
-            summed = jnp.sum(p, axis=0, keepdims=True)
-            total = summed if at == start else total + summed
-        return total
-
-    lses, at = [], 0
-    for block in range(cols // 128):
-        both = []
-        for i in range(pair):
-            start, count, peak, scale = parts[at]
-            total = weigh(parts[at])
-            lses.append(peak * (scale * LOG2E) + jnp.log2(total))
-            column = block * 128 + i * head
-            o = dot(vvt_ref[column : column + head, :], p_ref[start : start + count, :])
-            both.append(o * (1.0 / total))
-            at += 1
-        v2a = jnp.concatenate(both, axis=0).T
-        own_v2a_ref[:, block * 128 : (block + 1) * 128] = v2a[0:rows_audio]
-        for j, dst in enumerate(sends):
-            top = rows + block * rows_audio
-            dst[top : top + rows_audio, 0:128] = v2a[(j + 1) * rows_audio : (j + 2) * rows_audio].astype(BF16)
-    for j in range(n):
-        for h in range(width // DHV):
-            cut = slice(h * DHV, (h + 1) * DHV)
-            start, count, _, _ = parts[at]
-            total = weigh(parts[at])
-            o = dot(vt_ref[cut, :], p_ref[start : start + count, :]) * (1.0 / total)
-            dst = own_ref if j == 0 else sends[j - 1].at[0:rows, :]
-            dst[:, cut] = o.T.astype(BF16)
-            at += 1
-    relayed = 2 * cols // width * rows_audio
-    dst, src = sends[hops.index(1) - 1], blocks[hops.index(FORWARDED ^ 1)]
-    dst[dst.shape[0] - relayed :, :] = src[src.shape[0] - relayed :, :]
-    heads = len(lses)
-    lse = jnp.concatenate(lses, axis=0)
-    own_lse_ref[...] = lse
+        q = audio_block(ref, end, rows_audio, cols, block)
+        o, lse = audio_part(q, kv_ref[:, cut], vvt_ref[cut, :], head)
+        outs.append(o)
+        lses += lse
+    return outs, jnp.concatenate(lses, axis=0)
+
+
+def store_tail(dst, top, outs, lse):
+    rows_audio = outs[0].shape[0]
+    for i, o in enumerate(outs):
+        dst[top + i * rows_audio : top + (i + 1) * rows_audio, 0:128] = o.astype(BF16)
     pieces, left = [], lse
     for _ in range(3):
         pieces.append(left.astype(BF16).astype(F32))
         left = left - pieces[-1]
-    packed = jnp.concatenate(pieces + [jnp.zeros((LSE_ROWS - 3 * heads, lse.shape[1]), F32)], axis=0)
-    for j, dst in enumerate(sends):
-        top = rows + cols // 128 * rows_audio
-        dst[top : top + LSE_ROWS, 0:128] = pltpu.roll(packed, 128 - (j + 1) * rows_audio, 1).astype(BF16)
+    pieces.append(jnp.zeros((LSE_ROWS - 3 * lse.shape[0], 128), F32))
+    top += len(outs) * rows_audio
+    dst[top : top + LSE_ROWS, 0:128] = jnp.concatenate(pieces, axis=0).astype(BF16)
+
+
+def early_kernel(early, head, kv_ref, vv_ref, *rest):
+    count = len(early)
+    blocks, (part_ref, stats_ref, vt_ref, vvt_ref, own_v2a_ref, own_lse_ref) = rest[:count], rest[count : count + 6]
+    tails, (s_ref,) = rest[count + 6 : -1], rest[-1:]
+    rows, cols = kv_ref.shape
+    rows_audio = own_v2a_ref.shape[0]
+    for i, ref in enumerate(blocks):
+        vt_ref[:, i * rows : (i + 1) * rows] = turn(ref[2 * rows : 3 * rows, :])
+    for block in range(cols // 128):
+        cut = slice(block * 128, (block + 1) * 128)
+        vvt_ref[cut, :] = turn(vv_ref[:, cut])
+    scale = 1.0 / math.sqrt(DHV)
+    peaks = []
+    for j, ref in enumerate(blocks):
+        peak = None
+        for i, other in enumerate(blocks):
+            scores = dot_t(other[rows : 2 * rows, :], ref[0:rows, :])
+            s_ref[(j * count + i) * rows : (j * count + i + 1) * rows, :] = scores
+            top = jnp.max(scores, axis=0, keepdims=True)
+            peak = top if i == 0 else jnp.maximum(peak, top)
+        peaks.append(peak)
+    for j, peak in enumerate(peaks):
+        total, p = None, []
+        for i in range(count):
+            x = jnp.exp2((s_ref[(j * count + i) * rows : (j * count + i + 1) * rows, :] - peak) * (scale * LOG2E))
+            summed = jnp.sum(x, axis=0, keepdims=True)
+            total = summed if i == 0 else total + summed
+            p.append(x.astype(BF16))
+        part_ref[j * DHV : (j + 1) * DHV, :] = dot(vt_ref[...], jnp.concatenate(p, axis=0))
+        stats_ref[2 * j : 2 * j + 1, :] = peak
+        stats_ref[2 * j + 1 : 2 * j + 2, :] = total
+    for j, (hop, ref) in enumerate(zip(early, blocks)):
+        outs, lse = audio_parts(ref, 1 if hop == FORWARDED else 3, kv_ref, vvt_ref, rows_audio, head)
+        if j > 0:
+            store_tail(tails[j - 1], 0, outs, lse)
+            continue
+        own_lse_ref[...] = lse
+        for block, o in enumerate(outs):
+            own_v2a_ref[:, block * 128 : (block + 1) * 128] = o
+
+
+def late_kernel(early, hops, rows_audio, head, kv_ref, vvt_ref, part_ref, stats_ref, vt_ref, last_ref, *rest):
+    count, n = len(early), len(hops)
+    blocks, tails, outs, s_ref = rest[:count], rest[count : 2 * count - 1], rest[2 * count - 1 : -1], rest[-1]
+    by_hop = dict(zip(hops, outs))
+    rows = kv_ref.shape[0]
+    last = next(hop for hop in hops if hop not in early)
+    scale = 1.0 / math.sqrt(DHV)
+    keys = last_ref[rows : 2 * rows, :]
+    peaks = []
+    for j, ref in enumerate((*blocks, last_ref)):
+        scores = dot_t(keys, ref[0:rows, :])
+        s_ref[j * rows : (j + 1) * rows, :] = scores
+        top = jnp.max(scores, axis=0, keepdims=True)
+        peaks.append(jnp.maximum(top, stats_ref[2 * j : 2 * j + 1, :]) if j < count else top)
+    for i, other in enumerate(blocks):
+        scores = dot_t(other[rows : 2 * rows, :], last_ref[0:rows, :])
+        s_ref[(n + i) * rows : (n + i + 1) * rows, :] = scores
+        peaks[-1] = jnp.maximum(peaks[-1], jnp.max(scores, axis=0, keepdims=True))
+    values_t = turn(last_ref[2 * rows : 3 * rows, :])
+
+    def weigh(at, peak):
+        x = jnp.exp2((s_ref[at * rows : (at + 1) * rows, :] - peak) * (scale * LOG2E))
+        return x.astype(BF16), jnp.sum(x, axis=0, keepdims=True)
+
+    audio = audio_parts(last_ref, 3, kv_ref, vvt_ref, rows_audio, head)
+    total, p = None, []
+    for i in range(count):
+        x, summed = weigh(n + i, peaks[-1])
+        total = summed if i == 0 else total + summed
+        p.append(x)
+    x, summed = weigh(count, peaks[-1])
+    o = dot(vt_ref[...], jnp.concatenate(p, axis=0)) + dot(values_t, x)
+    by_hop[last][0:rows, :] = (o * (1.0 / (total + summed))).T.astype(BF16)
+    for j, hop in enumerate(early):
+        x, summed = weigh(j, peaks[j])
+        factor = jnp.exp2((stats_ref[2 * j : 2 * j + 1, :] - peaks[j]) * (scale * LOG2E))
+        total = stats_ref[2 * j + 1 : 2 * j + 2, :] * factor + summed
+        o = part_ref[j * DHV : (j + 1) * DHV, :] * factor + dot(values_t, x)
+        by_hop[hop][0:rows, :] = (o * (1.0 / total)).T.astype(BF16)
+    store_tail(by_hop[last], rows, *audio)
+    for hop, tail in zip(early[1:], tails):
+        by_hop[hop][rows : rows + tail.shape[0], :] = tail[...]
+    dst = by_hop[FORWARDED]
+    top = rows + tails[0].shape[0]
+    dst[top:, :] = blocks[0][blocks[0].shape[0] - (dst.shape[0] - top) :, :]
 
 
 def audio_allowed(hop, rows_audio, limit):
@@ -508,7 +545,7 @@
 def first_kernel(hops, rows_audio, head, limit_ref, q_ref, part_ref, stats_ref, own_ref, ws_ref, wa_ref, gain_ref, *rest):
     got, (self_ref, a2v_ref, out_ref, term_ref) = rest[: len(hops) - 1], rest[len(hops) - 1 :]
     rows, width = own_ref.shape
-    last_ref = got[hops.index(1) - 1]
+    last_ref = got[hops.index(FORWARDED) - 1]
     self_ref[:, columns(index_of("seq"), width)] = own_ref[...]
     for hop, ref in zip(hops[1:], got):
         self_ref[:, columns(index_of("seq") ^ hop, width)] = ref[0:rows, :]
@@ -624,17 +661,32 @@
         scratch=[pltpu.VMEM(x.shape, x.dtype) for x in (*steps, audio_gates)]
         + [pltpu.SemaphoreType.DMA((3 + len(late),))],
     )
-    back = rows + cross // 128 * rows_audio + LSE_ROWS
-    result = call(
-        functools.partial(attend_kernel, hops, DHC),
-        [shape(back + 2 * audio if hop == 1 else back, width) for hop in hops[1:]]
-        + [shape(rows, width), shape(rows_audio, cross, F32), shape(cross // DHC, 128, F32)],
-        (k_own, v_own, *blocks.values()),
-        flops=4 * n * n * rows * rows * width,
-        scratch=[pltpu.VMEM((width, n * rows), BF16), pltpu.VMEM((cross, rows), BF16)]
-        + [pltpu.VMEM((n * n * rows * width // DHV + cross // DHC * rows, 128), kind) for kind in (F32, BF16)],
-    )
-    sends, (own, own_v2a, own_lse) = result[: n - 1], result[n - 1 :]
+    tail = cross // 128 * rows_audio + LSE_ROWS
+    early = [hop for hop in hops if hop != LAST]
+    count = len(early)
+    part, stats, vt, vvt, own_v2a, own_lse, *tails = call(
+        functools.partial(early_kernel, early, DHC),
+        [
+            shape(count * width, rows, F32),
+            shape(2 * count, rows, F32),
+            shape(width, count * rows),
+            shape(cross, rows),
+            shape(rows_audio, cross, F32),
+            shape(cross // DHC, 128, F32),
+        ]
+        + [shape(tail, width)] * (count - 1),
+        (k_own, v_own, *(blocks[hop] for hop in early)),
+        flops=4 * count * count * rows * rows * width,
+        scratch=[pltpu.VMEM((count * count * rows, rows), F32)],
+    )
+    own, *sends = call(
+        functools.partial(late_kernel, early, hops, rows_audio, DHC),
+        [shape(rows, width)]
+        + [shape(rows + tail + (2 * audio if hop == FORWARDED else 0), width) for hop in hops[1:]],
+        (k_own, vvt, part, stats, vt, blocks[LAST], *(blocks[hop] for hop in early), *tails),
+        flops=4 * (2 * n - 1) * rows * rows * width,
+        scratch=[pltpu.VMEM(((2 * n - 1) * rows, rows), F32)],
+    )
     got = [trade(x, "seq", hop, n) for x, hop in zip(sends, hops[1:])]
     near = [hop for hop in hops if hop != FORWARDED]
     a2v_part, a2v_stats = call(
@@ -692,7 +744,7 @@
     fits = (
         n == SEQ
         and (mp, sub) == (2, 2)
-        and width % DHV == 0
+        and width == DHV == 128
         and cross % width == 0
         and 3 * (cross // DHC) <= LSE_ROWS
         and n * arrays[8].shape[0] == arrays[2].shape[0] == 128

time: 42.3 us -> 42.4 us (level)
  Pallas kernels: 10.2 us -> 11.9 us
  waiting for transfers between devices: 14.9 us -> 13.9 us
  starting transfers between devices: 14.5 us -> 13.8 us
    pallas_call x11 -> x12, Pallas kernels: 10.2 us -> 11.9 us  [call(): pl.pallas_call(kernel, out_shape=tuple(outs), in_specs=specs or [VMEM] *...]
    ppermute x11, waiting for transfers between devices: 14.9 us -> 13.9 us  [trade(): return lax.ppermute(x, axis, [(i, i ^ hop) for i in range(size)])]
    ppermute x11, starting transfers between devices: 14.5 us -> 13.8 us  [trade(): return lax.ppermute(x, axis, [(i, i ^ hop) for i in range(size)])]
  transfers between devices with their start and end apart: 11 -> 11, of which waited for: 4 -> 3; matrix products, arithmetic and copies ran while one was open for 3% -> 3% of each run, Pallas kernels for 14% -> 18%
where the time goes in v9:
time: 42.4 us; the launch traced here: 42.1 us
  waiting for transfers between devices  13.9 us (33%)
  starting transfers between devices  13.8 us (33%)
  Pallas kernels  11.9 us (28%)
  between operations  1.38 us (3%)
  local copies, waits for them, and re-layouts  1.1 us (3%)
    ppermute x11, waiting for transfers between devices, trade(): return lax.ppermute(x, axis, [(i, i ^ hop) for i in range(size)])  13.9 us
    ppermute x11, starting transfers between devices, trade(): return lax.ppermute(x, axis, [(i, i ^ hop) for i in range(size)])  13.8 us
    pallas_call x12, Pallas kernels, call(): pl.pallas_call(kernel, out_shape=tuple(outs), in_specs=specs or [VMEM] *...  11.9 us
    unnamed x1, local copies, waits for them, and re-layouts  1.1 us
  transfers between devices with their start and end apart: 11, of which 3 were waited for; matrix products, arithmetic and copies ran while one was open for 3% of the time, Pallas kernels for 18%

profile of v9, /device:TPU:0, one launch (start us, length us, event | category | flops | bytes accessed | tf_op | source)
XLA Modules:
  0.0 42.1 jit_solution(8559442369136825746)
XLA Ops:
  0.6 1.3 %shard_map.195 = (bf16[576,128]{1,0:T(8,128)(2,1)S(1)}, bf16[576,128]{1,0:T(8,128)(2,1)S(1)}, bf16[576,128]{1,0:T(8,128)(2,1)S(1)}) custom-call(bf16[128,512]{1,0:T(8,128)(2,1)} %q_ref.3, bf16[128,512]{1,0:T(8,128)(2,1)} %k_ref.3, bf16[128,512]{1,0:T(8,128)(2,1)} %v_ref.3, bf16[32,256]{1,0:T(8,128)(2,1)} %qa_ref.3, bf16[32,256]{1,0:T(8,128)(2,1)} %ka_ref.3, ...), custom_call_target="tpu_custom_call" | custom-call | bytes 884736 | tf_op jit(solution)/shard_map/pallas_call | solution.py:194
  1.9 3.1 %collective-permute-start.1 = (bf16[576,128]{1,0:T(8,128)(2,1)S(1)}, bf16[576,128]{1,0:T(8,128)(2,1)S(1)}, u32[]{:S(2)}, u32[]{:S(2)}) collective-permute-start(bf16[576,128]{1,0:T(8,128)(2,1)S(1)} %get-tuple-element.43), channel_id=1, source_target_pairs={{0,4},{4,0},{8,12},{12,8},{1,5},{5,1},{9,13},{13,9},{2,6},{6,2},{1... | collective-permute-start | bytes 442376 | tf_op jit(solution)/shard_map/ppermute | solution.py:632
  5.0 2.6 %collective-permute-start = (bf16[576,128]{1,0:T(8,128)(2,1)S(1)}, bf16[576,128]{1,0:T(8,128)(2,1)S(1)}, u32[]{:S(2)}, u32[]{:S(2)}) collective-permute-start(bf16[576,128]{1,0:T(8,128)(2,1)S(1)} %get-tuple-element.42), channel_id=1, source_target_pairs={{0,8},{4,12},{8,0},{12,4},{1,9},{5,13},{9,1},{13,5},{2,10},{6,14},... | collective-permute-start | bytes 442376 | tf_op jit(solution)/shard_map/ppermute | solution.py:632
  7.6 0.8 %shard_map.197 = bf16[448,128]{1,0:T(8,128)(2,1)S(1)} custom-call(bf16[128,512]{1,0:T(8,128)(2,1)} %q_ref.3, bf16[128,512]{1,0:T(8,128)(2,1)} %k_ref.3, bf16[128,512]{1,0:T(8,128)(2,1)} %v_ref.3, bf16[32,256]{1,0:T(8,128)(2,1)} %qa_ref.3, bf16[32,256]{1,0:T(8,128)(2,1)} %ka_ref.3, bf16[32,256]{1,0:T(8,128)(2,1)} %va_ref.3), custom_call_target="tpu_custom_call" | custom-call | bytes 557056 | tf_op jit(solution)/shard_map/pallas_call | solution.py:194
  9.2 1.1 %copy.21 = bf16[2,8,2,4096]{3,1,2,0:T(8,128)(2,1)S(1)} copy(bf16[2,8,2,4096]{3,2,1,0:T(2,128)(2,1)} %bitcast.5) | data formatting | bytes 524288
  10.3 3.4 %shard_map.194 = (bf16[128,8192]{1,0:T(8,128)(2,1)S(1)}, f32[32,512]{1,0:T(8,128)S(1)}, bf16[128,256]{1,0:T(8,128)(2,1)S(1)}, bf16[128,256]{1,0:T(8,128)(2,1)S(1...) custom-call(s32[1]{0:T(128)S(6)} %copy.22.limit_ref, ...), custom_call_target="tpu_custom_call" | custom-call | bytes 18154116 | tf_op jit(solution)/shard_map/pallas_call | solution.py:194
  13.7 3.1 %collective-permute-done.2.rest_1_ = bf16[448,128]{1,0:T(8,128)(2,1)S(1)} collective-permute-done((bf16[448,128]{1,0:T(8,128)(2,1)S(1)}, bf16[448,128]{1,0:T(8,128)(2,1)S(1)}, u32[]{:S(2)}, u32[]{:S(2)}) %collective-permute-start.2) | collective-permute-done | bytes 114720 | tf_op jit(solution)/shard_map/ppermute | solution.py:632
  16.8 1.8 %shard_map.198 = (f32[384,128]{1,0:T(8,128)S(1)}, f32[6,128]{1,0:T(8,128)S(1)}, bf16[128,384]{1,0:T(8,128)(2,1)S(1)}, bf16[256,128]{1,0:T(8,128)(2,1)S(1)}, f32[...) custom-call(bf16[128,256]{1,0:T(8,128)(2,1)S(1)} %get-tuple-element.46.kv_r, ...), custom_call_target="tpu_custom_call" | custom-call | flops 75497472 | bytes 979968 | tf_op jit(solution)/shard_map/pallas_call | solution.py:194
  18.6 0.8 %shard_map.199 = (bf16[128,128]{1,0:T(8,128)(2,1)S(1)}, bf16[336,128]{1,0:T(8,128)(2,1)S(1)}, bf16[208,128]{1,0:T(8,128)(2,1)S(1)}, bf16[208,128]{1,0:T(8,128)(2,1)S(1)}) custom-call(bf16[128,256]{1,0:T(8,128)(2,1)S(1)} %get-tuple-element.46.kv_ref, bf16[256,128]{1,0:T(8,128)(2,1)S(1)} %get-tuple-element.48.vvt_ref, ...), custom_call_target="tpu_custom_call" | custom-call | flops 58720256 | bytes 1252352 | tf_op jit(solution)/shard_map/pallas_call | solution.py:194
  19.4 1.9 %collective-permute-start.3 = (bf16[336,128]{1,0:T(8,128)(2,1)S(1)}, bf16[336,128]{1,0:T(8,128)(2,1)S(1)}, u32[]{:S(2)}, u32[]{:S(2)}) collective-permute-start(bf16[336,128]{1,0:T(8,128)(2,1)S(1)} %get-tuple-element.58), channel_id=1, source_target_pairs={{0,12},{4,8},{8,4},{12,0},{1,13},{5,9},{9,5},{13,1},{2,14},{6,10},... | collective-permute-start | bytes 258056 | tf_op jit(solution)/shard_map/ppermute | solution.py:632
  21.3 2.8 %collective-permute-start.4 = (bf16[208,128]{1,0:T(8,128)(2,1)S(1)}, bf16[208,128]{1,0:T(8,128)(2,1)S(1)}, u32[]{:S(2)}, u32[]{:S(2)}) collective-permute-start(bf16[208,128]{1,0:T(8,128)(2,1)S(1)} %get-tuple-element.59), channel_id=1, source_target_pairs={{0,8},{4,12},{8,0},{12,4},{1,9},{5,13},{9,1},{13,5},{2,10},{6,14},... | collective-permute-start | bytes 159752 | tf_op jit(solution)/shard_map/ppermute | solution.py:632
  24.1 0.1 collective-permute-start.5
  24.2 0.6 %shard_map.196 = (f32[256,128]{1,0:T(8,128)S(1)}, f32[4,256]{1,0:T(4,128)S(1)}) custom-call(s32[1]{0:T(128)S(6)} %copy.22.limit_ref, bf16[128,256]{1,0:T(8,128)(2,1)S(1)} %get-tuple-element.40.q_ref, bf16[576,128]{1,0:T(8,128)(2,1)S(1)} %get-tuple-element.41.rest_0_, bf16[576,128]{1,0:T(8,128)(2,1)S(1)} %collective-permute-done.rest_1_.last_ref, ...), custom_call_target="tpu_custom_call" | custom-call | flops 33554432 | bytes 643076 | tf_op jit(solution)/shard_map/pallas_call | solution.py:194
  24.8 4.0 %collective-permute-done.4.rest_1_ = bf16[208,128]{1,0:T(8,128)(2,1)S(1)} collective-permute-done((bf16[208,128]{1,0:T(8,128)(2,1)S(1)}, bf16[208,128]{1,0:T(8,128)(2,1)S(1)}, u32[]{:S(2)}, u32[]{:S(2)}) %collective-permute-start.4) | collective-permute-done | bytes 53280 | tf_op jit(solution)/shard_map/ppermute | solution.py:632
  28.8 0.7 %shard_map.200 = (bf16[128,512]{1,0:T(8,128)(2,1)S(1)}, bf16[128,256]{1,0:T(8,128)(2,1)S(1)}, bf16[128,512]{1,0:T(8,128)(2,1)S(1)}) custom-call(s32[1]{0:T(128)S(6)} %copy.22.limit_ref, bf16[128,256]{1,0:T(8,128)(2,1)S(1)} %get-tuple-element.40.q_ref, f32[256,128]{1,0:T(8,128)S(1)} %get-tuple-element.44.part_ref, f32[4,256]{1,0:T(4,128)S(1)} %get-tuple-element.45.stats_ref, ...), custom_call_target="tpu_custom_call" | custom-call | flops 100663296 | bytes 9142276 | tf_op jit(solution)/shard_map/pallas_call | solution.py:194
  29.5 0.6 %shard_map.201 = (bf16[160,512]{1,0:T(8,128)(2,1)S(1)}, bf16[32,256]{1,0:T(8,128)(2,1)S(1)}, f32[128,512]{1,0:T(8,128)S(1)}) custom-call(bf16[128,512]{1,0:T(8,128)(2,1)S(1)} %get-tuple-element.61.self_ref, bf16[128,256]{1,0:T(8,128)(2,1)S(1)} %get-tuple-element.62.a2v_ref, bf16[512,4096]{1,0:T(8,128)(2,1)S(1)} %get-tuple-element.55.ws_ref, ...), custom_call_target="tpu_custom_call" | custom-call | flops 201326592 | bytes 10303488 | tf_op jit(solution)/shard_map/pallas_call | solution.py:194
  30.1 0.8 %shard_map.202 = (bf16[288,512]{1,0:T(8,128)(2,1)S(1)}, f32[288,512]{1,0:T(8,128)S(1)}) custom-call(bf16[128,512]{1,0:T(8,128)(2,1)S(1)} %get-tuple-element.61.self_ref, bf16[128,256]{1,0:T(8,128)(2,1)S(1)} %get-tuple-element.62.a2v_ref, bf16[32,256]{1,0:T(8,128)(2,1)S(1)} %get-tuple-element.66.audio_ref, bf16[512,4096]{1,0:T(8,128)(2,1)S(1)} %get-tuple-element.55.ws_ref, ...), custom_call_target="tpu_custom_call" | custom-call | flops 402653184 | bytes 10534912 | tf_op jit(solution)/shard_map/pallas_call | solution.py:194
  30.9 0.5 %collective-permute-start.6 = (bf16[288,512]{1,0:T(8,128)(2,1)S(1)}, bf16[288,512]{1,0:T(8,128)(2,1)S(1)}, u32[]{:S(2)}, u32[]{:S(2)}) collective-permute-start(bf16[288,512]{1,0:T(8,128)(2,1)S(1)} %get-tuple-element.68), channel_id=1, source_target_pairs={{0,1},{1,0},{2,3},{3,2},{4,5},{5,4},{6,7},{7,6},{8,9},{9,8},{10,11... | collective-permute-start | bytes 884744 | tf_op jit(solution)/shard_map/ppermute | solution.py:632
  31.4 0.1 collective-permute-start.7
  31.5 0.3 shard_map.204
  31.8 1.6 %collective-permute-start.10 = (bf16[160,512]{1,0:T(8,128)(2,1)S(1)}, bf16[160,512]{1,0:T(8,128)(2,1)S(1)}, u32[]{:S(2)}, u32[]{:S(2)}) collective-permute-start(bf16[160,512]{1,0:T(8,128)(2,1)S(1)} %shard_map.204), channel_id=1, source_target_pairs={{0,2},{2,0},{1,3},{3,1},{4,6},{6,4},{5,7},{7,5},{8,10},{10,8},{9,1... | collective-permute-start | bytes 491528 | tf_op jit(solution)/shard_map/ppermute | solution.py:632
  33.4 1.0 %collective-permute-start.8 = (bf16[128,512]{1,0:T(8,128)(2,1)S(1)}, bf16[128,512]{1,0:T(8,128)(2,1)S(1)}, u32[]{:S(2)}, u32[]{:S(2)}) collective-permute-start(bf16[128,512]{1,0:T(8,128)(2,1)S(1)} %shard_map.203), channel_id=1, source_target_pairs={{0,2},{2,0},{1,3},{3,1},{4,6},{6,4},{5,7},{7,5},{8,10},{10,8},{9,1... | collective-permute-start | bytes 393224 | tf_op jit(solution)/shard_map/ppermute | solution.py:632
  34.4 6.8 %collective-permute-done.8.low_ref = bf16[128,512]{1,0:T(8,128)(2,1)S(1)} collective-permute-done((bf16[128,512]{1,0:T(8,128)(2,1)S(1)}, bf16[128,512]{1,0:T(8,128)(2,1)S(1)}, u32[]{:S(2)}, u32[]{:S(2)}) %collective-permute-start.8) | collective-permute-done | bytes 131104 | tf_op jit(solution)/shard_map/ppermute | solution.py:632
  41.3 0.8 %shard_map.205 = (bf16[128,1024]{1,0:T(8,128)(2,1)}, bf16[32,512]{1,0:T(8,128)(2,1)}) custom-call(bf16[128,1024]{1,0:T(8,128)(2,1)S(1)} %get-tuple-element.37.video_ref, bf16[32,512]{1,0:T(8,128)(2,1)S(1)} %get-tuple-element.38.audio_ref, f32[32,512]{1,0:T(8,128)S(1)} %get-tuple-element.39.gain_ref, f32[288,512]{1,0:T(8,128)S(1)} %get-tuple-element.67.own_ref, ...), custom_call_target="tpu_custom_call" | custom-call | bytes 1835008 | tf_op jit(solution)/shard_map/pallas_call | solution.py:194
  (11 shorter events, 0.2 us)
Async XLA Ops:
  1.9 14.9 %collective-permute-start.1 = (bf16[576,128]{1,0:T(8,128)(2,1)S(1)}, bf16[576,128]{1,0:T(8,128)(2,1)S(1)}, u32[]{:S(2)}, u32[]{:S(2)}) collective-permute-start(bf16[576,128]{1,0:T(8,128)(2,1)S(1)} %get-tuple-element.43), channel_id=1, source_target_pairs={{0,4},{4,0},{8,12},{12,8},{1,5},{5,1},{9,13},{13,9},{2,6},{6,2},{1... | collective-permute-start | bytes 442376 | tf_op jit(solution)/shard_map/ppermute | solution.py:632
  5.0 13.6 %collective-permute-start = (bf16[576,128]{1,0:T(8,128)(2,1)S(1)}, bf16[576,128]{1,0:T(8,128)(2,1)S(1)}, u32[]{:S(2)}, u32[]{:S(2)}) collective-permute-start(bf16[576,128]{1,0:T(8,128)(2,1)S(1)} %get-tuple-element.42), channel_id=1, source_target_pairs={{0,8},{4,12},{8,0},{12,4},{1,9},{5,13},{9,1},{13,5},{2,10},{6,14},... | collective-permute-start | bytes 442376 | tf_op jit(solution)/shard_map/ppermute | solution.py:632
  8.5 8.3 %collective-permute-start.2 = (bf16[448,128]{1,0:T(8,128)(2,1)S(1)}, bf16[448,128]{1,0:T(8,128)(2,1)S(1)}, u32[]{:S(2)}, u32[]{:S(2)}) collective-permute-start(bf16[448,128]{1,0:T(8,128)(2,1)S(1)} %shard_map.197), channel_id=1, source_target_pairs={{0,12},{4,8},{8,4},{12,0},{1,13},{5,9},{9,5},{13,1},{2,14},{6,10},... | collective-permute-start | bytes 344072 | tf_op jit(solution)/shard_map/ppermute | solution.py:632
  19.4 9.4 %collective-permute-start.3 = (bf16[336,128]{1,0:T(8,128)(2,1)S(1)}, bf16[336,128]{1,0:T(8,128)(2,1)S(1)}, u32[]{:S(2)}, u32[]{:S(2)}) collective-permute-start(bf16[336,128]{1,0:T(8,128)(2,1)S(1)} %get-tuple-element.58), channel_id=1, source_target_pairs={{0,12},{4,8},{8,4},{12,0},{1,13},{5,9},{9,5},{13,1},{2,14},{6,10},... | collective-permute-start | bytes 258056 | tf_op jit(solution)/shard_map/ppermute | solution.py:632
  21.3 7.4 %collective-permute-start.4 = (bf16[208,128]{1,0:T(8,128)(2,1)S(1)}, bf16[208,128]{1,0:T(8,128)(2,1)S(1)}, u32[]{:S(2)}, u32[]{:S(2)}) collective-permute-start(bf16[208,128]{1,0:T(8,128)(2,1)S(1)} %get-tuple-element.59), channel_id=1, source_target_pairs={{0,8},{4,12},{8,0},{12,4},{1,9},{5,13},{9,1},{13,5},{2,10},{6,14},... | collective-permute-start | bytes 159752 | tf_op jit(solution)/shard_map/ppermute | solution.py:632
  24.1 4.7 %collective-permute-start.5 = (bf16[208,128]{1,0:T(8,128)(2,1)S(1)}, bf16[208,128]{1,0:T(8,128)(2,1)S(1)}, u32[]{:S(2)}, u32[]{:S(2)}) collective-permute-start(bf16[208,128]{1,0:T(8,128)(2,1)S(1)} %get-tuple-element.60), channel_id=1, source_target_pairs={{0,4},{4,0},{8,12},{12,8},{1,5},{5,1},{9,13},{13,9},{2,6},{6,2},{1... | collective-permute-start | bytes 159752 | tf_op jit(solution)/shard_map/ppermute | solution.py:632
  30.1 1.5 %collective-permute-start.9 = (bf16[160,512]{1,0:T(8,128)(2,1)S(1)}, bf16[160,512]{1,0:T(8,128)(2,1)S(1)}, u32[]{:S(2)}, u32[]{:S(2)}) collective-permute-start(bf16[160,512]{1,0:T(8,128)(2,1)S(1)} %get-tuple-element.71), channel_id=1, source_target_pairs={{0,1},{1,0},{2,3},{3,2},{4,5},{5,4},{6,7},{7,6},{8,9},{9,8},{10,11... | collective-permute-start | bytes 491528 | tf_op jit(solution)/shard_map/ppermute | solution.py:632
  30.9 10.3 %collective-permute-start.6 = (bf16[288,512]{1,0:T(8,128)(2,1)S(1)}, bf16[288,512]{1,0:T(8,128)(2,1)S(1)}, u32[]{:S(2)}, u32[]{:S(2)}) collective-permute-start(bf16[288,512]{1,0:T(8,128)(2,1)S(1)} %get-tuple-element.68), channel_id=1, source_target_pairs={{0,1},{1,0},{2,3},{3,2},{4,5},{5,4},{6,7},{7,6},{8,9},{9,8},{10,11... | collective-permute-start | bytes 884744 | tf_op jit(solution)/shard_map/ppermute | solution.py:632
  31.4 2.0 %collective-permute-start.7 = (bf16[128,512]{1,0:T(8,128)(2,1)S(1)}, bf16[128,512]{1,0:T(8,128)(2,1)S(1)}, u32[]{:S(2)}, u32[]{:S(2)}) collective-permute-start(bf16[128,512]{1,0:T(8,128)(2,1)S(1)} %get-tuple-element.70), channel_id=1, source_target_pairs={{0,1},{1,0},{2,3},{3,2},{4,5},{5,4},{6,7},{7,6},{8,9},{9,8},{10,11... | collective-permute-start | bytes 393224 | tf_op jit(solution)/shard_map/ppermute | solution.py:632
  31.8 9.4 %collective-permute-start.10 = (bf16[160,512]{1,0:T(8,128)(2,1)S(1)}, bf16[160,512]{1,0:T(8,128)(2,1)S(1)}, u32[]{:S(2)}, u32[]{:S(2)}) collective-permute-start(bf16[160,512]{1,0:T(8,128)(2,1)S(1)} %shard_map.204), channel_id=1, source_target_pairs={{0,2},{2,0},{1,3},{3,1},{4,6},{6,4},{5,7},{7,5},{8,10},{10,8},{9,1... | collective-permute-start | bytes 491528 | tf_op jit(solution)/shard_map/ppermute | solution.py:632
  33.4 7.8 %collective-permute-start.8 = (bf16[128,512]{1,0:T(8,128)(2,1)S(1)}, bf16[128,512]{1,0:T(8,128)(2,1)S(1)}, u32[]{:S(2)}, u32[]{:S(2)}) collective-permute-start(bf16[128,512]{1,0:T(8,128)(2,1)S(1)} %shard_map.203), channel_id=1, source_target_pairs={{0,2},{2,0},{1,3},{3,1},{4,6},{6,4},{5,7},{7,5},{8,10},{10,8},{9,1... | collective-permute-start | bytes 393224 | tf_op jit(solution)/shard_map/ppermute | solution.py:632

commit v10 on v9

--- a/solution.py
+++ b/solution.py
@@ -361,6 +361,16 @@
     for block in range(cols // 128):
         cut = slice(block * 128, (block + 1) * 128)
         vvt_ref[cut, :] = turn(vv_ref[:, cut])
+    tops = []
+    for block in range(cols // 128):
+        ends = [1 if hop == FORWARDED else 3 for hop in early]
+        q = [audio_block(ref, end, rows_audio, cols, block) for ref, end in zip(blocks, ends)]
+        q = jnp.concatenate(q + [q[0]] * (128 // rows_audio - count), axis=0)
+        scores = dot_t(kv_ref[:, block * 128 : (block + 1) * 128], pair_rows(q, head))
+        for i in range(128 // head):
+            row = (count * count + block * (128 // head) + i) * rows
+            s_ref[row : row + rows, :] = scores[:, i * 128 : (i + 1) * 128]
+        tops.append(jnp.max(scores, axis=0, keepdims=True))
     scale = 1.0 / math.sqrt(DHV)
     peaks = []
     for j, ref in enumerate(blocks):
@@ -381,14 +391,28 @@
         part_ref[j * DHV : (j + 1) * DHV, :] = dot(vt_ref[...], jnp.concatenate(p, axis=0))
         stats_ref[2 * j : 2 * j + 1, :] = peak
         stats_ref[2 * j + 1 : 2 * j + 2, :] = total
-    for j, (hop, ref) in enumerate(zip(early, blocks)):
-        outs, lse = audio_parts(ref, 1 if hop == FORWARDED else 3, kv_ref, vvt_ref, rows_audio, head)
-        if j > 0:
-            store_tail(tails[j - 1], 0, outs, lse)
-            continue
-        own_lse_ref[...] = lse
-        for block, o in enumerate(outs):
-            own_v2a_ref[:, block * 128 : (block + 1) * 128] = o
+    pair, scale = 128 // head, 1.0 / math.sqrt(head)
+    outs, lses = [], []
+    for block in range(cols // 128):
+        cut = slice(block * 128, (block + 1) * 128)
+        peak = tops[block]
+        both = []
+        for i in range(pair):
+            at = slice(i * 128, (i + 1) * 128)
+            row = (count * count + block * pair + i) * rows
+            p = jnp.exp2((s_ref[row : row + rows, :] - peak[:, at]) * (scale * LOG2E))
+            total = jnp.sum(p, axis=0, keepdims=True)
+            lses.append(peak[:, at] * (scale * LOG2E) + jnp.log2(total))
+            column = block * 128 + i * head
+            both.append(dot(vvt_ref[column : column + head, :], p.astype(BF16)) * (1.0 / total))
+        outs.append(jnp.concatenate(both, axis=0).T)
+    lse = jnp.concatenate(lses, axis=0)
+    own_lse_ref[...] = lse
+    for block, o in enumerate(outs):
+        own_v2a_ref[:, block * 128 : (block + 1) * 128] = o[0:rows_audio]
+    for j in range(1, count):
+        mine = [o[j * rows_audio : (j + 1) * rows_audio] for o in outs]
+        store_tail(tails[j - 1], 0, mine, pltpu.roll(lse, 128 - j * rows_audio, 1))
 
 
 def late_kernel(early, hops, rows_audio, head, kv_ref, vvt_ref, part_ref, stats_ref, vt_ref, last_ref, *rest):
@@ -677,7 +701,7 @@
         + [shape(tail, width)] * (count - 1),
         (k_own, v_own, *(blocks[hop] for hop in early)),
         flops=4 * count * count * rows * rows * width,
-        scratch=[pltpu.VMEM((count * count * rows, rows), F32)],
+        scratch=[pltpu.VMEM(((count * count + cross // DHC) * rows, rows), F32)],
     )
     own, *sends = call(
         functools.partial(late_kernel, early, hops, rows_audio, DHC),

time: 42.4 us -> 41.4 us (0.976)
  Pallas kernels: 11.9 us -> 10.7 us
  waiting for transfers between devices: 13.9 us -> 14.4 us
    pallas_call x12, Pallas kernels: 11.9 us -> 10.7 us  [call(): pl.pallas_call(kernel, out_shape=tuple(outs), in_specs=specs or [VMEM] *...]
    ppermute x11, waiting for transfers between devices: 13.9 us -> 14.4 us  [trade(): return lax.ppermute(x, axis, [(i, i ^ hop) for i in range(size)])]
  transfers between devices with their start and end apart: 11 -> 11, of which waited for: 3 -> 4; matrix products, arithmetic and copies ran while one was open for 3% -> 3% of each run, Pallas kernels for 18% -> 16%
where the time goes in v10:
time: 41.4 us; the launch traced here: 41.1 us
  waiting for transfers between devices  14.4 us (35%)
  starting transfers between devices  13.5 us (33%)
  Pallas kernels  10.7 us (26%)
  between operations  1.38 us (3%)
  local copies, waits for them, and re-layouts  1.1 us (3%)
    ppermute x11, waiting for transfers between devices, trade(): return lax.ppermute(x, axis, [(i, i ^ hop) for i in range(size)])  14.4 us
    ppermute x11, starting transfers between devices, trade(): return lax.ppermute(x, axis, [(i, i ^ hop) for i in range(size)])  13.5 us
    pallas_call x12, Pallas kernels, call(): pl.pallas_call(kernel, out_shape=tuple(outs), in_specs=specs or [VMEM] *...  10.7 us
    unnamed x1, local copies, waits for them, and re-layouts  1.1 us
  transfers between devices with their start and end apart: 11, of which 4 were waited for; matrix products, arithmetic and copies ran while one was open for 3% of the time, Pallas kernels for 16%

profile of v10, /device:TPU:0, one launch (start us, length us, event | category | flops | bytes accessed | tf_op | source)
XLA Modules:
  0.0 41.1 jit_solution(12936461340327983881)
XLA Ops:
  0.6 1.3 %shard_map.195 = (bf16[576,128]{1,0:T(8,128)(2,1)S(1)}, bf16[576,128]{1,0:T(8,128)(2,1)S(1)}, bf16[576,128]{1,0:T(8,128)(2,1)S(1)}) custom-call(bf16[128,512]{1,0:T(8,128)(2,1)} %q_ref.3, bf16[128,512]{1,0:T(8,128)(2,1)} %k_ref.3, bf16[128,512]{1,0:T(8,128)(2,1)} %v_ref.3, bf16[32,256]{1,0:T(8,128)(2,1)} %qa_ref.3, bf16[32,256]{1,0:T(8,128)(2,1)} %ka_ref.3, ...), custom_call_target="tpu_custom_call" | custom-call | bytes 884736 | tf_op jit(solution)/shard_map/pallas_call | solution.py:194
  1.9 3.1 %collective-permute-start.1 = (bf16[576,128]{1,0:T(8,128)(2,1)S(1)}, bf16[576,128]{1,0:T(8,128)(2,1)S(1)}, u32[]{:S(2)}, u32[]{:S(2)}) collective-permute-start(bf16[576,128]{1,0:T(8,128)(2,1)S(1)} %get-tuple-element.43), channel_id=1, source_target_pairs={{0,4},{4,0},{8,12},{12,8},{1,5},{5,1},{9,13},{13,9},{2,6},{6,2},{1... | collective-permute-start | bytes 442376 | tf_op jit(solution)/shard_map/ppermute | solution.py:656
  5.0 2.6 %collective-permute-start = (bf16[576,128]{1,0:T(8,128)(2,1)S(1)}, bf16[576,128]{1,0:T(8,128)(2,1)S(1)}, u32[]{:S(2)}, u32[]{:S(2)}) collective-permute-start(bf16[576,128]{1,0:T(8,128)(2,1)S(1)} %get-tuple-element.42), channel_id=1, source_target_pairs={{0,8},{4,12},{8,0},{12,4},{1,9},{5,13},{9,1},{13,5},{2,10},{6,14},... | collective-permute-start | bytes 442376 | tf_op jit(solution)/shard_map/ppermute | solution.py:656
  7.6 0.8 %shard_map.197 = bf16[448,128]{1,0:T(8,128)(2,1)S(1)} custom-call(bf16[128,512]{1,0:T(8,128)(2,1)} %q_ref.3, bf16[128,512]{1,0:T(8,128)(2,1)} %k_ref.3, bf16[128,512]{1,0:T(8,128)(2,1)} %v_ref.3, bf16[32,256]{1,0:T(8,128)(2,1)} %qa_ref.3, bf16[32,256]{1,0:T(8,128)(2,1)} %ka_ref.3, bf16[32,256]{1,0:T(8,128)(2,1)} %va_ref.3), custom_call_target="tpu_custom_call" | custom-call | bytes 557056 | tf_op jit(solution)/shard_map/pallas_call | solution.py:194
  9.2 1.1 %copy.21 = bf16[2,8,2,4096]{3,1,2,0:T(8,128)(2,1)S(1)} copy(bf16[2,8,2,4096]{3,2,1,0:T(2,128)(2,1)} %bitcast.5) | data formatting | bytes 524288
  10.3 3.4 %shard_map.194 = (bf16[128,8192]{1,0:T(8,128)(2,1)S(1)}, f32[32,512]{1,0:T(8,128)S(1)}, bf16[128,256]{1,0:T(8,128)(2,1)S(1)}, bf16[128,256]{1,0:T(8,128)(2,1)S(1...) custom-call(s32[1]{0:T(128)S(6)} %copy.22.limit_ref, ...), custom_call_target="tpu_custom_call" | custom-call | bytes 18154116 | tf_op jit(solution)/shard_map/pallas_call | solution.py:194
  13.7 3.1 %collective-permute-done.2.rest_1_ = bf16[448,128]{1,0:T(8,128)(2,1)S(1)} collective-permute-done((bf16[448,128]{1,0:T(8,128)(2,1)S(1)}, bf16[448,128]{1,0:T(8,128)(2,1)S(1)}, u32[]{:S(2)}, u32[]{:S(2)}) %collective-permute-start.2) | collective-permute-done | bytes 114720 | tf_op jit(solution)/shard_map/ppermute | solution.py:656
  16.8 0.7 %shard_map.198 = (f32[384,128]{1,0:T(8,128)S(1)}, f32[6,128]{1,0:T(8,128)S(1)}, bf16[128,384]{1,0:T(8,128)(2,1)S(1)}, bf16[256,128]{1,0:T(8,128)(2,1)S(1)}, f32[...) custom-call(bf16[128,256]{1,0:T(8,128)(2,1)S(1)} %get-tuple-element.46.kv_r, ...), custom_call_target="tpu_custom_call" | custom-call | flops 75497472 | bytes 979968 | tf_op jit(solution)/shard_map/pallas_call | solution.py:194
  17.5 0.5 %collective-permute-done.rest_1_.last_ref = bf16[576,128]{1,0:T(8,128)(2,1)S(1)} collective-permute-done((bf16[576,128]{1,0:T(8,128)(2,1)S(1)}, bf16[576,128]{1,0:T(8,128)(2,1)S(1)}, u32[]{:S(2)}, u32[]{:S(2)}) %collective-permute-start) | collective-permute-done | bytes 147488 | tf_op jit(solution)/shard_map/ppermute | solution.py:656
  18.1 0.7 %shard_map.199 = (bf16[128,128]{1,0:T(8,128)(2,1)S(1)}, bf16[336,128]{1,0:T(8,128)(2,1)S(1)}, bf16[208,128]{1,0:T(8,128)(2,1)S(1)}, bf16[208,128]{1,0:T(8,128)(2,1)S(1)}) custom-call(bf16[128,256]{1,0:T(8,128)(2,1)S(1)} %get-tuple-element.46.kv_ref, bf16[256,128]{1,0:T(8,128)(2,1)S(1)} %get-tuple-element.48.vvt_ref, ...), custom_call_target="tpu_custom_call" | custom-call | flops 58720256 | bytes 1252352 | tf_op jit(solution)/shard_map/pallas_call | solution.py:194
  18.8 2.5 %collective-permute-start.3 = (bf16[336,128]{1,0:T(8,128)(2,1)S(1)}, bf16[336,128]{1,0:T(8,128)(2,1)S(1)}, u32[]{:S(2)}, u32[]{:S(2)}) collective-permute-start(bf16[336,128]{1,0:T(8,128)(2,1)S(1)} %get-tuple-element.58), channel_id=1, source_target_pairs={{0,12},{4,8},{8,4},{12,0},{1,13},{5,9},{9,5},{13,1},{2,14},{6,10},... | collective-permute-start | bytes 258056 | tf_op jit(solution)/shard_map/ppermute | solution.py:656
  21.3 1.6 %collective-permute-start.4 = (bf16[208,128]{1,0:T(8,128)(2,1)S(1)}, bf16[208,128]{1,0:T(8,128)(2,1)S(1)}, u32[]{:S(2)}, u32[]{:S(2)}) collective-permute-start(bf16[208,128]{1,0:T(8,128)(2,1)S(1)} %get-tuple-element.59), channel_id=1, source_target_pairs={{0,8},{4,12},{8,0},{12,4},{1,9},{5,13},{9,1},{13,5},{2,10},{6,14},... | collective-permute-start | bytes 159752 | tf_op jit(solution)/shard_map/ppermute | solution.py:656
  22.9 0.3 collective-permute-start.5
  23.3 0.6 %shard_map.196 = (f32[256,128]{1,0:T(8,128)S(1)}, f32[4,256]{1,0:T(4,128)S(1)}) custom-call(s32[1]{0:T(128)S(6)} %copy.22.limit_ref, bf16[128,256]{1,0:T(8,128)(2,1)S(1)} %get-tuple-element.40.q_ref, bf16[576,128]{1,0:T(8,128)(2,1)S(1)} %get-tuple-element.41.rest_0_, bf16[576,128]{1,0:T(8,128)(2,1)S(1)} %collective-permute-done.rest_1_.last_ref, ...), custom_call_target="tpu_custom_call" | custom-call | flops 33554432 | bytes 643076 | tf_op jit(solution)/shard_map/pallas_call | solution.py:194
  23.9 3.9 %collective-permute-done.4.rest_1_ = bf16[208,128]{1,0:T(8,128)(2,1)S(1)} collective-permute-done((bf16[208,128]{1,0:T(8,128)(2,1)S(1)}, bf16[208,128]{1,0:T(8,128)(2,1)S(1)}, u32[]{:S(2)}, u32[]{:S(2)}) %collective-permute-start.4) | collective-permute-done | bytes 53280 | tf_op jit(solution)/shard_map/ppermute | solution.py:656
  27.8 0.7 %shard_map.200 = (bf16[128,512]{1,0:T(8,128)(2,1)S(1)}, bf16[128,256]{1,0:T(8,128)(2,1)S(1)}, bf16[128,512]{1,0:T(8,128)(2,1)S(1)}) custom-call(s32[1]{0:T(128)S(6)} %copy.22.limit_ref, bf16[128,256]{1,0:T(8,128)(2,1)S(1)} %get-tuple-element.40.q_ref, f32[256,128]{1,0:T(8,128)S(1)} %get-tuple-element.44.part_ref, f32[4,256]{1,0:T(4,128)S(1)} %get-tuple-element.45.stats_ref, ...), custom_call_target="tpu_custom_call" | custom-call | flops 100663296 | bytes 9142276 | tf_op jit(solution)/shard_map/pallas_call | solution.py:194
  28.5 0.6 %shard_map.201 = (bf16[160,512]{1,0:T(8,128)(2,1)S(1)}, bf16[32,256]{1,0:T(8,128)(2,1)S(1)}, f32[128,512]{1,0:T(8,128)S(1)}) custom-call(bf16[128,512]{1,0:T(8,128)(2,1)S(1)} %get-tuple-element.61.self_ref, bf16[128,256]{1,0:T(8,128)(2,1)S(1)} %get-tuple-element.62.a2v_ref, bf16[512,4096]{1,0:T(8,128)(2,1)S(1)} %get-tuple-element.55.ws_ref, ...), custom_call_target="tpu_custom_call" | custom-call | flops 201326592 | bytes 10303488 | tf_op jit(solution)/shard_map/pallas_call | solution.py:194
  29.2 0.8 %shard_map.202 = (bf16[288,512]{1,0:T(8,128)(2,1)S(1)}, f32[288,512]{1,0:T(8,128)S(1)}) custom-call(bf16[128,512]{1,0:T(8,128)(2,1)S(1)} %get-tuple-element.61.self_ref, bf16[128,256]{1,0:T(8,128)(2,1)S(1)} %get-tuple-element.62.a2v_ref, bf16[32,256]{1,0:T(8,128)(2,1)S(1)} %get-tuple-element.66.audio_ref, bf16[512,4096]{1,0:T(8,128)(2,1)S(1)} %get-tuple-element.55.ws_ref, ...), custom_call_target="tpu_custom_call" | custom-call | flops 402653184 | bytes 10534912 | tf_op jit(solution)/shard_map/pallas_call | solution.py:194
  29.9 0.5 %collective-permute-start.6 = (bf16[288,512]{1,0:T(8,128)(2,1)S(1)}, bf16[288,512]{1,0:T(8,128)(2,1)S(1)}, u32[]{:S(2)}, u32[]{:S(2)}) collective-permute-start(bf16[288,512]{1,0:T(8,128)(2,1)S(1)} %get-tuple-element.68), channel_id=1, source_target_pairs={{0,1},{1,0},{2,3},{3,2},{4,5},{5,4},{6,7},{7,6},{8,9},{9,8},{10,11... | collective-permute-start | bytes 884744 | tf_op jit(solution)/shard_map/ppermute | solution.py:656
  30.5 0.3 shard_map.204
  30.9 1.6 %collective-permute-start.10 = (bf16[160,512]{1,0:T(8,128)(2,1)S(1)}, bf16[160,512]{1,0:T(8,128)(2,1)S(1)}, u32[]{:S(2)}, u32[]{:S(2)}) collective-permute-start(bf16[160,512]{1,0:T(8,128)(2,1)S(1)} %shard_map.204), channel_id=1, source_target_pairs={{0,2},{2,0},{1,3},{3,1},{4,6},{6,4},{5,7},{7,5},{8,10},{10,8},{9,1... | collective-permute-start | bytes 491528 | tf_op jit(solution)/shard_map/ppermute | solution.py:656
  32.5 1.0 %collective-permute-start.8 = (bf16[128,512]{1,0:T(8,128)(2,1)S(1)}, bf16[128,512]{1,0:T(8,128)(2,1)S(1)}, u32[]{:S(2)}, u32[]{:S(2)}) collective-permute-start(bf16[128,512]{1,0:T(8,128)(2,1)S(1)} %shard_map.203), channel_id=1, source_target_pairs={{0,2},{2,0},{1,3},{3,1},{4,6},{6,4},{5,7},{7,5},{8,10},{10,8},{9,1... | collective-permute-start | bytes 393224 | tf_op jit(solution)/shard_map/ppermute | solution.py:656
  33.5 6.8 %collective-permute-done.8.low_ref = bf16[128,512]{1,0:T(8,128)(2,1)S(1)} collective-permute-done((bf16[128,512]{1,0:T(8,128)(2,1)S(1)}, bf16[128,512]{1,0:T(8,128)(2,1)S(1)}, u32[]{:S(2)}, u32[]{:S(2)}) %collective-permute-start.8) | collective-permute-done | bytes 131104 | tf_op jit(solution)/shard_map/ppermute | solution.py:656
  40.3 0.8 %shard_map.205 = (bf16[128,1024]{1,0:T(8,128)(2,1)}, bf16[32,512]{1,0:T(8,128)(2,1)}) custom-call(bf16[128,1024]{1,0:T(8,128)(2,1)S(1)} %get-tuple-element.37.video_ref, bf16[32,512]{1,0:T(8,128)(2,1)S(1)} %get-tuple-element.38.audio_ref, f32[32,512]{1,0:T(8,128)S(1)} %get-tuple-element.39.gain_ref, f32[288,512]{1,0:T(8,128)S(1)} %get-tuple-element.67.own_ref, ...), custom_call_target="tpu_custom_call" | custom-call | bytes 1835008 | tf_op jit(solution)/shard_map/pallas_call | solution.py:194
  (11 shorter events, 0.3 us)
Async XLA Ops:
  1.9 14.9 %collective-permute-start.1 = (bf16[576,128]{1,0:T(8,128)(2,1)S(1)}, bf16[576,128]{1,0:T(8,128)(2,1)S(1)}, u32[]{:S(2)}, u32[]{:S(2)}) collective-permute-start(bf16[576,128]{1,0:T(8,128)(2,1)S(1)} %get-tuple-element.43), channel_id=1, source_target_pairs={{0,4},{4,0},{8,12},{12,8},{1,5},{5,1},{9,13},{13,9},{2,6},{6,2},{1... | collective-permute-start | bytes 442376 | tf_op jit(solution)/shard_map/ppermute | solution.py:656
  5.0 13.0 %collective-permute-start = (bf16[576,128]{1,0:T(8,128)(2,1)S(1)}, bf16[576,128]{1,0:T(8,128)(2,1)S(1)}, u32[]{:S(2)}, u32[]{:S(2)}) collective-permute-start(bf16[576,128]{1,0:T(8,128)(2,1)S(1)} %get-tuple-element.42), channel_id=1, source_target_pairs={{0,8},{4,12},{8,0},{12,4},{1,9},{5,13},{9,1},{13,5},{2,10},{6,14},... | collective-permute-start | bytes 442376 | tf_op jit(solution)/shard_map/ppermute | solution.py:656
  8.5 8.3 %collective-permute-start.2 = (bf16[448,128]{1,0:T(8,128)(2,1)S(1)}, bf16[448,128]{1,0:T(8,128)(2,1)S(1)}, u32[]{:S(2)}, u32[]{:S(2)}) collective-permute-start(bf16[448,128]{1,0:T(8,128)(2,1)S(1)} %shard_map.197), channel_id=1, source_target_pairs={{0,12},{4,8},{8,4},{12,0},{1,13},{5,9},{9,5},{13,1},{2,14},{6,10},... | collective-permute-start | bytes 344072 | tf_op jit(solution)/shard_map/ppermute | solution.py:656
  18.8 9.0 %collective-permute-start.3 = (bf16[336,128]{1,0:T(8,128)(2,1)S(1)}, bf16[336,128]{1,0:T(8,128)(2,1)S(1)}, u32[]{:S(2)}, u32[]{:S(2)}) collective-permute-start(bf16[336,128]{1,0:T(8,128)(2,1)S(1)} %get-tuple-element.58), channel_id=1, source_target_pairs={{0,12},{4,8},{8,4},{12,0},{1,13},{5,9},{9,5},{13,1},{2,14},{6,10},... | collective-permute-start | bytes 258056 | tf_op jit(solution)/shard_map/ppermute | solution.py:656
  21.3 6.5 %collective-permute-start.4 = (bf16[208,128]{1,0:T(8,128)(2,1)S(1)}, bf16[208,128]{1,0:T(8,128)(2,1)S(1)}, u32[]{:S(2)}, u32[]{:S(2)}) collective-permute-start(bf16[208,128]{1,0:T(8,128)(2,1)S(1)} %get-tuple-element.59), channel_id=1, source_target_pairs={{0,8},{4,12},{8,0},{12,4},{1,9},{5,13},{9,1},{13,5},{2,10},{6,14},... | collective-permute-start | bytes 159752 | tf_op jit(solution)/shard_map/ppermute | solution.py:656
  22.9 4.9 %collective-permute-start.5 = (bf16[208,128]{1,0:T(8,128)(2,1)S(1)}, bf16[208,128]{1,0:T(8,128)(2,1)S(1)}, u32[]{:S(2)}, u32[]{:S(2)}) collective-permute-start(bf16[208,128]{1,0:T(8,128)(2,1)S(1)} %get-tuple-element.60), channel_id=1, source_target_pairs={{0,4},{4,0},{8,12},{12,8},{1,5},{5,1},{9,13},{13,9},{2,6},{6,2},{1... | collective-permute-start | bytes 159752 | tf_op jit(solution)/shard_map/ppermute | solution.py:656
  29.1 1.5 %collective-permute-start.9 = (bf16[160,512]{1,0:T(8,128)(2,1)S(1)}, bf16[160,512]{1,0:T(8,128)(2,1)S(1)}, u32[]{:S(2)}, u32[]{:S(2)}) collective-permute-start(bf16[160,512]{1,0:T(8,128)(2,1)S(1)} %get-tuple-element.71), channel_id=1, source_target_pairs={{0,1},{1,0},{2,3},{3,2},{4,5},{5,4},{6,7},{7,6},{8,9},{9,8},{10,11... | collective-permute-start | bytes 491528 | tf_op jit(solution)/shard_map/ppermute | solution.py:656
  29.9 10.3 %collective-permute-start.6 = (bf16[288,512]{1,0:T(8,128)(2,1)S(1)}, bf16[288,512]{1,0:T(8,128)(2,1)S(1)}, u32[]{:S(2)}, u32[]{:S(2)}) collective-permute-start(bf16[288,512]{1,0:T(8,128)(2,1)S(1)} %get-tuple-element.68), channel_id=1, source_target_pairs={{0,1},{1,0},{2,3},{3,2},{4,5},{5,4},{6,7},{7,6},{8,9},{9,8},{10,11... | collective-permute-start | bytes 884744 | tf_op jit(solution)/shard_map/ppermute | solution.py:656
  30.5 2.0 %collective-permute-start.7 = (bf16[128,512]{1,0:T(8,128)(2,1)S(1)}, bf16[128,512]{1,0:T(8,128)(2,1)S(1)}, u32[]{:S(2)}, u32[]{:S(2)}) collective-permute-start(bf16[128,512]{1,0:T(8,128)(2,1)S(1)} %get-tuple-element.70), channel_id=1, source_target_pairs={{0,1},{1,0},{2,3},{3,2},{4,5},{5,4},{6,7},{7,6},{8,9},{9,8},{10,11... | collective-permute-start | bytes 393224 | tf_op jit(solution)/shard_map/ppermute | solution.py:656
  30.9 9.4 %collective-permute-start.10 = (bf16[160,512]{1,0:T(8,128)(2,1)S(1)}, bf16[160,512]{1,0:T(8,128)(2,1)S(1)}, u32[]{:S(2)}, u32[]{:S(2)}) collective-permute-start(bf16[160,512]{1,0:T(8,128)(2,1)S(1)} %shard_map.204), channel_id=1, source_target_pairs={{0,2},{2,0},{1,3},{3,1},{4,6},{6,4},{5,7},{7,5},{8,10},{10,8},{9,1... | collective-permute-start | bytes 491528 | tf_op jit(solution)/shard_map/ppermute | solution.py:656
  32.5 7.8 %collective-permute-start.8 = (bf16[128,512]{1,0:T(8,128)(2,1)S(1)}, bf16[128,512]{1,0:T(8,128)(2,1)S(1)}, u32[]{:S(2)}, u32[]{:S(2)}) collective-permute-start(bf16[128,512]{1,0:T(8,128)(2,1)S(1)} %shard_map.203), channel_id=1, source_target_pairs={{0,2},{2,0},{1,3},{3,1},{4,6},{6,4},{5,7},{7,5},{8,10},{10,8},{9,1... | collective-permute-start | bytes 393224 | tf_op jit(solution)/shard_map/ppermute | solution.py:656

commit v11 on v10

--- a/solution.py
+++ b/solution.py
@@ -180,7 +180,7 @@
 SMEM = pl.BlockSpec(memory_space=pltpu.SMEM)
 HBM = pl.BlockSpec(memory_space=pltpu.HBM)
 BF16, F32 = jnp.bfloat16, jnp.float32
-LSE_ROWS = 16
+LSE_ROWS, PARTS = 16, 4
 LEAST = float(jnp.finfo(jnp.float32).min)
 SEQ, FORWARDED, OUT_ORDER, LAST = 4, 3, [3, 2, 1], 2
 
@@ -457,9 +457,10 @@
     store_tail(by_hop[last], rows, *audio)
     for hop, tail in zip(early[1:], tails):
         by_hop[hop][rows : rows + tail.shape[0], :] = tail[...]
-    dst = by_hop[FORWARDED]
     top = rows + tails[0].shape[0]
-    dst[top:, :] = blocks[0][blocks[0].shape[0] - (dst.shape[0] - top) :, :]
+    extra = by_hop[FORWARDED].shape[0] - top
+    by_hop[FORWARDED][top:, :] = blocks[0][blocks[0].shape[0] - extra :, :]
+    by_hop[1][top:, :] = last_ref[last_ref.shape[0] - 2 * extra : last_ref.shape[0] - extra, :]
 
 
 def audio_allowed(hop, rows_audio, limit):
@@ -490,20 +491,20 @@
         stats_ref[2 * block + 1 : 2 * block + 2, :] = total
 
 
-def finish_audio(head, limit, q_ref, part_ref, stats_ref, last_ref, rows_audio, out_ref):
+def finish_audio(head, limit, q_ref, part_ref, stats_ref, keys_ref, values_ref, rows_audio, out_ref):
     cols = q_ref.shape[1]
     scale = 1.0 / math.sqrt(head)
     allowed = audio_allowed(FORWARDED, rows_audio, limit)
     for block in range(cols // 128):
         cut = slice(block * 128, (block + 1) * 128)
         q = pair_rows(q_ref[:, cut], head)
-        scores = jnp.where(allowed, dot_t(audio_block(last_ref, 2, rows_audio, cols, block), q), LEAST)
+        scores = jnp.where(allowed, dot_t(audio_block(keys_ref, 1, rows_audio, cols, block), q), LEAST)
         before, summed = stats_ref[2 * block : 2 * block + 1, :], stats_ref[2 * block + 1 : 2 * block + 2, :]
         peak = jnp.maximum(before, jnp.max(scores, axis=0, keepdims=True))
         factor = jnp.exp2((before - peak) * (scale * LOG2E))
         p = jnp.exp2((scores - peak) * (scale * LOG2E))
         inverse = 1.0 / (summed * factor + jnp.sum(p, axis=0, keepdims=True))
-        vt = turn(audio_block(last_ref, 1, rows_audio, cols, block))
+        vt = turn(audio_block(values_ref, 1, rows_audio, cols, block))
         last = pair_columns(dot(vt, p.astype(BF16)), head)
         both = part_ref[cut, :] * spread(factor, head) + last
         out_ref[:, cut] = (both * spread(inverse, head)).T.astype(BF16)
@@ -545,83 +546,92 @@
     return (1 - mp if far else mp) * 2 + (1 - sub if other else sub)
 
 
-def project_self(block, half, att_ref, ws_ref, gain_ref):
-    cut = ws_ref.shape[1] // 8
-    at = columns(block * 2 + half, cut)
+def project_self(block, part, att_ref, ws_ref, gain_ref):
+    cut = ws_ref.shape[1] // (4 * PARTS)
+    at = columns(block * PARTS + part, cut)
     return gain_ref[:, at].astype(F32) * dot(att_ref[...], ws_ref[:, at])
 
 
-def project_a2v(block, half, a2v_ref, wa_ref, gain_ref):
-    cut = wa_ref.shape[1] // 8
-    gain = gain_ref[:, columns(block * 2 + half + 8, cut)].astype(F32)
-    return gain * dot(a2v_ref[...], wa_ref[:, columns(block * 2 + half, cut)])
-
-
-def project(block, half, heads, weights, gain_ref):
-    term = project_self(block, half, heads[0], weights[0], gain_ref)
-    return term + project_a2v(block, half, heads[1], weights[1], gain_ref)
+def project_a2v(block, part, a2v_ref, wa_ref, gain_ref):
+    cut = wa_ref.shape[1] // (4 * PARTS)
+    gain = gain_ref[:, columns((block + 4) * PARTS + part, cut)].astype(F32)
+    return gain * dot(a2v_ref[...], wa_ref[:, columns(block * PARTS + part, cut)])
 
 
 def project_audio(block, v2a_ref, wv_ref):
     return dot(v2a_ref[...], wv_ref[:, columns(block, wv_ref.shape[1] // 4)])
+
+
+def project(block, parts, heads, weights, out, extra=None):
+    (self_ref, a2v_ref, audio_ref), (ws_ref, wa_ref, wv_ref, gain_ref) = heads, weights
+    rows, cut = self_ref.shape[0], out.shape[1]
+
+    def store(at, term):
+        if extra is not None:
+            term = term + extra[at : at + term.shape[0], :].astype(F32)
+        out[at : at + term.shape[0], :] = term.astype(out.dtype)
+
+    for i, part in enumerate(parts):
+        term = project_self(block, part, self_ref, ws_ref, gain_ref)
+        store(i * rows, term + project_a2v(block, part, a2v_ref, wa_ref, gain_ref))
+    term, rows_audio = project_audio(block, audio_ref, wv_ref), audio_ref.shape[0]
+    for i in range(term.shape[1] // cut):
+        store(len(parts) * rows + i * rows_audio, term[:, i * cut : (i + 1) * cut])
 
 
 def first_kernel(hops, rows_audio, head, limit_ref, q_ref, part_ref, stats_ref, own_ref, ws_ref, wa_ref, gain_ref, *rest):
     got, (self_ref, a2v_ref, out_ref, term_ref) = rest[: len(hops) - 1], rest[len(hops) - 1 :]
     rows, width = own_ref.shape
-    last_ref = got[hops.index(FORWARDED) - 1]
+    keys_ref, values_ref = got[hops.index(1) - 1], got[hops.index(FORWARDED) - 1]
     self_ref[:, columns(index_of("seq"), width)] = own_ref[...]
     for hop, ref in zip(hops[1:], got):
         self_ref[:, columns(index_of("seq") ^ hop, width)] = ref[0:rows, :]
     block = block_of(True, True)
     term_ref[...] = project_self(block, 0, self_ref, ws_ref, gain_ref)
-    finish_audio(head, limit_ref[0], q_ref, part_ref, stats_ref, last_ref, rows_audio, a2v_ref)
+    finish_audio(head, limit_ref[0], q_ref, part_ref, stats_ref, keys_ref, values_ref, rows_audio, a2v_ref)
     out_ref[...] = (term_ref[...] + project_a2v(block, 0, a2v_ref, wa_ref, gain_ref)).astype(BF16)
 
 
 def second_kernel(head, self_ref, a2v_ref, ws_ref, wa_ref, wv_ref, gain_ref, v2a_ref, lse_ref, *rest):
     got, (out_ref, audio_ref, low_ref) = rest[:-3], rest[-3:]
-    rows = self_ref.shape[0]
-    block = block_of(True, True)
-    out_ref[0:rows, :] = project(block, 1, (self_ref, a2v_ref), (ws_ref, wa_ref), gain_ref).astype(BF16)
-    merge_audio(head, rows, v2a_ref, lse_ref, got, audio_ref)
-    out_ref[rows:, :] = project_audio(block, audio_ref, wv_ref).astype(BF16)
-    low_ref[...] = project(block_of(True, False), 0, (self_ref, a2v_ref), (ws_ref, wa_ref), gain_ref)
+    merge_audio(head, self_ref.shape[0], v2a_ref, lse_ref, got, audio_ref)
+    heads, weights = (self_ref, a2v_ref, audio_ref), (ws_ref, wa_ref, wv_ref, gain_ref)
+    project(block_of(True, True), range(1, PARTS), heads, weights, out_ref)
+    block = block_of(True, False)
+    term = project_self(block, 0, self_ref, ws_ref, gain_ref)
+    low_ref[...] = term + project_a2v(block, 0, a2v_ref, wa_ref, gain_ref)
 
 
 def far_low_kernel(low_ref, extra_ref, out_ref):
     out_ref[...] = (low_ref[...] + extra_ref[...].astype(F32)).astype(BF16)
 
 
-def near_kernel(self_ref, a2v_ref, audio_ref, ws_ref, wa_ref, wv_ref, gain_ref, send_ref, own_ref):
-    rows = self_ref.shape[0]
-    for out, other in ((send_ref, True), (own_ref, False)):
-        block = block_of(False, other)
-        for half in range(2):
-            term = project(block, half, (self_ref, a2v_ref), (ws_ref, wa_ref), gain_ref)
-            out[half * rows : (half + 1) * rows, :] = term.astype(out.dtype)
-        out[2 * rows :, :] = project_audio(block, audio_ref, wv_ref).astype(out.dtype)
-
-
-def far_high_kernel(self_ref, a2v_ref, ws_ref, wa_ref, gain_ref, extra_ref, audio_ref, wv_ref, out_ref):
-    rows = self_ref.shape[0]
-    block = block_of(True, False)
-    term = project(block, 1, (self_ref, a2v_ref), (ws_ref, wa_ref), gain_ref)
-    out_ref[0:rows, :] = (term + extra_ref[0:rows, :].astype(F32)).astype(BF16)
-    term = project_audio(block, audio_ref, wv_ref)
-    out_ref[rows:, :] = (term + extra_ref[rows:, :].astype(F32)).astype(BF16)
+def near_kernel(*refs):
+    heads, weights, (send_ref, own_ref) = refs[:3], refs[3:7], refs[7:]
+    project(block_of(False, True), range(PARTS), heads, weights, send_ref)
+    project(block_of(False, False), range(PARTS), heads, weights, own_ref)
+
+
+def far_high_kernel(*refs):
+    heads, weights, (extra_ref, out_ref) = refs[:3], refs[3:7], refs[7:]
+    project(block_of(True, False), range(1, PARTS), heads, weights, out_ref, extra_ref)
 
 
 def finish_kernel(video_ref, audio_ref, gain_ref, own_ref, core_ref, low_ref, high_ref, video_out, audio_out):
-    rows = video_ref.shape[0]
-    cut = video_ref.shape[1] // 2
-    near = own_ref[...] + core_ref[...].astype(F32)
-    for half, ref in enumerate((low_ref, high_ref)):
-        at = slice(half * cut, (half + 1) * cut)
-        term = near[half * rows : (half + 1) * rows] + ref[0:rows, :].astype(F32)
+    rows, cut = low_ref.shape
+    rows_audio = audio_ref.shape[0]
+    for part in range(PARTS):
+        at = slice(part * cut, (part + 1) * cut)
+        here = slice(part * rows, (part + 1) * rows)
+        far = low_ref[...] if part == 0 else high_ref[(part - 1) * rows : part * rows, :]
+        term = own_ref[here, :] + core_ref[here, :].astype(F32) + far.astype(F32)
         video_out[:, at] = (video_ref[:, at].astype(F32) + term).astype(BF16)
-    term = near[2 * rows :] + high_ref[rows:, :].astype(F32)
-    audio_out[...] = (audio_ref[...].astype(F32) + gain_ref[...] * term).astype(BF16)
+    for i in range(audio_ref.shape[1] // cut):
+        at = slice(i * cut, (i + 1) * cut)
+        top = PARTS * rows + i * rows_audio
+        here, there = slice(top, top + rows_audio), slice(top - rows, top - rows + rows_audio)
+        term = own_ref[here, :] + core_ref[here, :].astype(F32) + high_ref[there, :].astype(F32)
+        audio_out[:, at] = (audio_ref[:, at].astype(F32) + gain_ref[:, at] * term).astype(BF16)
 
 
 def on_device_heads(
@@ -706,7 +716,7 @@
     own, *sends = call(
         functools.partial(late_kernel, early, hops, rows_audio, DHC),
         [shape(rows, width)]
-        + [shape(rows + tail + (2 * audio if hop == FORWARDED else 0), width) for hop in hops[1:]],
+        + [shape(rows + tail + (0 if hop == LAST else audio), width) for hop in hops[1:]],
         (k_own, vvt, part, stats, vt, blocks[LAST], *(blocks[hop] for hop in early), *tails),
         flops=4 * (2 * n - 1) * rows * rows * width,
         scratch=[pltpu.VMEM(((2 * n - 1) * rows, rows), F32)],
@@ -721,38 +731,36 @@
         flops=8 * n * rows * rows_audio * cross,
     )
 
-    half = video_in.shape[1] // 2
-    flops = 2 * rows * (cols + cross) * half
+    cut = video_in.shape[1] // PARTS
+    below = rows_audio * audio_in.shape[1] // cut
+    flops = 2 * rows * (cols + cross) * cut
     self_att, a2v_att, first = call(
         functools.partial(first_kernel, hops, rows_audio, DHC),
-        [shape(rows, cols), shape(rows, cross), shape(rows, half)],
+        [shape(rows, cols), shape(rows, cross), shape(rows, cut)],
         (audio_len, q_own, a2v_part, a2v_stats, own, ws, wa, gain, *got),
         [SMEM] + [VMEM] * (n + 6),
         flops=flops,
-        scratch=[pltpu.VMEM((rows, half), F32)],
+        scratch=[pltpu.VMEM((rows, cut), F32)],
     )
     first = trade(first, "sub", 1, 2)
+    high_rows = (PARTS - 1) * rows + below
     second, v2a_att, own_low = call(
         functools.partial(second_kernel, DHC),
-        [shape(rows + rows_audio, half), shape(rows_audio, cross), shape(rows, half, F32)],
+        [shape(high_rows, cut), shape(rows_audio, cross), shape(rows, cut, F32)],
         (self_att, a2v_att, ws, wa, wv, gain, own_v2a, own_lse, *got),
-        flops=2 * flops,
+        flops=PARTS * flops,
     )
     second = trade(second, "sub", 1, 2)
-    (low,) = call(far_low_kernel, [shape(rows, half)], (own_low, first))
+    operands = (self_att, a2v_att, v2a_att, ws, wa, wv, gain)
+    (low,) = call(far_low_kernel, [shape(rows, cut)], (own_low, first))
     low = trade(low, "mp", 1, 2)
-    (high,) = call(
-        far_high_kernel,
-        [shape(rows + rows_audio, half)],
-        (self_att, a2v_att, ws, wa, gain, second, v2a_att, wv),
-        flops=flops,
-    )
+    (high,) = call(far_high_kernel, [shape(high_rows, cut)], (*operands, second), flops=3 * flops)
     high = trade(high, "mp", 1, 2)
     near, own_sum = call(
         near_kernel,
-        [shape(2 * rows + rows_audio, half), shape(2 * rows + rows_audio, half, F32)],
-        (self_att, a2v_att, v2a_att, ws, wa, wv, gain),
-        flops=4 * flops,
+        [shape(rows + high_rows, cut), shape(rows + high_rows, cut, F32)],
+        operands,
+        flops=2 * PARTS * flops,
     )
     near = trade(near, "sub", 1, 2)
     return call(
@@ -773,6 +781,7 @@
         and 3 * (cross // DHC) <= LSE_ROWS
         and n * arrays[8].shape[0] == arrays[2].shape[0] == 128
         and arrays[0].shape[1] == 2 * arrays[1].shape[1]
+        and arrays[0].shape[1] % (PARTS * 128) == 0
     )
     if fits:
         return on_device_heads(*arrays, n=n)

time: 41.4 us -> 41.9 us (1.012)
  waiting for transfers between devices: 14.4 us -> 15.2 us
  starting transfers between devices: 13.5 us -> 13 us
    ppermute x11, waiting for transfers between devices: 14.4 us -> 15.2 us  [trade(): return lax.ppermute(x, axis, [(i, i ^ hop) for i in range(size)])]
    ppermute x11, starting transfers between devices: 13.5 us -> 13 us  [trade(): return lax.ppermute(x, axis, [(i, i ^ hop) for i in range(size)])]
  transfers between devices with their start and end apart: 11 -> 11, of which waited for: 4 -> 6; matrix products, arithmetic and copies ran while one was open for 3% -> 3% of each run, Pallas kernels for 16% -> 16%
where the time goes in v11:
time: 41.9 us; the launch traced here: 41.6 us
  waiting for transfers between devices  15.2 us (36%)
  starting transfers between devices  13 us (31%)
  Pallas kernels  10.9 us (26%)
  between operations  1.38 us (3%)
  local copies, waits for them, and re-layouts  1.1 us (3%)
    ppermute x11, waiting for transfers between devices, trade(): return lax.ppermute(x, axis, [(i, i ^ hop) for i in range(size)])  15.2 us
    ppermute x11, starting transfers between devices, trade(): return lax.ppermute(x, axis, [(i, i ^ hop) for i in range(size)])  13 us
    pallas_call x12, Pallas kernels, call(): pl.pallas_call(kernel, out_shape=tuple(outs), in_specs=specs or [VMEM] *...  10.9 us
    unnamed x1, local copies, waits for them, and re-layouts  1.1 us
  transfers between devices with their start and end apart: 11, of which 6 were waited for; matrix products, arithmetic and copies ran while one was open for 3% of the time, Pallas kernels for 16%

profile of v11, /device:TPU:0, one launch (start us, length us, event | category | flops | bytes accessed | tf_op | source)
XLA Modules:
  0.0 41.6 jit_solution(2506177499637429461)
XLA Ops:
  0.6 1.3 %shard_map.195 = (bf16[576,128]{1,0:T(8,128)(2,1)S(1)}, bf16[576,128]{1,0:T(8,128)(2,1)S(1)}, bf16[576,128]{1,0:T(8,128)(2,1)S(1)}) custom-call(bf16[128,512]{1,0:T(8,128)(2,1)} %q_ref.3, bf16[128,512]{1,0:T(8,128)(2,1)} %k_ref.3, bf16[128,512]{1,0:T(8,128)(2,1)} %v_ref.3, bf16[32,256]{1,0:T(8,128)(2,1)} %qa_ref.3, bf16[32,256]{1,0:T(8,128)(2,1)} %ka_ref.3, ...), custom_call_target="tpu_custom_call" | custom-call | bytes 884736 | tf_op jit(solution)/shard_map/pallas_call | solution.py:194
  1.9 3.1 %collective-permute-start.1 = (bf16[576,128]{1,0:T(8,128)(2,1)S(1)}, bf16[576,128]{1,0:T(8,128)(2,1)S(1)}, u32[]{:S(2)}, u32[]{:S(2)}) collective-permute-start(bf16[576,128]{1,0:T(8,128)(2,1)S(1)} %get-tuple-element.43), channel_id=1, source_target_pairs={{0,4},{4,0},{8,12},{12,8},{1,5},{5,1},{9,13},{13,9},{2,6},{6,2},{1... | collective-permute-start | bytes 442376 | tf_op jit(solution)/shard_map/ppermute | solution.py:666
  5.0 2.6 %collective-permute-start = (bf16[576,128]{1,0:T(8,128)(2,1)S(1)}, bf16[576,128]{1,0:T(8,128)(2,1)S(1)}, u32[]{:S(2)}, u32[]{:S(2)}) collective-permute-start(bf16[576,128]{1,0:T(8,128)(2,1)S(1)} %get-tuple-element.42), channel_id=1, source_target_pairs={{0,8},{4,12},{8,0},{12,4},{1,9},{5,13},{9,1},{13,5},{2,10},{6,14},... | collective-permute-start | bytes 442376 | tf_op jit(solution)/shard_map/ppermute | solution.py:666
  7.6 0.8 %shard_map.197 = bf16[448,128]{1,0:T(8,128)(2,1)S(1)} custom-call(bf16[128,512]{1,0:T(8,128)(2,1)} %q_ref.3, bf16[128,512]{1,0:T(8,128)(2,1)} %k_ref.3, bf16[128,512]{1,0:T(8,128)(2,1)} %v_ref.3, bf16[32,256]{1,0:T(8,128)(2,1)} %qa_ref.3, bf16[32,256]{1,0:T(8,128)(2,1)} %ka_ref.3, bf16[32,256]{1,0:T(8,128)(2,1)} %va_ref.3), custom_call_target="tpu_custom_call" | custom-call | bytes 557056 | tf_op jit(solution)/shard_map/pallas_call | solution.py:194
  9.2 1.1 %copy.21 = bf16[2,8,2,4096]{3,1,2,0:T(8,128)(2,1)S(1)} copy(bf16[2,8,2,4096]{3,2,1,0:T(2,128)(2,1)} %bitcast.5) | data formatting | bytes 524288
  10.3 3.4 %shard_map.194 = (bf16[128,8192]{1,0:T(8,128)(2,1)S(1)}, f32[32,512]{1,0:T(8,128)S(1)}, bf16[128,256]{1,0:T(8,128)(2,1)S(1)}, bf16[128,256]{1,0:T(8,128)(2,1)S(1...) custom-call(s32[1]{0:T(128)S(6)} %copy.22.limit_ref, ...), custom_call_target="tpu_custom_call" | custom-call | bytes 18154116 | tf_op jit(solution)/shard_map/pallas_call | solution.py:194
  13.7 3.1 %collective-permute-done.2.rest_1_ = bf16[448,128]{1,0:T(8,128)(2,1)S(1)} collective-permute-done((bf16[448,128]{1,0:T(8,128)(2,1)S(1)}, bf16[448,128]{1,0:T(8,128)(2,1)S(1)}, u32[]{:S(2)}, u32[]{:S(2)}) %collective-permute-start.2) | collective-permute-done | bytes 114720 | tf_op jit(solution)/shard_map/ppermute | solution.py:666
  16.8 0.7 %shard_map.198 = (f32[384,128]{1,0:T(8,128)S(1)}, f32[6,128]{1,0:T(8,128)S(1)}, bf16[128,384]{1,0:T(8,128)(2,1)S(1)}, bf16[256,128]{1,0:T(8,128)(2,1)S(1)}, f32[...) custom-call(bf16[128,256]{1,0:T(8,128)(2,1)S(1)} %get-tuple-element.46.kv_r, ...), custom_call_target="tpu_custom_call" | custom-call | flops 75497472 | bytes 979968 | tf_op jit(solution)/shard_map/pallas_call | solution.py:194
  17.5 0.5 %collective-permute-done.rest_1_.last_ref = bf16[576,128]{1,0:T(8,128)(2,1)S(1)} collective-permute-done((bf16[576,128]{1,0:T(8,128)(2,1)S(1)}, bf16[576,128]{1,0:T(8,128)(2,1)S(1)}, u32[]{:S(2)}, u32[]{:S(2)}) %collective-permute-start) | collective-permute-done | bytes 147488 | tf_op jit(solution)/shard_map/ppermute | solution.py:666
  18.1 0.7 %shard_map.199 = (bf16[128,128]{1,0:T(8,128)(2,1)S(1)}, bf16[272,128]{1,0:T(8,128)(2,1)S(1)}, bf16[208,128]{1,0:T(8,128)(2,1)S(1)}, bf16[272,128]{1,0:T(8,128)(2,1)S(1)}) custom-call(bf16[128,256]{1,0:T(8,128)(2,1)S(1)} %get-tuple-element.46.kv_ref, bf16[256,128]{1,0:T(8,128)(2,1)S(1)} %get-tuple-element.48.vvt_ref, ...), custom_call_target="tpu_custom_call" | custom-call | flops 58720256 | bytes 1252352 | tf_op jit(solution)/shard_map/pallas_call | solution.py:194
  18.8 2.5 %collective-permute-start.3 = (bf16[272,128]{1,0:T(8,128)(2,1)S(1)}, bf16[272,128]{1,0:T(8,128)(2,1)S(1)}, u32[]{:S(2)}, u32[]{:S(2)}) collective-permute-start(bf16[272,128]{1,0:T(8,128)(2,1)S(1)} %get-tuple-element.58), channel_id=1, source_target_pairs={{0,12},{4,8},{8,4},{12,0},{1,13},{5,9},{9,5},{13,1},{2,14},{6,10},... | collective-permute-start | bytes 208904 | tf_op jit(solution)/shard_map/ppermute | solution.py:666
  21.3 1.7 %collective-permute-start.5 = (bf16[272,128]{1,0:T(8,128)(2,1)S(1)}, bf16[272,128]{1,0:T(8,128)(2,1)S(1)}, u32[]{:S(2)}, u32[]{:S(2)}) collective-permute-start(bf16[272,128]{1,0:T(8,128)(2,1)S(1)} %get-tuple-element.60), channel_id=1, source_target_pairs={{0,4},{4,0},{8,12},{12,8},{1,5},{5,1},{9,13},{13,9},{2,6},{6,2},{1... | collective-permute-start | bytes 208904 | tf_op jit(solution)/shard_map/ppermute | solution.py:666
  23.3 0.6 %shard_map.196 = (f32[256,128]{1,0:T(8,128)S(1)}, f32[4,256]{1,0:T(4,128)S(1)}) custom-call(s32[1]{0:T(128)S(6)} %copy.22.limit_ref, bf16[128,256]{1,0:T(8,128)(2,1)S(1)} %get-tuple-element.40.q_ref, bf16[576,128]{1,0:T(8,128)(2,1)S(1)} %get-tuple-element.41.rest_0_, bf16[576,128]{1,0:T(8,128)(2,1)S(1)} %collective-permute-done.rest_1_.last_ref, ...), custom_call_target="tpu_custom_call" | custom-call | flops 33554432 | bytes 643076 | tf_op jit(solution)/shard_map/pallas_call | solution.py:194
  23.9 4.5 %collective-permute-done.4.rest_1_ = bf16[208,128]{1,0:T(8,128)(2,1)S(1)} collective-permute-done((bf16[208,128]{1,0:T(8,128)(2,1)S(1)}, bf16[208,128]{1,0:T(8,128)(2,1)S(1)}, u32[]{:S(2)}, u32[]{:S(2)}) %collective-permute-start.4) | collective-permute-done | bytes 53280 | tf_op jit(solution)/shard_map/ppermute | solution.py:666
  28.4 0.8 %shard_map.200 = (bf16[128,512]{1,0:T(8,128)(2,1)S(1)}, bf16[128,256]{1,0:T(8,128)(2,1)S(1)}, bf16[128,256]{1,0:T(8,128)(2,1)S(1)}) custom-call(s32[1]{0:T(128)S(6)} %copy.22.limit_ref, bf16[128,256]{1,0:T(8,128)(2,1)S(1)} %get-tuple-element.40.q_ref, f32[256,128]{1,0:T(8,128)S(1)} %get-tuple-element.44.part_ref, f32[4,256]{1,0:T(4,128)S(1)} %get-tuple-element.45.stats_ref, ...), custom_call_target="tpu_custom_call" | custom-call | flops 50331648 | bytes 9076740 | tf_op jit(solution)/shard_map/pallas_call | solution.py:194
  29.2 0.6 %shard_map.201 = (bf16[448,256]{1,0:T(8,128)(2,1)S(1)}, bf16[32,256]{1,0:T(8,128)(2,1)S(1)}, f32[128,256]{1,0:T(8,128)S(1)}) custom-call(bf16[128,512]{1,0:T(8,128)(2,1)S(1)} %get-tuple-element.61.self_ref.refs_0_, bf16[128,256]{1,0:T(8,128)(2,1)S(1)} %get-tuple-element.62.a2v_ref.refs_1_, bf16[512,4096]{1,0:T(8,128)(2,1)S(1)} %get-tuple-element.55.ws_ref.refs_3_, ...), custom_call_target="tpu_custom_call" | custom-call | flops 201326592 | bytes 10237952 | tf_op jit(solution)/shard_map/pallas_call | solution.py:194
  29.8 0.8 %shard_map.202 = (bf16[576,256]{1,0:T(8,128)(2,1)S(1)}, f32[576,256]{1,0:T(8,128)S(1)}) custom-call(bf16[128,512]{1,0:T(8,128)(2,1)S(1)} %get-tuple-element.61.self_ref.refs_0_, bf16[128,256]{1,0:T(8,128)(2,1)S(1)} %get-tuple-element.62.a2v_ref.refs_1_, bf16[32,256]{1,0:T(8,128)(2,1)S(1)} %get-tuple-element.66.refs_2_, ...), custom_call_target="tpu_custom_call" | custom-call | flops 402653184 | bytes 10534912 | tf_op jit(solution)/shard_map/pallas_call | solution.py:194
  30.6 0.6 %collective-permute-start.6 = (bf16[576,256]{1,0:T(8,128)(2,1)S(1)}, bf16[576,256]{1,0:T(8,128)(2,1)S(1)}, u32[]{:S(2)}, u32[]{:S(2)}) collective-permute-start(bf16[576,256]{1,0:T(8,128)(2,1)S(1)} %get-tuple-element.68), channel_id=1, source_target_pairs={{0,1},{1,0},{2,3},{3,2},{4,5},{5,4},{6,7},{7,6},{8,9},{9,8},{10,11... | collective-permute-start | bytes 884744 | tf_op jit(solution)/shard_map/ppermute | solution.py:666
  31.3 0.4 shard_map.204
  31.7 1.6 %collective-permute-start.10 = (bf16[448,256]{1,0:T(8,128)(2,1)S(1)}, bf16[448,256]{1,0:T(8,128)(2,1)S(1)}, u32[]{:S(2)}, u32[]{:S(2)}) collective-permute-start(bf16[448,256]{1,0:T(8,128)(2,1)S(1)} %shard_map.204), channel_id=1, source_target_pairs={{0,2},{2,0},{1,3},{3,1},{4,6},{6,4},{5,7},{7,5},{8,10},{10,8},{9,1... | collective-permute-start | bytes 688136 | tf_op jit(solution)/shard_map/ppermute | solution.py:666
  33.2 1.3 %collective-permute-done.7.extra_ref = bf16[128,256]{1,0:T(8,128)(2,1)S(1)} collective-permute-done((bf16[128,256]{1,0:T(8,128)(2,1)S(1)}, bf16[128,256]{1,0:T(8,128)(2,1)S(1)}, u32[]{:S(2)}, u32[]{:S(2)}) %collective-permute-start.7) | collective-permute-done | bytes 65568 | tf_op jit(solution)/shard_map/ppermute | solution.py:666
  34.5 0.6 %collective-permute-start.8 = (bf16[128,256]{1,0:T(8,128)(2,1)S(1)}, bf16[128,256]{1,0:T(8,128)(2,1)S(1)}, u32[]{:S(2)}, u32[]{:S(2)}) collective-permute-start(bf16[128,256]{1,0:T(8,128)(2,1)S(1)} %shard_map.203), channel_id=1, source_target_pairs={{0,2},{2,0},{1,3},{3,1},{4,6},{6,4},{5,7},{7,5},{8,10},{10,8},{9,1... | collective-permute-start | bytes 196616 | tf_op jit(solution)/shard_map/ppermute | solution.py:666
  35.1 5.7 %collective-permute-done.8.low_ref = bf16[128,256]{1,0:T(8,128)(2,1)S(1)} collective-permute-done((bf16[128,256]{1,0:T(8,128)(2,1)S(1)}, bf16[128,256]{1,0:T(8,128)(2,1)S(1)}, u32[]{:S(2)}, u32[]{:S(2)}) %collective-permute-start.8) | collective-permute-done | bytes 65568 | tf_op jit(solution)/shard_map/ppermute | solution.py:666
  40.8 0.8 %shard_map.205 = (bf16[128,1024]{1,0:T(8,128)(2,1)}, bf16[32,512]{1,0:T(8,128)(2,1)}) custom-call(bf16[128,1024]{1,0:T(8,128)(2,1)S(1)} %get-tuple-element.37.video_ref, bf16[32,512]{1,0:T(8,128)(2,1)S(1)} %get-tuple-element.38.audio_ref, f32[32,512]{1,0:T(8,128)S(1)} %get-tuple-element.39.gain_ref, f32[576,256]{1,0:T(8,128)S(1)} %get-tuple-element.67.own_ref, ...), custom_call_target="tpu_custom_call" | custom-call | bytes 1835008 | tf_op jit(solution)/shard_map/pallas_call | solution.py:194
  (11 shorter events, 0.5 us)
Async XLA Ops:
  1.9 14.9 %collective-permute-start.1 = (bf16[576,128]{1,0:T(8,128)(2,1)S(1)}, bf16[576,128]{1,0:T(8,128)(2,1)S(1)}, u32[]{:S(2)}, u32[]{:S(2)}) collective-permute-start(bf16[576,128]{1,0:T(8,128)(2,1)S(1)} %get-tuple-element.43), channel_id=1, source_target_pairs={{0,4},{4,0},{8,12},{12,8},{1,5},{5,1},{9,13},{13,9},{2,6},{6,2},{1... | collective-permute-start | bytes 442376 | tf_op jit(solution)/shard_map/ppermute | solution.py:666
  5.0 13.0 %collective-permute-start = (bf16[576,128]{1,0:T(8,128)(2,1)S(1)}, bf16[576,128]{1,0:T(8,128)(2,1)S(1)}, u32[]{:S(2)}, u32[]{:S(2)}) collective-permute-start(bf16[576,128]{1,0:T(8,128)(2,1)S(1)} %get-tuple-element.42), channel_id=1, source_target_pairs={{0,8},{4,12},{8,0},{12,4},{1,9},{5,13},{9,1},{13,5},{2,10},{6,14},... | collective-permute-start | bytes 442376 | tf_op jit(solution)/shard_map/ppermute | solution.py:666
  8.5 8.3 %collective-permute-start.2 = (bf16[448,128]{1,0:T(8,128)(2,1)S(1)}, bf16[448,128]{1,0:T(8,128)(2,1)S(1)}, u32[]{:S(2)}, u32[]{:S(2)}) collective-permute-start(bf16[448,128]{1,0:T(8,128)(2,1)S(1)} %shard_map.197), channel_id=1, source_target_pairs={{0,12},{4,8},{8,4},{12,0},{1,13},{5,9},{9,5},{13,1},{2,14},{6,10},... | collective-permute-start | bytes 344072 | tf_op jit(solution)/shard_map/ppermute | solution.py:666
  18.8 9.6 %collective-permute-start.3 = (bf16[272,128]{1,0:T(8,128)(2,1)S(1)}, bf16[272,128]{1,0:T(8,128)(2,1)S(1)}, u32[]{:S(2)}, u32[]{:S(2)}) collective-permute-start(bf16[272,128]{1,0:T(8,128)(2,1)S(1)} %get-tuple-element.58), channel_id=1, source_target_pairs={{0,12},{4,8},{8,4},{12,0},{1,13},{5,9},{9,5},{13,1},{2,14},{6,10},... | collective-permute-start | bytes 208904 | tf_op jit(solution)/shard_map/ppermute | solution.py:666
  21.3 7.1 %collective-permute-start.5 = (bf16[272,128]{1,0:T(8,128)(2,1)S(1)}, bf16[272,128]{1,0:T(8,128)(2,1)S(1)}, u32[]{:S(2)}, u32[]{:S(2)}) collective-permute-start(bf16[272,128]{1,0:T(8,128)(2,1)S(1)} %get-tuple-element.60), channel_id=1, source_target_pairs={{0,4},{4,0},{8,12},{12,8},{1,5},{5,1},{9,13},{13,9},{2,6},{6,2},{1... | collective-permute-start | bytes 208904 | tf_op jit(solution)/shard_map/ppermute | solution.py:666
  23.1 5.4 %collective-permute-start.4 = (bf16[208,128]{1,0:T(8,128)(2,1)S(1)}, bf16[208,128]{1,0:T(8,128)(2,1)S(1)}, u32[]{:S(2)}, u32[]{:S(2)}) collective-permute-start(bf16[208,128]{1,0:T(8,128)(2,1)S(1)} %get-tuple-element.59), channel_id=1, source_target_pairs={{0,8},{4,12},{8,0},{12,4},{1,9},{5,13},{9,1},{13,5},{2,10},{6,14},... | collective-permute-start | bytes 159752 | tf_op jit(solution)/shard_map/ppermute | solution.py:666
  29.7 1.6 %collective-permute-start.9 = (bf16[448,256]{1,0:T(8,128)(2,1)S(1)}, bf16[448,256]{1,0:T(8,128)(2,1)S(1)}, u32[]{:S(2)}, u32[]{:S(2)}) collective-permute-start(bf16[448,256]{1,0:T(8,128)(2,1)S(1)} %get-tuple-element.71), channel_id=1, source_target_pairs={{0,1},{1,0},{2,3},{3,2},{4,5},{5,4},{6,7},{7,6},{8,9},{9,8},{10,11... | collective-permute-start | bytes 688136 | tf_op jit(solution)/shard_map/ppermute | solution.py:666
  30.6 10.2 %collective-permute-start.6 = (bf16[576,256]{1,0:T(8,128)(2,1)S(1)}, bf16[576,256]{1,0:T(8,128)(2,1)S(1)}, u32[]{:S(2)}, u32[]{:S(2)}) collective-permute-start(bf16[576,256]{1,0:T(8,128)(2,1)S(1)} %get-tuple-element.68), channel_id=1, source_target_pairs={{0,1},{1,0},{2,3},{3,2},{4,5},{5,4},{6,7},{7,6},{8,9},{9,8},{10,11... | collective-permute-start | bytes 884744 | tf_op jit(solution)/shard_map/ppermute | solution.py:666
  31.7 9.1 %collective-permute-start.10 = (bf16[448,256]{1,0:T(8,128)(2,1)S(1)}, bf16[448,256]{1,0:T(8,128)(2,1)S(1)}, u32[]{:S(2)}, u32[]{:S(2)}) collective-permute-start(bf16[448,256]{1,0:T(8,128)(2,1)S(1)} %shard_map.204), channel_id=1, source_target_pairs={{0,2},{2,0},{1,3},{3,1},{4,6},{6,4},{5,7},{7,5},{8,10},{10,8},{9,1... | collective-permute-start | bytes 688136 | tf_op jit(solution)/shard_map/ppermute | solution.py:666
  33.2 1.3 %collective-permute-start.7 = (bf16[128,256]{1,0:T(8,128)(2,1)S(1)}, bf16[128,256]{1,0:T(8,128)(2,1)S(1)}, u32[]{:S(2)}, u32[]{:S(2)}) collective-permute-start(bf16[128,256]{1,0:T(8,128)(2,1)S(1)} %get-tuple-element.70), channel_id=1, source_target_pairs={{0,1},{1,0},{2,3},{3,2},{4,5},{5,4},{6,7},{7,6},{8,9},{9,8},{10,11... | collective-permute-start | bytes 196616 | tf_op jit(solution)/shard_map/ppermute | solution.py:666
  34.5 6.3 %collective-permute-start.8 = (bf16[128,256]{1,0:T(8,128)(2,1)S(1)}, bf16[128,256]{1,0:T(8,128)(2,1)S(1)}, u32[]{:S(2)}, u32[]{:S(2)}) collective-permute-start(bf16[128,256]{1,0:T(8,128)(2,1)S(1)} %shard_map.203), channel_id=1, source_target_pairs={{0,2},{2,0},{1,3},{3,1},{4,6},{6,4},{5,7},{7,5},{8,10},{10,8},{9,1... | collective-permute-start | bytes 196616 | tf_op jit(solution)/shard_map/ppermute | solution.py:666

commit v12 on v11

--- a/solution.py
+++ b/solution.py
@@ -417,7 +417,7 @@
 
 def late_kernel(early, hops, rows_audio, head, kv_ref, vvt_ref, part_ref, stats_ref, vt_ref, last_ref, *rest):
     count, n = len(early), len(hops)
-    blocks, tails, outs, s_ref = rest[:count], rest[count : 2 * count - 1], rest[2 * count - 1 : -1], rest[-1]
+    blocks, tails, outs, (relay_ref, s_ref) = rest[:count], rest[count : 2 * count - 1], rest[2 * count - 1 : -2], rest[-2:]
     by_hop = dict(zip(hops, outs))
     rows = kv_ref.shape[0]
     last = next(hop for hop in hops if hop not in early)
@@ -457,10 +457,7 @@
     store_tail(by_hop[last], rows, *audio)
     for hop, tail in zip(early[1:], tails):
         by_hop[hop][rows : rows + tail.shape[0], :] = tail[...]
-    top = rows + tails[0].shape[0]
-    extra = by_hop[FORWARDED].shape[0] - top
-    by_hop[FORWARDED][top:, :] = blocks[0][blocks[0].shape[0] - extra :, :]
-    by_hop[1][top:, :] = last_ref[last_ref.shape[0] - 2 * extra : last_ref.shape[0] - extra, :]
+    relay_ref[...] = last_ref[last_ref.shape[0] - relay_ref.shape[0] :, :]
 
 
 def audio_allowed(hop, rows_audio, limit):
@@ -491,20 +488,20 @@
         stats_ref[2 * block + 1 : 2 * block + 2, :] = total
 
 
-def finish_audio(head, limit, q_ref, part_ref, stats_ref, keys_ref, values_ref, rows_audio, out_ref):
+def join_kernel(head, rows_audio, limit_ref, q_ref, part_ref, stats_ref, last_ref, out_ref):
     cols = q_ref.shape[1]
     scale = 1.0 / math.sqrt(head)
-    allowed = audio_allowed(FORWARDED, rows_audio, limit)
+    allowed = audio_allowed(FORWARDED, rows_audio, limit_ref[0])
     for block in range(cols // 128):
         cut = slice(block * 128, (block + 1) * 128)
         q = pair_rows(q_ref[:, cut], head)
-        scores = jnp.where(allowed, dot_t(audio_block(keys_ref, 1, rows_audio, cols, block), q), LEAST)
+        scores = jnp.where(allowed, dot_t(audio_block(last_ref, 2, rows_audio, cols, block), q), LEAST)
         before, summed = stats_ref[2 * block : 2 * block + 1, :], stats_ref[2 * block + 1 : 2 * block + 2, :]
         peak = jnp.maximum(before, jnp.max(scores, axis=0, keepdims=True))
         factor = jnp.exp2((before - peak) * (scale * LOG2E))
         p = jnp.exp2((scores - peak) * (scale * LOG2E))
         inverse = 1.0 / (summed * factor + jnp.sum(p, axis=0, keepdims=True))
-        vt = turn(audio_block(values_ref, 1, rows_audio, cols, block))
+        vt = turn(audio_block(last_ref, 1, rows_audio, cols, block))
         last = pair_columns(dot(vt, p.astype(BF16)), head)
         both = part_ref[cut, :] * spread(factor, head) + last
         out_ref[:, cut] = (both * spread(inverse, head)).T.astype(BF16)
@@ -579,17 +576,15 @@
         store(len(parts) * rows + i * rows_audio, term[:, i * cut : (i + 1) * cut])
 
 
-def first_kernel(hops, rows_audio, head, limit_ref, q_ref, part_ref, stats_ref, own_ref, ws_ref, wa_ref, gain_ref, *rest):
-    got, (self_ref, a2v_ref, out_ref, term_ref) = rest[: len(hops) - 1], rest[len(hops) - 1 :]
+def first_kernel(hops, own_ref, a2v_ref, ws_ref, wa_ref, gain_ref, *rest):
+    got, (self_ref, out_ref) = rest[: len(hops) - 1], rest[len(hops) - 1 :]
     rows, width = own_ref.shape
-    keys_ref, values_ref = got[hops.index(1) - 1], got[hops.index(FORWARDED) - 1]
-    self_ref[:, columns(index_of("seq"), width)] = own_ref[...]
+    block, me = block_of(True, True), index_of("seq")
+    term = project_a2v(block, 0, a2v_ref, wa_ref, gain_ref)
+    self_ref[:, columns(me, width)] = own_ref[...]
     for hop, ref in zip(hops[1:], got):
-        self_ref[:, columns(index_of("seq") ^ hop, width)] = ref[0:rows, :]
-    block = block_of(True, True)
-    term_ref[...] = project_self(block, 0, self_ref, ws_ref, gain_ref)
-    finish_audio(head, limit_ref[0], q_ref, part_ref, stats_ref, keys_ref, values_ref, rows_audio, a2v_ref)
-    out_ref[...] = (term_ref[...] + project_a2v(block, 0, a2v_ref, wa_ref, gain_ref)).astype(BF16)
+        self_ref[:, columns(me ^ hop, width)] = ref[0:rows, :]
+    out_ref[...] = (project_self(block, 0, self_ref, ws_ref, gain_ref) + term).astype(BF16)
 
 
 def second_kernel(head, self_ref, a2v_ref, ws_ref, wa_ref, wv_ref, gain_ref, v2a_ref, lse_ref, *rest):
@@ -713,15 +708,17 @@
         flops=4 * count * count * rows * rows * width,
         scratch=[pltpu.VMEM(((count * count + cross // DHC) * rows, rows), F32)],
     )
-    own, *sends = call(
+    own, *sends, relay = call(
         functools.partial(late_kernel, early, hops, rows_audio, DHC),
         [shape(rows, width)]
-        + [shape(rows + tail + (0 if hop == LAST else audio), width) for hop in hops[1:]],
+        + [shape(rows + tail, width)] * (n - 1)
+        + [shape(2 * audio, width)],
         (k_own, vvt, part, stats, vt, blocks[LAST], *(blocks[hop] for hop in early), *tails),
         flops=4 * (2 * n - 1) * rows * rows * width,
         scratch=[pltpu.VMEM(((2 * n - 1) * rows, rows), F32)],
     )
     got = [trade(x, "seq", hop, n) for x, hop in zip(sends, hops[1:])]
+    forwarded = trade(relay, "seq", FORWARDED ^ LAST, n)
     near = [hop for hop in hops if hop != FORWARDED]
     a2v_part, a2v_stats = call(
         functools.partial(attend_audio_kernel, near, rows_audio, DHC),
@@ -731,16 +728,22 @@
         flops=8 * n * rows * rows_audio * cross,
     )
 
+    (a2v_att,) = call(
+        functools.partial(join_kernel, DHC, rows_audio),
+        [shape(rows, cross)],
+        (audio_len, q_own, a2v_part, a2v_stats, forwarded),
+        [SMEM] + [VMEM] * 4,
+        flops=4 * rows * rows_audio * cross,
+    )
+
     cut = video_in.shape[1] // PARTS
     below = rows_audio * audio_in.shape[1] // cut
     flops = 2 * rows * (cols + cross) * cut
-    self_att, a2v_att, first = call(
-        functools.partial(first_kernel, hops, rows_audio, DHC),
-        [shape(rows, cols), shape(rows, cross), shape(rows, cut)],
-        (audio_len, q_own, a2v_part, a2v_stats, own, ws, wa, gain, *got),
-        [SMEM] + [VMEM] * (n + 6),
+    self_att, first = call(
+        functools.partial(first_kernel, hops),
+        [shape(rows, cols), shape(rows, cut)],
+        (own, a2v_att, ws, wa, gain, *got),
         flops=flops,
-        scratch=[pltpu.VMEM((rows, cut), F32)],
     )
     first = trade(first, "sub", 1, 2)
     high_rows = (PARTS - 1) * rows + below

time: 41.9 us -> 41.1 us (0.981)
  waiting for transfers between devices: 15.2 us -> 12.6 us
  starting transfers between devices: 13 us -> 14.7 us
    ppermute x11 -> x12, waiting for transfers between devices: 15.2 us -> 12.6 us  [trade(): return lax.ppermute(x, axis, [(i, i ^ hop) for i in range(size)])]
    ppermute x11 -> x12, starting transfers between devices: 13 us -> 14.7 us  [trade(): return lax.ppermute(x, axis, [(i, i ^ hop) for i in range(size)])]
    pallas_call x12 -> x13, Pallas kernels: 10.9 us -> 11 us  [call(): pl.pallas_call(kernel, out_shape=tuple(outs), in_specs=specs or [VMEM] *...]
  transfers between devices with their start and end apart: 11 -> 12, of which waited for: 6 -> 6; matrix products, arithmetic and copies ran while one was open for 3% -> 3% of each run, Pallas kernels for 16% -> 18%
where the time goes in v12:
time: 41.1 us; the launch traced here: 40.8 us
  starting transfers between devices  14.7 us (36%)
  waiting for transfers between devices  12.6 us (31%)
  Pallas kernels  11 us (27%)
  between operations  1.41 us (3%)
  local copies, waits for them, and re-layouts  1.1 us (3%)
    ppermute x12, starting transfers between devices, trade(): return lax.ppermute(x, axis, [(i, i ^ hop) for i in range(size)])  14.7 us
    ppermute x12, waiting for transfers between devices, trade(): return lax.ppermute(x, axis, [(i, i ^ hop) for i in range(size)])  12.6 us
    pallas_call x13, Pallas kernels, call(): pl.pallas_call(kernel, out_shape=tuple(outs), in_specs=specs or [VMEM] *...  11 us
    unnamed x1, local copies, waits for them, and re-layouts  1.1 us
  transfers between devices with their start and end apart: 12, of which 6 were waited for; matrix products, arithmetic and copies ran while one was open for 3% of the time, Pallas kernels for 18%

profile of v12, /device:TPU:0, one launch (start us, length us, event | category | flops | bytes accessed | tf_op | source)
XLA Modules:
  0.0 40.8 jit_solution(305952125234494825)
XLA Ops:
  0.6 1.3 %shard_map.195 = (bf16[576,128]{1,0:T(8,128)(2,1)S(1)}, bf16[576,128]{1,0:T(8,128)(2,1)S(1)}, bf16[576,128]{1,0:T(8,128)(2,1)S(1)}) custom-call(bf16[128,512]{1,0:T(8,128)(2,1)} %q_ref.3, bf16[128,512]{1,0:T(8,128)(2,1)} %k_ref.3, bf16[128,512]{1,0:T(8,128)(2,1)} %v_ref.3, bf16[32,256]{1,0:T(8,128)(2,1)} %qa_ref.3, bf16[32,256]{1,0:T(8,128)(2,1)} %ka_ref.3, ...), custom_call_target="tpu_custom_call" | custom-call | bytes 884736 | tf_op jit(solution)/shard_map/pallas_call | solution.py:194
  1.9 3.1 %collective-permute-start.1 = (bf16[576,128]{1,0:T(8,128)(2,1)S(1)}, bf16[576,128]{1,0:T(8,128)(2,1)S(1)}, u32[]{:S(2)}, u32[]{:S(2)}) collective-permute-start(bf16[576,128]{1,0:T(8,128)(2,1)S(1)} %get-tuple-element.43), channel_id=1, source_target_pairs={{0,4},{4,0},{8,12},{12,8},{1,5},{5,1},{9,13},{13,9},{2,6},{6,2},{1... | collective-permute-start | bytes 442376 | tf_op jit(solution)/shard_map/ppermute | solution.py:661
  5.0 2.6 %collective-permute-start.2 = (bf16[576,128]{1,0:T(8,128)(2,1)S(1)}, bf16[576,128]{1,0:T(8,128)(2,1)S(1)}, u32[]{:S(2)}, u32[]{:S(2)}) collective-permute-start(bf16[576,128]{1,0:T(8,128)(2,1)S(1)} %get-tuple-element.48), channel_id=1, source_target_pairs={{0,8},{4,12},{8,0},{12,4},{1,9},{5,13},{9,1},{13,5},{2,10},{6,14},... | collective-permute-start | bytes 442376 | tf_op jit(solution)/shard_map/ppermute | solution.py:661
  7.6 0.8 %shard_map.196 = bf16[448,128]{1,0:T(8,128)(2,1)S(1)} custom-call(bf16[128,512]{1,0:T(8,128)(2,1)} %q_ref.3, bf16[128,512]{1,0:T(8,128)(2,1)} %k_ref.3, bf16[128,512]{1,0:T(8,128)(2,1)} %v_ref.3, bf16[32,256]{1,0:T(8,128)(2,1)} %qa_ref.3, bf16[32,256]{1,0:T(8,128)(2,1)} %ka_ref.3, bf16[32,256]{1,0:T(8,128)(2,1)} %va_ref.3), custom_call_target="tpu_custom_call" | custom-call | bytes 557056 | tf_op jit(solution)/shard_map/pallas_call | solution.py:194
  9.2 1.1 %copy.21 = bf16[2,8,2,4096]{3,1,2,0:T(8,128)(2,1)S(1)} copy(bf16[2,8,2,4096]{3,2,1,0:T(2,128)(2,1)} %bitcast.5) | data formatting | bytes 524288
  10.3 3.4 %shard_map.194 = (bf16[128,8192]{1,0:T(8,128)(2,1)S(1)}, f32[32,512]{1,0:T(8,128)S(1)}, bf16[128,256]{1,0:T(8,128)(2,1)S(1)}, bf16[128,256]{1,0:T(8,128)(2,1)S(1...) custom-call(s32[1]{0:T(128)S(6)} %copy.22.limit_ref, ...), custom_call_target="tpu_custom_call" | custom-call | bytes 18154116 | tf_op jit(solution)/shard_map/pallas_call | solution.py:194
  13.7 3.1 %collective-permute-done.rest_1_ = bf16[448,128]{1,0:T(8,128)(2,1)S(1)} collective-permute-done((bf16[448,128]{1,0:T(8,128)(2,1)S(1)}, bf16[448,128]{1,0:T(8,128)(2,1)S(1)}, u32[]{:S(2)}, u32[]{:S(2)}) %collective-permute-start) | collective-permute-done | bytes 114720 | tf_op jit(solution)/shard_map/ppermute | solution.py:661
  16.8 0.7 %shard_map.197 = (f32[384,128]{1,0:T(8,128)S(1)}, f32[6,128]{1,0:T(8,128)S(1)}, bf16[128,384]{1,0:T(8,128)(2,1)S(1)}, bf16[256,128]{1,0:T(8,128)(2,1)S(1)}, f32[...) custom-call(bf16[128,256]{1,0:T(8,128)(2,1)S(1)} %get-tuple-element.40.kv_r, ...), custom_call_target="tpu_custom_call" | custom-call | flops 75497472 | bytes 979968 | tf_op jit(solution)/shard_map/pallas_call | solution.py:194
  17.5 0.5 %collective-permute-done.2.last_ref.rest_1_ = bf16[576,128]{1,0:T(8,128)(2,1)S(1)} collective-permute-done((bf16[576,128]{1,0:T(8,128)(2,1)S(1)}, bf16[576,128]{1,0:T(8,128)(2,1)S(1)}, u32[]{:S(2)}, u32[]{:S(2)}) %collective-permute-start.2) | collective-permute-done | bytes 147488 | tf_op jit(solution)/shard_map/ppermute | solution.py:661
  18.1 0.7 %shard_map.198 = (bf16[128,128]{1,0:T(8,128)(2,1)S(1)}, bf16[208,128]{1,0:T(8,128)(2,1)S(1)}, bf16[208,128]{1,0:T(8,128)(2,1)S(1)}, bf16[208,128]{1,0:T(8,128)(2,1)S(1)}, bf16[128,128]{1,0:T(8,128)(2,1)S(1)}) custom-call(bf16[128,256]{1,0:T(8,128)(2,1)S(1)} %get-tuple-element.40.kv_ref, bf16[256,128]{1,0:T(8,128)(2,1)S(1)} %get-tuple-element.44.vvt_ref, ...), custom_call_target="tpu_custom_call" | custom-call | flops 58720256 | bytes 1252352 | tf_op jit(solution)/shard_map/pallas_call | solution.py:194
  18.8 2.5 %collective-permute-start.4 = (bf16[208,128]{1,0:T(8,128)(2,1)S(1)}, bf16[208,128]{1,0:T(8,128)(2,1)S(1)}, u32[]{:S(2)}, u32[]{:S(2)}) collective-permute-start(bf16[208,128]{1,0:T(8,128)(2,1)S(1)} %get-tuple-element.59), channel_id=1, source_target_pairs={{0,12},{4,8},{8,4},{12,0},{1,13},{5,9},{9,5},{13,1},{2,14},{6,10},... | collective-permute-start | bytes 159752 | tf_op jit(solution)/shard_map/ppermute | solution.py:661
  21.3 1.6 %collective-permute-start.5 = (bf16[208,128]{1,0:T(8,128)(2,1)S(1)}, bf16[208,128]{1,0:T(8,128)(2,1)S(1)}, u32[]{:S(2)}, u32[]{:S(2)}) collective-permute-start(bf16[208,128]{1,0:T(8,128)(2,1)S(1)} %get-tuple-element.60), channel_id=1, source_target_pairs={{0,8},{4,12},{8,0},{12,4},{1,9},{5,13},{9,1},{13,5},{2,10},{6,14},... | collective-permute-start | bytes 159752 | tf_op jit(solution)/shard_map/ppermute | solution.py:661
  23.3 1.7 %collective-permute-start.3 = (bf16[128,128]{1,0:T(8,128)(2,1)S(1)}, bf16[128,128]{1,0:T(8,128)(2,1)S(1)}, u32[]{:S(2)}, u32[]{:S(2)}) collective-permute-start(bf16[128,128]{1,0:T(8,128)(2,1)S(1)} %get-tuple-element.55), channel_id=1, source_target_pairs={{0,4},{4,0},{8,12},{12,8},{1,5},{5,1},{9,13},{13,9},{2,6},{6,2},{1... | collective-permute-start | bytes 98312 | tf_op jit(solution)/shard_map/ppermute | solution.py:661
  25.0 0.6 %shard_map.199 = (f32[256,128]{1,0:T(8,128)S(1)}, f32[4,256]{1,0:T(4,128)S(1)}) custom-call(s32[1]{0:T(128)S(6)} %copy.22.limit_ref, bf16[128,256]{1,0:T(8,128)(2,1)S(1)} %get-tuple-element.52.q_ref, bf16[576,128]{1,0:T(8,128)(2,1)S(1)} %get-tuple-element.42.rest_0_, bf16[576,128]{1,0:T(8,128)(2,1)S(1)} %collective-permute-done.2.last_ref.rest_1_, ...), custom_call_target="tpu_custom_call" | custom-call | flops 33554432 | bytes 643076 | tf_op jit(solution)/shard_map/pallas_call | solution.py:194
  25.6 1.9 %collective-permute-done.3.last_ref = bf16[128,128]{1,0:T(8,128)(2,1)S(1)} collective-permute-done((bf16[128,128]{1,0:T(8,128)(2,1)S(1)}, bf16[128,128]{1,0:T(8,128)(2,1)S(1)}, u32[]{:S(2)}, u32[]{:S(2)}) %collective-permute-start.3) | collective-permute-done | bytes 32800 | tf_op jit(solution)/shard_map/ppermute | solution.py:661
  27.4 0.6 %shard_map.200.a2v_ref.refs_1_ = bf16[128,256]{1,0:T(8,128)(2,1)S(1)} custom-call(s32[1]{0:T(128)S(6)} %copy.22.limit_ref, bf16[128,256]{1,0:T(8,128)(2,1)S(1)} %get-tuple-element.52.q_ref, f32[256,128]{1,0:T(8,128)S(1)} %get-tuple-element.53.part_ref, f32[4,256]{1,0:T(4,128)S(1)} %get-tuple-element.54.stats_ref, ...), custom_call_target="tpu_custom_call" | custom-call | flops 4194304 | bytes 299012 | tf_op jit(solution)/shard_map/pallas_call | solution.py:194
  28.3 0.5 %shard_map.202 = (bf16[448,256]{1,0:T(8,128)(2,1)S(1)}, bf16[32,256]{1,0:T(8,128)(2,1)S(1)}, f32[128,256]{1,0:T(8,128)S(1)}) custom-call(bf16[128,512]{1,0:T(8,128)(2,1)S(1)} %get-tuple-element.62.self_ref.refs_0_, bf16[128,256]{1,0:T(8,128)(2,1)S(1)} %shard_map.200.a2v_ref.refs_1_, bf16[512,4096]{1,0:T(8,128)(2,1)S(1)} %get-tuple-element.56.ws_ref.refs_3_, ...), custom_call_target="tpu_custom_call" | custom-call | flops 201326592 | bytes 10205184 | tf_op jit(solution)/shard_map/pallas_call | solution.py:194
  29.0 0.8 %shard_map.203 = (bf16[576,256]{1,0:T(8,128)(2,1)S(1)}, f32[576,256]{1,0:T(8,128)S(1)}) custom-call(bf16[128,512]{1,0:T(8,128)(2,1)S(1)} %get-tuple-element.62.self_ref.refs_0_, bf16[128,256]{1,0:T(8,128)(2,1)S(1)} %shard_map.200.a2v_ref.refs_1_, bf16[32,256]{1,0:T(8,128)(2,1)S(1)} %get-tuple-element.66.refs_2_, ...), custom_call_target="tpu_custom_call" | custom-call | flops 402653184 | bytes 10534912 | tf_op jit(solution)/shard_map/pallas_call | solution.py:194
  29.8 0.6 %collective-permute-start.7 = (bf16[576,256]{1,0:T(8,128)(2,1)S(1)}, bf16[576,256]{1,0:T(8,128)(2,1)S(1)}, u32[]{:S(2)}, u32[]{:S(2)}) collective-permute-start(bf16[576,256]{1,0:T(8,128)(2,1)S(1)} %get-tuple-element.68), channel_id=1, source_target_pairs={{0,1},{1,0},{2,3},{3,2},{4,5},{5,4},{6,7},{7,6},{8,9},{9,8},{10,11... | collective-permute-start | bytes 884744 | tf_op jit(solution)/shard_map/ppermute | solution.py:661
  30.8 1.6 %collective-permute-start.11 = (bf16[448,256]{1,0:T(8,128)(2,1)S(1)}, bf16[448,256]{1,0:T(8,128)(2,1)S(1)}, u32[]{:S(2)}, u32[]{:S(2)}) collective-permute-start(bf16[448,256]{1,0:T(8,128)(2,1)S(1)} %shard_map.205), channel_id=1, source_target_pairs={{0,2},{2,0},{1,3},{3,1},{4,6},{6,4},{5,7},{7,5},{8,10},{10,8},{9,1... | collective-permute-start | bytes 688136 | tf_op jit(solution)/shard_map/ppermute | solution.py:661
  32.4 1.3 %collective-permute-done.8.extra_ref = bf16[128,256]{1,0:T(8,128)(2,1)S(1)} collective-permute-done((bf16[128,256]{1,0:T(8,128)(2,1)S(1)}, bf16[128,256]{1,0:T(8,128)(2,1)S(1)}, u32[]{:S(2)}, u32[]{:S(2)}) %collective-permute-start.8) | collective-permute-done | bytes 65568 | tf_op jit(solution)/shard_map/ppermute | solution.py:661
  33.7 0.6 %collective-permute-start.9 = (bf16[128,256]{1,0:T(8,128)(2,1)S(1)}, bf16[128,256]{1,0:T(8,128)(2,1)S(1)}, u32[]{:S(2)}, u32[]{:S(2)}) collective-permute-start(bf16[128,256]{1,0:T(8,128)(2,1)S(1)} %shard_map.204), channel_id=1, source_target_pairs={{0,2},{2,0},{1,3},{3,1},{4,6},{6,4},{5,7},{7,5},{8,10},{10,8},{9,1... | collective-permute-start | bytes 196616 | tf_op jit(solution)/shard_map/ppermute | solution.py:661
  34.3 5.7 %collective-permute-done.9.low_ref = bf16[128,256]{1,0:T(8,128)(2,1)S(1)} collective-permute-done((bf16[128,256]{1,0:T(8,128)(2,1)S(1)}, bf16[128,256]{1,0:T(8,128)(2,1)S(1)}, u32[]{:S(2)}, u32[]{:S(2)}) %collective-permute-start.9) | collective-permute-done | bytes 65568 | tf_op jit(solution)/shard_map/ppermute | solution.py:661
  40.0 0.8 %shard_map.206 = (bf16[128,1024]{1,0:T(8,128)(2,1)}, bf16[32,512]{1,0:T(8,128)(2,1)}) custom-call(bf16[128,1024]{1,0:T(8,128)(2,1)S(1)} %get-tuple-element.37.video_ref, bf16[32,512]{1,0:T(8,128)(2,1)S(1)} %get-tuple-element.38.audio_ref, f32[32,512]{1,0:T(8,128)S(1)} %get-tuple-element.39.gain_ref, f32[576,256]{1,0:T(8,128)S(1)} %get-tuple-element.67.own_ref, ...), custom_call_target="tpu_custom_call" | custom-call | bytes 1835008 | tf_op jit(solution)/shard_map/pallas_call | solution.py:194
  (14 shorter events, 1.2 us)
Async XLA Ops:
  1.9 14.9 %collective-permute-start.1 = (bf16[576,128]{1,0:T(8,128)(2,1)S(1)}, bf16[576,128]{1,0:T(8,128)(2,1)S(1)}, u32[]{:S(2)}, u32[]{:S(2)}) collective-permute-start(bf16[576,128]{1,0:T(8,128)(2,1)S(1)} %get-tuple-element.43), channel_id=1, source_target_pairs={{0,4},{4,0},{8,12},{12,8},{1,5},{5,1},{9,13},{13,9},{2,6},{6,2},{1... | collective-permute-start | bytes 442376 | tf_op jit(solution)/shard_map/ppermute | solution.py:661
  5.0 13.0 %collective-permute-start.2 = (bf16[576,128]{1,0:T(8,128)(2,1)S(1)}, bf16[576,128]{1,0:T(8,128)(2,1)S(1)}, u32[]{:S(2)}, u32[]{:S(2)}) collective-permute-start(bf16[576,128]{1,0:T(8,128)(2,1)S(1)} %get-tuple-element.48), channel_id=1, source_target_pairs={{0,8},{4,12},{8,0},{12,4},{1,9},{5,13},{9,1},{13,5},{2,10},{6,14},... | collective-permute-start | bytes 442376 | tf_op jit(solution)/shard_map/ppermute | solution.py:661
  8.5 8.3 %collective-permute-start = (bf16[448,128]{1,0:T(8,128)(2,1)S(1)}, bf16[448,128]{1,0:T(8,128)(2,1)S(1)}, u32[]{:S(2)}, u32[]{:S(2)}) collective-permute-start(bf16[448,128]{1,0:T(8,128)(2,1)S(1)} %shard_map.196), channel_id=1, source_target_pairs={{0,12},{4,8},{8,4},{12,0},{1,13},{5,9},{9,5},{13,1},{2,14},{6,10},... | collective-permute-start | bytes 344072 | tf_op jit(solution)/shard_map/ppermute | solution.py:661
  18.8 9.2 %collective-permute-start.4 = (bf16[208,128]{1,0:T(8,128)(2,1)S(1)}, bf16[208,128]{1,0:T(8,128)(2,1)S(1)}, u32[]{:S(2)}, u32[]{:S(2)}) collective-permute-start(bf16[208,128]{1,0:T(8,128)(2,1)S(1)} %get-tuple-element.59), channel_id=1, source_target_pairs={{0,12},{4,8},{8,4},{12,0},{1,13},{5,9},{9,5},{13,1},{2,14},{6,10},... | collective-permute-start | bytes 159752 | tf_op jit(solution)/shard_map/ppermute | solution.py:661
  21.3 6.7 %collective-permute-start.5 = (bf16[208,128]{1,0:T(8,128)(2,1)S(1)}, bf16[208,128]{1,0:T(8,128)(2,1)S(1)}, u32[]{:S(2)}, u32[]{:S(2)}) collective-permute-start(bf16[208,128]{1,0:T(8,128)(2,1)S(1)} %get-tuple-element.60), channel_id=1, source_target_pairs={{0,8},{4,12},{8,0},{12,4},{1,9},{5,13},{9,1},{13,5},{2,10},{6,14},... | collective-permute-start | bytes 159752 | tf_op jit(solution)/shard_map/ppermute | solution.py:661
  22.9 5.1 %collective-permute-start.6 = (bf16[208,128]{1,0:T(8,128)(2,1)S(1)}, bf16[208,128]{1,0:T(8,128)(2,1)S(1)}, u32[]{:S(2)}, u32[]{:S(2)}) collective-permute-start(bf16[208,128]{1,0:T(8,128)(2,1)S(1)} %get-tuple-element.61), channel_id=1, source_target_pairs={{0,4},{4,0},{8,12},{12,8},{1,5},{5,1},{9,13},{13,9},{2,6},{6,2},{1... | collective-permute-start | bytes 159752 | tf_op jit(solution)/shard_map/ppermute | solution.py:661
  23.3 4.2 %collective-permute-start.3 = (bf16[128,128]{1,0:T(8,128)(2,1)S(1)}, bf16[128,128]{1,0:T(8,128)(2,1)S(1)}, u32[]{:S(2)}, u32[]{:S(2)}) collective-permute-start(bf16[128,128]{1,0:T(8,128)(2,1)S(1)} %get-tuple-element.55), channel_id=1, source_target_pairs={{0,4},{4,0},{8,12},{12,8},{1,5},{5,1},{9,13},{13,9},{2,6},{6,2},{1... | collective-permute-start | bytes 98312 | tf_op jit(solution)/shard_map/ppermute | solution.py:661
  28.9 1.6 %collective-permute-start.10 = (bf16[448,256]{1,0:T(8,128)(2,1)S(1)}, bf16[448,256]{1,0:T(8,128)(2,1)S(1)}, u32[]{:S(2)}, u32[]{:S(2)}) collective-permute-start(bf16[448,256]{1,0:T(8,128)(2,1)S(1)} %get-tuple-element.71), channel_id=1, source_target_pairs={{0,1},{1,0},{2,3},{3,2},{4,5},{5,4},{6,7},{7,6},{8,9},{9,8},{10,11... | collective-permute-start | bytes 688136 | tf_op jit(solution)/shard_map/ppermute | solution.py:661
  29.8 10.2 %collective-permute-start.7 = (bf16[576,256]{1,0:T(8,128)(2,1)S(1)}, bf16[576,256]{1,0:T(8,128)(2,1)S(1)}, u32[]{:S(2)}, u32[]{:S(2)}) collective-permute-start(bf16[576,256]{1,0:T(8,128)(2,1)S(1)} %get-tuple-element.68), channel_id=1, source_target_pairs={{0,1},{1,0},{2,3},{3,2},{4,5},{5,4},{6,7},{7,6},{8,9},{9,8},{10,11... | collective-permute-start | bytes 884744 | tf_op jit(solution)/shard_map/ppermute | solution.py:661
  30.8 9.1 %collective-permute-start.11 = (bf16[448,256]{1,0:T(8,128)(2,1)S(1)}, bf16[448,256]{1,0:T(8,128)(2,1)S(1)}, u32[]{:S(2)}, u32[]{:S(2)}) collective-permute-start(bf16[448,256]{1,0:T(8,128)(2,1)S(1)} %shard_map.205), channel_id=1, source_target_pairs={{0,2},{2,0},{1,3},{3,1},{4,6},{6,4},{5,7},{7,5},{8,10},{10,8},{9,1... | collective-permute-start | bytes 688136 | tf_op jit(solution)/shard_map/ppermute | solution.py:661
  32.4 1.3 %collective-permute-start.8 = (bf16[128,256]{1,0:T(8,128)(2,1)S(1)}, bf16[128,256]{1,0:T(8,128)(2,1)S(1)}, u32[]{:S(2)}, u32[]{:S(2)}) collective-permute-start(bf16[128,256]{1,0:T(8,128)(2,1)S(1)} %get-tuple-element.70), channel_id=1, source_target_pairs={{0,1},{1,0},{2,3},{3,2},{4,5},{5,4},{6,7},{7,6},{8,9},{9,8},{10,11... | collective-permute-start | bytes 196616 | tf_op jit(solution)/shard_map/ppermute | solution.py:661
  33.7 6.3 %collective-permute-start.9 = (bf16[128,256]{1,0:T(8,128)(2,1)S(1)}, bf16[128,256]{1,0:T(8,128)(2,1)S(1)}, u32[]{:S(2)}, u32[]{:S(2)}) collective-permute-start(bf16[128,256]{1,0:T(8,128)(2,1)S(1)} %shard_map.204), channel_id=1, source_target_pairs={{0,2},{2,0},{1,3},{3,1},{4,6},{6,4},{5,7},{7,5},{8,10},{10,8},{9,1... | collective-permute-start | bytes 196616 | tf_op jit(solution)/shard_map/ppermute | solution.py:661

commit v13 on v12

--- a/solution.py
+++ b/solution.py
@@ -417,7 +417,7 @@
 
 def late_kernel(early, hops, rows_audio, head, kv_ref, vvt_ref, part_ref, stats_ref, vt_ref, last_ref, *rest):
     count, n = len(early), len(hops)
-    blocks, tails, outs, (relay_ref, s_ref) = rest[:count], rest[count : 2 * count - 1], rest[2 * count - 1 : -2], rest[-2:]
+    blocks, tails, outs, s_ref = rest[:count], rest[count : 2 * count - 1], rest[2 * count - 1 : -1], rest[-1]
     by_hop = dict(zip(hops, outs))
     rows = kv_ref.shape[0]
     last = next(hop for hop in hops if hop not in early)
@@ -457,7 +457,9 @@
     store_tail(by_hop[last], rows, *audio)
     for hop, tail in zip(early[1:], tails):
         by_hop[hop][rows : rows + tail.shape[0], :] = tail[...]
-    relay_ref[...] = last_ref[last_ref.shape[0] - relay_ref.shape[0] :, :]
+    dst, src = by_hop[last], blocks[early.index(FORWARDED ^ last)]
+    extra = dst.shape[0] - rows - tails[0].shape[0]
+    dst[dst.shape[0] - extra :, :] = src[src.shape[0] - extra :, :]
 
 
 def audio_allowed(hop, rows_audio, limit):
@@ -708,17 +710,15 @@
         flops=4 * count * count * rows * rows * width,
         scratch=[pltpu.VMEM(((count * count + cross // DHC) * rows, rows), F32)],
     )
-    own, *sends, relay = call(
+    own, *sends = call(
         functools.partial(late_kernel, early, hops, rows_audio, DHC),
         [shape(rows, width)]
-        + [shape(rows + tail, width)] * (n - 1)
-        + [shape(2 * audio, width)],
+        + [shape(rows + tail + (2 * audio if hop == LAST else 0), width) for hop in hops[1:]],
         (k_own, vvt, part, stats, vt, blocks[LAST], *(blocks[hop] for hop in early), *tails),
         flops=4 * (2 * n - 1) * rows * rows * width,
         scratch=[pltpu.VMEM(((2 * n - 1) * rows, rows), F32)],
     )
     got = [trade(x, "seq", hop, n) for x, hop in zip(sends, hops[1:])]
-    forwarded = trade(relay, "seq", FORWARDED ^ LAST, n)
     near = [hop for hop in hops if hop != FORWARDED]
     a2v_part, a2v_stats = call(
         functools.partial(attend_audio_kernel, near, rows_audio, DHC),
@@ -731,7 +731,7 @@
     (a2v_att,) = call(
         functools.partial(join_kernel, DHC, rows_audio),
         [shape(rows, cross)],
-        (audio_len, q_own, a2v_part, a2v_stats, forwarded),
+        (audio_len, q_own, a2v_part, a2v_stats, got[hops.index(LAST) - 1]),
         [SMEM] + [VMEM] * 4,
         flops=4 * rows * rows_audio * cross,
     )

time: 41.1 us -> 41.6 us (1.012)
  waiting for transfers between devices: 12.6 us -> 14.2 us
  starting transfers between devices: 14.7 us -> 13.6 us
    ppermute x12 -> x11, waiting for transfers between devices: 12.6 us -> 14.2 us  [trade(): return lax.ppermute(x, axis, [(i, i ^ hop) for i in range(size)])]
    ppermute x12 -> x11, starting transfers between devices: 14.7 us -> 13.6 us  [trade(): return lax.ppermute(x, axis, [(i, i ^ hop) for i in range(size)])]
  transfers between devices with their start and end apart: 12 -> 11, of which waited for: 6 -> 7; matrix products, arithmetic and copies ran while one was open for 3% -> 3% of each run, Pallas kernels for 18% -> 18%
where the time goes in v13:
time: 41.6 us; the launch traced here: 41.3 us
  waiting for transfers between devices  14.2 us (34%)
  starting transfers between devices  13.6 us (33%)
  Pallas kernels  11 us (26%)
  between operations  1.38 us (3%)
  local copies, waits for them, and re-layouts  1.1 us (3%)
    ppermute x11, waiting for transfers between devices, trade(): return lax.ppermute(x, axis, [(i, i ^ hop) for i in range(size)])  14.2 us
    ppermute x11, starting transfers between devices, trade(): return lax.ppermute(x, axis, [(i, i ^ hop) for i in range(size)])  13.6 us
    pallas_call x13, Pallas kernels, call(): pl.pallas_call(kernel, out_shape=tuple(outs), in_specs=specs or [VMEM] *...  11 us
    unnamed x1, local copies, waits for them, and re-layouts  1.1 us
  transfers between devices with their start and end apart: 11, of which 7 were waited for; matrix products, arithmetic and copies ran while one was open for 3% of the time, Pallas kernels for 18%

profile of v13, /device:TPU:0, one launch (start us, length us, event | category | flops | bytes accessed | tf_op | source)
XLA Modules:
  0.0 41.3 jit_solution(6663745618680404881)
XLA Ops:
  0.6 1.3 %shard_map.195 = (bf16[576,128]{1,0:T(8,128)(2,1)S(1)}, bf16[576,128]{1,0:T(8,128)(2,1)S(1)}, bf16[576,128]{1,0:T(8,128)(2,1)S(1)}) custom-call(bf16[128,512]{1,0:T(8,128)(2,1)} %q_ref.3, bf16[128,512]{1,0:T(8,128)(2,1)} %k_ref.3, bf16[128,512]{1,0:T(8,128)(2,1)} %v_ref.3, bf16[32,256]{1,0:T(8,128)(2,1)} %qa_ref.3, bf16[32,256]{1,0:T(8,128)(2,1)} %ka_ref.3, ...), custom_call_target="tpu_custom_call" | custom-call | bytes 884736 | tf_op jit(solution)/shard_map/pallas_call | solution.py:194
  1.9 3.1 %collective-permute-start.1 = (bf16[576,128]{1,0:T(8,128)(2,1)S(1)}, bf16[576,128]{1,0:T(8,128)(2,1)S(1)}, u32[]{:S(2)}, u32[]{:S(2)}) collective-permute-start(bf16[576,128]{1,0:T(8,128)(2,1)S(1)} %get-tuple-element.42), channel_id=1, source_target_pairs={{0,4},{4,0},{8,12},{12,8},{1,5},{5,1},{9,13},{13,9},{2,6},{6,2},{1... | collective-permute-start | bytes 442376 | tf_op jit(solution)/shard_map/ppermute | solution.py:663
  5.0 2.6 %collective-permute-start.2 = (bf16[576,128]{1,0:T(8,128)(2,1)S(1)}, bf16[576,128]{1,0:T(8,128)(2,1)S(1)}, u32[]{:S(2)}, u32[]{:S(2)}) collective-permute-start(bf16[576,128]{1,0:T(8,128)(2,1)S(1)} %get-tuple-element.47), channel_id=1, source_target_pairs={{0,8},{4,12},{8,0},{12,4},{1,9},{5,13},{9,1},{13,5},{2,10},{6,14},... | collective-permute-start | bytes 442376 | tf_op jit(solution)/shard_map/ppermute | solution.py:663
  7.6 0.8 %shard_map.196 = bf16[448,128]{1,0:T(8,128)(2,1)S(1)} custom-call(bf16[128,512]{1,0:T(8,128)(2,1)} %q_ref.3, bf16[128,512]{1,0:T(8,128)(2,1)} %k_ref.3, bf16[128,512]{1,0:T(8,128)(2,1)} %v_ref.3, bf16[32,256]{1,0:T(8,128)(2,1)} %qa_ref.3, bf16[32,256]{1,0:T(8,128)(2,1)} %ka_ref.3, bf16[32,256]{1,0:T(8,128)(2,1)} %va_ref.3), custom_call_target="tpu_custom_call" | custom-call | bytes 557056 | tf_op jit(solution)/shard_map/pallas_call | solution.py:194
  9.2 1.1 %copy.21 = bf16[2,8,2,4096]{3,1,2,0:T(8,128)(2,1)S(1)} copy(bf16[2,8,2,4096]{3,2,1,0:T(2,128)(2,1)} %bitcast.5) | data formatting | bytes 524288
  10.3 3.4 %shard_map.194 = (bf16[128,8192]{1,0:T(8,128)(2,1)S(1)}, f32[32,512]{1,0:T(8,128)S(1)}, bf16[128,256]{1,0:T(8,128)(2,1)S(1)}, bf16[128,256]{1,0:T(8,128)(2,1)S(1...) custom-call(s32[1]{0:T(128)S(6)} %copy.22.limit_ref, ...), custom_call_target="tpu_custom_call" | custom-call | bytes 18154116 | tf_op jit(solution)/shard_map/pallas_call | solution.py:194
  13.7 3.1 %collective-permute-done.rest_1_ = bf16[448,128]{1,0:T(8,128)(2,1)S(1)} collective-permute-done((bf16[448,128]{1,0:T(8,128)(2,1)S(1)}, bf16[448,128]{1,0:T(8,128)(2,1)S(1)}, u32[]{:S(2)}, u32[]{:S(2)}) %collective-permute-start) | collective-permute-done | bytes 114720 | tf_op jit(solution)/shard_map/ppermute | solution.py:663
  16.8 0.7 %shard_map.197 = (f32[384,128]{1,0:T(8,128)S(1)}, f32[6,128]{1,0:T(8,128)S(1)}, bf16[128,384]{1,0:T(8,128)(2,1)S(1)}, bf16[256,128]{1,0:T(8,128)(2,1)S(1)}, f32[...) custom-call(bf16[128,256]{1,0:T(8,128)(2,1)S(1)} %get-tuple-element.39.kv_r, ...), custom_call_target="tpu_custom_call" | custom-call | flops 75497472 | bytes 979968 | tf_op jit(solution)/shard_map/pallas_call | solution.py:194
  17.5 0.5 %collective-permute-done.2.last_ref.rest_1_ = bf16[576,128]{1,0:T(8,128)(2,1)S(1)} collective-permute-done((bf16[576,128]{1,0:T(8,128)(2,1)S(1)}, bf16[576,128]{1,0:T(8,128)(2,1)S(1)}, u32[]{:S(2)}, u32[]{:S(2)}) %collective-permute-start.2) | collective-permute-done | bytes 147488 | tf_op jit(solution)/shard_map/ppermute | solution.py:663
  18.1 0.7 %shard_map.198 = (bf16[128,128]{1,0:T(8,128)(2,1)S(1)}, bf16[208,128]{1,0:T(8,128)(2,1)S(1)}, bf16[336,128]{1,0:T(8,128)(2,1)S(1)}, bf16[208,128]{1,0:T(8,128)(2,1)S(1)}) custom-call(bf16[128,256]{1,0:T(8,128)(2,1)S(1)} %get-tuple-element.39.kv_ref, bf16[256,128]{1,0:T(8,128)(2,1)S(1)} %get-tuple-element.43.vvt_ref, ...), custom_call_target="tpu_custom_call" | custom-call | flops 58720256 | bytes 1252352 | tf_op jit(solution)/shard_map/pallas_call | solution.py:194
  18.8 3.7 %collective-permute-start.3 = (bf16[336,128]{1,0:T(8,128)(2,1)S(1)}, bf16[336,128]{1,0:T(8,128)(2,1)S(1)}, u32[]{:S(2)}, u32[]{:S(2)}) collective-permute-start(bf16[336,128]{1,0:T(8,128)(2,1)S(1)} %get-tuple-element.54), channel_id=1, source_target_pairs={{0,8},{4,12},{8,0},{12,4},{1,9},{5,13},{9,1},{13,5},{2,10},{6,14},... | collective-permute-start | bytes 258056 | tf_op jit(solution)/shard_map/ppermute | solution.py:663
  22.5 1.4 %collective-permute-start.4 = (bf16[208,128]{1,0:T(8,128)(2,1)S(1)}, bf16[208,128]{1,0:T(8,128)(2,1)S(1)}, u32[]{:S(2)}, u32[]{:S(2)}) collective-permute-start(bf16[208,128]{1,0:T(8,128)(2,1)S(1)} %get-tuple-element.58), channel_id=1, source_target_pairs={{0,12},{4,8},{8,4},{12,0},{1,13},{5,9},{9,5},{13,1},{2,14},{6,10},... | collective-permute-start | bytes 159752 | tf_op jit(solution)/shard_map/ppermute | solution.py:663
  23.8 0.6 %shard_map.199 = (f32[256,128]{1,0:T(8,128)S(1)}, f32[4,256]{1,0:T(4,128)S(1)}) custom-call(s32[1]{0:T(128)S(6)} %copy.22.limit_ref, bf16[128,256]{1,0:T(8,128)(2,1)S(1)} %get-tuple-element.51.q_ref, bf16[576,128]{1,0:T(8,128)(2,1)S(1)} %get-tuple-element.41.rest_0_, bf16[576,128]{1,0:T(8,128)(2,1)S(1)} %collective-permute-done.2.last_ref.rest_1_, ...), custom_call_target="tpu_custom_call" | custom-call | flops 33554432 | bytes 643076 | tf_op jit(solution)/shard_map/pallas_call | solution.py:194
  24.4 2.7 %collective-permute-done.3.last_ref.rest_1_ = bf16[336,128]{1,0:T(8,128)(2,1)S(1)} collective-permute-done((bf16[336,128]{1,0:T(8,128)(2,1)S(1)}, bf16[336,128]{1,0:T(8,128)(2,1)S(1)}, u32[]{:S(2)}, u32[]{:S(2)}) %collective-permute-start.3) | collective-permute-done | bytes 86048 | tf_op jit(solution)/shard_map/ppermute | solution.py:663
  27.1 0.6 %shard_map.200.a2v_ref.refs_1_ = bf16[128,256]{1,0:T(8,128)(2,1)S(1)} custom-call(s32[1]{0:T(128)S(6)} %copy.22.limit_ref, bf16[128,256]{1,0:T(8,128)(2,1)S(1)} %get-tuple-element.51.q_ref, f32[256,128]{1,0:T(8,128)S(1)} %get-tuple-element.52.part_ref, f32[4,256]{1,0:T(4,128)S(1)} %get-tuple-element.53.stats_ref, ...), custom_call_target="tpu_custom_call" | custom-call | flops 4194304 | bytes 352260 | tf_op jit(solution)/shard_map/pallas_call | solution.py:194
  27.7 0.8 %collective-permute-done.4.rest_0_ = bf16[208,128]{1,0:T(8,128)(2,1)S(1)} collective-permute-done((bf16[208,128]{1,0:T(8,128)(2,1)S(1)}, bf16[208,128]{1,0:T(8,128)(2,1)S(1)}, u32[]{:S(2)}, u32[]{:S(2)}) %collective-permute-start.4) | collective-permute-done | bytes 53280 | tf_op jit(solution)/shard_map/ppermute | solution.py:663
  28.8 0.6 %shard_map.202 = (bf16[448,256]{1,0:T(8,128)(2,1)S(1)}, bf16[32,256]{1,0:T(8,128)(2,1)S(1)}, f32[128,256]{1,0:T(8,128)S(1)}) custom-call(bf16[128,512]{1,0:T(8,128)(2,1)S(1)} %get-tuple-element.60.self_ref.refs_0_, bf16[128,256]{1,0:T(8,128)(2,1)S(1)} %shard_map.200.a2v_ref.refs_1_, bf16[512,4096]{1,0:T(8,128)(2,1)S(1)} %get-tuple-element.55.ws_ref.refs_3_, ...), custom_call_target="tpu_custom_call" | custom-call | flops 201326592 | bytes 10237952 | tf_op jit(solution)/shard_map/pallas_call | solution.py:194
  29.4 0.8 %shard_map.203 = (bf16[576,256]{1,0:T(8,128)(2,1)S(1)}, f32[576,256]{1,0:T(8,128)S(1)}) custom-call(bf16[128,512]{1,0:T(8,128)(2,1)S(1)} %get-tuple-element.60.self_ref.refs_0_, bf16[128,256]{1,0:T(8,128)(2,1)S(1)} %shard_map.200.a2v_ref.refs_1_, bf16[32,256]{1,0:T(8,128)(2,1)S(1)} %get-tuple-element.64.refs_2_, ...), custom_call_target="tpu_custom_call" | custom-call | flops 402653184 | bytes 10534912 | tf_op jit(solution)/shard_map/pallas_call | solution.py:194
  30.3 0.6 %collective-permute-start.6 = (bf16[576,256]{1,0:T(8,128)(2,1)S(1)}, bf16[576,256]{1,0:T(8,128)(2,1)S(1)}, u32[]{:S(2)}, u32[]{:S(2)}) collective-permute-start(bf16[576,256]{1,0:T(8,128)(2,1)S(1)} %get-tuple-element.66), channel_id=1, source_target_pairs={{0,1},{1,0},{2,3},{3,2},{4,5},{5,4},{6,7},{7,6},{8,9},{9,8},{10,11... | collective-permute-start | bytes 884744 | tf_op jit(solution)/shard_map/ppermute | solution.py:663
  31.3 1.6 %collective-permute-start.10 = (bf16[448,256]{1,0:T(8,128)(2,1)S(1)}, bf16[448,256]{1,0:T(8,128)(2,1)S(1)}, u32[]{:S(2)}, u32[]{:S(2)}) collective-permute-start(bf16[448,256]{1,0:T(8,128)(2,1)S(1)} %shard_map.205), channel_id=1, source_target_pairs={{0,2},{2,0},{1,3},{3,1},{4,6},{6,4},{5,7},{7,5},{8,10},{10,8},{9,1... | collective-permute-start | bytes 688136 | tf_op jit(solution)/shard_map/ppermute | solution.py:663
  32.8 1.3 %collective-permute-done.7.extra_ref = bf16[128,256]{1,0:T(8,128)(2,1)S(1)} collective-permute-done((bf16[128,256]{1,0:T(8,128)(2,1)S(1)}, bf16[128,256]{1,0:T(8,128)(2,1)S(1)}, u32[]{:S(2)}, u32[]{:S(2)}) %collective-permute-start.7) | collective-permute-done | bytes 65568 | tf_op jit(solution)/shard_map/ppermute | solution.py:663
  34.1 0.6 %collective-permute-start.8 = (bf16[128,256]{1,0:T(8,128)(2,1)S(1)}, bf16[128,256]{1,0:T(8,128)(2,1)S(1)}, u32[]{:S(2)}, u32[]{:S(2)}) collective-permute-start(bf16[128,256]{1,0:T(8,128)(2,1)S(1)} %shard_map.204), channel_id=1, source_target_pairs={{0,2},{2,0},{1,3},{3,1},{4,6},{6,4},{5,7},{7,5},{8,10},{10,8},{9,1... | collective-permute-start | bytes 196616 | tf_op jit(solution)/shard_map/ppermute | solution.py:663
  34.7 5.7 %collective-permute-done.8.low_ref = bf16[128,256]{1,0:T(8,128)(2,1)S(1)} collective-permute-done((bf16[128,256]{1,0:T(8,128)(2,1)S(1)}, bf16[128,256]{1,0:T(8,128)(2,1)S(1)}, u32[]{:S(2)}, u32[]{:S(2)}) %collective-permute-start.8) | collective-permute-done | bytes 65568 | tf_op jit(solution)/shard_map/ppermute | solution.py:663
  40.4 0.8 %shard_map.206 = (bf16[128,1024]{1,0:T(8,128)(2,1)}, bf16[32,512]{1,0:T(8,128)(2,1)}) custom-call(bf16[128,1024]{1,0:T(8,128)(2,1)S(1)} %get-tuple-element.36.video_ref, bf16[32,512]{1,0:T(8,128)(2,1)S(1)} %get-tuple-element.37.audio_ref, f32[32,512]{1,0:T(8,128)S(1)} %get-tuple-element.38.gain_ref, f32[576,256]{1,0:T(8,128)S(1)} %get-tuple-element.65.own_ref, ...), custom_call_target="tpu_custom_call" | custom-call | bytes 1835008 | tf_op jit(solution)/shard_map/pallas_call | solution.py:194
  (12 shorter events, 0.9 us)
Async XLA Ops:
  1.9 14.9 %collective-permute-start.1 = (bf16[576,128]{1,0:T(8,128)(2,1)S(1)}, bf16[576,128]{1,0:T(8,128)(2,1)S(1)}, u32[]{:S(2)}, u32[]{:S(2)}) collective-permute-start(bf16[576,128]{1,0:T(8,128)(2,1)S(1)} %get-tuple-element.42), channel_id=1, source_target_pairs={{0,4},{4,0},{8,12},{12,8},{1,5},{5,1},{9,13},{13,9},{2,6},{6,2},{1... | collective-permute-start | bytes 442376 | tf_op jit(solution)/shard_map/ppermute | solution.py:663
  5.0 13.0 %collective-permute-start.2 = (bf16[576,128]{1,0:T(8,128)(2,1)S(1)}, bf16[576,128]{1,0:T(8,128)(2,1)S(1)}, u32[]{:S(2)}, u32[]{:S(2)}) collective-permute-start(bf16[576,128]{1,0:T(8,128)(2,1)S(1)} %get-tuple-element.47), channel_id=1, source_target_pairs={{0,8},{4,12},{8,0},{12,4},{1,9},{5,13},{9,1},{13,5},{2,10},{6,14},... | collective-permute-start | bytes 442376 | tf_op jit(solution)/shard_map/ppermute | solution.py:663
  8.5 8.3 %collective-permute-start = (bf16[448,128]{1,0:T(8,128)(2,1)S(1)}, bf16[448,128]{1,0:T(8,128)(2,1)S(1)}, u32[]{:S(2)}, u32[]{:S(2)}) collective-permute-start(bf16[448,128]{1,0:T(8,128)(2,1)S(1)} %shard_map.196), channel_id=1, source_target_pairs={{0,12},{4,8},{8,4},{12,0},{1,13},{5,9},{9,5},{13,1},{2,14},{6,10},... | collective-permute-start | bytes 344072 | tf_op jit(solution)/shard_map/ppermute | solution.py:663
  18.8 8.3 %collective-permute-start.3 = (bf16[336,128]{1,0:T(8,128)(2,1)S(1)}, bf16[336,128]{1,0:T(8,128)(2,1)S(1)}, u32[]{:S(2)}, u32[]{:S(2)}) collective-permute-start(bf16[336,128]{1,0:T(8,128)(2,1)S(1)} %get-tuple-element.54), channel_id=1, source_target_pairs={{0,8},{4,12},{8,0},{12,4},{1,9},{5,13},{9,1},{13,5},{2,10},{6,14},... | collective-permute-start | bytes 258056 | tf_op jit(solution)/shard_map/ppermute | solution.py:663
  22.5 6.0 %collective-permute-start.4 = (bf16[208,128]{1,0:T(8,128)(2,1)S(1)}, bf16[208,128]{1,0:T(8,128)(2,1)S(1)}, u32[]{:S(2)}, u32[]{:S(2)}) collective-permute-start(bf16[208,128]{1,0:T(8,128)(2,1)S(1)} %get-tuple-element.58), channel_id=1, source_target_pairs={{0,12},{4,8},{8,4},{12,0},{1,13},{5,9},{9,5},{13,1},{2,14},{6,10},... | collective-permute-start | bytes 159752 | tf_op jit(solution)/shard_map/ppermute | solution.py:663
  23.8 4.7 %collective-permute-start.5 = (bf16[208,128]{1,0:T(8,128)(2,1)S(1)}, bf16[208,128]{1,0:T(8,128)(2,1)S(1)}, u32[]{:S(2)}, u32[]{:S(2)}) collective-permute-start(bf16[208,128]{1,0:T(8,128)(2,1)S(1)} %get-tuple-element.59), channel_id=1, source_target_pairs={{0,4},{4,0},{8,12},{12,8},{1,5},{5,1},{9,13},{13,9},{2,6},{6,2},{1... | collective-permute-start | bytes 159752 | tf_op jit(solution)/shard_map/ppermute | solution.py:663
  29.4 1.6 %collective-permute-start.9 = (bf16[448,256]{1,0:T(8,128)(2,1)S(1)}, bf16[448,256]{1,0:T(8,128)(2,1)S(1)}, u32[]{:S(2)}, u32[]{:S(2)}) collective-permute-start(bf16[448,256]{1,0:T(8,128)(2,1)S(1)} %get-tuple-element.69), channel_id=1, source_target_pairs={{0,1},{1,0},{2,3},{3,2},{4,5},{5,4},{6,7},{7,6},{8,9},{9,8},{10,11... | collective-permute-start | bytes 688136 | tf_op jit(solution)/shard_map/ppermute | solution.py:663
  30.3 10.2 %collective-permute-start.6 = (bf16[576,256]{1,0:T(8,128)(2,1)S(1)}, bf16[576,256]{1,0:T(8,128)(2,1)S(1)}, u32[]{:S(2)}, u32[]{:S(2)}) collective-permute-start(bf16[576,256]{1,0:T(8,128)(2,1)S(1)} %get-tuple-element.66), channel_id=1, source_target_pairs={{0,1},{1,0},{2,3},{3,2},{4,5},{5,4},{6,7},{7,6},{8,9},{9,8},{10,11... | collective-permute-start | bytes 884744 | tf_op jit(solution)/shard_map/ppermute | solution.py:663
  31.3 9.1 %collective-permute-start.10 = (bf16[448,256]{1,0:T(8,128)(2,1)S(1)}, bf16[448,256]{1,0:T(8,128)(2,1)S(1)}, u32[]{:S(2)}, u32[]{:S(2)}) collective-permute-start(bf16[448,256]{1,0:T(8,128)(2,1)S(1)} %shard_map.205), channel_id=1, source_target_pairs={{0,2},{2,0},{1,3},{3,1},{4,6},{6,4},{5,7},{7,5},{8,10},{10,8},{9,1... | collective-permute-start | bytes 688136 | tf_op jit(solution)/shard_map/ppermute | solution.py:663
  32.8 1.3 %collective-permute-start.7 = (bf16[128,256]{1,0:T(8,128)(2,1)S(1)}, bf16[128,256]{1,0:T(8,128)(2,1)S(1)}, u32[]{:S(2)}, u32[]{:S(2)}) collective-permute-start(bf16[128,256]{1,0:T(8,128)(2,1)S(1)} %get-tuple-element.68), channel_id=1, source_target_pairs={{0,1},{1,0},{2,3},{3,2},{4,5},{5,4},{6,7},{7,6},{8,9},{9,8},{10,11... | collective-permute-start | bytes 196616 | tf_op jit(solution)/shard_map/ppermute | solution.py:663
  34.1 6.3 %collective-permute-start.8 = (bf16[128,256]{1,0:T(8,128)(2,1)S(1)}, bf16[128,256]{1,0:T(8,128)(2,1)S(1)}, u32[]{:S(2)}, u32[]{:S(2)}) collective-permute-start(bf16[128,256]{1,0:T(8,128)(2,1)S(1)} %shard_map.204), channel_id=1, source_target_pairs={{0,2},{2,0},{1,3},{3,1},{4,6},{6,4},{5,7},{7,5},{8,10},{10,8},{9,1... | collective-permute-start | bytes 196616 | tf_op jit(solution)/shard_map/ppermute | solution.py:663
